TPU v7x, 32 devices: a whole 2x2x4 slice. The times are simulated.
32 devices in a mesh: groups: 2 (over y), blk: 4 (over z), leaf: 2 (over x), sample: 2 (over core).
Axes of the slice: x: 2, y: 2, z: 4, core: 2. Of those that a mesh axis runs over, the one named last changes fastest.
Arguments:
- residual: float32 [256, 128, 256], P(('groups', 'blk', 'leaf'), 'sample'), parts along dimension 0, may hold values from -60 to 60
- direction: bfloat16 [256, 128, 256], P(('groups', 'blk', 'leaf'), 'sample'), parts along dimension 0, may hold values from -60 to 60
- step: float32 [256], P(('groups', 'sample')), parts along dimension 0, may hold values from 0.2 to 0.8
- coords: bfloat16 [256, 3, 256], P(('groups', 'blk', 'leaf')), parts along dimension 0, may hold values from 0 to 1
- order: int32 [256, 256], P(('groups', 'blk', 'leaf')), parts along dimension 0, may hold values from 0 to 255, each once within a row
- basis: bfloat16 [256, 64, 256], P(('groups', 'blk', 'leaf')), parts along dimension 0, may hold values from -0.5 to 0.5
- leaf_transfer: bfloat16 [256, 64, 64], P(('groups', 'blk', 'leaf')), parts along dimension 0, may hold values from -0.75 to 0.75
- node_transfer: bfloat16 [16, 64, 64], P(('groups', 'blk', 'leaf')), parts along dimension 0, may hold values from -0.75 to 0.75
- near_list: int32 [256, 12], P(('groups', 'blk', 'leaf')), parts along dimension 0, may hold values from 0 to 127, as said below
- coupling_list: int32 [256, 8], P(('groups', 'blk', 'leaf')), parts along dimension 0, may hold values from 0 to 127, as said below
- coupling: bfloat16 [256, 8, 64, 64], P(('groups', 'blk', 'leaf')), parts along dimension 0, may hold values from -0.25 to 0.25
- top_list: int32 [8, 4], P(('groups', 'blk')), parts along dimension 0, may hold values from 0 to 3, as said below
- top_coupling: bfloat16 [8, 4, 64, 64], P(('groups', 'blk')), parts along dimension 0, may hold values from -0.0625 to 0.0625
Outputs:
- residual_next: float32 [256, 128, 256], P(('groups', 'blk', 'leaf'), 'sample'), parts along dimension 0
- direction_next: bfloat16 [256, 128, 256], P(('groups', 'blk', 'leaf'), 'sample'), parts along dimension 0
There are 2 independent parts, one for each index of `groups`. A program takes and returns all parts, laid end to end along the dimension named above; each array names one. Nothing has to cross between parts.
Inputs may be any that keep to these rules, and one draw needn't show every extreme that they name: `near_list`: entry 0 of leaf g is g itself; the other entries are distinct leaves other than g, each at most 16 positions from g around the cycle of 128 leaves; some leaf names both g - 16 and g + 16 (mod 128). `coupling_list`: the entries of leaf g are distinct leaves of the aligned blocks of 16 leaves just before and just after g's own block, around the cycle of 128 leaves, each more than 16 positions from g. `top_list`: the entries of top cluster b name clusters other than b; they may repeat.
All inputs are finite; a program needn't handle non-finite values.
Results may differ from a plain program's by a relative error of at most 0.0065.
Values may be sent and summed in bfloat16 or wider, within the bound.
No kernel may reach another device: no remote copies, remote signals or barrier semaphores. Data moves between devices by JAX's collectives and lax.ppermute only.
A program may use at most 64 MiB of HBM per device.

v0:
```python
import math

import jax
import jax.numpy as jnp
from jax import lax
from jax.sharding import PartitionSpec as P

LEAF_DEV = 16


ROOT_THREE = math.sqrt(3.0)
LENGTH = 0.3
AMPLITUDE = 0.25
NUGGET = 0.5


def padded(array, sides, width):
    for axis, dim in sides:
        count, length = (lax.axis_size(axis), array.shape[dim])
        up = [(i, (i + 1) % count) for i in range(count)]
        down = [(j, i) for i, j in up]
        last = lax.slice_in_dim(array, length - width, length, axis=dim)
        initial = lax.slice_in_dim(array, 0, width, axis=dim)
        before = lax.ppermute(last, axis, up)
        after = lax.ppermute(initial, axis, down)
        array = jnp.concatenate([before, array, after], axis=dim)
    return array


def swapped(array, axis, bit):
    return lax.ppermute(array, axis, [(i, i ^ 1 << bit) for i in range(lax.axis_size(axis))])


def matern(own_offsets, near_offsets, gap_leaves, spread):
    gap_x = (
        own_offsets[0][:, None] - near_offsets[0][None, :] + gap_leaves.astype(jnp.float32) * spread
    )
    gap_y = own_offsets[1][:, None] - near_offsets[1][None, :]
    gap_z = own_offsets[2][:, None] - near_offsets[2][None, :]
    scaled = jnp.sqrt(gap_x * gap_x + gap_y * gap_y + gap_z * gap_z) * (ROOT_THREE / LENGTH)
    return AMPLITUDE * (1.0 + scaled) * jnp.exp(-scaled)


def tile_block(own_offsets, near_offsets, gap_leaves, spread):
    inner = jax.vmap(matern, in_axes=(None, 0, 0, None))
    return jax.vmap(inner, in_axes=(0, 0, 0, None))(own_offsets, near_offsets, gap_leaves, spread)


def on_device(
    residual,
    direction,
    step,
    coords,
    order,
    basis,
    leaf_transfer,
    node_transfer,
    near_list,
    coupling_list,
    coupling,
    top_list,
    top_coupling,
):
    leaf_dev = direction.shape[0]
    samples = direction.shape[1]
    points = direction.shape[2]
    blk_count = lax.axis_size("blk")
    leaf_count = lax.axis_size("leaf")
    leaf_total = leaf_dev * blk_count * leaf_count
    device = lax.axis_index("blk") * leaf_count + lax.axis_index("leaf")
    first_leaf = device * leaf_dev
    spread = 0.5 / LEAF_DEV
    old_norm = lax.psum(jnp.sum(residual * residual, axis=(0, 2)), ("blk", "leaf"))
    packed = jnp.concatenate([direction, coords], axis=1)
    widened = padded(packed, ((("blk", "leaf"), 0),), leaf_dev)
    anchor = first_leaf - leaf_dev
    own_offsets_all = coords.astype(jnp.float32)
    slot_ids = jnp.mod(near_list - anchor, leaf_total)
    window_values = widened[:, :samples, :]
    window_offsets = widened[:, samples:, :]
    half_rows = leaf_dev // 2
    side = lax.axis_index("sample")
    partner_values = swapped(window_values, "sample", 0)
    all_columns = jnp.where(
        side == 0,
        jnp.concatenate([window_values, partner_values], axis=1),
        jnp.concatenate([partner_values, window_values], axis=1),
    )
    base = side * half_rows
    blocks = 4
    columns = all_columns.shape[1]

    def near_block(block_index):
        start_at = base + block_index * blocks
        slot_rows = lax.dynamic_slice_in_dim(slot_ids, start_at, blocks, 0)
        name_rows = lax.dynamic_slice_in_dim(near_list, start_at, blocks, 0)
        leaf_ids = first_leaf + start_at + jnp.arange(blocks, dtype=jnp.int32)
        near_values = all_columns[slot_rows]
        near_offsets = window_offsets[slot_rows].astype(jnp.float32)
        own_offsets = lax.dynamic_slice_in_dim(own_offsets_all, start_at, blocks, 0)
        gap_leaves = (
            jnp.mod(leaf_ids[:, None] - name_rows + leaf_total // 2, leaf_total) - leaf_total // 2
        )
        kernel_tiles = tile_block(own_offsets, near_offsets, gap_leaves, spread).astype(
            jnp.bfloat16
        )
        return jnp.einsum(
            "lkab,lksb->lsa", kernel_tiles, near_values, preferred_element_type=jnp.float32
        )

    mapped = lax.map(near_block, jnp.arange(half_rows // blocks, dtype=jnp.int32))
    own_rows = mapped.reshape(half_rows, columns, points)
    kept_part = lax.dynamic_slice_in_dim(own_rows, side * samples, samples, 1)
    given_part = lax.dynamic_slice_in_dim(own_rows, (1 - side) * samples, samples, 1)
    received = swapped(given_part.astype(jnp.bfloat16), "sample", 0).astype(given_part.dtype)
    near_field = jnp.where(
        side == 0,
        jnp.concatenate([kept_part, received], axis=0),
        jnp.concatenate([received, kept_part], axis=0),
    )
    inverse = jnp.argsort(order, axis=1)
    natural_values = jnp.take_along_axis(basis, inverse[:, None, :], axis=2)
    expansion_weights = jnp.einsum(
        "ejt,ekt->ekj", natural_values, direction, preferred_element_type=jnp.float32
    ).astype(jnp.bfloat16)
    node_coef = jnp.einsum(
        "lrk,lsk->sr", leaf_transfer, expansion_weights, preferred_element_type=jnp.float32
    ).astype(jnp.bfloat16)
    lifted = jnp.einsum(
        "rk,sk->sr", node_transfer[0], node_coef, preferred_element_type=jnp.float32
    )
    top_node = lax.psum(lifted, "leaf").astype(jnp.bfloat16)
    every_top = lax.all_gather(top_node[None], "blk", axis=0, tiled=True)
    chosen = every_top[top_list[0]]
    incoming = jnp.einsum(
        "krj,ksj->sr", top_coupling[0], chosen, preferred_element_type=jnp.float32
    )
    incoming = incoming.astype(jnp.bfloat16)
    down_coef = jnp.einsum(
        "rk,sr->sk", node_transfer[0], incoming, preferred_element_type=jnp.float32
    ).astype(jnp.bfloat16)
    coef_wide = padded(expansion_weights, ((("blk", "leaf"), 0),), leaf_dev)
    paired_block = coef_wide[jnp.mod(coupling_list - (first_leaf - leaf_dev), leaf_total)]
    upward_gathered = jnp.einsum(
        "lrk,sr->lsk", leaf_transfer, down_coef, preferred_element_type=jnp.float32
    )
    upward_gathered = upward_gathered + jnp.einsum(
        "ohvd,ohgd->ogv", coupling, paired_block, preferred_element_type=jnp.float32
    )
    upward_gathered = upward_gathered.astype(jnp.bfloat16)
    distant_field = jnp.einsum(
        "bfw,baf->baw", natural_values, upward_gathered, preferred_element_type=jnp.float32
    )
    product_image = NUGGET * direction.astype(jnp.float32) + near_field + distant_field
    residual_next = residual - step[None, :, None] * product_image
    new_square = jnp.sum(residual_next * residual_next, axis=(0, 2))
    new_norm = lax.psum(new_square, ("blk", "leaf"))
    beta_ratio = new_norm / old_norm
    direction_next = (
        residual_next + beta_ratio[None, :, None] * direction.astype(jnp.float32)
    ).astype(jnp.bfloat16)
    return (residual_next, direction_next)


def solution(mesh):
    in_specs = (
        P(("groups", "blk", "leaf"), "sample", None),
        P(("groups", "blk", "leaf"), "sample", None),
        P(("groups", "sample")),
        P(("groups", "blk", "leaf"), None, None),
        P(("groups", "blk", "leaf"), None),
        P(("groups", "blk", "leaf"), None, None),
        P(("groups", "blk", "leaf"), None, None),
        P(("groups", "blk", "leaf"), None, None),
        P(("groups", "blk", "leaf"), None),
        P(("groups", "blk", "leaf"), None),
        P(("groups", "blk", "leaf"), None, None, None),
        P(("groups", "blk"), None),
        P(("groups", "blk"), None, None, None),
    )
    out_specs = (
        P(("groups", "blk", "leaf"), "sample", None),
        P(("groups", "blk", "leaf"), "sample", None),
    )
    return jax.shard_map(
        on_device, mesh=mesh, in_specs=in_specs, out_specs=out_specs, check_vma=False
    )
```

profile of v0, /device:TPU:0, one launch (start us, length us, event | category | flops | bytes accessed | tf_op | source)
XLA Modules:
  0.0 217.2 jit_solution(16189384715876912534)
XLA Ops:
  7.2 1.5 copy_dynamic-update-slice_fusion
  8.7 1.4 fusion.37
  10.1 2.9 %collective-permute-start = (bf16[16,67,256]{2,0,1:T(8,128)(2,1)S(1)}, bf16[16,67,256]{2,0,1:T(8,128)(2,1)S(1)}, u32[]{:S(2)}, u32[]{:S(2)}) collective-permute-start(bf16[16,67,256]{2,0,1:T(8,128)(2,1)S(1)} %get-tuple-element.173), channel_id=1, source_target_pairs={{0,2},{2,4},{4,6},{6,8},{8,10},{10,12},{12,14},{14,0},{1,3},{3,5},... | collective-permute-start | bytes 1646600 | tf_op jit(solution)/shard_map/ppermute | solution.py:24
  13.1 3.0 %collective-permute-start.1 = (bf16[16,67,256]{2,0,1:T(8,128)(2,1)S(1)}, bf16[16,67,256]{2,0,1:T(8,128)(2,1)}, u32[]{:S(2)}, u32[]{:S(2)}) collective-permute-start(bf16[16,67,256]{2,0,1:T(8,128)(2,1)S(1)} %get-tuple-element.173), channel_id=1, source_target_pairs={{2,0},{4,2},{6,4},{8,6},{10,8},{12,10},{14,12},{0,14},{3,1},{5,3},... | collective-permute-start | bytes 1646600 | tf_op jit(solution)/shard_map/ppermute | solution.py:25
  17.6 1.9 multiply_reduce_fusion
  20.2 16.4 %collective-permute-done = bf16[16,67,256]{2,0,1:T(8,128)(2,1)S(1)} collective-permute-done((bf16[16,67,256]{2,0,1:T(8,128)(2,1)S(1)}, bf16[16,67,256]{2,0,1:T(8,128)(2,1)S(1)}, u32[]{:S(2)}, u32[]{:S(2)}) %collective-permute-start) | collective-permute-done | bytes 548896 | tf_op jit(solution)/shard_map/ppermute | solution.py:24
  36.5 2.3 %collective-permute-done.1 = bf16[16,67,256]{2,0,1:T(8,128)(2,1)} collective-permute-done((bf16[16,67,256]{2,0,1:T(8,128)(2,1)S(1)}, bf16[16,67,256]{2,0,1:T(8,128)(2,1)}, u32[]{:S(2)}, u32[]{:S(2)}) %collective-permute-start.1) | collective-permute-done | bytes 548896 | tf_op jit(solution)/shard_map/ppermute | solution.py:25
  38.9 1.2 pad_maximum_fusion
  40.0 1.3 slice.57
  43.1 1.5 copy.38
  45.4 40.6 %gather_fusion.4 = bf16[4096,64]{1,0:T(8,128)(2,1)} fusion(bf16[16,64,256]{1,2,0:T(8,128)(2,1)S(1)} %copy.38, s32[4096]{0:T(1024)S(1)} %bitcast.104), kind=kCustom, calls=%fused_computation.4 | custom fusion | bytes 1081344 | tf_op jit(solution)/shard_map/jit(take_along_axis)/gather | solution.py:122
  86.0 2.4 %copy.39 = bf16[16,256,64]{1,2,0:T(8,128)(2,1)} copy(bf16[16,256,64]{2,1,0:T(8,128)(2,1)} %bitcast.109) | data formatting | bytes 1048576 | tf_op jit(solution)/shard_map/jit(take_along_axis)/gather | solution.py:122
  88.4 2.2 %fusion.12 = bf16[16,64,64]{1,2,0:T(8,128)(2,1)} fusion(bf16[16,64,256]{2,1,0:T(8,128)(2,1)} %param.16, bf16[16,256,64]{1,2,0:T(8,128)(2,1)} %copy.39, pred[16,256]{1,0:T(8,128)(4,1)S(1)} %compare_and_fusion), kind=kOutput, calls=%fused_computation.37 | convolution fusion | flops 33882112 | bytes 1183744 | tf_op jit(solution)/shard_map/ejt,ekt->ekj/dot_general | solution.py:123
  91.0 4.3 %collective-permute-start.5 = (bf16[16,64,64]{1,2,0:T(8,128)(2,1)}, bf16[16,64,64]{1,2,0:T(8,128)(2,1)}, u32[]{:S(2)}, u32[]{:S(2)}) collective-permute-start(bf16[16,64,64]{1,2,0:T(8,128)(2,1)} %fusion.12), channel_id=1, source_target_pairs={{2,0},{4,2},{6,4},{8,6},{10,8},{12,10},{14,12},{0,14},{3,1},{5,3},... | collective-permute-start | bytes 393224 | tf_op jit(solution)/shard_map/ppermute | solution.py:25
  95.4 1.3 fusion.17
  96.7 11.0 %psum.21 = bf16[64,64]{1,0:T(8,128)(2,1)S(1)} all-reduce(f32[64,64]{1,0:T(8,128)S(1)} %fusion.17), channel_id=1, replica_groups=mesh['groups'=2,'blk'=4,'leaf'=2,'sample'=2] {'leaf'}, use_global_device_ids=true, to_apply=%region_3.4 | all-reduce | flops 4096 | bytes 24576 | tf_op jit(solution)/shard_map/psum | solution.py:132
  107.7 13.5 %all-gather = bf16[256,64]{1,0:T(8,128)(2,1)S(1)} all-gather(bf16[64,64]{1,0:T(8,128)(2,1)S(1)} %psum.21), channel_id=2, replica_groups=mesh['groups'=2,'blk'=4,'leaf'=2,'sample'=2] {'blk'}, dimensions={0}, use_global_device_ids=true | all-gather | bytes 40960 | tf_op jit(solution)/shard_map/all_gather | solution.py:133
  121.2 1.3 gather_fusion.2
  124.5 3.1 %maximum_select_fusion = bf16[48,128,256]{2,0,1:T(8,128)(2,1)S(1)} fusion(bf16[48,64,256]{2,0,1:T(8,128)(2,1)} %collective-permute-done.2, bf16[48,64,256]{2,0,1:T(8,128)(2,1)} %slice.57, pred[]{:T(512)S(6)} %eq.12), kind=kLoop, calls=%fused_computation.28 | loop fusion | flops 4718592 | bytes 6291457 | tf_op jit(solution)/shard_map/jit(_where)/select_n | solution.py:84
  127.7 2.8 %copy.36 = bf16[48,128,256]{2,1,0:T(8,128)(2,1)} copy(bf16[48,128,256]{2,0,1:T(8,128)(2,1)S(1)} %maximum_select_fusion) | data formatting | bytes 6291456 | tf_op jit(solution)/shard_map/while | solution.py:111
  130.4 42.3 %while.12 = (s32[]{:T(128)}, f32[2,4,128,256]{3,2,1,0:T(8,128)}, s32[2]{0:T(128)S(1)}, s32[]{:T(128)}, s32[16,12]{1,0:T(8,128)}, /*index=5*/bf16[48,128,256]{2,1...) while((s32[]{:T(128)}, f32[2,4,128,256]{3,2,1,0:T(8,128)}, ...), condition=%wide.region_1.0_spmd, body=%wide.region_0.0_spmd.sunk | while | flops 852494208 | bytes 11184823 | solution.py:111
  134.2 4.4 %gather_fusion = bf16[48,128,256]{2,1,0:T(8,128)(2,1)} fusion(bf16[48,128,256]{2,1,0:T(8,128)(2,1)} %get-tuple-element.290, s32[1024]{0:T(1024)S(1)} %pad_clamp_fusion.4), kind=kCustom, calls=%fused_computation.clone.1 | custom fusion | bytes 6291648 | tf_op jit(solution)/shard_map/while/body/eval_jaxpr/gather | solution.py:98
  139.4 12.2 %fusion.54 = f32[2,4,128,256]{3,2,1,0:T(8,128)} fusion(f32[2,4,128,256]{3,2,1,0:T(8,128)} %get-tuple-element.270, s32[]{:T(128)} %get-tuple-element.269, bf16[4,12,128,256]{3,2,1,0:T(8,128)(2,1)} %bitcast.105, f32[4,12,256]{2,1,0:T(8,128)S(1)} %copy.62, f32[4,256]{1,0:T(4,128)S(1)} %get-tuple-element.248, f32[4,12,256]{2,1,0:T(8,128)S(1)} %copy.63, ...), kind=kOutput, calls=%fused_computation.8.clone.1 | convolution fusion | flops 852492288 | bytes 3830464 | tf_op jit(solution)/shard_map/while/body/eval_jaxpr/lkab,lksb->lsa/dot_general | solution.py:107
  155.4 4.4 %gather_fusion = bf16[48,128,256]{2,1,0:T(8,128)(2,1)} fusion(bf16[48,128,256]{2,1,0:T(8,128)(2,1)} %get-tuple-element.290, s32[1024]{0:T(1024)S(1)} %pad_clamp_fusion.4), kind=kCustom, calls=%fused_computation.clone.1 | custom fusion | bytes 6291648 | tf_op jit(solution)/shard_map/while/body/eval_jaxpr/gather | solution.py:98
  160.6 12.1 %fusion.54 = f32[2,4,128,256]{3,2,1,0:T(8,128)} fusion(f32[2,4,128,256]{3,2,1,0:T(8,128)} %get-tuple-element.270, s32[]{:T(128)} %get-tuple-element.269, bf16[4,12,128,256]{3,2,1,0:T(8,128)(2,1)} %bitcast.105, f32[4,12,256]{2,1,0:T(8,128)S(1)} %copy.62, f32[4,256]{1,0:T(4,128)S(1)} %get-tuple-element.248, f32[4,12,256]{2,1,0:T(8,128)S(1)} %copy.63, ...), kind=kOutput, calls=%fused_computation.8.clone.1 | convolution fusion | flops 852492288 | bytes 3830464 | tf_op jit(solution)/shard_map/while/body/eval_jaxpr/lkab,lksb->lsa/dot_general | solution.py:107
  172.7 1.8 dynamic-slice_convert_fusion
  175.5 1.3 pad_maximum_fusion.1
  176.8 2.1 gather_fusion.3
  179.0 1.9 constant_dynamic-slice_fusion
  181.9 4.6 %multiply_reduce_fusion.1 = (f32[64]{0:T(128)S(1)}, f32[16,64,256]{2,1,0:T(8,128)}) fusion(f32[16,64,256]{2,1,0:T(8,128)} %param.15, bf16[16,256,64]{1,2,0:T(8,128)(2,1)} %copy.39, pred[16,256]{1,0:T(8,128)(4,1)S(1)} %copy-done.12, f32[16,64,64]{2,1,0:T(8,128)} %convolution_bitcast_fusion.1, bf16[16,8,64,64]{2,3,1,0:T(8,128)(2,1)} %bitcast.107, ...), kind=kOutput, calls=%fused_computation.54 | convolution fusion | flops 103940032 | bytes 6558209 | tf_op jit(solution)/shard_map/bfw,baf->baw/dot_general | solution.py:151
  186.5 21.7 %all-reduce = (f32[64]{0:T(128)S(1)}, f32[64]{0:T(128)S(1)}) all-reduce(f32[64]{0:T(128)S(1)} %get-tuple-element.174, f32[64]{0:T(128)S(1)} %copy-done.14), channel_id=1, replica_groups=mesh['groups'=2,'blk'=4,'leaf'=2,'sample'=2] {'blk','leaf'}, use_global_device_ids=true, to_apply=%region_5.6 | all-reduce | flops 128 | bytes 1024 | tf_op jit(solution)/shard_map/psum | solution.py:157
  208.2 2.2 %fusion.23 = bf16[16,64,256]{2,1,0:T(8,128)(2,1)} fusion(f32[16,64,256]{2,1,0:T(8,128)} %get-tuple-element.175, bf16[16,64,256]{2,1,0:T(8,128)(2,1)S(1)} %copy-done.3, f32[64]{0:T(128)S(1)} %div.3), kind=kLoop, calls=%fused_computation.51 | loop fusion | flops 1048576 | bytes 2097408 | tf_op jit(solution)/shard_map/convert_element_type | solution.py:161
  (87 shorter events, 16.8 us)
Async XLA Ops:
  7.2 174.7 %copy-start = (bf16[16,8,64,64]{3,2,1,0:T(8,128)(2,1)S(1)}, bf16[16,8,64,64]{3,2,1,0:T(8,128)(2,1)}, u32[]{:S(2)}) copy-start(bf16[16,8,64,64]{3,2,1,0:T(8,128)(2,1)} %param.25) | copy-start | bytes 3145732
  7.2 37.5 %sort.19.cloned.1.call-start = ((), (), s32[]{:S(2)}) async-start(), calls=%async_computation | async-start | bytes 98336 | tf_op jit(solution)/shard_map/jit(argsort)/sort | solution.py:121
  10.1 31.2 %copy-start.1 = (bf16[16,67,256]{2,0,1:T(8,128)(2,1)}, bf16[16,67,256]{2,0,1:T(8,128)(2,1)S(1)}, u32[]{:S(2)}) copy-start(bf16[16,67,256]{2,0,1:T(8,128)(2,1)S(1)} %get-tuple-element.173) | copy-start | bytes 1646596
  10.1 26.4 %collective-permute-start = (bf16[16,67,256]{2,0,1:T(8,128)(2,1)S(1)}, bf16[16,67,256]{2,0,1:T(8,128)(2,1)S(1)}, u32[]{:S(2)}, u32[]{:S(2)}) collective-permute-start(bf16[16,67,256]{2,0,1:T(8,128)(2,1)S(1)} %get-tuple-element.173), channel_id=1, source_target_pairs={{0,2},{2,4},{4,6},{6,8},{8,10},{10,12},{12,14},{14,0},{1,3},{3,5},... | collective-permute-start | bytes 1646600 | tf_op jit(solution)/shard_map/ppermute | solution.py:24
  13.1 25.8 %collective-permute-start.1 = (bf16[16,67,256]{2,0,1:T(8,128)(2,1)S(1)}, bf16[16,67,256]{2,0,1:T(8,128)(2,1)}, u32[]{:S(2)}, u32[]{:S(2)}) collective-permute-start(bf16[16,67,256]{2,0,1:T(8,128)(2,1)S(1)} %get-tuple-element.173), channel_id=1, source_target_pairs={{2,0},{4,2},{6,4},{8,6},{10,8},{12,10},{14,12},{0,14},{3,1},{5,3},... | collective-permute-start | bytes 1646600 | tf_op jit(solution)/shard_map/ppermute | solution.py:25
  20.2 21.7 %copy-start.9 = (s32[16,12]{1,0:T(8,128)S(1)}, s32[16,12]{1,0:T(8,128)}, u32[]{:S(2)}) copy-start(s32[16,12]{1,0:T(8,128)} %param.23) | copy-start | bytes 2308
  36.5 4.8 %copy-start.4 = (bf16[16,67,256]{2,0,1:T(8,128)(2,1)}, bf16[16,67,256]{2,0,1:T(8,128)(2,1)S(1)}, u32[]{:S(2)}) copy-start(bf16[16,67,256]{2,0,1:T(8,128)(2,1)S(1)} %collective-permute-done) | copy-start | bytes 1646596
  41.3 83.2 %collective-permute-start.2 = (bf16[48,64,256]{2,0,1:T(8,128)(2,1)}, bf16[48,64,256]{2,0,1:T(8,128)(2,1)}, u32[]{:S(2)}, u32[]{:S(2)}) collective-permute-start(bf16[48,64,256]{2,0,1:T(8,128)(2,1)} %slice.57), channel_id=1, source_target_pairs={{0,1},{1,0},{2,3},{3,2},{4,5},{5,4},{6,7},{7,6},{8,9},{9,8},{10,11... | collective-permute-start | bytes 4718600 | tf_op jit(solution)/shard_map/ppermute | solution.py:31
  45.4 43.0 %copy-start.8 = (s32[16,256]{1,0:T(8,128)S(1)}, s32[16,256]{1,0:T(8,128)}, u32[]{:S(2)}) copy-start(s32[16,256]{1,0:T(8,128)} %get-tuple-element.131) | copy-start | bytes 49156
  45.4 50.0 %copy-start.7 = (bf16[1,64,64]{2,1,0:T(8,128)(2,1)S(1)}, bf16[1,64,64]{2,1,0:T(8,128)(2,1)}, u32[]{:S(2)}) copy-start(bf16[1,64,64]{2,1,0:T(8,128)(2,1)} %param.22) | copy-start | bytes 24580
  86.0 9.4 %copy-start.6 = (bf16[16,64,64]{2,1,0:T(8,128)(2,1)S(1)}, bf16[16,64,64]{2,1,0:T(8,128)(2,1)}, u32[]{:S(2)}) copy-start(bf16[16,64,64]{2,1,0:T(8,128)(2,1)} %param.21) | copy-start | bytes 393220
  86.0 37.7 %copy-start.2 = (bf16[16,67,256]{2,0,1:T(8,128)(2,1)S(1)}, bf16[16,67,256]{2,0,1:T(8,128)(2,1)}, u32[]{:S(2)}) copy-start(bf16[16,67,256]{2,0,1:T(8,128)(2,1)} %copy-done.1) | copy-start | bytes 1646596
  86.0 37.7 %copy-start.5 = (bf16[16,67,256]{2,0,1:T(8,128)(2,1)S(1)}, bf16[16,67,256]{2,0,1:T(8,128)(2,1)}, u32[]{:S(2)}) copy-start(bf16[16,67,256]{2,0,1:T(8,128)(2,1)} %copy-done.4) | copy-start | bytes 1646596
  88.4 2.6 %copy-start.11 = (pred[16,256]{1,0:T(8,128)(4,1)}, pred[16,256]{1,0:T(8,128)(4,1)S(1)}, u32[]{:S(2)}) copy-start(pred[16,256]{1,0:T(8,128)(4,1)S(1)} %compare_and_fusion) | copy-start | bytes 12292
  90.6 84.9 %collective-permute-start.4 = (bf16[16,64,64]{1,2,0:T(8,128)(2,1)}, bf16[16,64,64]{1,2,0:T(8,128)(2,1)}, u32[]{:S(2)}, u32[]{:S(2)}) collective-permute-start(bf16[16,64,64]{1,2,0:T(8,128)(2,1)} %fusion.12), channel_id=1, source_target_pairs={{0,2},{2,4},{4,6},{6,8},{8,10},{10,12},{12,14},{14,0},{1,3},{3,5},... | collective-permute-start | bytes 393224 | tf_op jit(solution)/shard_map/ppermute | solution.py:24
  91.0 84.5 %collective-permute-start.5 = (bf16[16,64,64]{1,2,0:T(8,128)(2,1)}, bf16[16,64,64]{1,2,0:T(8,128)(2,1)}, u32[]{:S(2)}, u32[]{:S(2)}) collective-permute-start(bf16[16,64,64]{1,2,0:T(8,128)(2,1)} %fusion.12), channel_id=1, source_target_pairs={{2,0},{4,2},{6,4},{8,6},{10,8},{12,10},{14,12},{0,14},{3,1},{5,3},... | collective-permute-start | bytes 393224 | tf_op jit(solution)/shard_map/ppermute | solution.py:25
  130.4 46.4 %copy-start.10 = (s32[1024]{0:T(1024)S(1)}, s32[1024]{0:T(1024)}, u32[]{:S(2)}) copy-start(s32[1024]{0:T(1024)} %pad_clamp_fusion.1) | copy-start | bytes 12292
  174.5 6.4 %collective-permute-start.3 = (bf16[8,64,256]{2,1,0:T(8,128)(2,1)}, bf16[8,64,256]{2,1,0:T(8,128)(2,1)}, u32[]{:S(2)}, u32[]{:S(2)}) collective-permute-start(bf16[8,64,256]{2,1,0:T(8,128)(2,1)} %dynamic-slice_convert_fusion), channel_id=1, source_target_pairs={{0,1},{1,0},{2,3},{3,2},{4,5},{5,4},{6,7},{7,6},{8,9},{9,8},{10,11... | collective-permute-start | bytes 786440 | tf_op jit(solution)/shard_map/ppermute | solution.py:31
  176.8 5.1 %copy-start.3 = (bf16[16,64,256]{2,1,0:T(8,128)(2,1)S(1)}, bf16[16,64,256]{2,1,0:T(8,128)(2,1)}, u32[]{:S(2)}) copy-start(bf16[16,64,256]{2,1,0:T(8,128)(2,1)} %param.16) | copy-start | bytes 1572868
  176.8 5.1 %copy-start.12 = (pred[16,256]{1,0:T(8,128)(4,1)S(1)}, pred[16,256]{1,0:T(8,128)(4,1)}, u32[]{:S(2)}) copy-start(pred[16,256]{1,0:T(8,128)(4,1)} %copy-done.11) | copy-start | bytes 12292
  176.8 5.1 %copy-start.13 = (f32[64]{0:T(128)S(1)}, f32[64]{0:T(128)}, u32[]{:S(2)}) copy-start(f32[64]{0:T(128)} %param.17) | copy-start | bytes 772
  181.9 4.6 %copy-start.14 = (f32[64]{0:T(128)S(1)}, f32[64]{0:T(128)}, u32[]{:S(2)}) copy-start(f32[64]{0:T(128)} %multiply_reduce_fusion) | copy-start | bytes 772
Sparse Core Ops, SparseCore 0:
  16.9 2.5 sort.21.cloned.1.call-done
  (1 shorter events, 0.0 us)
where the time goes:
time: 218 us; the launch traced here: 217 us
  local copies, waits for them, and re-layouts  71.6 us (33%)
  blocking collectives  46.2 us (21%)
  matrix products  34.6 us (16%)
  other arithmetic  19.7 us (9%)
  waiting for transfers between devices  18.7 us (9%)
  between operations  14.3 us (7%)
  starting transfers between devices  10.7 us (5%)
    gather x2, local copies, waits for them, and re-layouts, on_device(): natural_values = jnp.take_along_axis(basis, inverse[:, None, :], axis=2)  43 us
    dot_general x2, matrix products, near_block(): jnp.einsum('lkab,lksb->lsa', kernel_tiles, near_values, preferred_element...  24.3 us
    psum x1, blocking collectives, on_device(): new_norm = lax.psum(new_square, ('blk', 'leaf'))  21.7 us
    ppermute x2, waiting for transfers between devices, padded(): before = lax.ppermute(last, axis, up)  16.4 us
    all_gather x1, blocking collectives, on_device(): every_top = lax.all_gather(top_node[None], 'blk', axis=0, tiled=True)  13.5 us
    psum x1, blocking collectives, on_device(): top_node = lax.psum(lifted, 'leaf').astype(jnp.bfloat16)  11 us
    gather x2, local copies, waits for them, and re-layouts, near_block(): near_values = all_columns[slot_rows]  8.85 us
    ppermute x2, starting transfers between devices, padded(): after = lax.ppermute(initial, axis, down)  7.38 us
  transfers between devices with their start and end apart: 6, of which 2 were waited for; matrix products, arithmetic and copies ran while one was open for 52% of the time, Pallas kernels for 0%

commit v1 on v0

v1 whole, which is shorter than its diff:
```python
import functools
import math

import jax
import jax.numpy as jnp
from jax import lax
from jax.experimental import pallas as pl
from jax.experimental.pallas import tpu as pltpu
from jax.sharding import PartitionSpec as P

LEAF_DEV = 16

ROOT_THREE = math.sqrt(3.0)
LENGTH = 0.3
AMPLITUDE = 0.25
NUGGET = 0.5
SPREAD = 0.5 / LEAF_DEV
KAPPA = (ROOT_THREE / LENGTH) ** 2
LOG2E = 1.4426950408889634

RING = ("blk", "leaf")
BF = jnp.bfloat16
F32 = jnp.float32
MIB = 1 << 20


def shifted(array, axis, by):
    if isinstance(axis, tuple):
        count = math.prod(lax.axis_size(name) for name in axis)
    else:
        count = lax.axis_size(axis)
    return lax.ppermute(array, axis, [(i, (i + by) % count) for i in range(count)])


def partner(array):
    return lax.ppermute(array, "sample", [(0, 1), (1, 0)])


def thirds(value):
    high = value.astype(BF).astype(F32)
    rest = value - high
    middle = rest.astype(BF).astype(F32)
    return high, middle, rest - middle


def nt(left, right):
    return lax.dot_general(left, right, (((1,), (1,)), ((), ())), preferred_element_type=F32)


def nn(left, right):
    return jnp.dot(left, right, preferred_element_type=F32)


def call(kernel, outs, flops, moved, vmem=40, **kwargs):
    return pl.pallas_call(
        kernel,
        out_shape=outs,
        compiler_params=pltpu.CompilerParams(vmem_limit_bytes=vmem * MIB),
        cost_estimate=pl.CostEstimate(flops=flops, bytes_accessed=moved, transcendentals=0),
        **kwargs,
    )


def up_kernel(order, basis, direction, leaf_transfer, node_transfer, natural, coef, lifted):
    leaves, rank, points = basis.shape
    samples = direction.shape[1]
    rows = lax.broadcasted_iota(jnp.int32, (points, points), 0)
    node = jnp.zeros((samples, rank), F32)
    for g in range(leaves):
        place = jnp.where(rows == order[g : g + 1, :], 1.0, 0.0).astype(BF)
        own = nt(basis[g], place).astype(BF)
        natural[g] = own
        weights = nt(direction[g], own).astype(BF)
        coef[g] = weights
        node = node + nt(weights, leaf_transfer[g])
    lifted[...] = nt(node.astype(BF), node_transfer[0])


def features(offsets):
    x, y, z = (offsets[i : i + 1, :] for i in range(3))
    square = thirds(KAPPA * (x * x + y * y + z * z))
    row = lax.broadcasted_iota(jnp.int32, (8, x.shape[1]), 0)
    packed = jnp.zeros((8, x.shape[1]), F32)
    for i, value in enumerate((x, y, z, jnp.ones_like(x)) + square):
        packed = jnp.where(row == i, value, packed)
    return packed.astype(BF)


def tile_kernel(near, prev, own, after, tiles, spread_x):
    half = tiles.shape[0] * pl.num_programs(0)
    entries = near.shape[1]
    points = own.shape[2]
    leaves = own.shape[0]
    total = leaves * lax.axis_size("blk") * lax.axis_size("leaf")
    device = lax.axis_index("blk") * lax.axis_size("leaf") + lax.axis_index("leaf")
    anchor = (device - 1) * leaves

    @pl.when(pl.program_id(0) == 0)
    def _():
        lane = lax.broadcasted_iota(jnp.int32, (8, 128), 1)
        source = jnp.where(
            lane < 9,
            lane // 3,
            jnp.where(lane < 12, lane - 5, jnp.where(lane < 16, 7, jnp.where(lane < 64, 3, 0))),
        )
        source = jnp.where(lane < 112, source, 7)
        row = lax.broadcasted_iota(jnp.int32, (8, 128), 0)
        pick = jnp.where((row == source) & (row < 7), 1.0, 0.0).astype(BF)
        for side, ref in enumerate((prev, own, after)):
            for j in range(leaves):
                feats = features(ref[j].astype(F32))
                spread_x[side * leaves + j] = lax.dot_general(
                    feats, pick, (((0,), (0,)), ((), ())), preferred_element_type=F32
                ).astype(BF)

    g = lax.axis_index("sample") * half + pl.program_id(0)
    offsets = own[g].astype(F32)
    x, y, z = (offsets[i : i + 1, :] for i in range(3))
    row = lax.broadcasted_iota(jnp.int32, (16, points), 0)
    first = jnp.where((row >= 9) & (row < 12), 1.0, jnp.zeros((16, points), F32))
    at = 0
    for value in (x, y, z):
        for part in thirds(value * (-2.0 * KAPPA)):
            first = jnp.where(row == at, part, first)
            at += 1
    slots = []
    gap = jnp.zeros((16, points), F32)
    for e in range(entries):
        slot = lax.rem(near[g, e] - anchor + 2 * total, total)
        slots.append(slot)
        gap = jnp.where(row == e, (leaves + g - slot).astype(F32) * SPREAD, gap)
    moved = x + gap
    fixed = thirds(KAPPA * (moved * moved + y * y + z * z))
    gaps = thirds(gap * (-2.0 * KAPPA))
    weights = jnp.concatenate(
        [part.astype(BF) for part in (first,) + fixed + gaps + (jnp.zeros((16, points), F32),)],
        axis=0,
    )
    lane = lax.broadcasted_iota(jnp.int32, (1, 128), 1)
    for e in range(entries):
        keep = jnp.where((lane < 16) | (lane % 16 == e), 1.0, 0.0).astype(BF)
        square = jnp.maximum(nn(spread_x[slots[e]] * keep, weights), 1e-30)
        scaled = square * lax.rsqrt(square)
        value = (1.0 + scaled) * jnp.exp2(scaled * (-LOG2E))
        tiles[0, e * points : (e + 1) * points, :] = value.astype(BF)


def down_kernel(
    top_list,
    coupling_list,
    tops,
    top_coupling,
    node_transfer,
    leaf_transfer,
    before,
    after,
    coupling,
    natural,
    direction,
    base,
    window,
):
    leaves, samples, points = direction.shape
    rank = natural.shape[1]
    clusters = lax.axis_size("blk")
    here = lax.axis_index("blk")
    total = leaves * clusters * lax.axis_size("leaf")
    anchor = (here * lax.axis_size("leaf") + lax.axis_index("leaf") - 1) * leaves
    window[:leaves] = before[...]
    window[leaves:] = after[...]
    incoming = jnp.zeros((samples, rank), F32)
    for e in range(top_list.shape[1]):
        place = lax.rem(here - top_list[0, e] + clusters, clusters)
        incoming = incoming + nt(tops[place], top_coupling[0, e])
    down = nn(incoming.astype(BF), node_transfer[0]).astype(BF)
    for g in range(leaves):
        inward = nn(down, leaf_transfer[g])
        for c in range(coupling_list.shape[1]):
            slot = lax.rem(coupling_list[g, c] - anchor + 2 * total, total)
            slot = jnp.where(slot >= 2 * leaves, slot - leaves, slot)
            slot = jnp.minimum(slot, 2 * leaves - 1)
            inward = inward + nt(window[slot], coupling[g, c])
        far = nn(inward.astype(BF), natural[g])
        base[g] = NUGGET * direction[g].astype(F32) + far


def near_kernel(near, *refs):
    pieces, (tiles, kept, given, window, sems) = refs[:6], refs[6:]
    leaves = window.shape[0] // 3
    samples = kept.shape[1]
    points = kept.shape[2]
    total = leaves * lax.axis_size("blk") * lax.axis_size("leaf")
    device = lax.axis_index("blk") * lax.axis_size("leaf") + lax.axis_index("leaf")
    anchor = (device - 1) * leaves

    @pl.when(pl.program_id(0) == 0)
    def _():
        copies = []
        for i, piece in enumerate(pieces):
            side, columns = i // 2, i % 2
            copies.append(
                pltpu.make_async_copy(
                    piece,
                    window.at[
                        side * leaves : (side + 1) * leaves,
                        columns * samples : (columns + 1) * samples,
                    ],
                    sems.at[i],
                )
            )
        for copy in copies:
            copy.start()
        for copy in copies:
            copy.wait()

    g = lax.axis_index("sample") * pl.num_programs(0) + pl.program_id(0)
    values = []
    for e in range(near.shape[1]):
        values.append(window[lax.rem(near[g, e] - anchor + 2 * total, total)])
    field = nn(jnp.concatenate(values, axis=1), tiles[0]) * AMPLITUDE
    kept[0] = field[:samples]
    given[0] = field[samples:].astype(BF)


def residual_kernel(core, step, base, kept, received, residual, updated, norms):
    block = pl.program_id(0)
    mine = block // (pl.num_programs(0) // 2) == core[0]

    @pl.when(block == 0)
    def _():
        norms[...] = jnp.zeros_like(norms)

    def finish(near):
        old = residual[...]
        new = old - step[...][None] * (base[...] + near)
        updated[...] = new
        norms[0] += jnp.sum(jnp.sum(old * old, axis=0), axis=1, keepdims=True)
        norms[1] += jnp.sum(jnp.sum(new * new, axis=0), axis=1, keepdims=True)

    @pl.when(mine)
    def _():
        finish(kept[...])

    @pl.when(jnp.logical_not(mine))
    def _():
        finish(received[...].astype(F32))


def on_device(
    residual,
    direction,
    step,
    coords,
    order,
    basis,
    leaf_transfer,
    node_transfer,
    near_list,
    coupling_list,
    coupling,
    top_list,
    top_coupling,
):
    leaves, samples, points = direction.shape
    rank = basis.shape[1]
    entries = near_list.shape[1]
    half = leaves // 2
    blk_count = lax.axis_size("blk")
    leaf_count = lax.axis_size("leaf")
    shape = jax.ShapeDtypeStruct
    smem = pl.BlockSpec(memory_space=pltpu.SMEM)
    vmem = pl.BlockSpec(memory_space=pltpu.VMEM)
    anywhere = pl.BlockSpec(memory_space=pl.ANY)

    coords_prev = shifted(coords, RING, 1)
    coords_after = shifted(coords, RING, -1)
    direction_prev = shifted(direction, RING, 1)
    direction_after = shifted(direction, RING, -1)
    direction_other = partner(direction)

    natural, coef, lifted = call(
        up_kernel,
        (
            shape((leaves, rank, points), BF),
            shape((leaves, samples, rank), BF),
            shape((samples, rank), F32),
        ),
        4 * leaves * rank * points * points,
        6 * MIB,
        in_specs=[vmem] * 5,
        out_specs=(vmem,) * 3,
    )(order, basis, direction, leaf_transfer, node_transfer)

    coef_prev = shifted(coef, RING, 1)
    coef_after = shifted(coef, RING, -1)
    top = lifted
    for by in range(1, leaf_count):
        top = top + shifted(lifted, "leaf", by)
    top = top.astype(BF)
    if blk_count <= 8:
        tops = jnp.stack([top] + [shifted(top, "blk", by) for by in range(1, blk_count)])
    else:
        tops = lax.all_gather(top[None], "blk", axis=0, tiled=True)
        places = jnp.mod(lax.axis_index("blk") - jnp.arange(blk_count, dtype=jnp.int32), blk_count)
        tops = tops[places]

    tiles = call(
        tile_kernel,
        shape((half, entries * points, points), BF),
        40 * half * entries * points * points,
        half * entries * points * points * 2,
        grid=(half,),
        in_specs=[smem] + [vmem] * 3,
        out_specs=pl.BlockSpec((1, entries * points, points), lambda i: (i, 0, 0)),
        scratch_shapes=[pltpu.VMEM((3 * leaves, points, 128), BF)],
    )(near_list, coords_prev, coords, coords_after)

    base = call(
        down_kernel,
        shape((leaves, samples, points), F32),
        2 * leaves * samples * rank * (points + 9 * rank),
        8 * MIB,
        in_specs=[smem] * 2 + [vmem] * 9,
        out_specs=vmem,
        scratch_shapes=[pltpu.VMEM((2 * leaves, samples, rank), BF)],
    )(
        top_list,
        coupling_list,
        tops,
        top_coupling,
        node_transfer,
        leaf_transfer,
        coef_prev,
        coef_after,
        coupling,
        natural,
        direction,
    )

    own = pl.BlockSpec((1, samples, points), lambda i: (i, 0, 0))
    kept, given = call(
        near_kernel,
        (shape((half, samples, points), F32), shape((half, samples, points), BF)),
        4 * half * entries * samples * points * points,
        half * entries * points * points * 2,
        grid=(half,),
        in_specs=[smem]
        + [anywhere] * 6
        + [pl.BlockSpec((1, entries * points, points), lambda i: (i, 0, 0))],
        out_specs=(own, own),
        scratch_shapes=[
            pltpu.VMEM((3 * leaves, 2 * samples, points), BF),
            pltpu.SemaphoreType.DMA((6,)),
        ],
    )(
        near_list,
        direction_prev,
        partner(direction_prev),
        direction,
        direction_other,
        direction_after,
        partner(direction_after),
        tiles,
    )
    received = partner(given)

    side = lax.axis_index("sample").astype(jnp.int32).reshape(1)
    steps = 4
    chunk = leaves // steps
    slab = pl.BlockSpec((chunk, samples, points), lambda i, core: (i, 0, 0))
    per_side = steps // 2

    def of_side(flip):
        def index(i, core):
            owner = core[0] if not flip else 1 - core[0]
            return (jnp.clip(i - owner * per_side, 0, per_side - 1), 0, 0)

        return pl.BlockSpec((chunk, samples, points), index)

    residual_next, norms = pl.pallas_call(
        residual_kernel,
        out_shape=(shape((leaves, samples, points), F32), shape((2, samples, 1), F32)),
        grid_spec=pltpu.PrefetchScalarGridSpec(
            num_scalar_prefetch=1,
            grid=(steps,),
            in_specs=[
                pl.BlockSpec((samples, 1), lambda i, core: (0, 0)),
                slab,
                of_side(False),
                of_side(True),
                slab,
            ],
            out_specs=(slab, pl.BlockSpec((2, samples, 1), lambda i, core: (0, 0, 0))),
        ),
        cost_estimate=pl.CostEstimate(flops=4 * MIB, bytes_accessed=5 * MIB, transcendentals=0),
    )(side, step[:, None], base, kept, received, residual)

    devices = blk_count * leaf_count
    shared = jnp.broadcast_to(norms.reshape(1, 2, samples), (devices, 2, samples))
    sums = jnp.sum(lax.all_to_all(shared, RING, 0, 0), axis=0)
    ratio = sums[1] / sums[0]
    direction_next = (residual_next + ratio[None, :, None] * direction.astype(F32)).astype(BF)
    return (residual_next, direction_next)


def solution(mesh):
    in_specs = (
        P(("groups", "blk", "leaf"), "sample", None),
        P(("groups", "blk", "leaf"), "sample", None),
        P(("groups", "sample")),
        P(("groups", "blk", "leaf"), None, None),
        P(("groups", "blk", "leaf"), None),
        P(("groups", "blk", "leaf"), None, None),
        P(("groups", "blk", "leaf"), None, None),
        P(("groups", "blk", "leaf"), None, None),
        P(("groups", "blk", "leaf"), None),
        P(("groups", "blk", "leaf"), None),
        P(("groups", "blk", "leaf"), None, None, None),
        P(("groups", "blk"), None),
        P(("groups", "blk"), None, None, None),
    )
    out_specs = (
        P(("groups", "blk", "leaf"), "sample", None),
        P(("groups", "blk", "leaf"), "sample", None),
    )
    return jax.shard_map(
        on_device, mesh=mesh, in_specs=in_specs, out_specs=out_specs, check_vma=False
    )
```

time: 218 us -> 110 us (0.50)
  local copies, waits for them, and re-layouts: 71.6 us -> 14.3 us
  blocking collectives: 46.2 us -> 10.8 us
  matrix products: 34.6 us -> 0 us
  Pallas kernels: 0 us -> 34.5 us
  other arithmetic: 19.7 us -> 4.59 us
  between operations: 14.3 us -> 0.87 us
  waiting for transfers between devices: 18.7 us -> 27.4 us
  starting transfers between devices: 10.7 us -> 17 us
    gather x8 -> x0, local copies, waits for them, and re-layouts: 56.6 us -> none  [the longest x2 43 us: on_device(): natural_values = jnp.take_along_axis(basis, inverse[:, None, :], axis=2)]
    dot_general x7 -> x0, matrix products: 34.6 us -> none  [the longest x2 24.3 us: near_block(): jnp.einsum('lkab,lksb->lsa', kernel_tiles, near_values, preferred_element...]
    pallas_call x0 -> x5, Pallas kernels: none -> 34.5 us  [the longest x1 11.3 us: on_device(): call(tile_kernel, shape((half, entries * points, points), BF), 40 * half...]
    psum x2 -> x0, blocking collectives: 32.7 us -> none  [the longest x1 21.7 us: on_device(): new_norm = lax.psum(new_square, ('blk', 'leaf'))]
    all_gather x1 -> x0, blocking collectives: 13.5 us -> none  [on_device(): every_top = lax.all_gather(top_node[None], 'blk', axis=0, tiled=True)]
    all_to_all x0 -> x1, blocking collectives: none -> 10.8 us  [on_device(): sums = jnp.sum(lax.all_to_all(shared, RING, 0, 0), axis=0)]
    unnamed x34 -> x38, local copies, waits for them, and re-layouts: 3.11 us -> 12.5 us
    ppermute x6 -> x14, waiting for transfers between devices: 18.7 us -> 27.4 us  [the longest x10 27.4 us: shifted(): lax.ppermute(array, axis, [(i, (i + by) % count) for i in range(count)])]
  transfers between devices with their start and end apart: 6 -> 14, of which waited for: 2 -> 4; matrix products, arithmetic and copies ran while one was open for 52% -> 3% of each run, Pallas kernels for 0% -> 28%
where the time goes in v1:
time: 110 us
  Pallas kernels  34.5 us (31%)
  waiting for transfers between devices  27.4 us (25%)
  starting transfers between devices  17 us (15%)
  local copies, waits for them, and re-layouts  14.3 us (13%)
  blocking collectives  10.8 us (10%)
  other arithmetic  4.59 us (4%)
    ppermute x10, waiting for transfers between devices, shifted(): lax.ppermute(array, axis, [(i, (i + by) % count) for i in range(count)])  27.4 us
    ppermute x10, starting transfers between devices, shifted(): lax.ppermute(array, axis, [(i, (i + by) % count) for i in range(count)])  16.7 us
    unnamed x38, local copies, waits for them, and re-layouts  12.5 us
    pallas_call x1, Pallas kernels, on_device(): call(tile_kernel, shape((half, entries * points, points), BF), 40 * half...  11.3 us
    all_to_all x1, blocking collectives, on_device(): sums = jnp.sum(lax.all_to_all(shared, RING, 0, 0), axis=0)  10.8 us
    pallas_call x1, Pallas kernels, on_device(): call(near_kernel, (shape((half, samples, points), F32), shape((half, samp...  9.13 us
    pallas_call x1, Pallas kernels, on_device(): call(down_kernel, shape((leaves, samples, points), F32), 2 * leaves * sam...  5.68 us
    pallas_call x1, Pallas kernels, on_device(): call(up_kernel, (shape((leaves, rank, points), BF), shape((leaves, sample...  4.39 us
  transfers between devices with their start and end apart: 14, of which 4 were waited for; matrix products, arithmetic and copies ran while one was open for 3% of the time, Pallas kernels for 28%

profile of v1, /device:TPU:0, one launch (start us, length us, event | category | flops | bytes accessed | tf_op | source)
XLA Modules:
  0.0 109.6 jit_solution(8669102136084732199)
XLA Ops:
  0.6 6.0 %collective-permute-start.9 = (bf16[16,64,256]{2,1,0:T(8,128)(2,1)}, bf16[16,64,256]{2,1,0:T(8,128)(2,1)S(1)}, u32[]{:S(2)}, u32[]{:S(2)}) collective-permute-start(bf16[16,64,256]{2,1,0:T(8,128)(2,1)} %refs_2_.1), channel_id=1, source_target_pairs={{0,14},{2,0},{4,2},{6,4},{8,6},{10,8},{12,10},{14,12},{1,15},{3,1}... | collective-permute-start | bytes 1572872 | tf_op jit(solution)/shard_map/ppermute | solution.py:32
  6.7 20.3 %collective-permute-done.9.refs_4_ = bf16[16,64,256]{2,1,0:T(8,128)(2,1)S(1)} collective-permute-done((bf16[16,64,256]{2,1,0:T(8,128)(2,1)}, bf16[16,64,256]{2,1,0:T(8,128)(2,1)S(1)}, u32[]{:S(2)}, u32[]{:S(2)}) %collective-permute-start.9) | collective-permute-done | bytes 524320 | tf_op jit(solution)/shard_map/ppermute | solution.py:32
  27.0 0.3 collective-permute-done.6.refs_0_
  27.3 0.3 collective-permute-start.7
  27.5 0.8 copy.31.own
  28.3 2.2 %collective-permute-start.11 = (bf16[16,3,256]{2,1,0:T(4,128)(2,1)S(1)}, bf16[16,3,256]{2,1,0:T(4,128)(2,1)S(1)}, u32[]{:S(2)}, u32[]{:S(2)}) collective-permute-start(bf16[16,3,256]{2,1,0:T(4,128)(2,1)S(1)} %copy.31.own), channel_id=1, source_target_pairs={{0,2},{2,4},{4,6},{6,8},{8,10},{10,12},{12,14},{14,0},{1,3},{3,5},... | collective-permute-start | bytes 73736 | tf_op jit(solution)/shard_map/ppermute | solution.py:32
  30.5 2.6 %collective-permute-start.12 = (bf16[16,3,256]{2,1,0:T(4,128)(2,1)S(1)}, bf16[16,3,256]{2,1,0:T(4,128)(2,1)S(1)}, u32[]{:S(2)}, u32[]{:S(2)}) collective-permute-start(bf16[16,3,256]{2,1,0:T(4,128)(2,1)S(1)} %copy.31.own), channel_id=1, source_target_pairs={{0,14},{2,0},{4,2},{6,4},{8,6},{10,8},{12,10},{14,12},{1,15},{3,1}... | collective-permute-start | bytes 73736 | tf_op jit(solution)/shard_map/ppermute | solution.py:32
  33.1 1.0 copy-done.1
  34.1 0.9 copy-done.5
  35.1 1.0 copy-done.8
  36.1 0.7 copy-done.10
  36.8 0.7 copy-done.14
  37.5 4.4 %shard_map.140 = (bf16[16,64,256]{2,1,0:T(8,128)(2,1)S(1)}, bf16[16,64,64]{2,1,0:T(8,128)(2,1)}, f32[64,64]{1,0:T(8,128)S(1)}) custom-call(s32[16,256]{1,0:T(8,128)S(1)} %copy-done.14, bf16[16,64,256]{2,1,0:T(8,128)(2,1)S(1)} %copy-done.8, bf16[16,64,256]{2,1,0:T(8,128)(2,1)S(1)} %copy-done.1, bf16[16,64,64]{2,1,0:T(8,128)(2,1)S(1)} %copy-done.5, ...), custom_call_target="tpu_custom_call" | custom-call | flops 268435456 | bytes 6291456 | tf_op jit(solution)/shard_map/pallas_call | solution.py:281
  42.0 4.7 %collective-permute-start.5 = (bf16[16,64,64]{2,1,0:T(8,128)(2,1)}, bf16[16,64,64]{2,1,0:T(8,128)(2,1)}, u32[]{:S(2)}, u32[]{:S(2)}) collective-permute-start(bf16[16,64,64]{2,1,0:T(8,128)(2,1)} %get-tuple-element.10), channel_id=1, source_target_pairs={{0,14},{2,0},{4,2},{6,4},{8,6},{10,8},{12,10},{14,12},{1,15},{3,1}... | collective-permute-start | bytes 393224 | tf_op jit(solution)/shard_map/ppermute | solution.py:32
  46.8 0.7 copy-done.12
  47.4 11.3 %shard_map.142.refs_6_ = bf16[8,3072,256]{2,1,0:T(8,128)(2,1)S(1)} custom-call(s32[16,12]{1,0:T(8,128)S(1)} %copy-done.12, bf16[16,3,256]{2,1,0:T(4,128)(2,1)S(1)} %collective-permute-done.11.prev, bf16[16,3,256]{2,1,0:T(4,128)(2,1)S(1)} %copy.31.own, bf16[16,3,256]{2,1,0:T(4,128)(2,1)S(1)} %collective-permute-done.12.after), custom_call_target="tpu_custom_call" | custom-call | flops 251658240 | bytes 12582912 | tf_op jit(solution)/shard_map/pallas_call | solution.py:307
  58.7 4.5 %copy-done = bf16[8,3072,256]{2,1,0:T(8,128)(2,1)} copy-done((bf16[8,3072,256]{2,1,0:T(8,128)(2,1)}, bf16[8,3072,256]{2,1,0:T(8,128)(2,1)S(1)}, u32[]{:S(2)}) %copy-start) | copy-done | bytes 12582936
  63.3 9.1 %shard_map.143 = (f32[8,64,256]{2,1,0:T(8,128)S(1)}, bf16[8,64,256]{2,1,0:T(8,128)(2,1)}) custom-call(s32[16,12]{1,0:T(8,128)S(1)} %copy-done.13, bf16[16,64,256]{2,1,0:T(8,128)(2,1)S(1)} %collective-permute-done.6.refs_0_, bf16[16,64,256]{2,1,0:T(8,128)(2,1)S(1)} %collective-permute-done.7.refs_1_, bf16[16,64,256]{2,1,0:T(8,128)(2,1)S(1)} %copy-done.2, ...), custom_call_target="tpu_custom_call" | custom-call | flops 1610612736 | bytes 12582912 | tf_op jit(solution)/shard_map/pallas_call | solution.py:341
  72.4 0.8 copy-done.7
  73.3 1.1 %collective-permute-start.2 = (bf16[64,64]{1,0:T(8,128)(2,1)S(1)}, bf16[64,64]{1,0:T(8,128)(2,1)S(1)}, u32[]{:S(2)}, u32[]{:S(2)}) collective-permute-start(bf16[64,64]{1,0:T(8,128)(2,1)S(1)} %add_convert_fusion.1), channel_id=1, source_target_pairs={{0,8},{4,12},{8,0},{12,4},{1,9},{5,13},{9,1},{13,5},{2,10},{6,14},... | collective-permute-start | bytes 24584 | tf_op jit(solution)/shard_map/ppermute | solution.py:32
  74.4 4.4 %collective-permute-done.1 = bf16[64,64]{1,0:T(8,128)(2,1)S(1)} collective-permute-done((bf16[64,64]{1,0:T(8,128)(2,1)S(1)}, bf16[64,64]{1,0:T(8,128)(2,1)S(1)}, u32[]{:S(2)}, u32[]{:S(2)}) %collective-permute-start.1) | collective-permute-done | bytes 8224 | tf_op jit(solution)/shard_map/ppermute | solution.py:32
  78.9 1.3 %copy.34.step = f32[64,1]{1,0:T(8,128)} copy(f32[64,1]{0,1:T(1,128)} %bitcast.11) | data formatting | bytes 512 | tf_op jit(solution)/shard_map/broadcast_in_dim | solution.py:396
  80.3 2.4 %collective-permute-done.3 = bf16[64,64]{1,0:T(8,128)(2,1)} collective-permute-done((bf16[64,64]{1,0:T(8,128)(2,1)S(1)}, bf16[64,64]{1,0:T(8,128)(2,1)}, u32[]{:S(2)}, u32[]{:S(2)}) %collective-permute-start.3) | collective-permute-done | bytes 8224 | tf_op jit(solution)/shard_map/ppermute | solution.py:32
  82.7 0.7 pad_maximum_fusion.tops
  83.5 5.7 %shard_map.141.base = f32[16,64,256]{2,1,0:T(8,128)S(1)} custom-call(s32[1,4]{1,0:T(1,128)S(1)} %copy-done.15, s32[16,8]{1,0:T(8,128)S(1)} %copy.30.coupling_list, bf16[4,64,64]{2,1,0:T(8,128)(2,1)S(1)} %pad_maximum_fusion.tops, bf16[1,4,64,64]{3,2,1,0:T(8,128)(2,1)S(1)} %copy-done.9, bf16[1,64,64]{2,1,0:T(8,128)(2,1)S(1)} %copy-done.11, ...), custom_call_target="tpu_custom_call" | custom-call | flops 109051904 | bytes 8388608 | tf_op jit(solution)/shard_map/pallas_call | solution.py:318
  89.2 1.0 copy-done.3
  90.2 4.1 %shard_map.144 = (f32[16,64,256]{2,1,0:T(8,128)}, f32[2,64,1]{2,1,0:T(8,128)}) custom-call(s32[1]{0:T(128)} %bitcast.core, f32[64,1]{1,0:T(8,128)} %copy.34.step, f32[16,64,256]{2,1,0:T(8,128)} %copy-done.3, f32[8,64,256]{2,1,0:T(8,128)} %copy-done.7, bf16[8,64,256]{2,1,0:T(8,128)(2,1)} %collective-permute-done.13.received, f32[16,64,256]{2,1,0:T(8,128)} %residual.1), custom_call_target="tpu_custom_call" | custom-call | flops 4194304 | bytes 5242880 | tf_op jit(solution)/shard_map/pallas_call | solution.py:380
  94.2 0.9 reduce
  95.3 10.8 %all_to_all.5 = f32[8,1,128]{2,1,0:T(1,128)S(1)} all-to-all(f32[8,1,128]{2,1,0:T(1,128)S(1)} %reshape.21), channel_id=1, replica_groups=mesh['groups'=2,'blk'=4,'leaf'=2,'sample'=2] {'blk','leaf'}, dimensions={0} | all-to-all | bytes 8192 | tf_op jit(solution)/shard_map/all_to_all | solution.py:400
  106.0 0.5 broadcast.1
  106.6 0.7 reduce.1
  107.3 2.2 %add_convert_fusion = bf16[16,64,256]{2,1,0:T(8,128)(2,1)} fusion(f32[16,64,256]{2,1,0:T(8,128)} %get-tuple-element.7, bf16[16,64,256]{2,1,0:T(8,128)(2,1)S(1)} %copy-done.2, f32[64]{0:T(128)S(1)} %fusion), kind=kLoop, calls=%fused_computation | loop fusion | flops 1048576 | bytes 2097408 | tf_op jit(solution)/shard_map/convert_element_type | solution.py:402
  (50 shorter events, 0.5 us)
Async XLA Ops:
  0.6 62.6 %copy-start.13 = (s32[16,12]{1,0:T(8,128)S(1)}, s32[16,12]{1,0:T(8,128)}, u32[]{:S(2)}) copy-start(s32[16,12]{1,0:T(8,128)} %near.3) | copy-start | bytes 2308
  0.6 26.4 %collective-permute-start.9 = (bf16[16,64,256]{2,1,0:T(8,128)(2,1)}, bf16[16,64,256]{2,1,0:T(8,128)(2,1)S(1)}, u32[]{:S(2)}, u32[]{:S(2)}) collective-permute-start(bf16[16,64,256]{2,1,0:T(8,128)(2,1)} %refs_2_.1), channel_id=1, source_target_pairs={{0,14},{2,0},{4,2},{6,4},{8,6},{10,8},{12,10},{14,12},{1,15},{3,1}... | collective-permute-start | bytes 1572872 | tf_op jit(solution)/shard_map/ppermute | solution.py:32
  6.7 20.6 %collective-permute-start.6 = (bf16[16,64,256]{2,1,0:T(8,128)(2,1)}, bf16[16,64,256]{2,1,0:T(8,128)(2,1)S(1)}, u32[]{:S(2)}, u32[]{:S(2)}) collective-permute-start(bf16[16,64,256]{2,1,0:T(8,128)(2,1)} %refs_2_.1), channel_id=1, source_target_pairs={{0,2},{2,4},{4,6},{6,8},{8,10},{10,12},{12,14},{14,0},{1,3},{3,5},... | collective-permute-start | bytes 1572872 | tf_op jit(solution)/shard_map/ppermute | solution.py:32
  6.7 56.6 %collective-permute-start.8 = (bf16[16,64,256]{2,1,0:T(8,128)(2,1)}, bf16[16,64,256]{2,1,0:T(8,128)(2,1)S(1)}, u32[]{:S(2)}, u32[]{:S(2)}) collective-permute-start(bf16[16,64,256]{2,1,0:T(8,128)(2,1)} %refs_2_.1), channel_id=1, source_target_pairs={{0,1},{1,0},{2,3},{3,2},{4,5},{5,4},{6,7},{7,6},{8,9},{9,8},{10,11... | collective-permute-start | bytes 1572872 | tf_op jit(solution)/shard_map/ppermute | solution.py:36
  27.0 36.2 %collective-permute-start.10 = (bf16[16,64,256]{2,1,0:T(8,128)(2,1)S(1)}, bf16[16,64,256]{2,1,0:T(8,128)(2,1)S(1)}, u32[]{:S(2)}, u32[]{:S(2)}) collective-permute-start(bf16[16,64,256]{2,1,0:T(8,128)(2,1)S(1)} %collective-permute-done.9.refs_4_), channel_id=1, source_target_pairs={{0,1},{1,0},{2,3},{3,2},{4,5},{5,4},{6,7},{7,6},{8,9},{9,8},{10,11... | collective-permute-start | bytes 1572872 | tf_op jit(solution)/shard_map/ppermute | solution.py:36
  27.3 36.0 %collective-permute-start.7 = (bf16[16,64,256]{2,1,0:T(8,128)(2,1)S(1)}, bf16[16,64,256]{2,1,0:T(8,128)(2,1)S(1)}, u32[]{:S(2)}, u32[]{:S(2)}) collective-permute-start(bf16[16,64,256]{2,1,0:T(8,128)(2,1)S(1)} %collective-permute-done.6.refs_0_), channel_id=1, source_target_pairs={{0,1},{1,0},{2,3},{3,2},{4,5},{5,4},{6,7},{7,6},{8,9},{9,8},{10,11... | collective-permute-start | bytes 1572872 | tf_op jit(solution)/shard_map/ppermute | solution.py:36
  28.3 13.7 %collective-permute-start.11 = (bf16[16,3,256]{2,1,0:T(4,128)(2,1)S(1)}, bf16[16,3,256]{2,1,0:T(4,128)(2,1)S(1)}, u32[]{:S(2)}, u32[]{:S(2)}) collective-permute-start(bf16[16,3,256]{2,1,0:T(4,128)(2,1)S(1)} %copy.31.own), channel_id=1, source_target_pairs={{0,2},{2,4},{4,6},{6,8},{8,10},{10,12},{12,14},{14,0},{1,3},{3,5},... | collective-permute-start | bytes 73736 | tf_op jit(solution)/shard_map/ppermute | solution.py:32
  30.5 11.6 %collective-permute-start.12 = (bf16[16,3,256]{2,1,0:T(4,128)(2,1)S(1)}, bf16[16,3,256]{2,1,0:T(4,128)(2,1)S(1)}, u32[]{:S(2)}, u32[]{:S(2)}) collective-permute-start(bf16[16,3,256]{2,1,0:T(4,128)(2,1)S(1)} %copy.31.own), channel_id=1, source_target_pairs={{0,14},{2,0},{4,2},{6,4},{8,6},{10,8},{12,10},{14,12},{1,15},{3,1}... | collective-permute-start | bytes 73736 | tf_op jit(solution)/shard_map/ppermute | solution.py:32
  33.1 1.0 copy-start.1
  34.1 0.9 copy-start.5
  35.1 1.0 copy-start.8
  36.1 0.7 copy-start.10
  36.8 0.7 copy-start.14
  37.5 25.7 %copy-start.2 = (bf16[16,64,256]{2,1,0:T(8,128)(2,1)S(1)}, bf16[16,64,256]{2,1,0:T(8,128)(2,1)}, u32[]{:S(2)}) copy-start(bf16[16,64,256]{2,1,0:T(8,128)(2,1)} %refs_2_.1) | copy-start | bytes 1572868
  41.9 41.5 %copy-start.15 = (s32[1,4]{1,0:T(1,128)S(1)}, s32[1,4]{1,0:T(1,128)}, u32[]{:S(2)}) copy-start(s32[1,4]{1,0:T(1,128)} %top_list.1) | copy-start | bytes 52
  41.9 41.5 %copy-start.4 = (bf16[16,8,64,64]{3,2,1,0:T(8,128)(2,1)S(1)}, bf16[16,8,64,64]{3,2,1,0:T(8,128)(2,1)}, u32[]{:S(2)}) copy-start(bf16[16,8,64,64]{3,2,1,0:T(8,128)(2,1)} %coupling.1) | copy-start | bytes 3145732
  41.9 41.5 %copy-start.6 = (bf16[16,64,64]{2,1,0:T(8,128)(2,1)S(1)}, bf16[16,64,64]{2,1,0:T(8,128)(2,1)}, u32[]{:S(2)}) copy-start(bf16[16,64,64]{2,1,0:T(8,128)(2,1)} %leaf_transfer.3) | copy-start | bytes 393220
  41.9 41.5 %copy-start.9 = (bf16[1,4,64,64]{3,2,1,0:T(8,128)(2,1)S(1)}, bf16[1,4,64,64]{3,2,1,0:T(8,128)(2,1)}, u32[]{:S(2)}) copy-start(bf16[1,4,64,64]{3,2,1,0:T(8,128)(2,1)} %top_coupling.1) | copy-start | bytes 98308
  42.0 41.5 %copy-start.11 = (bf16[1,64,64]{2,1,0:T(8,128)(2,1)S(1)}, bf16[1,64,64]{2,1,0:T(8,128)(2,1)}, u32[]{:S(2)}) copy-start(bf16[1,64,64]{2,1,0:T(8,128)(2,1)} %node_transfer.3) | copy-start | bytes 24580
  42.0 41.4 %collective-permute-start.4 = (bf16[16,64,64]{2,1,0:T(8,128)(2,1)}, bf16[16,64,64]{2,1,0:T(8,128)(2,1)}, u32[]{:S(2)}, u32[]{:S(2)}) collective-permute-start(bf16[16,64,64]{2,1,0:T(8,128)(2,1)} %get-tuple-element.10), channel_id=1, source_target_pairs={{0,2},{2,4},{4,6},{6,8},{8,10},{10,12},{12,14},{14,0},{1,3},{3,5},... | collective-permute-start | bytes 393224 | tf_op jit(solution)/shard_map/ppermute | solution.py:32
  42.0 41.4 %collective-permute-start.5 = (bf16[16,64,64]{2,1,0:T(8,128)(2,1)}, bf16[16,64,64]{2,1,0:T(8,128)(2,1)}, u32[]{:S(2)}, u32[]{:S(2)}) collective-permute-start(bf16[16,64,64]{2,1,0:T(8,128)(2,1)} %get-tuple-element.10), channel_id=1, source_target_pairs={{0,14},{2,0},{4,2},{6,4},{8,6},{10,8},{12,10},{14,12},{1,15},{3,1}... | collective-permute-start | bytes 393224 | tf_op jit(solution)/shard_map/ppermute | solution.py:32
  46.7 0.7 copy-start.12
  47.4 31.4 %copy-start.16 = (s32[16,8]{0,1:T(8,128)S(1)}, s32[16,8]{0,1:T(8,128)}, u32[]{:S(2)}) copy-start(s32[16,8]{0,1:T(8,128)} %param.22) | copy-start | bytes 1540
  58.7 4.5 %copy-start = (bf16[8,3072,256]{2,1,0:T(8,128)(2,1)}, bf16[8,3072,256]{2,1,0:T(8,128)(2,1)S(1)}, u32[]{:S(2)}) copy-start(bf16[8,3072,256]{2,1,0:T(8,128)(2,1)S(1)} %shard_map.142.refs_6_) | copy-start | bytes 37748740
  63.2 10.0 %collective-permute-start = (f32[64,64]{1,0:T(8,128)S(1)}, f32[64,64]{1,0:T(8,128)S(1)}, u32[]{:S(2)}, u32[]{:S(2)}) collective-permute-start(f32[64,64]{1,0:T(8,128)S(1)} %get-tuple-element.9), channel_id=1, source_target_pairs={{0,2},{2,0},{1,3},{3,1},{4,6},{6,4},{5,7},{7,5},{8,10},{10,8},{9,1... | collective-permute-start | bytes 49160 | tf_op jit(solution)/shard_map/ppermute | solution.py:32
  72.4 0.8 copy-start.7
  73.2 17.0 %collective-permute-start.13 = (bf16[8,64,256]{2,1,0:T(8,128)(2,1)}, bf16[8,64,256]{2,1,0:T(8,128)(2,1)}, u32[]{:S(2)}, u32[]{:S(2)}) collective-permute-start(bf16[8,64,256]{2,1,0:T(8,128)(2,1)} %get-tuple-element.13), channel_id=1, source_target_pairs={{0,1},{1,0},{2,3},{3,2},{4,5},{5,4},{6,7},{7,6},{8,9},{9,8},{10,11... | collective-permute-start | bytes 786440 | tf_op jit(solution)/shard_map/ppermute | solution.py:36
  73.2 5.6 %collective-permute-start.1 = (bf16[64,64]{1,0:T(8,128)(2,1)S(1)}, bf16[64,64]{1,0:T(8,128)(2,1)S(1)}, u32[]{:S(2)}, u32[]{:S(2)}) collective-permute-start(bf16[64,64]{1,0:T(8,128)(2,1)S(1)} %add_convert_fusion.1), channel_id=1, source_target_pairs={{0,4},{4,8},{8,12},{12,0},{1,5},{5,9},{9,13},{13,1},{2,6},{6,10},{... | collective-permute-start | bytes 24584 | tf_op jit(solution)/shard_map/ppermute | solution.py:32
  73.3 7.0 %collective-permute-start.2 = (bf16[64,64]{1,0:T(8,128)(2,1)S(1)}, bf16[64,64]{1,0:T(8,128)(2,1)S(1)}, u32[]{:S(2)}, u32[]{:S(2)}) collective-permute-start(bf16[64,64]{1,0:T(8,128)(2,1)S(1)} %add_convert_fusion.1), channel_id=1, source_target_pairs={{0,8},{4,12},{8,0},{12,4},{1,9},{5,13},{9,1},{13,5},{2,10},{6,14},... | collective-permute-start | bytes 24584 | tf_op jit(solution)/shard_map/ppermute | solution.py:32
  78.8 3.8 %collective-permute-start.3 = (bf16[64,64]{1,0:T(8,128)(2,1)S(1)}, bf16[64,64]{1,0:T(8,128)(2,1)}, u32[]{:S(2)}, u32[]{:S(2)}) collective-permute-start(bf16[64,64]{1,0:T(8,128)(2,1)S(1)} %add_convert_fusion.1), channel_id=1, source_target_pairs={{0,12},{4,0},{8,4},{12,8},{1,13},{5,1},{9,5},{13,9},{2,14},{6,2},{... | collective-permute-start | bytes 24584 | tf_op jit(solution)/shard_map/ppermute | solution.py:32
  89.2 1.0 copy-start.3

commit v2 on v1

v2 whole, which is shorter than its diff:
```python
import functools
import math

import jax
import jax.numpy as jnp
from jax import lax
from jax.experimental import pallas as pl
from jax.experimental.pallas import tpu as pltpu
from jax.sharding import PartitionSpec as P

LEAF_DEV = 16

ROOT_THREE = math.sqrt(3.0)
LENGTH = 0.3
AMPLITUDE = 0.25
NUGGET = 0.5
SPREAD = 0.5 / LEAF_DEV
KAPPA = (ROOT_THREE / LENGTH) ** 2
LOG2E = 1.4426950408889634

RING = ("blk", "leaf")
BF = jnp.bfloat16
F32 = jnp.float32
MIB = 1 << 20


def shifted(array, axis, by):
    if isinstance(axis, tuple):
        count = math.prod(lax.axis_size(name) for name in axis)
    else:
        count = lax.axis_size(axis)
    return lax.ppermute(array, axis, [(i, (i + by) % count) for i in range(count)])


def partner(array):
    return lax.ppermute(array, "sample", [(0, 1), (1, 0)])


def ordered(array, *first):
    return lax.optimization_barrier((array,) + first)[0]


def column(row):
    size = row.shape[1]
    shape = (size, size)
    here = lax.broadcasted_iota(jnp.int32, shape, 0) == lax.broadcasted_iota(jnp.int32, shape, 1)
    return jnp.sum(jnp.where(here, row, 0.0), axis=1, keepdims=True)


def thirds(value):
    high = value.astype(BF).astype(F32)
    rest = value - high
    middle = rest.astype(BF).astype(F32)
    return high, middle, rest - middle


def nt(left, right):
    return lax.dot_general(left, right, (((1,), (1,)), ((), ())), preferred_element_type=F32)


def nn(left, right):
    return jnp.dot(left, right, preferred_element_type=F32)


def call(kernel, outs, flops, moved, vmem=40, **kwargs):
    return pl.pallas_call(
        kernel,
        out_shape=outs,
        compiler_params=pltpu.CompilerParams(vmem_limit_bytes=vmem * MIB),
        cost_estimate=pl.CostEstimate(flops=flops, bytes_accessed=moved, transcendentals=0),
        **kwargs,
    )


def up_kernel(order, basis, direction, leaf_transfer, node_transfer, natural, coef, lifted):
    leaves, rank, points = basis.shape
    samples = direction.shape[1]
    rows = lax.broadcasted_iota(jnp.int32, (points, points), 0)
    node = jnp.zeros((samples, rank), F32)
    for g in range(leaves):
        place = jnp.where(rows == order[g : g + 1, :], 1.0, 0.0).astype(BF)
        own = nt(basis[g], place).astype(BF)
        natural[g] = own
        weights = nt(direction[g], own).astype(BF)
        coef[g] = weights
        node = node + nt(weights, leaf_transfer[g])
    lifted[...] = nt(node.astype(BF), node_transfer[0])


def features(offsets):
    x, y, z = (offsets[i : i + 1, :] for i in range(3))
    square = thirds(KAPPA * (x * x + y * y + z * z))
    row = lax.broadcasted_iota(jnp.int32, (8, x.shape[1]), 0)
    packed = jnp.zeros((8, x.shape[1]), F32)
    for i, value in enumerate((x, y, z, jnp.ones_like(x)) + square):
        packed = jnp.where(row == i, value, packed)
    return packed.astype(BF)


def spread_features(offsets):
    lane = lax.broadcasted_iota(jnp.int32, (8, 128), 1)
    source = jnp.where(
        lane < 9,
        lane // 3,
        jnp.where(lane < 12, lane - 5, jnp.where(lane < 16, 7, jnp.where(lane < 64, 3, 0))),
    )
    source = jnp.where(lane < 112, source, 7)
    row = lax.broadcasted_iota(jnp.int32, (8, 128), 0)
    pick = jnp.where((row == source) & (row < 7), 1.0, 0.0).astype(BF)
    return lax.dot_general(
        features(offsets), pick, (((0,), (0,)), ((), ())), preferred_element_type=F32
    ).astype(BF)


def tile_kernel(start, near, prev, own, after, tiles, spread_x):
    count = tiles.shape[0]
    entries = near.shape[1]
    points = own.shape[2]
    leaves = own.shape[0]
    total = leaves * lax.axis_size("blk") * lax.axis_size("leaf")
    device = lax.axis_index("blk") * lax.axis_size("leaf") + lax.axis_index("leaf")
    anchor = (device - 1) * leaves
    for side, ref in enumerate((prev, own, after)):
        for j in range(leaves):
            spread_x[side * leaves + j] = spread_features(ref[j].astype(F32))
    row = lax.broadcasted_iota(jnp.int32, (16, points), 0)
    lane = lax.broadcasted_iota(jnp.int32, (1, 128), 1)

    def leaf(i, carry):
        g = lax.axis_index("sample") * (leaves // 2) + start + i
        offsets = own[g].astype(F32)
        x, y, z = (offsets[k : k + 1, :] for k in range(3))
        first = jnp.where((row >= 9) & (row < 12), 1.0, jnp.zeros((16, points), F32))
        at = 0
        for value in (x, y, z):
            for part in thirds(value * (-2.0 * KAPPA)):
                first = jnp.where(row == at, part, first)
                at += 1
        slots = []
        gap = jnp.zeros((16, points), F32)
        for e in range(entries):
            slot = lax.rem(near[g, e] - anchor + 2 * total, total)
            slots.append(slot)
            gap = jnp.where(row == e, (leaves + g - slot).astype(F32) * SPREAD, gap)
        moved = x + gap
        fixed = thirds(KAPPA * (moved * moved + y * y + z * z))
        gaps = thirds(gap * (-2.0 * KAPPA))
        weights = jnp.concatenate(
            [part.astype(BF) for part in (first,) + fixed + gaps + (jnp.zeros_like(first),)],
            axis=0,
        )
        for e in range(entries):
            keep = jnp.where((lane < 16) | (lane % 16 == e), 1.0, 0.0).astype(BF)
            square = jnp.maximum(nn(spread_x[slots[e]] * keep, weights), 1e-30)
            scaled = square * lax.rsqrt(square)
            value = (1.0 + scaled) * jnp.exp2(scaled * (-LOG2E))
            tiles[i, e * points : (e + 1) * points, :] = value.astype(BF)
        return carry

    lax.fori_loop(0, count, leaf, 0)


def down_kernel(
    top_list,
    coupling_list,
    tops,
    top_coupling,
    node_transfer,
    leaf_transfer,
    before,
    after,
    coupling,
    natural,
    direction,
    base,
    window,
):
    leaves, samples, points = direction.shape
    rank = natural.shape[1]
    clusters = lax.axis_size("blk")
    here = lax.axis_index("blk")
    total = leaves * clusters * lax.axis_size("leaf")
    anchor = (here * lax.axis_size("leaf") + lax.axis_index("leaf") - 1) * leaves
    window[:leaves] = before[...]
    window[leaves:] = after[...]
    incoming = jnp.zeros((samples, rank), F32)
    for e in range(top_list.shape[1]):
        place = lax.rem(here - top_list[0, e] + clusters, clusters)
        incoming = incoming + nt(tops[place], top_coupling[0, e])
    down = nn(incoming.astype(BF), node_transfer[0]).astype(BF)
    for g in range(leaves):
        inward = nn(down, leaf_transfer[g])
        for c in range(coupling_list.shape[1]):
            slot = lax.rem(coupling_list[g, c] - anchor + 2 * total, total)
            slot = jnp.where(slot >= 2 * leaves, slot - leaves, slot)
            slot = jnp.minimum(slot, 2 * leaves - 1)
            inward = inward + nt(window[slot], coupling[g, c])
        far = nn(inward.astype(BF), natural[g])
        base[g] = NUGGET * direction[g].astype(F32) + far


def near_kernel(near, *refs):
    pieces, tiles, (kept, given, window, sems) = refs[:6], refs[6:-4], refs[-4:]
    leaves = window.shape[0] // 3
    samples = kept.shape[1]
    total = leaves * lax.axis_size("blk") * lax.axis_size("leaf")
    device = lax.axis_index("blk") * lax.axis_size("leaf") + lax.axis_index("leaf")
    anchor = (device - 1) * leaves
    copies = []
    for i, piece in enumerate(pieces):
        side, columns = i // 2, i % 2
        copies.append(
            pltpu.make_async_copy(
                piece,
                window.at[
                    side * leaves : (side + 1) * leaves,
                    columns * samples : (columns + 1) * samples,
                ],
                sems.at[i],
            )
        )
    for copy in copies:
        copy.start()
    for copy in copies:
        copy.wait()
    at = 0
    for part in tiles:

        def leaf(i, carry, part=part, at=at):
            g = lax.axis_index("sample") * kept.shape[0] + at + i
            values = []
            for e in range(near.shape[1]):
                values.append(window[lax.rem(near[g, e] - anchor + 2 * total, total)])
            field = nn(jnp.concatenate(values, axis=1), part[i]) * AMPLITUDE
            kept[at + i] = field[:samples]
            given[at + i] = field[samples:].astype(BF)
            return carry

        lax.fori_loop(0, part.shape[0], leaf, 0)
        at += part.shape[0]


def residual_kernel(step, base, kept, received, residual, updated, norms):
    half = kept.shape[0]
    core = lax.axis_index("sample")
    steps = column(step[...])
    totals = [jnp.zeros((step.shape[1], 1), F32)] * 2
    for i in range(half):
        for theirs in range(2):
            g = (core ^ theirs) * half + i
            near = received[i].astype(F32) if theirs else kept[i]
            old = residual[g]
            new = old - steps * (base[g] + near)
            updated[g] = new
            for k, value in enumerate((old, new)):
                totals[k] = totals[k] + jnp.sum(value * value, axis=1, keepdims=True)
    samples = steps.shape[0]
    lane = lax.broadcasted_iota(jnp.int32, (samples, 128), 1)
    sub = lax.broadcasted_iota(jnp.int32, (samples, 128), 0)
    rows = [jnp.sum(jnp.where(lane == sub, part, 0.0), axis=0, keepdims=True) for part in totals]
    row = lax.broadcasted_iota(jnp.int32, norms.shape[1:], 0)
    packed = jnp.where(row == 0, rows[0], jnp.where(row == 1, rows[1], 0.0))
    for i in range(norms.shape[0]):
        norms[i] = packed


def direction_kernel(norms, updated, direction, result, held, sems):
    leaves, samples, points = updated.shape
    sums = norms[0]
    for i in range(1, norms.shape[0]):
        sums = sums + norms[i]
    ratio = column((sums[1:2, :] / sums[0:1, :])[:, :samples])
    chunks = sems.shape[0]
    size = leaves // chunks
    copies = []
    for c in range(chunks):
        for g in range(c * size, (c + 1) * size):
            held[g] = (updated[g] + ratio * direction[g].astype(F32)).astype(BF)
        part = pl.ds(c * size, size)
        copies.append(pltpu.make_async_copy(held.at[part], result.at[part], sems.at[c]))
        copies[-1].start()
    for copy in copies:
        copy.wait()


def on_device(
    residual,
    direction,
    step,
    coords,
    order,
    basis,
    leaf_transfer,
    node_transfer,
    near_list,
    coupling_list,
    coupling,
    top_list,
    top_coupling,
):
    leaves, samples, points = direction.shape
    rank = basis.shape[1]
    entries = near_list.shape[1]
    half = leaves // 2
    blk_count = lax.axis_size("blk")
    leaf_count = lax.axis_size("leaf")
    shape = jax.ShapeDtypeStruct
    smem = pl.BlockSpec(memory_space=pltpu.SMEM)
    vmem = pl.BlockSpec(memory_space=pltpu.VMEM)
    anywhere = pl.BlockSpec(memory_space=pl.ANY)

    coords_prev = shifted(coords, RING, 1)
    coords_after = shifted(coords, RING, -1)
    direction_prev = shifted(direction, RING, 1)
    direction_after = shifted(direction, RING, -1)
    direction_other = partner(direction)

    natural, coef, lifted = call(
        up_kernel,
        (
            shape((leaves, rank, points), BF),
            shape((leaves, samples, rank), BF),
            shape((samples, rank), F32),
        ),
        4 * leaves * rank * points * points,
        6 * MIB,
        in_specs=[vmem] * 5,
        out_specs=(vmem,) * 3,
    )(order, basis, direction, leaf_transfer, node_transfer)

    coef_prev = shifted(coef, RING, 1)
    coef_after = shifted(coef, RING, -1)
    top = lifted
    for by in range(1, leaf_count):
        top = top + shifted(lifted, "leaf", by)
    top = top.astype(BF)
    if blk_count <= 8:
        tops = jnp.stack([top] + [shifted(top, "blk", by) for by in range(1, blk_count)])
    else:
        tops = lax.all_gather(top[None], "blk", axis=0, tiled=True)
        places = jnp.mod(lax.axis_index("blk") - jnp.arange(blk_count, dtype=jnp.int32), blk_count)
        tops = tops[places]

    def make_tiles(start, near):
        count = half // 2
        return call(
            functools.partial(tile_kernel, start),
            shape((count, entries * points, points), BF),
            40 * count * entries * points * points,
            count * entries * points * points * 2,
            in_specs=[smem] + [vmem] * 3,
            out_specs=vmem,
            scratch_shapes=[pltpu.VMEM((3 * leaves, points, 128), BF)],
            vmem=16,
        )(near, coords_prev, coords, coords_after)

    tiles_low = make_tiles(0, ordered(near_list, natural))
    tiles_high = make_tiles(half // 2, ordered(near_list, tiles_low, top))

    base = call(
        down_kernel,
        shape((leaves, samples, points), F32),
        2 * leaves * samples * rank * (points + 9 * rank),
        8 * MIB,
        in_specs=[smem] * 2 + [vmem] * 9,
        out_specs=vmem,
        scratch_shapes=[pltpu.VMEM((2 * leaves, samples, rank), BF)],
        vmem=16,
    )(
        ordered(top_list, tiles_high),
        coupling_list,
        tops,
        top_coupling,
        node_transfer,
        leaf_transfer,
        coef_prev,
        coef_after,
        coupling,
        natural,
        direction,
    )

    direction_prev = ordered(direction_prev, base)
    direction_after = ordered(direction_after, base)
    kept, given = call(
        near_kernel,
        (shape((half, samples, points), F32), shape((half, samples, points), BF)),
        4 * half * entries * samples * points * points,
        half * entries * points * points * 2,
        in_specs=[smem] + [anywhere] * 6 + [vmem] * 2,
        out_specs=(vmem, vmem),
        scratch_shapes=[
            pltpu.VMEM((3 * leaves, 2 * samples, points), BF),
            pltpu.SemaphoreType.DMA((6,)),
        ],
        vmem=16,
    )(
        near_list,
        direction_prev,
        partner(direction_prev),
        direction,
        direction_other,
        direction_after,
        partner(direction_after),
        tiles_low,
        tiles_high,
    )
    received = partner(given)

    devices = blk_count * leaf_count
    residual_next, norms = call(
        residual_kernel,
        (shape((leaves, samples, points), F32), shape((devices, 8, 128), F32)),
        4 * MIB,
        5 * MIB,
        in_specs=[vmem] * 5,
        out_specs=(vmem, vmem),
        vmem=16,
    )(step[None, :], base, kept, received, residual)
    norms = lax.all_to_all(norms, RING, 0, 0)
    direction_next = call(
        direction_kernel,
        shape((leaves, samples, points), BF),
        MIB,
        2 * MIB,
        in_specs=[vmem] * 3,
        out_specs=anywhere,
        scratch_shapes=[
            pltpu.VMEM((leaves, samples, points), BF),
            pltpu.SemaphoreType.DMA((4,)),
        ],
        vmem=16,
    )(norms, residual_next, direction)
    return (residual_next, direction_next)


def solution(mesh):
    in_specs = (
        P(("groups", "blk", "leaf"), "sample", None),
        P(("groups", "blk", "leaf"), "sample", None),
        P(("groups", "sample")),
        P(("groups", "blk", "leaf"), None, None),
        P(("groups", "blk", "leaf"), None),
        P(("groups", "blk", "leaf"), None, None),
        P(("groups", "blk", "leaf"), None, None),
        P(("groups", "blk", "leaf"), None, None),
        P(("groups", "blk", "leaf"), None),
        P(("groups", "blk", "leaf"), None),
        P(("groups", "blk", "leaf"), None, None, None),
        P(("groups", "blk"), None),
        P(("groups", "blk"), None, None, None),
    )
    out_specs = (
        P(("groups", "blk", "leaf"), "sample", None),
        P(("groups", "blk", "leaf"), "sample", None),
    )
    return jax.shard_map(
        on_device, mesh=mesh, in_specs=in_specs, out_specs=out_specs, check_vma=False
    )
```

time: 110 us -> 87 us (0.79)
  waiting for transfers between devices: 27.4 us -> 15.7 us
  Pallas kernels: 34.5 us -> 28.2 us
  local copies, waits for them, and re-layouts: 14.3 us -> 8.19 us
  other arithmetic: 4.59 us -> 0.03 us
  starting transfers between devices: 17 us -> 21.3 us
  blocking collectives: 10.8 us -> 12.3 us
    ppermute x10, waiting for transfers between devices: 27.4 us -> 12.3 us  [shifted(): lax.ppermute(array, axis, [(i, (i + by) % count) for i in range(count)])]
    pallas_call x1, Pallas kernels: 9.13 us -> 3.99 us  [on_device(): call(near_kernel, (shape((half, samples, points), F32), shape((half, samp...]
    unnamed x38 -> x34, local copies, waits for them, and re-layouts: 12.5 us -> 8.19 us
    ppermute x10, starting transfers between devices: 16.7 us -> 20.3 us  [shifted(): lax.ppermute(array, axis, [(i, (i + by) % count) for i in range(count)])]
    ppermute x4, waiting for transfers between devices: 0.01 us -> 3.33 us  [partner(): return lax.ppermute(array, 'sample', [(0, 1), (1, 0)])]
    convert_element_type x1 -> x0, other arithmetic: 2.23 us -> none  [on_device(): (residual_next + ratio[None, :, None] * direction.astype(F32)).astype(BF)]
    all_to_all x1, blocking collectives: 10.8 us -> 12.3 us  [on_device(): norms = lax.all_to_all(norms, RING, 0, 0)]
    broadcast_in_dim x2 -> x0, local copies, waits for them, and re-layouts: 1.35 us -> none  [the longest x1 1.35 us: on_device(): step[:, None]]
  transfers between devices with their start and end apart: 14 -> 14, of which waited for: 4 -> 8; matrix products, arithmetic and copies ran while one was open for 3% -> 2% of each run, Pallas kernels for 28% -> 25%
where the time goes in v2:
time: 87 us; the launch traced here: 86.5 us
  Pallas kernels  28.2 us (32%)
  starting transfers between devices  21.3 us (24%)
  waiting for transfers between devices  15.7 us (18%)
  blocking collectives  12.3 us (14%)
  local copies, waits for them, and re-layouts  8.19 us (9%)
    ppermute x10, starting transfers between devices, shifted(): lax.ppermute(array, axis, [(i, (i + by) % count) for i in range(count)])  20.3 us
    pallas_call x2, Pallas kernels, make_tiles(): call(functools.partial(tile_kernel, start), shape((count, entries * point...  12.8 us
    ppermute x10, waiting for transfers between devices, shifted(): lax.ppermute(array, axis, [(i, (i + by) % count) for i in range(count)])  12.3 us
    all_to_all x1, blocking collectives, on_device(): norms = lax.all_to_all(norms, RING, 0, 0)  12.3 us
    unnamed x34, local copies, waits for them, and re-layouts  8.19 us
    pallas_call x1, Pallas kernels, on_device(): call(down_kernel, shape((leaves, samples, points), F32), 2 * leaves * sam...  5.3 us
    pallas_call x1, Pallas kernels, on_device(): call(near_kernel, (shape((half, samples, points), F32), shape((half, samp...  3.99 us
    pallas_call x1, Pallas kernels, on_device(): call(up_kernel, (shape((leaves, rank, points), BF), shape((leaves, sample...  3.9 us
  transfers between devices with their start and end apart: 14, of which 8 were waited for; matrix products, arithmetic and copies ran while one was open for 2% of the time, Pallas kernels for 25%

profile of v2, /device:TPU:0, one launch (start us, length us, event | category | flops | bytes accessed | tf_op | source)
XLA Modules:
  0.0 86.5 jit_solution(16042157388256593346)
XLA Ops:
  0.6 6.0 %collective-permute-start.11 = (bf16[16,64,256]{2,1,0:T(8,128)(2,1)}, bf16[16,64,256]{2,1,0:T(8,128)(2,1)S(1)}, u32[]{:S(2)}, u32[]{:S(2)}) collective-permute-start(bf16[16,64,256]{2,1,0:T(8,128)(2,1)} %direction.5), channel_id=1, source_target_pairs={{0,14},{2,0},{4,2},{6,4},{8,6},{10,8},{12,10},{14,12},{1,15},{3,1}... | collective-permute-start | bytes 1572872 | tf_op jit(solution)/shard_map/ppermute | solution.py:32
  6.7 1.1 %copy-done = bf16[16,64,256]{2,1,0:T(8,128)(2,1)S(1)} copy-done((bf16[16,64,256]{2,1,0:T(8,128)(2,1)S(1)}, bf16[16,64,256]{2,1,0:T(8,128)(2,1)}, u32[]{:S(2)}) %copy-start) | copy-done | bytes 524312
  7.8 0.9 %copy-done.5 = bf16[16,64,64]{2,1,0:T(8,128)(2,1)S(1)} copy-done((bf16[16,64,64]{2,1,0:T(8,128)(2,1)S(1)}, bf16[16,64,64]{2,1,0:T(8,128)(2,1)}, u32[]{:S(2)}) %copy-start.5) | copy-done | bytes 131096
  8.7 1.0 %copy-done.7 = bf16[16,64,256]{2,1,0:T(8,128)(2,1)S(1)} copy-done((bf16[16,64,256]{2,1,0:T(8,128)(2,1)S(1)}, bf16[16,64,256]{2,1,0:T(8,128)(2,1)}, u32[]{:S(2)}) %copy-start.7) | copy-done | bytes 524312
  9.8 0.7 copy-done.11
  10.5 0.7 copy-done.13
  11.2 3.9 %shard_map.140 = (bf16[16,64,256]{2,1,0:T(8,128)(2,1)S(1)}, bf16[16,64,64]{2,1,0:T(8,128)(2,1)S(1)}, f32[64,64]{1,0:T(8,128)S(1)}) custom-call(s32[16,256]{1,0:T(8,128)S(1)} %copy-done.13, bf16[16,64,256]{2,1,0:T(8,128)(2,1)S(1)} %copy-done.7, bf16[16,64,256]{2,1,0:T(8,128)(2,1)S(1)} %copy-done, bf16[16,64,64]{2,1,0:T(8,128)(2,1)S(1)} %copy-done.5, ...), custom_call_target="tpu_custom_call" | custom-call | flops 268435456 | bytes 6291456 | tf_op jit(solution)/shard_map/pallas_call | solution.py:318
  15.1 0.8 copy.15.own
  15.9 4.7 %collective-permute-start.1 = (bf16[16,3,256]{2,1,0:T(4,128)(2,1)S(1)}, bf16[16,3,256]{2,1,0:T(4,128)(2,1)S(1)}, u32[]{:S(2)}, u32[]{:S(2)}) collective-permute-start(bf16[16,3,256]{2,1,0:T(4,128)(2,1)S(1)} %copy.15.own), channel_id=1, source_target_pairs={{0,14},{2,0},{4,2},{6,4},{8,6},{10,8},{12,10},{14,12},{1,15},{3,1}... | collective-permute-start | bytes 73736 | tf_op jit(solution)/shard_map/ppermute | solution.py:32
  20.6 7.9 %collective-permute-done.2 = f32[64,64]{1,0:T(8,128)S(1)} collective-permute-done((f32[64,64]{1,0:T(8,128)S(1)}, f32[64,64]{1,0:T(8,128)S(1)}, u32[]{:S(2)}, u32[]{:S(2)}) %collective-permute-start.2) | collective-permute-done | bytes 16416 | tf_op jit(solution)/shard_map/ppermute | solution.py:32
  28.6 3.4 %collective-permute-start.5 = (bf16[64,64]{1,0:T(8,128)(2,1)S(1)}, bf16[64,64]{1,0:T(8,128)(2,1)S(1)}, u32[]{:S(2)}, u32[]{:S(2)}) collective-permute-start(bf16[64,64]{1,0:T(8,128)(2,1)S(1)} %add_convert_fusion), channel_id=1, source_target_pairs={{0,12},{4,0},{8,4},{12,8},{1,13},{5,1},{9,5},{13,9},{2,14},{6,2},{... | collective-permute-start | bytes 24584 | tf_op jit(solution)/shard_map/ppermute | solution.py:32
  32.0 1.4 %collective-permute-done.5 = bf16[64,64]{1,0:T(8,128)(2,1)S(1)} collective-permute-done((bf16[64,64]{1,0:T(8,128)(2,1)S(1)}, bf16[64,64]{1,0:T(8,128)(2,1)S(1)}, u32[]{:S(2)}, u32[]{:S(2)}) %collective-permute-start.5) | collective-permute-done | bytes 8224 | tf_op jit(solution)/shard_map/ppermute | solution.py:32
  33.7 0.8 copy.19.coupling_list
  34.4 2.2 %collective-permute-done.4 = bf16[64,64]{1,0:T(8,128)(2,1)S(1)} collective-permute-done((bf16[64,64]{1,0:T(8,128)(2,1)S(1)}, bf16[64,64]{1,0:T(8,128)(2,1)S(1)}, u32[]{:S(2)}, u32[]{:S(2)}) %collective-permute-start.4) | collective-permute-done | bytes 8224 | tf_op jit(solution)/shard_map/ppermute | solution.py:32
  36.6 2.1 %collective-permute-start = (bf16[16,3,256]{2,1,0:T(4,128)(2,1)S(1)}, bf16[16,3,256]{2,1,0:T(4,128)(2,1)S(1)}, u32[]{:S(2)}, u32[]{:S(2)}) collective-permute-start(bf16[16,3,256]{2,1,0:T(4,128)(2,1)S(1)} %copy.15.own), channel_id=1, source_target_pairs={{0,2},{2,4},{4,6},{6,8},{8,10},{10,12},{12,14},{14,0},{1,3},{3,5},... | collective-permute-start | bytes 73736 | tf_op jit(solution)/shard_map/ppermute | solution.py:32
  38.7 0.5 collective-permute-done.3
  39.2 3.7 %collective-permute-start.7 = (bf16[16,64,64]{2,1,0:T(8,128)(2,1)S(1)}, bf16[16,64,64]{2,1,0:T(8,128)(2,1)S(1)}, u32[]{:S(2)}, u32[]{:S(2)}) collective-permute-start(bf16[16,64,64]{2,1,0:T(8,128)(2,1)S(1)} %get-tuple-element.19), channel_id=1, source_target_pairs={{0,14},{2,0},{4,2},{6,4},{8,6},{10,8},{12,10},{14,12},{1,15},{3,1}... | collective-permute-start | bytes 393224 | tf_op jit(solution)/shard_map/ppermute | solution.py:32
  43.0 0.3 collective-permute-done.prev
  43.3 0.9 copy-done.8
  44.2 6.4 %shard_map.141.refs_6_ = bf16[4,3072,256]{2,1,0:T(8,128)(2,1)S(1)} custom-call(s32[16,12]{1,0:T(8,128)S(1)} %copy-done.8, bf16[16,3,256]{2,1,0:T(4,128)(2,1)S(1)} %collective-permute-done.prev, bf16[16,3,256]{2,1,0:T(4,128)(2,1)S(1)} %copy.15.own, bf16[16,3,256]{2,1,0:T(4,128)(2,1)S(1)} %collective-permute-done.1.after), custom_call_target="tpu_custom_call" | custom-call | flops 125829120 | bytes 6291456 | tf_op jit(solution)/shard_map/pallas_call | solution.py:346
  50.5 6.4 %shard_map.142.refs_7_ = bf16[4,3072,256]{2,1,0:T(8,128)(2,1)S(1)} custom-call(s32[16,12]{1,0:T(8,128)S(1)} %copy-done.8, bf16[16,3,256]{2,1,0:T(4,128)(2,1)S(1)} %collective-permute-done.prev, bf16[16,3,256]{2,1,0:T(4,128)(2,1)S(1)} %copy.15.own, bf16[16,3,256]{2,1,0:T(4,128)(2,1)S(1)} %collective-permute-done.1.after), custom_call_target="tpu_custom_call" | custom-call | flops 125829120 | bytes 6291456 | tf_op jit(solution)/shard_map/pallas_call | solution.py:346
  57.0 5.3 %shard_map.143.base = f32[16,64,256]{2,1,0:T(8,128)S(1)} custom-call(s32[1,4]{1,0:T(1,128)S(1)} %copy-done.15, s32[16,8]{1,0:T(8,128)S(1)} %copy.19.coupling_list, bf16[4,64,64]{2,1,0:T(8,128)(2,1)S(1)} %pad_maximum_fusion.tops, bf16[1,4,64,64]{3,2,1,0:T(8,128)(2,1)S(1)} %copy-done.10, bf16[1,64,64]{2,1,0:T(8,128)(2,1)S(1)} %copy-done.12, ...), custom_call_target="tpu_custom_call" | custom-call | flops 109051904 | bytes 8388608 | tf_op jit(solution)/shard_map/pallas_call | solution.py:360
  62.4 0.4 collective-permute-start.9
  63.0 1.4 %collective-permute-done.9.refs_1_ = bf16[16,64,256]{2,1,0:T(8,128)(2,1)S(1)} collective-permute-done((bf16[16,64,256]{2,1,0:T(8,128)(2,1)S(1)}, bf16[16,64,256]{2,1,0:T(8,128)(2,1)S(1)}, u32[]{:S(2)}, u32[]{:S(2)}) %collective-permute-start.9) | collective-permute-done | bytes 524320 | tf_op jit(solution)/shard_map/ppermute | solution.py:36
  64.4 0.7 collective-permute-done.12.refs_5_
  65.1 4.0 %shard_map.144 = (f32[8,64,256]{2,1,0:T(8,128)S(1)}, bf16[8,64,256]{2,1,0:T(8,128)(2,1)S(1)}) custom-call(s32[16,12]{1,0:T(8,128)S(1)} %copy-done.9, bf16[16,64,256]{2,1,0:T(8,128)(2,1)S(1)} %collective-permute-done.8.refs_0_, bf16[16,64,256]{2,1,0:T(8,128)(2,1)S(1)} %collective-permute-done.9.refs_1_, bf16[16,64,256]{2,1,0:T(8,128)(2,1)S(1)} %copy-done.1, ...), custom_call_target="tpu_custom_call" | custom-call | flops 1610612736 | bytes 12582912 | tf_op jit(solution)/shard_map/pallas_call | solution.py:385
  69.1 0.4 collective-permute-start.13
  69.5 1.2 %collective-permute-done.13.received = bf16[8,64,256]{2,1,0:T(8,128)(2,1)S(1)} collective-permute-done((bf16[8,64,256]{2,1,0:T(8,128)(2,1)S(1)}, bf16[8,64,256]{2,1,0:T(8,128)(2,1)S(1)}, u32[]{:S(2)}, u32[]{:S(2)}) %collective-permute-start.13) | collective-permute-done | bytes 262176 | tf_op jit(solution)/shard_map/ppermute | solution.py:36
  70.7 1.3 %shard_map.145 = (f32[16,64,256]{2,1,0:T(8,128)}, f32[8,8,128]{2,1,0:T(8,128)S(1)}) custom-call(f32[1,64]{1,0:T(1,128)S(1)} %bitcast.5, f32[16,64,256]{2,1,0:T(8,128)S(1)} %shard_map.143.base, f32[8,64,256]{2,1,0:T(8,128)S(1)} %get-tuple-element.22.kept, bf16[8,64,256]{2,1,0:T(8,128)(2,1)S(1)} %collective-permute-done.13.received, f32[16,64,256]{2,1,0:T(8,128)S(1)} %copy-done.3), custom_call_target="tpu_custom_call" | custom-call | flops 4194304 | bytes 5242880 | tf_op jit(solution)/shard_map/pallas_call | solution.py:411
  72.0 12.3 %all_to_all.5.norms = f32[8,8,128]{2,1,0:T(8,128)S(1)} all-to-all(f32[8,8,128]{2,1,0:T(8,128)S(1)} %get-tuple-element.25), channel_id=1, replica_groups=mesh['groups'=2,'blk'=4,'leaf'=2,'sample'=2] {'blk','leaf'}, dimensions={0} | all-to-all | bytes 65536 | tf_op jit(solution)/shard_map/all_to_all | solution.py:420
  84.3 1.2 %copy-done.4 = f32[16,64,256]{2,1,0:T(8,128)S(1)} copy-done((f32[16,64,256]{2,1,0:T(8,128)S(1)}, f32[16,64,256]{2,1,0:T(8,128)}, u32[]{:S(2)}) %copy-start.4) | copy-done | bytes 1048600
  85.5 0.9 %shard_map.146 = bf16[16,64,256]{2,1,0:T(8,128)(2,1)} custom-call(f32[8,8,128]{2,1,0:T(8,128)S(1)} %all_to_all.5.norms, f32[16,64,256]{2,1,0:T(8,128)S(1)} %copy-done.4, bf16[16,64,256]{2,1,0:T(8,128)(2,1)S(1)} %copy-done.1), custom_call_target="tpu_custom_call" | custom-call | flops 1048576 | bytes 2097152 | tf_op jit(solution)/shard_map/pallas_call | solution.py:421
  (40 shorter events, 0.5 us)
Async XLA Ops:
  0.6 61.7 %collective-permute-start.11 = (bf16[16,64,256]{2,1,0:T(8,128)(2,1)}, bf16[16,64,256]{2,1,0:T(8,128)(2,1)S(1)}, u32[]{:S(2)}, u32[]{:S(2)}) collective-permute-start(bf16[16,64,256]{2,1,0:T(8,128)(2,1)} %direction.5), channel_id=1, source_target_pairs={{0,14},{2,0},{4,2},{6,4},{8,6},{10,8},{12,10},{14,12},{1,15},{3,1}... | collective-permute-start | bytes 1572872 | tf_op jit(solution)/shard_map/ppermute | solution.py:32
  6.7 55.7 %collective-permute-start.8 = (bf16[16,64,256]{2,1,0:T(8,128)(2,1)}, bf16[16,64,256]{2,1,0:T(8,128)(2,1)S(1)}, u32[]{:S(2)}, u32[]{:S(2)}) collective-permute-start(bf16[16,64,256]{2,1,0:T(8,128)(2,1)} %direction.5), channel_id=1, source_target_pairs={{0,2},{2,4},{4,6},{6,8},{8,10},{10,12},{12,14},{14,0},{1,3},{3,5},... | collective-permute-start | bytes 1572872 | tf_op jit(solution)/shard_map/ppermute | solution.py:32
  6.7 1.1 %copy-start = (bf16[16,64,256]{2,1,0:T(8,128)(2,1)S(1)}, bf16[16,64,256]{2,1,0:T(8,128)(2,1)}, u32[]{:S(2)}) copy-start(bf16[16,64,256]{2,1,0:T(8,128)(2,1)} %direction.5) | copy-start | bytes 1572868
  7.8 0.9 %copy-start.5 = (bf16[16,64,64]{2,1,0:T(8,128)(2,1)S(1)}, bf16[16,64,64]{2,1,0:T(8,128)(2,1)}, u32[]{:S(2)}) copy-start(bf16[16,64,64]{2,1,0:T(8,128)(2,1)} %leaf_transfer.3) | copy-start | bytes 393220
  8.7 1.0 %copy-start.7 = (bf16[16,64,256]{2,1,0:T(8,128)(2,1)S(1)}, bf16[16,64,256]{2,1,0:T(8,128)(2,1)}, u32[]{:S(2)}) copy-start(bf16[16,64,256]{2,1,0:T(8,128)(2,1)} %basis.1) | copy-start | bytes 1572868
  9.8 0.7 copy-start.11
  10.5 0.7 copy-start.13
  15.1 13.4 %collective-permute-start.2 = (f32[64,64]{1,0:T(8,128)S(1)}, f32[64,64]{1,0:T(8,128)S(1)}, u32[]{:S(2)}, u32[]{:S(2)}) collective-permute-start(f32[64,64]{1,0:T(8,128)S(1)} %get-tuple-element.16), channel_id=1, source_target_pairs={{0,2},{2,0},{1,3},{3,1},{4,6},{6,4},{5,7},{7,5},{8,10},{10,8},{9,1... | collective-permute-start | bytes 49160 | tf_op jit(solution)/shard_map/ppermute | solution.py:32
  15.9 27.1 %collective-permute-start.1 = (bf16[16,3,256]{2,1,0:T(4,128)(2,1)S(1)}, bf16[16,3,256]{2,1,0:T(4,128)(2,1)S(1)}, u32[]{:S(2)}, u32[]{:S(2)}) collective-permute-start(bf16[16,3,256]{2,1,0:T(4,128)(2,1)S(1)} %copy.15.own), channel_id=1, source_target_pairs={{0,14},{2,0},{4,2},{6,4},{8,6},{10,8},{12,10},{14,12},{1,15},{3,1}... | collective-permute-start | bytes 73736 | tf_op jit(solution)/shard_map/ppermute | solution.py:32
  28.6 4.8 %collective-permute-start.5 = (bf16[64,64]{1,0:T(8,128)(2,1)S(1)}, bf16[64,64]{1,0:T(8,128)(2,1)S(1)}, u32[]{:S(2)}, u32[]{:S(2)}) collective-permute-start(bf16[64,64]{1,0:T(8,128)(2,1)S(1)} %add_convert_fusion), channel_id=1, source_target_pairs={{0,12},{4,0},{8,4},{12,8},{1,13},{5,1},{9,5},{13,9},{2,14},{6,2},{... | collective-permute-start | bytes 24584 | tf_op jit(solution)/shard_map/ppermute | solution.py:32
  31.9 4.6 %collective-permute-start.4 = (bf16[64,64]{1,0:T(8,128)(2,1)S(1)}, bf16[64,64]{1,0:T(8,128)(2,1)S(1)}, u32[]{:S(2)}, u32[]{:S(2)}) collective-permute-start(bf16[64,64]{1,0:T(8,128)(2,1)S(1)} %add_convert_fusion), channel_id=1, source_target_pairs={{0,8},{4,12},{8,0},{12,4},{1,9},{5,13},{9,1},{13,5},{2,10},{6,14},... | collective-permute-start | bytes 24584 | tf_op jit(solution)/shard_map/ppermute | solution.py:32
  33.4 5.8 %collective-permute-start.3 = (bf16[64,64]{1,0:T(8,128)(2,1)S(1)}, bf16[64,64]{1,0:T(8,128)(2,1)S(1)}, u32[]{:S(2)}, u32[]{:S(2)}) collective-permute-start(bf16[64,64]{1,0:T(8,128)(2,1)S(1)} %add_convert_fusion), channel_id=1, source_target_pairs={{0,4},{4,8},{8,12},{12,0},{1,5},{5,9},{9,13},{13,1},{2,6},{6,10},{... | collective-permute-start | bytes 24584 | tf_op jit(solution)/shard_map/ppermute | solution.py:32
  36.6 6.7 %collective-permute-start = (bf16[16,3,256]{2,1,0:T(4,128)(2,1)S(1)}, bf16[16,3,256]{2,1,0:T(4,128)(2,1)S(1)}, u32[]{:S(2)}, u32[]{:S(2)}) collective-permute-start(bf16[16,3,256]{2,1,0:T(4,128)(2,1)S(1)} %copy.15.own), channel_id=1, source_target_pairs={{0,2},{2,4},{4,6},{6,8},{8,10},{10,12},{12,14},{14,0},{1,3},{3,5},... | collective-permute-start | bytes 73736 | tf_op jit(solution)/shard_map/ppermute | solution.py:32
  39.2 17.8 %collective-permute-start.7 = (bf16[16,64,64]{2,1,0:T(8,128)(2,1)S(1)}, bf16[16,64,64]{2,1,0:T(8,128)(2,1)S(1)}, u32[]{:S(2)}, u32[]{:S(2)}) collective-permute-start(bf16[16,64,64]{2,1,0:T(8,128)(2,1)S(1)} %get-tuple-element.19), channel_id=1, source_target_pairs={{0,14},{2,0},{4,2},{6,4},{8,6},{10,8},{12,10},{14,12},{1,15},{3,1}... | collective-permute-start | bytes 393224 | tf_op jit(solution)/shard_map/ppermute | solution.py:32
  42.9 14.0 %collective-permute-start.6 = (bf16[16,64,64]{2,1,0:T(8,128)(2,1)S(1)}, bf16[16,64,64]{2,1,0:T(8,128)(2,1)S(1)}, u32[]{:S(2)}, u32[]{:S(2)}) collective-permute-start(bf16[16,64,64]{2,1,0:T(8,128)(2,1)S(1)} %get-tuple-element.19), channel_id=1, source_target_pairs={{0,2},{2,4},{4,6},{6,8},{8,10},{10,12},{12,14},{14,0},{1,3},{3,5},... | collective-permute-start | bytes 393224 | tf_op jit(solution)/shard_map/ppermute | solution.py:32
  42.9 14.0 %copy-start.10 = (bf16[1,4,64,64]{3,2,1,0:T(8,128)(2,1)S(1)}, bf16[1,4,64,64]{3,2,1,0:T(8,128)(2,1)}, u32[]{:S(2)}) copy-start(bf16[1,4,64,64]{3,2,1,0:T(8,128)(2,1)} %top_coupling.1) | copy-start | bytes 98308
  42.9 14.0 %copy-start.12 = (bf16[1,64,64]{2,1,0:T(8,128)(2,1)S(1)}, bf16[1,64,64]{2,1,0:T(8,128)(2,1)}, u32[]{:S(2)}) copy-start(bf16[1,64,64]{2,1,0:T(8,128)(2,1)} %node_transfer.3) | copy-start | bytes 24580
  43.0 14.0 %copy-start.15 = (s32[1,4]{1,0:T(1,128)S(1)}, s32[1,4]{1,0:T(1,128)}, u32[]{:S(2)}) copy-start(s32[1,4]{1,0:T(1,128)} %top_list) | copy-start | bytes 52
  43.0 14.0 %copy-start.1 = (bf16[16,64,256]{2,1,0:T(8,128)(2,1)S(1)}, bf16[16,64,256]{2,1,0:T(8,128)(2,1)}, u32[]{:S(2)}) copy-start(bf16[16,64,256]{2,1,0:T(8,128)(2,1)} %direction.5) | copy-start | bytes 1572868
  43.0 14.0 %copy-start.2 = (bf16[16,8,64,64]{3,2,1,0:T(8,128)(2,1)S(1)}, bf16[16,8,64,64]{3,2,1,0:T(8,128)(2,1)}, u32[]{:S(2)}) copy-start(bf16[16,8,64,64]{3,2,1,0:T(8,128)(2,1)} %coupling.1) | copy-start | bytes 3145732
  43.0 14.0 %copy-start.6 = (bf16[16,64,64]{2,1,0:T(8,128)(2,1)S(1)}, bf16[16,64,64]{2,1,0:T(8,128)(2,1)}, u32[]{:S(2)}) copy-start(bf16[16,64,64]{2,1,0:T(8,128)(2,1)} %leaf_transfer.3) | copy-start | bytes 393220
  43.3 19.7 %collective-permute-start.10 = (bf16[16,64,256]{2,1,0:T(8,128)(2,1)}, bf16[16,64,256]{2,1,0:T(8,128)(2,1)S(1)}, u32[]{:S(2)}, u32[]{:S(2)}) collective-permute-start(bf16[16,64,256]{2,1,0:T(8,128)(2,1)} %direction.5), channel_id=1, source_target_pairs={{0,1},{1,0},{2,3},{3,2},{4,5},{5,4},{6,7},{7,6},{8,9},{9,8},{10,11... | collective-permute-start | bytes 1572872 | tf_op jit(solution)/shard_map/ppermute | solution.py:36
  43.3 0.9 copy-start.8
  50.5 14.6 %copy-start.9 = (s32[16,12]{1,0:T(8,128)S(1)}, s32[16,12]{1,0:T(8,128)}, u32[]{:S(2)}) copy-start(s32[16,12]{1,0:T(8,128)} %near.3) | copy-start | bytes 2308
  62.3 8.4 %copy-start.3 = (f32[16,64,256]{2,1,0:T(8,128)S(1)}, f32[16,64,256]{2,1,0:T(8,128)}, u32[]{:S(2)}) copy-start(f32[16,64,256]{2,1,0:T(8,128)} %residual.1) | copy-start | bytes 3145732
  62.4 8.4 %copy-start.14 = (f32[64]{0:T(128)S(1)}, f32[64]{0:T(128)}, u32[]{:S(2)}) copy-start(f32[64]{0:T(128)} %param.15) | copy-start | bytes 772
  62.4 2.0 %collective-permute-start.9 = (bf16[16,64,256]{2,1,0:T(8,128)(2,1)S(1)}, bf16[16,64,256]{2,1,0:T(8,128)(2,1)S(1)}, u32[]{:S(2)}, u32[]{:S(2)}) collective-permute-start(bf16[16,64,256]{2,1,0:T(8,128)(2,1)S(1)} %collective-permute-done.8.refs_0_), channel_id=1, source_target_pairs={{0,1},{1,0},{2,3},{3,2},{4,5},{5,4},{6,7},{7,6},{8,9},{9,8},{10,11... | collective-permute-start | bytes 1572872 | tf_op jit(solution)/shard_map/ppermute | solution.py:36
  62.8 2.3 %collective-permute-start.12 = (bf16[16,64,256]{2,1,0:T(8,128)(2,1)S(1)}, bf16[16,64,256]{2,1,0:T(8,128)(2,1)S(1)}, u32[]{:S(2)}, u32[]{:S(2)}) collective-permute-start(bf16[16,64,256]{2,1,0:T(8,128)(2,1)S(1)} %collective-permute-done.11.refs_4_), channel_id=1, source_target_pairs={{0,1},{1,0},{2,3},{3,2},{4,5},{5,4},{6,7},{7,6},{8,9},{9,8},{10,11... | collective-permute-start | bytes 1572872 | tf_op jit(solution)/shard_map/ppermute | solution.py:36
  69.1 1.6 %collective-permute-start.13 = (bf16[8,64,256]{2,1,0:T(8,128)(2,1)S(1)}, bf16[8,64,256]{2,1,0:T(8,128)(2,1)S(1)}, u32[]{:S(2)}, u32[]{:S(2)}) collective-permute-start(bf16[8,64,256]{2,1,0:T(8,128)(2,1)S(1)} %get-tuple-element.23), channel_id=1, source_target_pairs={{0,1},{1,0},{2,3},{3,2},{4,5},{5,4},{6,7},{7,6},{8,9},{9,8},{10,11... | collective-permute-start | bytes 786440 | tf_op jit(solution)/shard_map/ppermute | solution.py:36
  84.3 1.2 %copy-start.4 = (f32[16,64,256]{2,1,0:T(8,128)S(1)}, f32[16,64,256]{2,1,0:T(8,128)}, u32[]{:S(2)}) copy-start(f32[16,64,256]{2,1,0:T(8,128)} %get-tuple-element.12.updated) | copy-start | bytes 3145732

commit v3 on v2

--- a/solution.py
+++ b/solution.py
@@ -47,6 +47,10 @@
     return jnp.sum(jnp.where(here, row, 0.0), axis=1, keepdims=True)
 
 
+def in_hbm(*arrays):
+    return [pltpu.with_memory_space_constraint(array, pltpu.HBM) for array in arrays]
+
+
 def thirds(value):
     high = value.astype(BF).astype(F32)
     rest = value - high
@@ -72,19 +76,55 @@
     )
 
 
-def up_kernel(order, basis, direction, leaf_transfer, node_transfer, natural, coef, lifted):
+def up_kernel(order_h, basis_h, direction_h, transfer_h, node_h, natural_h, coef, lifted, mark, *scratch):
+    mark[...] = jnp.zeros_like(mark)
+    order, basis, direction, leaf_transfer, node_transfer, natural, sems = scratch
     leaves, rank, points = basis.shape
     samples = direction.shape[1]
+    chunks = sems.shape[1]
+    size = leaves // chunks
+    whole = [
+        pltpu.make_async_copy(order_h, order, sems.at[3, 0]),
+        pltpu.make_async_copy(node_h, node_transfer, sems.at[3, 1]),
+    ]
+    copies = []
+    for c in range(chunks):
+        part = pl.ds(c * size, size)
+        copies.append(
+            [
+                pltpu.make_async_copy(source.at[part], target.at[part], sems.at[i, c])
+                for i, (source, target) in enumerate(
+                    ((basis_h, basis), (direction_h, direction), (transfer_h, leaf_transfer))
+                )
+            ]
+        )
+    for copy in whole + sum(copies, []):
+        copy.start()
+    for copy in whole:
+        copy.wait()
     rows = lax.broadcasted_iota(jnp.int32, (points, points), 0)
     node = jnp.zeros((samples, rank), F32)
+    leaving = []
     for g in range(leaves):
+        if g % size == 0:
+            for copy in copies[g // size]:
+                copy.wait()
         place = jnp.where(rows == order[g : g + 1, :], 1.0, 0.0).astype(BF)
         own = nt(basis[g], place).astype(BF)
         natural[g] = own
         weights = nt(direction[g], own).astype(BF)
         coef[g] = weights
         node = node + nt(weights, leaf_transfer[g])
+        if g % size == size - 1:
+            part = pl.ds(g + 1 - size, size)
+            copy = pltpu.make_async_copy(
+                natural.at[part], natural_h.at[part], sems.at[4, g // size]
+            )
+            copy.start()
+            leaving.append(copy)
     lifted[...] = nt(node.astype(BF), node_transfer[0])
+    for copy in leaving:
+        copy.wait()
 
 
 def features(offsets):
@@ -112,7 +152,10 @@
     ).astype(BF)
 
 
-def tile_kernel(start, near, prev, own, after, tiles, spread_x):
+def tile_kernel(start, near_h, prev, own, after, tiles, mark, spread_x, near, sem):
+    listed = pltpu.make_async_copy(near_h, near, sem)
+    listed.start()
+    mark[...] = jnp.zeros_like(mark)
     count = tiles.shape[0]
     entries = near.shape[1]
     points = own.shape[2]
@@ -123,6 +166,7 @@
     for side, ref in enumerate((prev, own, after)):
         for j in range(leaves):
             spread_x[side * leaves + j] = spread_features(ref[j].astype(F32))
+    listed.wait()
     row = lax.broadcasted_iota(jnp.int32, (16, points), 0)
     lane = lax.broadcasted_iota(jnp.int32, (1, 128), 1)
 
@@ -160,35 +204,48 @@
     lax.fori_loop(0, count, leaf, 0)
 
 
-def down_kernel(
-    top_list,
-    coupling_list,
-    tops,
-    top_coupling,
-    node_transfer,
-    leaf_transfer,
-    before,
-    after,
-    coupling,
-    natural,
-    direction,
-    base,
-    window,
-):
+def down_kernel(*refs):
+    tops, before, after = refs[:3]
+    sources, base, targets, sems = refs[3:11], refs[11], refs[12:21], refs[21]
+    window, targets = targets[0], targets[1:]
+    top_list, coupling_list, top_coupling, node_transfer = targets[:4]
+    leaf_transfer, coupling, natural, direction = targets[4:]
     leaves, samples, points = direction.shape
     rank = natural.shape[1]
     clusters = lax.axis_size("blk")
     here = lax.axis_index("blk")
     total = leaves * clusters * lax.axis_size("leaf")
     anchor = (here * lax.axis_size("leaf") + lax.axis_index("leaf") - 1) * leaves
-    window[:leaves] = before[...]
-    window[leaves:] = after[...]
+    pairs = [(before, window.at[:leaves]), (after, window.at[leaves:])]
+    pairs += list(zip(sources[:4], targets[:4]))
+    whole = [
+        pltpu.make_async_copy(source, target, sems.at[0, i])
+        for i, (source, target) in enumerate(pairs)
+    ]
+    chunks = 4
+    size = leaves // chunks
+    parts = []
+    for c in range(chunks):
+        part = pl.ds(c * size, size)
+        parts.append(
+            [
+                pltpu.make_async_copy(source.at[part], target.at[part], sems.at[1 + c, i])
+                for i, (source, target) in enumerate(zip(sources[4:], targets[4:]))
+            ]
+        )
+    for copy in whole + sum(parts, []):
+        copy.start()
+    for copy in whole:
+        copy.wait()
     incoming = jnp.zeros((samples, rank), F32)
     for e in range(top_list.shape[1]):
         place = lax.rem(here - top_list[0, e] + clusters, clusters)
         incoming = incoming + nt(tops[place], top_coupling[0, e])
     down = nn(incoming.astype(BF), node_transfer[0]).astype(BF)
     for g in range(leaves):
+        if g % size == 0:
+            for copy in parts[g // size]:
+                copy.wait()
         inward = nn(down, leaf_transfer[g])
         for c in range(coupling_list.shape[1]):
             slot = lax.rem(coupling_list[g, c] - anchor + 2 * total, total)
@@ -199,14 +256,15 @@
         base[g] = NUGGET * direction[g].astype(F32) + far
 
 
-def near_kernel(near, *refs):
-    pieces, tiles, (kept, given, window, sems) = refs[:6], refs[6:-4], refs[-4:]
+def near_kernel(near_h, *refs):
+    pieces, tiles, (kept, given, mark, window, near, sems) = refs[:6], refs[6:-6], refs[-6:]
+    mark[...] = jnp.zeros_like(mark)
     leaves = window.shape[0] // 3
     samples = kept.shape[1]
     total = leaves * lax.axis_size("blk") * lax.axis_size("leaf")
     device = lax.axis_index("blk") * lax.axis_size("leaf") + lax.axis_index("leaf")
     anchor = (device - 1) * leaves
-    copies = []
+    copies = [pltpu.make_async_copy(near_h, near, sems.at[6])]
     for i, piece in enumerate(pieces):
         side, columns = i // 2, i % 2
         copies.append(
@@ -240,12 +298,30 @@
         at += part.shape[0]
 
 
-def residual_kernel(step, base, kept, received, residual, updated, norms):
+def residual_kernel(step, base, kept, received, residual_h, updated_h, updated, norms, *scratch):
+    residual, sems = scratch
     half = kept.shape[0]
+    chunks = sems.shape[1]
+    size = half // chunks
+    arrivals, leaving = [], []
+    for c in range(chunks):
+        for k in range(2):
+            part = pl.ds(k * half + c * size, size)
+            arrivals.append(
+                pltpu.make_async_copy(residual_h.at[part], residual.at[part], sems.at[k, c])
+            )
+            leaving.append(
+                pltpu.make_async_copy(updated.at[part], updated_h.at[part], sems.at[2 + k, c])
+            )
+    for copy in arrivals:
+        copy.start()
     core = lax.axis_index("sample")
     steps = column(step[...])
     totals = [jnp.zeros((step.shape[1], 1), F32)] * 2
     for i in range(half):
+        if i % size == 0:
+            for k in range(2):
+                arrivals[2 * (i // size) + k].wait()
         for theirs in range(2):
             g = (core ^ theirs) * half + i
             near = received[i].astype(F32) if theirs else kept[i]
@@ -254,6 +330,9 @@
             updated[g] = new
             for k, value in enumerate((old, new)):
                 totals[k] = totals[k] + jnp.sum(value * value, axis=1, keepdims=True)
+        if i % size == size - 1:
+            for k in range(2):
+                leaving[2 * (i // size) + k].start()
     samples = steps.shape[0]
     lane = lax.broadcasted_iota(jnp.int32, (samples, 128), 1)
     sub = lax.broadcasted_iota(jnp.int32, (samples, 128), 0)
@@ -262,6 +341,8 @@
     packed = jnp.where(row == 0, rows[0], jnp.where(row == 1, rows[1], 0.0))
     for i in range(norms.shape[0]):
         norms[i] = packed
+    for copy in leaving:
+        copy.wait()
 
 
 def direction_kernel(norms, updated, direction, result, held, sems):
@@ -305,118 +386,143 @@
     blk_count = lax.axis_size("blk")
     leaf_count = lax.axis_size("leaf")
     shape = jax.ShapeDtypeStruct
-    smem = pl.BlockSpec(memory_space=pltpu.SMEM)
+    token = shape((8, 128), F32)
     vmem = pl.BlockSpec(memory_space=pltpu.VMEM)
     anywhere = pl.BlockSpec(memory_space=pl.ANY)
+    hbm = pl.BlockSpec(memory_space=pltpu.HBM)
 
     coords_prev = shifted(coords, RING, 1)
     coords_after = shifted(coords, RING, -1)
-    direction_prev = shifted(direction, RING, 1)
-    direction_after = shifted(direction, RING, -1)
+    travelling, first = lax.optimization_barrier((direction, order, coords_prev, coords_after))[:2]
+    direction_prev = shifted(travelling, RING, 1)
+    direction_after = shifted(travelling, RING, -1)
     direction_other = partner(direction)
 
-    natural, coef, lifted = call(
+    natural, coef, lifted, up_mark = call(
         up_kernel,
         (
-            shape((leaves, rank, points), BF),
+            pltpu.HBM((leaves, rank, points), BF),
             shape((leaves, samples, rank), BF),
             shape((samples, rank), F32),
+            token,
         ),
         4 * leaves * rank * points * points,
         6 * MIB,
-        in_specs=[vmem] * 5,
-        out_specs=(vmem,) * 3,
-    )(order, basis, direction, leaf_transfer, node_transfer)
-
-    coef_prev = shifted(coef, RING, 1)
-    coef_after = shifted(coef, RING, -1)
-    top = lifted
-    for by in range(1, leaf_count):
-        top = top + shifted(lifted, "leaf", by)
-    top = top.astype(BF)
-    if blk_count <= 8:
-        tops = jnp.stack([top] + [shifted(top, "blk", by) for by in range(1, blk_count)])
-    else:
-        tops = lax.all_gather(top[None], "blk", axis=0, tiled=True)
-        places = jnp.mod(lax.axis_index("blk") - jnp.arange(blk_count, dtype=jnp.int32), blk_count)
-        tops = tops[places]
+        in_specs=[hbm] * 5,
+        out_specs=(hbm, vmem, vmem, vmem),
+        scratch_shapes=[
+            pltpu.VMEM(order.shape, jnp.int32),
+            pltpu.VMEM(basis.shape, BF),
+            pltpu.VMEM(direction.shape, BF),
+            pltpu.VMEM(leaf_transfer.shape, BF),
+            pltpu.VMEM(node_transfer.shape, BF),
+            pltpu.VMEM(basis.shape, BF),
+            pltpu.SemaphoreType.DMA((5, 4)),
+        ],
+        vmem=8,
+    )(*in_hbm(first, basis, direction, leaf_transfer, node_transfer))
 
     def make_tiles(start, near):
         count = half // 2
         return call(
             functools.partial(tile_kernel, start),
-            shape((count, entries * points, points), BF),
+            (shape((count, entries * points, points), BF), token),
             40 * count * entries * points * points,
             count * entries * points * points * 2,
-            in_specs=[smem] + [vmem] * 3,
-            out_specs=vmem,
-            scratch_shapes=[pltpu.VMEM((3 * leaves, points, 128), BF)],
-            vmem=16,
-        )(near, coords_prev, coords, coords_after)
-
-    tiles_low = make_tiles(0, ordered(near_list, natural))
-    tiles_high = make_tiles(half // 2, ordered(near_list, tiles_low, top))
-
+            in_specs=[hbm] + [vmem] * 3,
+            out_specs=(vmem, vmem),
+            scratch_shapes=[
+                pltpu.VMEM((3 * leaves, points, 128), BF),
+                pltpu.SMEM(near_list.shape, jnp.int32),
+                pltpu.SemaphoreType.DMA,
+            ],
+            vmem=8,
+        )(*in_hbm(near), coords_prev, coords, coords_after)
+
+    coef_prev = shifted(coef, RING, 1)
+    coef_after = shifted(coef, RING, -1)
+    terms = [shifted(lifted, "leaf", by) for by in range(1, leaf_count)]
+    tiles_low, low_mark = make_tiles(0, ordered(near_list, up_mark))
+    top = ordered(lifted, low_mark)
+    for term in terms:
+        top = top + term
+    top = top.astype(BF)
+    tiles_high, high_mark = make_tiles(
+        half // 2, ordered(near_list, low_mark, top, coef_prev, coef_after)
+    )
+    if blk_count <= 8:
+        others = [shifted(top, "blk", by) for by in range(1, blk_count)]
+    else:
+        others = lax.all_gather(top[None], "blk", axis=0, tiled=True)
+        places = jnp.mod(lax.axis_index("blk") - jnp.arange(blk_count, dtype=jnp.int32), blk_count)
+        others = list(others[places][1:])
+    direction_prev = ordered(direction_prev, high_mark, *others)
+    direction_after = ordered(direction_after, high_mark, *others)
+    kept, given, near_mark = call(
+        near_kernel,
+        (shape((half, samples, points), F32), shape((half, samples, points), BF), token),
+        4 * half * entries * samples * points * points,
+        half * entries * points * points * 2,
+        in_specs=[hbm] + [anywhere] * 6 + [vmem] * 2,
+        out_specs=(vmem,) * 3,
+        scratch_shapes=[
+            pltpu.VMEM((3 * leaves, 2 * samples, points), BF),
+            pltpu.SMEM(near_list.shape, jnp.int32),
+            pltpu.SemaphoreType.DMA((7,)),
+        ],
+        vmem=8,
+    )(
+        *in_hbm(near_list),
+        direction_prev,
+        partner(direction_prev),
+        *in_hbm(direction),
+        direction_other,
+        direction_after,
+        partner(direction_after),
+        tiles_low,
+        tiles_high,
+    )
+    tops = jnp.stack([top] + [ordered(other, near_mark) for other in others])
+    arrays = (
+        ordered(top_list, near_mark),
+        coupling_list,
+        top_coupling,
+        node_transfer,
+        leaf_transfer,
+        coupling,
+        natural,
+        direction,
+    )
+    spaces = (pltpu.SMEM,) * 2 + (pltpu.VMEM,) * 6
     base = call(
         down_kernel,
         shape((leaves, samples, points), F32),
         2 * leaves * samples * rank * (points + 9 * rank),
         8 * MIB,
-        in_specs=[smem] * 2 + [vmem] * 9,
+        in_specs=[vmem] + [hbm] * 10,
         out_specs=vmem,
-        scratch_shapes=[pltpu.VMEM((2 * leaves, samples, rank), BF)],
-        vmem=16,
-    )(
-        ordered(top_list, tiles_high),
-        coupling_list,
-        tops,
-        top_coupling,
-        node_transfer,
-        leaf_transfer,
-        coef_prev,
-        coef_after,
-        coupling,
-        natural,
-        direction,
-    )
-
-    direction_prev = ordered(direction_prev, base)
-    direction_after = ordered(direction_after, base)
-    kept, given = call(
-        near_kernel,
-        (shape((half, samples, points), F32), shape((half, samples, points), BF)),
-        4 * half * entries * samples * points * points,
-        half * entries * points * points * 2,
-        in_specs=[smem] + [anywhere] * 6 + [vmem] * 2,
-        out_specs=(vmem, vmem),
-        scratch_shapes=[
-            pltpu.VMEM((3 * leaves, 2 * samples, points), BF),
-            pltpu.SemaphoreType.DMA((6,)),
-        ],
-        vmem=16,
-    )(
-        near_list,
-        direction_prev,
-        partner(direction_prev),
-        direction,
-        direction_other,
-        direction_after,
-        partner(direction_after),
-        tiles_low,
-        tiles_high,
-    )
+        scratch_shapes=[pltpu.VMEM((2 * leaves, samples, rank), BF)]
+        + [space(array.shape, array.dtype) for space, array in zip(spaces, arrays)]
+        + [pltpu.SemaphoreType.DMA((5, 6))],
+        vmem=10,
+    )(tops, *in_hbm(coef_prev, coef_after, *arrays))
     received = partner(given)
 
     devices = blk_count * leaf_count
-    residual_next, norms = call(
+    whole = shape((leaves, samples, points), F32)
+    residual_next, updated, norms = call(
         residual_kernel,
-        (shape((leaves, samples, points), F32), shape((devices, 8, 128), F32)),
+        (whole, whole, shape((devices, 8, 128), F32)),
         4 * MIB,
         5 * MIB,
-        in_specs=[vmem] * 5,
-        out_specs=(vmem, vmem),
-        vmem=16,
-    )(step[None, :], base, kept, received, residual)
+        in_specs=[vmem] * 4 + [hbm],
+        out_specs=(hbm, vmem, vmem),
+        scratch_shapes=[
+            pltpu.VMEM((leaves, samples, points), F32),
+            pltpu.SemaphoreType.DMA((4, 2)),
+        ],
+        vmem=8,
+    )(step[None, :], base, kept, received, *in_hbm(residual))
     norms = lax.all_to_all(norms, RING, 0, 0)
     direction_next = call(
         direction_kernel,
@@ -429,8 +535,8 @@
             pltpu.VMEM((leaves, samples, points), BF),
             pltpu.SemaphoreType.DMA((4,)),
         ],
-        vmem=16,
-    )(norms, residual_next, direction)
+        vmem=8,
+    )(norms, updated, direction)
     return (residual_next, direction_next)
 
 

time: 87 us -> 85.2 us (0.979)
  local copies, waits for them, and re-layouts: 8.19 us -> 1.42 us
  Pallas kernels: 28.2 us -> 33.2 us
  blocking collectives: 12.3 us -> 11 us
  waiting for transfers between devices: 15.7 us -> 16.6 us
    unnamed x34 -> x12, local copies, waits for them, and re-layouts: 8.19 us -> 1.42 us
    pallas_call x4, Pallas kernels: 18 us -> 21.2 us  [the longest x2 12.4 us: make_tiles(): call(functools.partial(tile_kernel, start), (shape((count, entries * poin...]
    ppermute x10, waiting for transfers between devices: 12.3 us -> 13.9 us  [shifted(): lax.ppermute(array, axis, [(i, (i + by) % count) for i in range(count)])]
    all_to_all x1, blocking collectives: 12.3 us -> 11 us  [on_device(): norms = lax.all_to_all(norms, RING, 0, 0)]
    pallas_call x1, Pallas kernels: 5.3 us -> 6.39 us  [on_device(): call(down_kernel, shape((leaves, samples, points), F32), 2 * leaves * sam...]
  transfers between devices with their start and end apart: 14 -> 14, of which waited for: 8 -> 6; matrix products, arithmetic and copies ran while one was open for 2% -> 1% of each run, Pallas kernels for 25% -> 30%
where the time goes in v3:
time: 85.2 us; the launch traced here: 84.8 us
  Pallas kernels  33.2 us (39%)
  starting transfers between devices  21.7 us (25%)
  waiting for transfers between devices  16.6 us (19%)
  blocking collectives  11 us (13%)
  local copies, waits for them, and re-layouts  1.42 us (2%)
    ppermute x10, starting transfers between devices, shifted(): lax.ppermute(array, axis, [(i, (i + by) % count) for i in range(count)])  20.8 us
    ppermute x10, waiting for transfers between devices, shifted(): lax.ppermute(array, axis, [(i, (i + by) % count) for i in range(count)])  13.9 us
    pallas_call x2, Pallas kernels, make_tiles(): call(functools.partial(tile_kernel, start), (shape((count, entries * poin...  12.4 us
    all_to_all x1, blocking collectives, on_device(): norms = lax.all_to_all(norms, RING, 0, 0)  11 us
    pallas_call x1, Pallas kernels, on_device(): call(up_kernel, (pltpu.HBM((leaves, rank, points), BF), shape((leaves, sa...  6.46 us
    pallas_call x1, Pallas kernels, on_device(): call(down_kernel, shape((leaves, samples, points), F32), 2 * leaves * sam...  6.39 us
    pallas_call x1, Pallas kernels, on_device(): call(near_kernel, (shape((half, samples, points), F32), shape((half, samp...  4.73 us
    ppermute x4, waiting for transfers between devices, partner(): return lax.ppermute(array, 'sample', [(0, 1), (1, 0)])  2.73 us
  transfers between devices with their start and end apart: 14, of which 6 were waited for; matrix products, arithmetic and copies ran while one was open for 1% of the time, Pallas kernels for 30%

profile of v3, /device:TPU:0, one launch (start us, length us, event | category | flops | bytes accessed | tf_op | source)
XLA Modules:
  0.0 84.8 jit_solution(125815362544539749)
XLA Ops:
  0.6 0.8 copy.15.own
  1.4 3.0 %collective-permute-start = (bf16[16,3,256]{2,1,0:T(4,128)(2,1)S(1)}, bf16[16,3,256]{2,1,0:T(4,128)(2,1)S(1)}, u32[]{:S(2)}, u32[]{:S(2)}) collective-permute-start(bf16[16,3,256]{2,1,0:T(4,128)(2,1)S(1)} %copy.15.own), channel_id=1, source_target_pairs={{0,2},{2,4},{4,6},{6,8},{8,10},{10,12},{12,14},{14,0},{1,3},{3,5},... | collective-permute-start | bytes 73736 | tf_op jit(solution)/shard_map/ppermute | solution.py:32
  4.4 3.1 %collective-permute-start.1 = (bf16[16,3,256]{2,1,0:T(4,128)(2,1)S(1)}, bf16[16,3,256]{2,1,0:T(4,128)(2,1)S(1)}, u32[]{:S(2)}, u32[]{:S(2)}) collective-permute-start(bf16[16,3,256]{2,1,0:T(4,128)(2,1)S(1)} %copy.15.own), channel_id=1, source_target_pairs={{0,14},{2,0},{4,2},{6,4},{8,6},{10,8},{12,10},{14,12},{1,15},{3,1}... | collective-permute-start | bytes 73736 | tf_op jit(solution)/shard_map/ppermute | solution.py:32
  7.5 1.8 %collective-permute-done.prev = bf16[16,3,256]{2,1,0:T(4,128)(2,1)S(1)} collective-permute-done((bf16[16,3,256]{2,1,0:T(4,128)(2,1)S(1)}, bf16[16,3,256]{2,1,0:T(4,128)(2,1)S(1)}, u32[]{:S(2)}, u32[]{:S(2)}) %collective-permute-start) | collective-permute-done | bytes 24608 | tf_op jit(solution)/shard_map/ppermute | solution.py:32
  9.3 4.8 %collective-permute-start.11 = (bf16[16,64,256]{2,1,0:T(8,128)(2,1)}, bf16[16,64,256]{2,1,0:T(8,128)(2,1)S(1)}, u32[]{:S(2)}, u32[]{:S(2)}) collective-permute-start(bf16[16,64,256]{2,1,0:T(8,128)(2,1)} %direction.1), channel_id=1, source_target_pairs={{0,14},{2,0},{4,2},{6,4},{8,6},{10,8},{12,10},{14,12},{1,15},{3,1}... | collective-permute-start | bytes 1572872 | tf_op jit(solution)/shard_map/ppermute | solution.py:32
  14.1 6.5 %shard_map.140 = (bf16[16,64,256]{2,1,0:T(8,128)(2,1)}, bf16[16,64,64]{2,1,0:T(8,128)(2,1)S(1)}, f32[64,64]{1,0:T(8,128)S(1)}, f32[8,128]{1,0:T(8,128)}) custom-call(s32[16,256]{1,0:T(8,128)} %order_h, bf16[16,64,256]{2,1,0:T(8,128)(2,1)} %basis_h.1, bf16[16,64,256]{2,1,0:T(8,128)(2,1)} %direction.1, bf16[16,64,64]{2,1,0:T(8,128)(2,1)} %refs_7_.1, ...), custom_call_target="tpu_custom_call" | custom-call | flops 268435456 | bytes 6291456 | tf_op jit(solution)/shard_map/pallas_call | solution.py:401
  20.6 0.1 collective-permute-start.2
  20.6 2.0 %collective-permute-start.5 = (bf16[16,64,64]{2,1,0:T(8,128)(2,1)S(1)}, bf16[16,64,64]{2,1,0:T(8,128)(2,1)S(1)}, u32[]{:S(2)}, u32[]{:S(2)}) collective-permute-start(bf16[16,64,64]{2,1,0:T(8,128)(2,1)S(1)} %get-tuple-element.30), channel_id=1, source_target_pairs={{0,2},{2,4},{4,6},{6,8},{8,10},{10,12},{12,14},{14,0},{1,3},{3,5},... | collective-permute-start | bytes 393224 | tf_op jit(solution)/shard_map/ppermute | solution.py:32
  22.7 2.8 %collective-permute-start.6 = (bf16[16,64,64]{2,1,0:T(8,128)(2,1)S(1)}, bf16[16,64,64]{2,1,0:T(8,128)(2,1)S(1)}, u32[]{:S(2)}, u32[]{:S(2)}) collective-permute-start(bf16[16,64,64]{2,1,0:T(8,128)(2,1)S(1)} %get-tuple-element.30), channel_id=1, source_target_pairs={{0,14},{2,0},{4,2},{6,4},{8,6},{10,8},{12,10},{14,12},{1,15},{3,1}... | collective-permute-start | bytes 393224 | tf_op jit(solution)/shard_map/ppermute | solution.py:32
  25.5 6.2 %shard_map.141 = (bf16[4,3072,256]{2,1,0:T(8,128)(2,1)S(1)}, f32[8,128]{1,0:T(8,128)}) custom-call(s32[16,12]{1,0:T(8,128)} %near_h.3, bf16[16,3,256]{2,1,0:T(4,128)(2,1)S(1)} %collective-permute-done.prev, bf16[16,3,256]{2,1,0:T(4,128)(2,1)S(1)} %copy.15.own, bf16[16,3,256]{2,1,0:T(4,128)(2,1)S(1)} %collective-permute-done.1.after), custom_call_target="tpu_custom_call" | custom-call | flops 125829120 | bytes 6291456 | tf_op jit(solution)/shard_map/pallas_call | solution.py:427
  31.7 10.3 %collective-permute-done.2 = f32[64,64]{1,0:T(8,128)S(1)} collective-permute-done((f32[64,64]{1,0:T(8,128)S(1)}, f32[64,64]{1,0:T(8,128)S(1)}, u32[]{:S(2)}, u32[]{:S(2)}) %collective-permute-start.2) | collective-permute-done | bytes 16416 | tf_op jit(solution)/shard_map/ppermute | solution.py:32
  42.0 1.0 %collective-permute-start.3 = (bf16[64,64]{1,0:T(8,128)(2,1)S(1)}, bf16[64,64]{1,0:T(8,128)(2,1)S(1)}, u32[]{:S(2)}, u32[]{:S(2)}) collective-permute-start(bf16[64,64]{1,0:T(8,128)(2,1)S(1)} %add_convert_fusion), channel_id=1, source_target_pairs={{0,4},{4,8},{8,12},{12,0},{1,5},{5,9},{9,13},{13,1},{2,6},{6,10},{... | collective-permute-start | bytes 24584 | tf_op jit(solution)/shard_map/ppermute | solution.py:32
  43.0 1.8 %collective-permute-done.5.refs_1_ = bf16[16,64,64]{2,1,0:T(8,128)(2,1)S(1)} collective-permute-done((bf16[16,64,64]{2,1,0:T(8,128)(2,1)S(1)}, bf16[16,64,64]{2,1,0:T(8,128)(2,1)S(1)}, u32[]{:S(2)}, u32[]{:S(2)}) %collective-permute-start.5) | collective-permute-done | bytes 131104 | tf_op jit(solution)/shard_map/ppermute | solution.py:32
  44.8 1.7 %collective-permute-start.7 = (bf16[64,64]{1,0:T(8,128)(2,1)S(1)}, bf16[64,64]{1,0:T(8,128)(2,1)S(1)}, u32[]{:S(2)}, u32[]{:S(2)}) collective-permute-start(bf16[64,64]{1,0:T(8,128)(2,1)S(1)} %add_convert_fusion), channel_id=1, source_target_pairs={{0,8},{4,12},{8,0},{12,4},{1,9},{5,13},{9,1},{13,5},{2,10},{6,14},... | collective-permute-start | bytes 24584 | tf_op jit(solution)/shard_map/ppermute | solution.py:32
  46.5 2.3 %collective-permute-start.8 = (bf16[64,64]{1,0:T(8,128)(2,1)S(1)}, bf16[64,64]{1,0:T(8,128)(2,1)S(1)}, u32[]{:S(2)}, u32[]{:S(2)}) collective-permute-start(bf16[64,64]{1,0:T(8,128)(2,1)S(1)} %add_convert_fusion), channel_id=1, source_target_pairs={{0,12},{4,0},{8,4},{12,8},{1,13},{5,1},{9,5},{13,9},{2,14},{6,2},{... | collective-permute-start | bytes 24584 | tf_op jit(solution)/shard_map/ppermute | solution.py:32
  48.8 6.2 %shard_map.142 = (bf16[4,3072,256]{2,1,0:T(8,128)(2,1)S(1)}, f32[8,128]{1,0:T(8,128)}) custom-call(s32[16,12]{1,0:T(8,128)} %near_h.3, bf16[16,3,256]{2,1,0:T(4,128)(2,1)S(1)} %collective-permute-done.prev, bf16[16,3,256]{2,1,0:T(4,128)(2,1)S(1)} %copy.15.own, bf16[16,3,256]{2,1,0:T(4,128)(2,1)S(1)} %collective-permute-done.1.after), custom_call_target="tpu_custom_call" | custom-call | flops 125829120 | bytes 6291456 | tf_op jit(solution)/shard_map/pallas_call | solution.py:427
  55.1 0.1 collective-permute-start.10
  55.2 0.0 collective-permute-done.8
  55.2 0.0 collective-permute-done.11.refs_4_
  55.2 0.5 collective-permute-start.12
  55.7 0.1 collective-permute-start.9
  55.8 1.4 %collective-permute-done.10.refs_3_ = bf16[16,64,256]{2,1,0:T(8,128)(2,1)S(1)} collective-permute-done((bf16[16,64,256]{2,1,0:T(8,128)(2,1)}, bf16[16,64,256]{2,1,0:T(8,128)(2,1)S(1)}, u32[]{:S(2)}, u32[]{:S(2)}) %collective-permute-start.10) | collective-permute-done | bytes 524320 | tf_op jit(solution)/shard_map/ppermute | solution.py:36
  57.2 0.5 collective-permute-done.12.refs_5_
  57.8 0.7 collective-permute-done.9.refs_1_
  58.5 4.7 %shard_map.143 = (f32[8,64,256]{2,1,0:T(8,128)S(1)}, bf16[8,64,256]{2,1,0:T(8,128)(2,1)S(1)}, f32[8,128]{1,0:T(8,128)}) custom-call(s32[16,12]{1,0:T(8,128)} %near_h.3, bf16[16,64,256]{2,1,0:T(8,128)(2,1)S(1)} %collective-permute-done.4.refs_0_, bf16[16,64,256]{2,1,0:T(8,128)(2,1)S(1)} %collective-permute-done.9.refs_1_, bf16[16,64,256]{2,1,0:T(8,128)(2,1)} %direction.1, ...), custom_call_target="tpu_custom_call" | custom-call | flops 1610612736 | bytes 12582912 | tf_op jit(solution)/shard_map/pallas_call | solution.py:461
  63.3 0.0 copy-start
  63.3 0.2 collective-permute-start.13
  63.5 0.6 copy.19.refs_4_
  64.2 6.4 %shard_map.144.base = f32[16,64,256]{2,1,0:T(8,128)S(1)} custom-call(bf16[4,64,64]{2,1,0:T(8,128)(2,1)S(1)} %pad_maximum_fusion.refs_0_, bf16[16,64,64]{2,1,0:T(8,128)(2,1)} %copy-done.2, bf16[16,64,64]{2,1,0:T(8,128)(2,1)} %copy-done.3, s32[1,4]{1,0:T(1,128)} %refs_3_, s32[16,8]{1,0:T(8,128)} %copy.19.refs_4_, bf16[1,4,64,64]{3,2,1,0:T(8,128)(2,1)} %refs_5_.1, ...), custom_call_target="tpu_custom_call" | custom-call | flops 109051904 | bytes 8388608 | tf_op jit(solution)/shard_map/pallas_call | solution.py:497
  70.6 2.3 %shard_map.145 = (f32[16,64,256]{2,1,0:T(8,128)}, f32[16,64,256]{2,1,0:T(8,128)S(1)}, f32[8,8,128]{2,1,0:T(8,128)S(1)}) custom-call(f32[1,64]{1,0:T(1,128)S(1)} %bitcast.5, f32[16,64,256]{2,1,0:T(8,128)S(1)} %shard_map.144.base, f32[8,64,256]{2,1,0:T(8,128)S(1)} %get-tuple-element.43.kept, bf16[8,64,256]{2,1,0:T(8,128)(2,1)S(1)} %collective-permute-done.13.received, ...), custom_call_target="tpu_custom_call" | custom-call | flops 4194304 | bytes 5242880 | tf_op jit(solution)/shard_map/pallas_call | solution.py:513
  72.9 11.0 %all_to_all.5.norms = f32[8,8,128]{2,1,0:T(8,128)S(1)} all-to-all(f32[8,8,128]{2,1,0:T(8,128)S(1)} %get-tuple-element.46), channel_id=1, replica_groups=mesh['groups'=2,'blk'=4,'leaf'=2,'sample'=2] {'blk','leaf'}, dimensions={0} | all-to-all | bytes 65536 | tf_op jit(solution)/shard_map/all_to_all | solution.py:526
  83.9 0.9 %shard_map.146 = bf16[16,64,256]{2,1,0:T(8,128)(2,1)} custom-call(f32[8,8,128]{2,1,0:T(8,128)S(1)} %all_to_all.5.norms, f32[16,64,256]{2,1,0:T(8,128)S(1)} %get-tuple-element.47.updated, bf16[16,64,256]{2,1,0:T(8,128)(2,1)S(1)} %copy-done), custom_call_target="tpu_custom_call" | custom-call | flops 1048576 | bytes 2097152 | tf_op jit(solution)/shard_map/pallas_call | solution.py:527
  (18 shorter events, 0.1 us)
Async XLA Ops:
  1.4 7.9 %collective-permute-start = (bf16[16,3,256]{2,1,0:T(4,128)(2,1)S(1)}, bf16[16,3,256]{2,1,0:T(4,128)(2,1)S(1)}, u32[]{:S(2)}, u32[]{:S(2)}) collective-permute-start(bf16[16,3,256]{2,1,0:T(4,128)(2,1)S(1)} %copy.15.own), channel_id=1, source_target_pairs={{0,2},{2,4},{4,6},{6,8},{8,10},{10,12},{12,14},{14,0},{1,3},{3,5},... | collective-permute-start | bytes 73736 | tf_op jit(solution)/shard_map/ppermute | solution.py:32
  4.4 4.9 %collective-permute-start.1 = (bf16[16,3,256]{2,1,0:T(4,128)(2,1)S(1)}, bf16[16,3,256]{2,1,0:T(4,128)(2,1)S(1)}, u32[]{:S(2)}, u32[]{:S(2)}) collective-permute-start(bf16[16,3,256]{2,1,0:T(4,128)(2,1)S(1)} %copy.15.own), channel_id=1, source_target_pairs={{0,14},{2,0},{4,2},{6,4},{8,6},{10,8},{12,10},{14,12},{1,15},{3,1}... | collective-permute-start | bytes 73736 | tf_op jit(solution)/shard_map/ppermute | solution.py:32
  9.3 45.9 %collective-permute-start.11 = (bf16[16,64,256]{2,1,0:T(8,128)(2,1)}, bf16[16,64,256]{2,1,0:T(8,128)(2,1)S(1)}, u32[]{:S(2)}, u32[]{:S(2)}) collective-permute-start(bf16[16,64,256]{2,1,0:T(8,128)(2,1)} %direction.1), channel_id=1, source_target_pairs={{0,14},{2,0},{4,2},{6,4},{8,6},{10,8},{12,10},{14,12},{1,15},{3,1}... | collective-permute-start | bytes 1572872 | tf_op jit(solution)/shard_map/ppermute | solution.py:32
  14.1 41.6 %collective-permute-start.4 = (bf16[16,64,256]{2,1,0:T(8,128)(2,1)}, bf16[16,64,256]{2,1,0:T(8,128)(2,1)S(1)}, u32[]{:S(2)}, u32[]{:S(2)}) collective-permute-start(bf16[16,64,256]{2,1,0:T(8,128)(2,1)} %direction.1), channel_id=1, source_target_pairs={{0,2},{2,4},{4,6},{6,8},{8,10},{10,12},{12,14},{14,0},{1,3},{3,5},... | collective-permute-start | bytes 1572872 | tf_op jit(solution)/shard_map/ppermute | solution.py:32
  20.6 21.4 %collective-permute-start.2 = (f32[64,64]{1,0:T(8,128)S(1)}, f32[64,64]{1,0:T(8,128)S(1)}, u32[]{:S(2)}, u32[]{:S(2)}) collective-permute-start(f32[64,64]{1,0:T(8,128)S(1)} %get-tuple-element.28), channel_id=1, source_target_pairs={{0,2},{2,0},{1,3},{3,1},{4,6},{6,4},{5,7},{7,5},{8,10},{10,8},{9,1... | collective-permute-start | bytes 49160 | tf_op jit(solution)/shard_map/ppermute | solution.py:32
  20.6 24.1 %collective-permute-start.5 = (bf16[16,64,64]{2,1,0:T(8,128)(2,1)S(1)}, bf16[16,64,64]{2,1,0:T(8,128)(2,1)S(1)}, u32[]{:S(2)}, u32[]{:S(2)}) collective-permute-start(bf16[16,64,64]{2,1,0:T(8,128)(2,1)S(1)} %get-tuple-element.30), channel_id=1, source_target_pairs={{0,2},{2,4},{4,6},{6,8},{8,10},{10,12},{12,14},{14,0},{1,3},{3,5},... | collective-permute-start | bytes 393224 | tf_op jit(solution)/shard_map/ppermute | solution.py:32
  22.7 23.8 %collective-permute-start.6 = (bf16[16,64,64]{2,1,0:T(8,128)(2,1)S(1)}, bf16[16,64,64]{2,1,0:T(8,128)(2,1)S(1)}, u32[]{:S(2)}, u32[]{:S(2)}) collective-permute-start(bf16[16,64,64]{2,1,0:T(8,128)(2,1)S(1)} %get-tuple-element.30), channel_id=1, source_target_pairs={{0,14},{2,0},{4,2},{6,4},{8,6},{10,8},{12,10},{14,12},{1,15},{3,1}... | collective-permute-start | bytes 393224 | tf_op jit(solution)/shard_map/ppermute | solution.py:32
  42.0 13.1 %collective-permute-start.3 = (bf16[64,64]{1,0:T(8,128)(2,1)S(1)}, bf16[64,64]{1,0:T(8,128)(2,1)S(1)}, u32[]{:S(2)}, u32[]{:S(2)}) collective-permute-start(bf16[64,64]{1,0:T(8,128)(2,1)S(1)} %add_convert_fusion), channel_id=1, source_target_pairs={{0,4},{4,8},{8,12},{12,0},{1,5},{5,9},{9,13},{13,1},{2,6},{6,10},{... | collective-permute-start | bytes 24584 | tf_op jit(solution)/shard_map/ppermute | solution.py:32
  44.8 18.5 %copy-start.2 = (bf16[16,64,64]{2,1,0:T(8,128)(2,1)}, bf16[16,64,64]{2,1,0:T(8,128)(2,1)S(1)}, u32[]{:S(2)}) copy-start(bf16[16,64,64]{2,1,0:T(8,128)(2,1)S(1)} %collective-permute-done.5.refs_1_) | copy-start | bytes 393220
  44.8 10.4 %collective-permute-start.7 = (bf16[64,64]{1,0:T(8,128)(2,1)S(1)}, bf16[64,64]{1,0:T(8,128)(2,1)S(1)}, u32[]{:S(2)}, u32[]{:S(2)}) collective-permute-start(bf16[64,64]{1,0:T(8,128)(2,1)S(1)} %add_convert_fusion), channel_id=1, source_target_pairs={{0,8},{4,12},{8,0},{12,4},{1,9},{5,13},{9,1},{13,5},{2,10},{6,14},... | collective-permute-start | bytes 24584 | tf_op jit(solution)/shard_map/ppermute | solution.py:32
  46.5 16.8 %copy-start.3 = (bf16[16,64,64]{2,1,0:T(8,128)(2,1)}, bf16[16,64,64]{2,1,0:T(8,128)(2,1)S(1)}, u32[]{:S(2)}) copy-start(bf16[16,64,64]{2,1,0:T(8,128)(2,1)S(1)} %collective-permute-done.6.refs_2_) | copy-start | bytes 393220
  46.5 8.7 %collective-permute-start.8 = (bf16[64,64]{1,0:T(8,128)(2,1)S(1)}, bf16[64,64]{1,0:T(8,128)(2,1)S(1)}, u32[]{:S(2)}, u32[]{:S(2)}) collective-permute-start(bf16[64,64]{1,0:T(8,128)(2,1)S(1)} %add_convert_fusion), channel_id=1, source_target_pairs={{0,12},{4,0},{8,4},{12,8},{1,13},{5,1},{9,5},{13,9},{2,14},{6,2},{... | collective-permute-start | bytes 24584 | tf_op jit(solution)/shard_map/ppermute | solution.py:32
  55.1 2.2 %collective-permute-start.10 = (bf16[16,64,256]{2,1,0:T(8,128)(2,1)}, bf16[16,64,256]{2,1,0:T(8,128)(2,1)S(1)}, u32[]{:S(2)}, u32[]{:S(2)}) collective-permute-start(bf16[16,64,256]{2,1,0:T(8,128)(2,1)} %direction.1), channel_id=1, source_target_pairs={{0,1},{1,0},{2,3},{3,2},{4,5},{5,4},{6,7},{7,6},{8,9},{9,8},{10,11... | collective-permute-start | bytes 1572872 | tf_op jit(solution)/shard_map/ppermute | solution.py:36
  55.2 2.6 %collective-permute-start.12 = (bf16[16,64,256]{2,1,0:T(8,128)(2,1)S(1)}, bf16[16,64,256]{2,1,0:T(8,128)(2,1)S(1)}, u32[]{:S(2)}, u32[]{:S(2)}) collective-permute-start(bf16[16,64,256]{2,1,0:T(8,128)(2,1)S(1)} %collective-permute-done.11.refs_4_), channel_id=1, source_target_pairs={{0,1},{1,0},{2,3},{3,2},{4,5},{5,4},{6,7},{7,6},{8,9},{9,8},{10,11... | collective-permute-start | bytes 1572872 | tf_op jit(solution)/shard_map/ppermute | solution.py:36
  55.7 2.8 %collective-permute-start.9 = (bf16[16,64,256]{2,1,0:T(8,128)(2,1)S(1)}, bf16[16,64,256]{2,1,0:T(8,128)(2,1)S(1)}, u32[]{:S(2)}, u32[]{:S(2)}) collective-permute-start(bf16[16,64,256]{2,1,0:T(8,128)(2,1)S(1)} %collective-permute-done.4.refs_0_), channel_id=1, source_target_pairs={{0,1},{1,0},{2,3},{3,2},{4,5},{5,4},{6,7},{7,6},{8,9},{9,8},{10,11... | collective-permute-start | bytes 1572872 | tf_op jit(solution)/shard_map/ppermute | solution.py:36
  58.5 5.0 %copy-start.4 = (s32[16,8]{0,1:T(8,128)S(1)}, s32[16,8]{0,1:T(8,128)}, u32[]{:S(2)}) copy-start(s32[16,8]{0,1:T(8,128)} %param.22) | copy-start | bytes 1540
  58.5 12.1 %copy-start.1 = (f32[64]{0:T(128)S(1)}, f32[64]{0:T(128)}, u32[]{:S(2)}) copy-start(f32[64]{0:T(128)} %param.15) | copy-start | bytes 772
  63.3 20.6 %copy-start = (bf16[16,64,256]{2,1,0:T(8,128)(2,1)S(1)}, bf16[16,64,256]{2,1,0:T(8,128)(2,1)}, u32[]{:S(2)}) copy-start(bf16[16,64,256]{2,1,0:T(8,128)(2,1)} %direction.1) | copy-start | bytes 1572868
  63.3 7.3 %collective-permute-start.13 = (bf16[8,64,256]{2,1,0:T(8,128)(2,1)S(1)}, bf16[8,64,256]{2,1,0:T(8,128)(2,1)S(1)}, u32[]{:S(2)}, u32[]{:S(2)}) collective-permute-start(bf16[8,64,256]{2,1,0:T(8,128)(2,1)S(1)} %get-tuple-element.44), channel_id=1, source_target_pairs={{0,1},{1,0},{2,3},{3,2},{4,5},{5,4},{6,7},{7,6},{8,9},{9,8},{10,11... | collective-permute-start | bytes 786440 | tf_op jit(solution)/shard_map/ppermute | solution.py:36

commit v4 on v3

--- a/solution.py
+++ b/solution.py
@@ -76,7 +76,7 @@
     )
 
 
-def up_kernel(order_h, basis_h, direction_h, transfer_h, node_h, natural_h, coef, lifted, mark, *scratch):
+def up_kernel(order_h, basis_h, direction_h, transfer_h, node_h, natural_h, coef, mark, *scratch):
     mark[...] = jnp.zeros_like(mark)
     order, basis, direction, leaf_transfer, node_transfer, natural, sems = scratch
     leaves, rank, points = basis.shape
@@ -113,7 +113,7 @@
         own = nt(basis[g], place).astype(BF)
         natural[g] = own
         weights = nt(direction[g], own).astype(BF)
-        coef[g] = weights
+        coef[g // 2, :, (g % 2) * rank : (g % 2 + 1) * rank] = weights
         node = node + nt(weights, leaf_transfer[g])
         if g % size == size - 1:
             part = pl.ds(g + 1 - size, size)
@@ -122,7 +122,9 @@
             )
             copy.start()
             leaving.append(copy)
-    lifted[...] = nt(node.astype(BF), node_transfer[0])
+    for i, part in enumerate(thirds(nt(node.astype(BF), node_transfer[0]))):
+        at = leaves + i
+        coef[at // 2, :, (at % 2) * rank : (at % 2 + 1) * rank] = part.astype(BF)
     for copy in leaving:
         copy.wait()
 
@@ -152,7 +154,11 @@
     ).astype(BF)
 
 
-def tile_kernel(start, near_h, prev, own, after, tiles, mark, spread_x, near, sem):
+def tile_kernel(start, near_h, _, own, *refs):
+    if start == 0:
+        prev, after, tiles, mark, spread_x, near, sem = refs
+    else:
+        spread_x, tiles, mark, near, sem = refs
     listed = pltpu.make_async_copy(near_h, near, sem)
     listed.start()
     mark[...] = jnp.zeros_like(mark)
@@ -163,9 +169,10 @@
     total = leaves * lax.axis_size("blk") * lax.axis_size("leaf")
     device = lax.axis_index("blk") * lax.axis_size("leaf") + lax.axis_index("leaf")
     anchor = (device - 1) * leaves
-    for side, ref in enumerate((prev, own, after)):
-        for j in range(leaves):
-            spread_x[side * leaves + j] = spread_features(ref[j].astype(F32))
+    if start == 0:
+        for side, ref in enumerate((prev, own, after)):
+            for j in range(leaves):
+                spread_x[side * leaves + j] = spread_features(ref[j].astype(F32))
     listed.wait()
     row = lax.broadcasted_iota(jnp.int32, (16, points), 0)
     lane = lax.broadcasted_iota(jnp.int32, (1, 128), 1)
@@ -204,9 +211,25 @@
     lax.fori_loop(0, count, leaf, 0)
 
 
+def top_kernel(own, *refs):
+    sides, top = refs[:-2], refs[-1]
+    samples, rank = top.shape
+    at = own.shape[0] - 2
+
+    def term(ref):
+        first, second = ref[at].astype(F32), ref[at + 1].astype(F32)
+        return first[:, :rank] + first[:, rank:] + second[:, :rank]
+
+    total = term(own)
+    if sides:
+        low = lax.axis_index("leaf") == 0
+        total = total + jnp.where(low, term(sides[1]), term(sides[0]))
+    top[...] = total.astype(top.dtype)
+
+
 def down_kernel(*refs):
-    tops, before, after = refs[:3]
-    sources, base, targets, sems = refs[3:11], refs[11], refs[12:21], refs[21]
+    tops, before, after, residual_h = refs[:4]
+    sources, (base, residual), targets, sems = refs[4:12], refs[13:15], refs[15:24], refs[24]
     window, targets = targets[0], targets[1:]
     top_list, coupling_list, top_coupling, node_transfer = targets[:4]
     leaf_transfer, coupling, natural, direction = targets[4:]
@@ -216,8 +239,7 @@
     here = lax.axis_index("blk")
     total = leaves * clusters * lax.axis_size("leaf")
     anchor = (here * lax.axis_size("leaf") + lax.axis_index("leaf") - 1) * leaves
-    pairs = [(before, window.at[:leaves]), (after, window.at[leaves:])]
-    pairs += list(zip(sources[:4], targets[:4]))
+    pairs = list(zip(sources[:4], targets[:4]))
     whole = [
         pltpu.make_async_copy(source, target, sems.at[0, i])
         for i, (source, target) in enumerate(pairs)
@@ -233,8 +255,13 @@
                 for i, (source, target) in enumerate(zip(sources[4:], targets[4:]))
             ]
         )
-    for copy in whole + sum(parts, []):
+    ahead = pltpu.make_async_copy(residual_h, residual, sems.at[0, 6])
+    for copy in whole + sum(parts, []) + [ahead]:
         copy.start()
+    for side, packed in enumerate((before, after)):
+        for g in range(leaves):
+            part = packed[g // 2, :, (g % 2) * rank : (g % 2 + 1) * rank]
+            window[side * leaves + g] = part
     for copy in whole:
         copy.wait()
     incoming = jnp.zeros((samples, rank), F32)
@@ -247,17 +274,21 @@
             for copy in parts[g // size]:
                 copy.wait()
         inward = nn(down, leaf_transfer[g])
+        rows = []
         for c in range(coupling_list.shape[1]):
             slot = lax.rem(coupling_list[g, c] - anchor + 2 * total, total)
             slot = jnp.where(slot >= 2 * leaves, slot - leaves, slot)
             slot = jnp.minimum(slot, 2 * leaves - 1)
-            inward = inward + nt(window[slot], coupling[g, c])
+            rows.append(window[slot])
+        columns = [coupling[g, c] for c in range(coupling_list.shape[1])]
+        inward = inward + nt(jnp.concatenate(rows, axis=1), jnp.concatenate(columns, axis=1))
         far = nn(inward.astype(BF), natural[g])
         base[g] = NUGGET * direction[g].astype(F32) + far
+    ahead.wait()
 
 
 def near_kernel(near_h, *refs):
-    pieces, tiles, (kept, given, mark, window, near, sems) = refs[:6], refs[6:-6], refs[-6:]
+    pieces, tiles, (kept, given, mark, window, near, sems) = refs[:6], refs[6:8], refs[-6:]
     mark[...] = jnp.zeros_like(mark)
     leaves = window.shape[0] // 3
     samples = kept.shape[1]
@@ -298,30 +329,21 @@
         at += part.shape[0]
 
 
-def residual_kernel(step, base, kept, received, residual_h, updated_h, updated, norms, *scratch):
-    residual, sems = scratch
+def residual_kernel(step, base, kept, received, residual, updated_h, updated, norms, sems):
     half = kept.shape[0]
     chunks = sems.shape[1]
     size = half // chunks
-    arrivals, leaving = [], []
+    leaving = []
     for c in range(chunks):
         for k in range(2):
             part = pl.ds(k * half + c * size, size)
-            arrivals.append(
-                pltpu.make_async_copy(residual_h.at[part], residual.at[part], sems.at[k, c])
+            leaving.append(
+                pltpu.make_async_copy(updated.at[part], updated_h.at[part], sems.at[k, c])
             )
-            leaving.append(
-                pltpu.make_async_copy(updated.at[part], updated_h.at[part], sems.at[2 + k, c])
-            )
-    for copy in arrivals:
-        copy.start()
     core = lax.axis_index("sample")
     steps = column(step[...])
     totals = [jnp.zeros((step.shape[1], 1), F32)] * 2
     for i in range(half):
-        if i % size == 0:
-            for k in range(2):
-                arrivals[2 * (i // size) + k].wait()
         for theirs in range(2):
             g = (core ^ theirs) * half + i
             near = received[i].astype(F32) if theirs else kept[i]
@@ -398,18 +420,17 @@
     direction_after = shifted(travelling, RING, -1)
     direction_other = partner(direction)
 
-    natural, coef, lifted, up_mark = call(
+    natural, coef, up_mark = call(
         up_kernel,
         (
             pltpu.HBM((leaves, rank, points), BF),
-            shape((leaves, samples, rank), BF),
-            shape((samples, rank), F32),
+            shape((leaves // 2 + 2, samples, 2 * rank), BF),
             token,
         ),
         4 * leaves * rank * points * points,
         6 * MIB,
         in_specs=[hbm] * 5,
-        out_specs=(hbm, vmem, vmem, vmem),
+        out_specs=(hbm, vmem, vmem),
         scratch_shapes=[
             pltpu.VMEM(order.shape, jnp.int32),
             pltpu.VMEM(basis.shape, BF),
@@ -422,42 +443,33 @@
         vmem=8,
     )(*in_hbm(first, basis, direction, leaf_transfer, node_transfer))
 
-    def make_tiles(start, near):
+    def make_tiles(start, done, *operands):
         count = half // 2
+        outs = (pltpu.VMEM((count, entries * points, points), BF), token)
+        if start == 0:
+            outs += (shape((3 * leaves, points, 128), BF),)
         return call(
             functools.partial(tile_kernel, start),
-            (shape((count, entries * points, points), BF), token),
+            outs,
             40 * count * entries * points * points,
             count * entries * points * points * 2,
-            in_specs=[hbm] + [vmem] * 3,
-            out_specs=(vmem, vmem),
+            in_specs=[hbm, anywhere] + [vmem] * len(operands),
+            out_specs=(vmem,) * len(outs),
             scratch_shapes=[
-                pltpu.VMEM((3 * leaves, points, 128), BF),
                 pltpu.SMEM(near_list.shape, jnp.int32),
                 pltpu.SemaphoreType.DMA,
             ],
             vmem=8,
-        )(*in_hbm(near), coords_prev, coords, coords_after)
+        )(*in_hbm(near_list), done, *operands)
 
     coef_prev = shifted(coef, RING, 1)
     coef_after = shifted(coef, RING, -1)
-    terms = [shifted(lifted, "leaf", by) for by in range(1, leaf_count)]
-    tiles_low, low_mark = make_tiles(0, ordered(near_list, up_mark))
-    top = ordered(lifted, low_mark)
-    for term in terms:
-        top = top + term
-    top = top.astype(BF)
-    tiles_high, high_mark = make_tiles(
-        half // 2, ordered(near_list, low_mark, top, coef_prev, coef_after)
-    )
-    if blk_count <= 8:
-        others = [shifted(top, "blk", by) for by in range(1, blk_count)]
-    else:
-        others = lax.all_gather(top[None], "blk", axis=0, tiled=True)
-        places = jnp.mod(lax.axis_index("blk") - jnp.arange(blk_count, dtype=jnp.int32), blk_count)
-        others = list(others[places][1:])
-    direction_prev = ordered(direction_prev, high_mark, *others)
-    direction_after = ordered(direction_after, high_mark, *others)
+    tiles_low, low_mark, spread_x = make_tiles(
+        0, up_mark, coords, coords_prev, coords_after
+    )
+    tiles_high, high_mark = make_tiles(half // 2, low_mark, coords, spread_x)
+    direction_prev = ordered(direction_prev, high_mark)
+    direction_after = ordered(direction_after, high_mark)
     kept, given, near_mark = call(
         near_kernel,
         (shape((half, samples, points), F32), shape((half, samples, points), BF), token),
@@ -482,9 +494,29 @@
         tiles_low,
         tiles_high,
     )
-    tops = jnp.stack([top] + [ordered(other, near_mark) for other in others])
+
+    paired = leaf_count == 2
+    top = call(
+        top_kernel,
+        shape((samples, rank), BF if paired else F32),
+        MIB,
+        MIB,
+        in_specs=[vmem] * (3 if paired else 1) + [anywhere],
+        out_specs=vmem,
+        vmem=4,
+    )(coef, *((coef_prev, coef_after) if paired else ()), near_mark)
+    if not paired:
+        terms = [shifted(top, "leaf", by) for by in range(1, leaf_count)]
+        top = sum(terms, top).astype(BF)
+    if blk_count <= 8:
+        others = [shifted(top, "blk", by) for by in range(1, blk_count)]
+    else:
+        others = lax.all_gather(top[None], "blk", axis=0, tiled=True)
+        places = jnp.mod(lax.axis_index("blk") - jnp.arange(blk_count, dtype=jnp.int32), blk_count)
+        others = list(others[places][1:])
+    tops = jnp.stack([top] + others)
     arrays = (
-        ordered(top_list, near_mark),
+        top_list,
         coupling_list,
         top_coupling,
         node_transfer,
@@ -494,35 +526,32 @@
         direction,
     )
     spaces = (pltpu.SMEM,) * 2 + (pltpu.VMEM,) * 6
-    base = call(
+    whole = shape((leaves, samples, points), F32)
+    base, residual_here = call(
         down_kernel,
-        shape((leaves, samples, points), F32),
+        (whole, whole),
         2 * leaves * samples * rank * (points + 9 * rank),
         8 * MIB,
-        in_specs=[vmem] + [hbm] * 10,
-        out_specs=vmem,
+        in_specs=[vmem] * 3 + [hbm] * 9 + [anywhere],
+        out_specs=(vmem, vmem),
         scratch_shapes=[pltpu.VMEM((2 * leaves, samples, rank), BF)]
         + [space(array.shape, array.dtype) for space, array in zip(spaces, arrays)]
-        + [pltpu.SemaphoreType.DMA((5, 6))],
+        + [pltpu.SemaphoreType.DMA((5, 7))],
         vmem=10,
-    )(tops, *in_hbm(coef_prev, coef_after, *arrays))
+    )(tops, coef_prev, coef_after, *in_hbm(residual, *arrays), near_mark)
     received = partner(given)
 
     devices = blk_count * leaf_count
-    whole = shape((leaves, samples, points), F32)
     residual_next, updated, norms = call(
         residual_kernel,
         (whole, whole, shape((devices, 8, 128), F32)),
         4 * MIB,
         5 * MIB,
-        in_specs=[vmem] * 4 + [hbm],
+        in_specs=[vmem] * 5,
         out_specs=(hbm, vmem, vmem),
-        scratch_shapes=[
-            pltpu.VMEM((leaves, samples, points), F32),
-            pltpu.SemaphoreType.DMA((4, 2)),
-        ],
+        scratch_shapes=[pltpu.SemaphoreType.DMA((2, 4))],
         vmem=8,
-    )(step[None, :], base, kept, received, *in_hbm(residual))
+    )(step[None, :], base, kept, received, residual_here)
     norms = lax.all_to_all(norms, RING, 0, 0)
     direction_next = call(
         direction_kernel,

time: 85.2 us -> 70.3 us (0.83)
  waiting for transfers between devices: 16.6 us -> 8.13 us
  Pallas kernels: 33.2 us -> 28.7 us
  starting transfers between devices: 21.7 us -> 20.3 us
    ppermute x10 -> x9, waiting for transfers between devices: 13.9 us -> 8.12 us  [shifted(): lax.ppermute(array, axis, [(i, (i + by) % count) for i in range(count)])]
    pallas_call x4 -> x5, Pallas kernels: 25.3 us -> 22.1 us  [the longest x2 11.3 us: make_tiles(): call(functools.partial(tile_kernel, start), outs, 40 * count * entries *...]
    ppermute x4, waiting for transfers between devices: 2.73 us -> 0.01 us  [partner(): return lax.ppermute(array, 'sample', [(0, 1), (1, 0)])]
    ppermute x10 -> x9, starting transfers between devices: 20.8 us -> 19.7 us  [shifted(): lax.ppermute(array, axis, [(i, (i + by) % count) for i in range(count)])]
    pallas_call x1, Pallas kernels: 2.26 us -> 1.24 us  [on_device(): call(residual_kernel, (whole, whole, shape((devices, 8, 128), F32)), 4 *...]
  transfers between devices with their start and end apart: 14 -> 13, of which waited for: 6 -> 5; matrix products, arithmetic and copies ran while one was open for 1% -> 1% of each run, Pallas kernels for 30% -> 38%
where the time goes in v4:
time: 70.3 us; the launch traced here: 70 us
  Pallas kernels  28.7 us (41%)
  starting transfers between devices  20.3 us (29%)
  blocking collectives  10.6 us (15%)
  waiting for transfers between devices  8.13 us (12%)
  local copies, waits for them, and re-layouts  1.44 us (2%)
  between operations  0.76 us (1%)
    ppermute x9, starting transfers between devices, shifted(): lax.ppermute(array, axis, [(i, (i + by) % count) for i in range(count)])  19.7 us
    pallas_call x2, Pallas kernels, make_tiles(): call(functools.partial(tile_kernel, start), outs, 40 * count * entries *...  11.3 us
    all_to_all x1, blocking collectives, on_device(): norms = lax.all_to_all(norms, RING, 0, 0)  10.6 us
    ppermute x9, waiting for transfers between devices, shifted(): lax.ppermute(array, axis, [(i, (i + by) % count) for i in range(count)])  8.12 us
    pallas_call x1, Pallas kernels, on_device(): call(up_kernel, (pltpu.HBM((leaves, rank, points), BF), shape((leaves //...  5.94 us
    pallas_call x1, Pallas kernels, on_device(): call(down_kernel, (whole, whole), 2 * leaves * samples * rank * (points +...  4.79 us
    pallas_call x1, Pallas kernels, on_device(): call(near_kernel, (shape((half, samples, points), F32), shape((half, samp...  4.46 us
    unnamed x8, local copies, waits for them, and re-layouts  1.44 us
  transfers between devices with their start and end apart: 13, of which 5 were waited for; matrix products, arithmetic and copies ran while one was open for 1% of the time, Pallas kernels for 38%

profile of v4, /device:TPU:0, one launch (start us, length us, event | category | flops | bytes accessed | tf_op | source)
XLA Modules:
  0.0 70.0 jit_solution(6724268281612481895)
XLA Ops:
  0.6 0.8 %copy.15.own = bf16[16,3,256]{2,1,0:T(4,128)(2,1)S(1)} copy(bf16[16,3,256]{2,0,1:T(8,128)(2,1)} %param.16) | data formatting | bytes 49152 | tf_op args[3]
  1.4 3.0 %collective-permute-start = (bf16[16,3,256]{2,1,0:T(4,128)(2,1)S(1)}, bf16[16,3,256]{2,1,0:T(4,128)(2,1)S(1)}, u32[]{:S(2)}, u32[]{:S(2)}) collective-permute-start(bf16[16,3,256]{2,1,0:T(4,128)(2,1)S(1)} %copy.15.own), channel_id=1, source_target_pairs={{0,2},{2,4},{4,6},{6,8},{8,10},{10,12},{12,14},{14,0},{1,3},{3,5},... | collective-permute-start | bytes 73736 | tf_op jit(solution)/shard_map/ppermute | solution.py:32
  4.4 3.1 %collective-permute-start.1 = (bf16[16,3,256]{2,1,0:T(4,128)(2,1)S(1)}, bf16[16,3,256]{2,1,0:T(4,128)(2,1)S(1)}, u32[]{:S(2)}, u32[]{:S(2)}) collective-permute-start(bf16[16,3,256]{2,1,0:T(4,128)(2,1)S(1)} %copy.15.own), channel_id=1, source_target_pairs={{0,14},{2,0},{4,2},{6,4},{8,6},{10,8},{12,10},{14,12},{1,15},{3,1}... | collective-permute-start | bytes 73736 | tf_op jit(solution)/shard_map/ppermute | solution.py:32
  7.5 1.8 %collective-permute-done.refs_0_ = bf16[16,3,256]{2,1,0:T(4,128)(2,1)S(1)} collective-permute-done((bf16[16,3,256]{2,1,0:T(4,128)(2,1)S(1)}, bf16[16,3,256]{2,1,0:T(4,128)(2,1)S(1)}, u32[]{:S(2)}, u32[]{:S(2)}) %collective-permute-start) | collective-permute-done | bytes 24608 | tf_op jit(solution)/shard_map/ppermute | solution.py:32
  9.3 0.0 collective-permute-done.1.refs_1_
  9.3 4.8 %collective-permute-start.7 = (bf16[16,64,256]{2,1,0:T(8,128)(2,1)}, bf16[16,64,256]{2,1,0:T(8,128)(2,1)S(1)}, u32[]{:S(2)}, u32[]{:S(2)}) collective-permute-start(bf16[16,64,256]{2,1,0:T(8,128)(2,1)} %direction.1), channel_id=1, source_target_pairs={{0,14},{2,0},{4,2},{6,4},{8,6},{10,8},{12,10},{14,12},{1,15},{3,1}... | collective-permute-start | bytes 1572872 | tf_op jit(solution)/shard_map/ppermute | solution.py:32
  14.1 0.0 collective-permute-start.4
  14.1 0.0 collective-permute-start.6
  14.1 5.9 %shard_map.140 = (bf16[16,64,256]{2,1,0:T(8,128)(2,1)}, bf16[10,64,128]{2,1,0:T(8,128)(2,1)S(1)}, f32[8,128]{1,0:T(8,128)S(1)}) custom-call(s32[16,256]{1,0:T(8,128)} %order_h, bf16[16,64,256]{2,1,0:T(8,128)(2,1)} %basis_h.1, bf16[16,64,256]{2,1,0:T(8,128)(2,1)} %direction.1, bf16[16,64,64]{2,1,0:T(8,128)(2,1)} %refs_8_.1, bf16[1,64,64]{2,1,0:T(8,128)(2,1)} %refs_7_.1), custom_call_target="tpu_custom_call" | custom-call | flops 268435456 | bytes 6291456 | tf_op jit(solution)/shard_map/pallas_call | solution.py:423
  20.0 5.8 %shard_map.141 = (bf16[4,3072,256]{2,1,0:T(8,128)(2,1)S(1)}, f32[8,128]{1,0:T(8,128)S(1)}, bf16[48,256,128]{2,1,0:T(8,128)(2,1)S(1)}) custom-call(s32[16,12]{1,0:T(8,128)} %near_h.5, f32[8,128]{1,0:T(8,128)S(1)} %get-tuple-element.25._, bf16[16,3,256]{2,1,0:T(4,128)(2,1)S(1)} %copy.15.own, bf16[16,3,256]{2,1,0:T(4,128)(2,1)S(1)} %collective-permute-done.refs_0_, ...), custom_call_target="tpu_custom_call" | custom-call | flops 125829120 | bytes 6291456 | tf_op jit(solution)/shard_map/pallas_call | solution.py:451
  25.8 5.5 %shard_map.142 = (bf16[4,3072,256]{2,1,0:T(8,128)(2,1)S(1)}, f32[8,128]{1,0:T(8,128)}) custom-call(s32[16,12]{1,0:T(8,128)} %near_h.5, f32[8,128]{1,0:T(8,128)S(1)} %get-tuple-element.26._, bf16[16,3,256]{2,1,0:T(4,128)(2,1)S(1)} %copy.15.own, bf16[48,256,128]{2,1,0:T(8,128)(2,1)S(1)} %get-tuple-element.27.refs_0_), custom_call_target="tpu_custom_call" | custom-call | flops 125829120 | bytes 6291456 | tf_op jit(solution)/shard_map/pallas_call | solution.py:451
  31.4 2.3 %collective-permute-done.7.refs_4_ = bf16[16,64,256]{2,1,0:T(8,128)(2,1)S(1)} collective-permute-done((bf16[16,64,256]{2,1,0:T(8,128)(2,1)}, bf16[16,64,256]{2,1,0:T(8,128)(2,1)S(1)}, u32[]{:S(2)}, u32[]{:S(2)}) %collective-permute-start.7) | collective-permute-done | bytes 524320 | tf_op jit(solution)/shard_map/ppermute | solution.py:32
  33.7 0.5 collective-permute-start.5
  34.2 1.2 %collective-permute-start.2 = (bf16[10,64,128]{2,1,0:T(8,128)(2,1)S(1)}, bf16[10,64,128]{2,1,0:T(8,128)(2,1)S(1)}, u32[]{:S(2)}, u32[]{:S(2)}) collective-permute-start(bf16[10,64,128]{2,1,0:T(8,128)(2,1)S(1)} %get-tuple-element.23.own), channel_id=1, source_target_pairs={{0,2},{2,4},{4,6},{6,8},{8,10},{10,12},{12,14},{14,0},{1,3},{3,5},... | collective-permute-start | bytes 491528 | tf_op jit(solution)/shard_map/ppermute | solution.py:32
  35.3 3.6 %collective-permute-start.3 = (bf16[10,64,128]{2,1,0:T(8,128)(2,1)S(1)}, bf16[10,64,128]{2,1,0:T(8,128)(2,1)S(1)}, u32[]{:S(2)}, u32[]{:S(2)}) collective-permute-start(bf16[10,64,128]{2,1,0:T(8,128)(2,1)S(1)} %get-tuple-element.23.own), channel_id=1, source_target_pairs={{0,14},{2,0},{4,2},{6,4},{8,6},{10,8},{12,10},{14,12},{1,15},{3,1}... | collective-permute-start | bytes 491528 | tf_op jit(solution)/shard_map/ppermute | solution.py:32
  38.9 0.0 copy-start.2
  38.9 0.0 copy-start.1
  38.9 4.5 %shard_map.143 = (f32[8,64,256]{2,1,0:T(8,128)S(1)}, bf16[8,64,256]{2,1,0:T(8,128)(2,1)S(1)}, f32[8,128]{1,0:T(8,128)S(1)}) custom-call(s32[16,12]{1,0:T(8,128)} %near_h.5, bf16[16,64,256]{2,1,0:T(8,128)(2,1)S(1)} %collective-permute-done.4.refs_0_, bf16[16,64,256]{2,1,0:T(8,128)(2,1)S(1)} %collective-permute-done.5.refs_1_, bf16[16,64,256]{2,1,0:T(8,128)(2,1)} %direction.1, ...), custom_call_target="tpu_custom_call" | custom-call | flops 1610612736 | bytes 12582912 | tf_op jit(solution)/shard_map/pallas_call | solution.py:473
  43.4 0.0 copy-start
  43.4 0.1 collective-permute-start.12
  43.5 1.7 %collective-permute-done.3.refs_1_.refs_2_ = bf16[10,64,128]{2,1,0:T(8,128)(2,1)S(1)} collective-permute-done((bf16[10,64,128]{2,1,0:T(8,128)(2,1)S(1)}, bf16[10,64,128]{2,1,0:T(8,128)(2,1)S(1)}, u32[]{:S(2)}, u32[]{:S(2)}) %collective-permute-start.3) | collective-permute-done | bytes 163872 | tf_op jit(solution)/shard_map/ppermute | solution.py:32
  45.2 0.1 shard_map.144
  45.3 0.2 collective-permute-start.9
  45.4 3.2 %collective-permute-start.10 = (bf16[64,64]{1,0:T(8,128)(2,1)S(1)}, bf16[64,64]{1,0:T(8,128)(2,1)S(1)}, u32[]{:S(2)}, u32[]{:S(2)}) collective-permute-start(bf16[64,64]{1,0:T(8,128)(2,1)S(1)} %shard_map.144), channel_id=1, source_target_pairs={{0,8},{4,12},{8,0},{12,4},{1,9},{5,13},{9,1},{13,5},{2,10},{6,14},... | collective-permute-start | bytes 24584 | tf_op jit(solution)/shard_map/ppermute | solution.py:32
  48.6 0.8 %collective-permute-start.11 = (bf16[64,64]{1,0:T(8,128)(2,1)S(1)}, bf16[64,64]{1,0:T(8,128)(2,1)S(1)}, u32[]{:S(2)}, u32[]{:S(2)}) collective-permute-start(bf16[64,64]{1,0:T(8,128)(2,1)S(1)} %shard_map.144), channel_id=1, source_target_pairs={{0,12},{4,0},{8,4},{12,8},{1,13},{5,1},{9,5},{13,9},{2,14},{6,2},{... | collective-permute-start | bytes 24584 | tf_op jit(solution)/shard_map/ppermute | solution.py:32
  49.4 0.7 copy.19.refs_5_
  50.0 1.0 %collective-permute-done.9 = bf16[64,64]{1,0:T(8,128)(2,1)S(1)} collective-permute-done((bf16[64,64]{1,0:T(8,128)(2,1)S(1)}, bf16[64,64]{1,0:T(8,128)(2,1)S(1)}, u32[]{:S(2)}, u32[]{:S(2)}) %collective-permute-start.9) | collective-permute-done | bytes 8224 | tf_op jit(solution)/shard_map/ppermute | solution.py:32
  51.0 1.3 %collective-permute-done.11 = bf16[64,64]{1,0:T(8,128)(2,1)S(1)} collective-permute-done((bf16[64,64]{1,0:T(8,128)(2,1)S(1)}, bf16[64,64]{1,0:T(8,128)(2,1)S(1)}, u32[]{:S(2)}, u32[]{:S(2)}) %collective-permute-start.11) | collective-permute-done | bytes 8224 | tf_op jit(solution)/shard_map/ppermute | solution.py:32
  52.4 4.8 %shard_map.145 = (f32[16,64,256]{2,1,0:T(8,128)S(1)}, f32[16,64,256]{2,1,0:T(8,128)S(1)}) custom-call(bf16[4,64,64]{2,1,0:T(8,128)(2,1)S(1)} %pad_maximum_fusion.refs_0_, bf16[10,64,128]{2,1,0:T(8,128)(2,1)S(1)} %collective-permute-done.2.refs_0_.refs_1_, bf16[10,64,128]{2,1,0:T(8,128)(2,1)S(1)} %collective-permute-done.3.refs_1_.refs_2_, ...), custom_call_target="tpu_custom_call" | custom-call | flops 109051904 | bytes 8388608 | tf_op jit(solution)/shard_map/pallas_call | solution.py:530
  57.2 1.2 %shard_map.146 = (f32[16,64,256]{2,1,0:T(8,128)}, f32[16,64,256]{2,1,0:T(8,128)S(1)}, f32[8,8,128]{2,1,0:T(8,128)S(1)}) custom-call(f32[1,64]{1,0:T(1,128)S(1)} %bitcast.6, f32[16,64,256]{2,1,0:T(8,128)S(1)} %get-tuple-element.35.base, f32[8,64,256]{2,1,0:T(8,128)S(1)} %get-tuple-element.36.kept, bf16[8,64,256]{2,1,0:T(8,128)(2,1)S(1)} %collective-permute-done.12.received, ...), custom_call_target="tpu_custom_call" | custom-call | flops 4194304 | bytes 5242880 | tf_op jit(solution)/shard_map/pallas_call | solution.py:545
  58.5 10.6 %all_to_all.5.norms = f32[8,8,128]{2,1,0:T(8,128)S(1)} all-to-all(f32[8,8,128]{2,1,0:T(8,128)S(1)} %get-tuple-element.40), channel_id=1, replica_groups=mesh['groups'=2,'blk'=4,'leaf'=2,'sample'=2] {'blk','leaf'}, dimensions={0} | all-to-all | bytes 65536 | tf_op jit(solution)/shard_map/all_to_all | solution.py:555
  69.0 0.9 %shard_map.147 = bf16[16,64,256]{2,1,0:T(8,128)(2,1)} custom-call(f32[8,8,128]{2,1,0:T(8,128)S(1)} %all_to_all.5.norms, f32[16,64,256]{2,1,0:T(8,128)S(1)} %get-tuple-element.41.updated, bf16[16,64,256]{2,1,0:T(8,128)(2,1)S(1)} %copy-done), custom_call_target="tpu_custom_call" | custom-call | flops 1048576 | bytes 2097152 | tf_op jit(solution)/shard_map/pallas_call | solution.py:556
  (12 shorter events, 0.0 us)
Async XLA Ops:
  1.4 7.9 %collective-permute-start = (bf16[16,3,256]{2,1,0:T(4,128)(2,1)S(1)}, bf16[16,3,256]{2,1,0:T(4,128)(2,1)S(1)}, u32[]{:S(2)}, u32[]{:S(2)}) collective-permute-start(bf16[16,3,256]{2,1,0:T(4,128)(2,1)S(1)} %copy.15.own), channel_id=1, source_target_pairs={{0,2},{2,4},{4,6},{6,8},{8,10},{10,12},{12,14},{14,0},{1,3},{3,5},... | collective-permute-start | bytes 73736 | tf_op jit(solution)/shard_map/ppermute | solution.py:32
  4.4 4.9 %collective-permute-start.1 = (bf16[16,3,256]{2,1,0:T(4,128)(2,1)S(1)}, bf16[16,3,256]{2,1,0:T(4,128)(2,1)S(1)}, u32[]{:S(2)}, u32[]{:S(2)}) collective-permute-start(bf16[16,3,256]{2,1,0:T(4,128)(2,1)S(1)} %copy.15.own), channel_id=1, source_target_pairs={{0,14},{2,0},{4,2},{6,4},{8,6},{10,8},{12,10},{14,12},{1,15},{3,1}... | collective-permute-start | bytes 73736 | tf_op jit(solution)/shard_map/ppermute | solution.py:32
  9.3 24.3 %collective-permute-start.7 = (bf16[16,64,256]{2,1,0:T(8,128)(2,1)}, bf16[16,64,256]{2,1,0:T(8,128)(2,1)S(1)}, u32[]{:S(2)}, u32[]{:S(2)}) collective-permute-start(bf16[16,64,256]{2,1,0:T(8,128)(2,1)} %direction.1), channel_id=1, source_target_pairs={{0,14},{2,0},{4,2},{6,4},{8,6},{10,8},{12,10},{14,12},{1,15},{3,1}... | collective-permute-start | bytes 1572872 | tf_op jit(solution)/shard_map/ppermute | solution.py:32
  14.1 19.6 %collective-permute-start.4 = (bf16[16,64,256]{2,1,0:T(8,128)(2,1)}, bf16[16,64,256]{2,1,0:T(8,128)(2,1)S(1)}, u32[]{:S(2)}, u32[]{:S(2)}) collective-permute-start(bf16[16,64,256]{2,1,0:T(8,128)(2,1)} %direction.1), channel_id=1, source_target_pairs={{0,2},{2,4},{4,6},{6,8},{8,10},{10,12},{12,14},{14,0},{1,3},{3,5},... | collective-permute-start | bytes 1572872 | tf_op jit(solution)/shard_map/ppermute | solution.py:32
  14.1 24.8 %collective-permute-start.6 = (bf16[16,64,256]{2,1,0:T(8,128)(2,1)}, bf16[16,64,256]{2,1,0:T(8,128)(2,1)S(1)}, u32[]{:S(2)}, u32[]{:S(2)}) collective-permute-start(bf16[16,64,256]{2,1,0:T(8,128)(2,1)} %direction.1), channel_id=1, source_target_pairs={{0,1},{1,0},{2,3},{3,2},{4,5},{5,4},{6,7},{7,6},{8,9},{9,8},{10,11... | collective-permute-start | bytes 1572872 | tf_op jit(solution)/shard_map/ppermute | solution.py:36
  33.7 5.2 %collective-permute-start.8 = (bf16[16,64,256]{2,1,0:T(8,128)(2,1)S(1)}, bf16[16,64,256]{2,1,0:T(8,128)(2,1)S(1)}, u32[]{:S(2)}, u32[]{:S(2)}) collective-permute-start(bf16[16,64,256]{2,1,0:T(8,128)(2,1)S(1)} %collective-permute-done.7.refs_4_), channel_id=1, source_target_pairs={{0,1},{1,0},{2,3},{3,2},{4,5},{5,4},{6,7},{7,6},{8,9},{9,8},{10,11... | collective-permute-start | bytes 1572872 | tf_op jit(solution)/shard_map/ppermute | solution.py:36
  33.7 5.2 %collective-permute-start.5 = (bf16[16,64,256]{2,1,0:T(8,128)(2,1)S(1)}, bf16[16,64,256]{2,1,0:T(8,128)(2,1)S(1)}, u32[]{:S(2)}, u32[]{:S(2)}) collective-permute-start(bf16[16,64,256]{2,1,0:T(8,128)(2,1)S(1)} %collective-permute-done.4.refs_0_), channel_id=1, source_target_pairs={{0,1},{1,0},{2,3},{3,2},{4,5},{5,4},{6,7},{7,6},{8,9},{9,8},{10,11... | collective-permute-start | bytes 1572872 | tf_op jit(solution)/shard_map/ppermute | solution.py:36
  34.2 9.3 %collective-permute-start.2 = (bf16[10,64,128]{2,1,0:T(8,128)(2,1)S(1)}, bf16[10,64,128]{2,1,0:T(8,128)(2,1)S(1)}, u32[]{:S(2)}, u32[]{:S(2)}) collective-permute-start(bf16[10,64,128]{2,1,0:T(8,128)(2,1)S(1)} %get-tuple-element.23.own), channel_id=1, source_target_pairs={{0,2},{2,4},{4,6},{6,8},{8,10},{10,12},{12,14},{14,0},{1,3},{3,5},... | collective-permute-start | bytes 491528 | tf_op jit(solution)/shard_map/ppermute | solution.py:32
  35.3 9.8 %collective-permute-start.3 = (bf16[10,64,128]{2,1,0:T(8,128)(2,1)S(1)}, bf16[10,64,128]{2,1,0:T(8,128)(2,1)S(1)}, u32[]{:S(2)}, u32[]{:S(2)}) collective-permute-start(bf16[10,64,128]{2,1,0:T(8,128)(2,1)S(1)} %get-tuple-element.23.own), channel_id=1, source_target_pairs={{0,14},{2,0},{4,2},{6,4},{8,6},{10,8},{12,10},{14,12},{1,15},{3,1}... | collective-permute-start | bytes 491528 | tf_op jit(solution)/shard_map/ppermute | solution.py:32
  38.9 10.5 %copy-start.2 = (s32[16,8]{0,1:T(8,128)S(1)}, s32[16,8]{0,1:T(8,128)}, u32[]{:S(2)}) copy-start(s32[16,8]{0,1:T(8,128)} %param.22) | copy-start | bytes 1540
  38.9 18.3 %copy-start.1 = (f32[64]{0:T(128)S(1)}, f32[64]{0:T(128)}, u32[]{:S(2)}) copy-start(f32[64]{0:T(128)} %param.15) | copy-start | bytes 772
  43.4 25.6 %copy-start = (bf16[16,64,256]{2,1,0:T(8,128)(2,1)S(1)}, bf16[16,64,256]{2,1,0:T(8,128)(2,1)}, u32[]{:S(2)}) copy-start(bf16[16,64,256]{2,1,0:T(8,128)(2,1)} %direction.1) | copy-start | bytes 1572868
  43.4 13.8 %collective-permute-start.12 = (bf16[8,64,256]{2,1,0:T(8,128)(2,1)S(1)}, bf16[8,64,256]{2,1,0:T(8,128)(2,1)S(1)}, u32[]{:S(2)}, u32[]{:S(2)}) collective-permute-start(bf16[8,64,256]{2,1,0:T(8,128)(2,1)S(1)} %get-tuple-element.37), channel_id=1, source_target_pairs={{0,1},{1,0},{2,3},{3,2},{4,5},{5,4},{6,7},{7,6},{8,9},{9,8},{10,11... | collective-permute-start | bytes 786440 | tf_op jit(solution)/shard_map/ppermute | solution.py:36
  45.3 5.8 %collective-permute-start.9 = (bf16[64,64]{1,0:T(8,128)(2,1)S(1)}, bf16[64,64]{1,0:T(8,128)(2,1)S(1)}, u32[]{:S(2)}, u32[]{:S(2)}) collective-permute-start(bf16[64,64]{1,0:T(8,128)(2,1)S(1)} %shard_map.144), channel_id=1, source_target_pairs={{0,4},{4,8},{8,12},{12,0},{1,5},{5,9},{9,13},{13,1},{2,6},{6,10},{... | collective-permute-start | bytes 24584 | tf_op jit(solution)/shard_map/ppermute | solution.py:32
  45.4 5.6 %collective-permute-start.10 = (bf16[64,64]{1,0:T(8,128)(2,1)S(1)}, bf16[64,64]{1,0:T(8,128)(2,1)S(1)}, u32[]{:S(2)}, u32[]{:S(2)}) collective-permute-start(bf16[64,64]{1,0:T(8,128)(2,1)S(1)} %shard_map.144), channel_id=1, source_target_pairs={{0,8},{4,12},{8,0},{12,4},{1,9},{5,13},{9,1},{13,5},{2,10},{6,14},... | collective-permute-start | bytes 24584 | tf_op jit(solution)/shard_map/ppermute | solution.py:32
  48.6 3.7 %collective-permute-start.11 = (bf16[64,64]{1,0:T(8,128)(2,1)S(1)}, bf16[64,64]{1,0:T(8,128)(2,1)S(1)}, u32[]{:S(2)}, u32[]{:S(2)}) collective-permute-start(bf16[64,64]{1,0:T(8,128)(2,1)S(1)} %shard_map.144), channel_id=1, source_target_pairs={{0,12},{4,0},{8,4},{12,8},{1,13},{5,1},{9,5},{13,9},{2,14},{6,2},{... | collective-permute-start | bytes 24584 | tf_op jit(solution)/shard_map/ppermute | solution.py:32

commit v5 on v4

--- a/solution.py
+++ b/solution.py
@@ -130,7 +130,7 @@
 
 
 def features(offsets):
-    x, y, z = (offsets[i : i + 1, :] for i in range(3))
+    x, y, z = (offsets[i : i + 1] for i in range(3))
     square = thirds(KAPPA * (x * x + y * y + z * z))
     row = lax.broadcasted_iota(jnp.int32, (8, x.shape[1]), 0)
     packed = jnp.zeros((8, x.shape[1]), F32)
@@ -154,33 +154,36 @@
     ).astype(BF)
 
 
-def tile_kernel(start, near_h, _, own, *refs):
+def tile_kernel(start, near_h, _, *refs):
     if start == 0:
-        prev, after, tiles, mark, spread_x, near, sem = refs
+        own, prev, after, tiles, mark, spread_x, plain, near, sem = refs
     else:
-        spread_x, tiles, mark, near, sem = refs
+        plain, spread_x, tiles, mark, near, sem = refs
+        own = plain
     listed = pltpu.make_async_copy(near_h, near, sem)
     listed.start()
     mark[...] = jnp.zeros_like(mark)
     count = tiles.shape[0]
     entries = near.shape[1]
     points = own.shape[2]
-    leaves = own.shape[0]
+    leaves = own.shape[1]
     total = leaves * lax.axis_size("blk") * lax.axis_size("leaf")
     device = lax.axis_index("blk") * lax.axis_size("leaf") + lax.axis_index("leaf")
     anchor = (device - 1) * leaves
     if start == 0:
         for side, ref in enumerate((prev, own, after)):
+            offsets = ref[...].astype(F32)
             for j in range(leaves):
-                spread_x[side * leaves + j] = spread_features(ref[j].astype(F32))
+                spread_x[side * leaves + j] = spread_features(offsets[:, j])
+            if side == 1:
+                plain[...] = offsets
     listed.wait()
     row = lax.broadcasted_iota(jnp.int32, (16, points), 0)
     lane = lax.broadcasted_iota(jnp.int32, (1, 128), 1)
 
     def leaf(i, carry):
         g = lax.axis_index("sample") * (leaves // 2) + start + i
-        offsets = own[g].astype(F32)
-        x, y, z = (offsets[k : k + 1, :] for k in range(3))
+        x, y, z = (plain[k, pl.ds(g, 1), :] for k in range(3))
         first = jnp.where((row >= 9) & (row < 12), 1.0, jnp.zeros((16, points), F32))
         at = 0
         for value in (x, y, z):
@@ -275,12 +278,12 @@
                 copy.wait()
         inward = nn(down, leaf_transfer[g])
         rows = []
-        for c in range(coupling_list.shape[1]):
-            slot = lax.rem(coupling_list[g, c] - anchor + 2 * total, total)
+        for c in range(coupling_list.shape[0]):
+            slot = lax.rem(coupling_list[c, g] - anchor + 2 * total, total)
             slot = jnp.where(slot >= 2 * leaves, slot - leaves, slot)
             slot = jnp.minimum(slot, 2 * leaves - 1)
             rows.append(window[slot])
-        columns = [coupling[g, c] for c in range(coupling_list.shape[1])]
+        columns = [coupling[g, c] for c in range(coupling_list.shape[0])]
         inward = inward + nt(jnp.concatenate(rows, axis=1), jnp.concatenate(columns, axis=1))
         far = nn(inward.astype(BF), natural[g])
         base[g] = NUGGET * direction[g].astype(F32) + far
@@ -413,6 +416,7 @@
     anywhere = pl.BlockSpec(memory_space=pl.ANY)
     hbm = pl.BlockSpec(memory_space=pltpu.HBM)
 
+    coords = jnp.transpose(coords, (1, 0, 2))
     coords_prev = shifted(coords, RING, 1)
     coords_after = shifted(coords, RING, -1)
     travelling, first = lax.optimization_barrier((direction, order, coords_prev, coords_after))[:2]
@@ -447,7 +451,7 @@
         count = half // 2
         outs = (pltpu.VMEM((count, entries * points, points), BF), token)
         if start == 0:
-            outs += (shape((3 * leaves, points, 128), BF),)
+            outs += (shape((3 * leaves, points, 128), BF), shape(coords.shape, F32))
         return call(
             functools.partial(tile_kernel, start),
             outs,
@@ -464,18 +468,37 @@
 
     coef_prev = shifted(coef, RING, 1)
     coef_after = shifted(coef, RING, -1)
-    tiles_low, low_mark, spread_x = make_tiles(
+    tiles_low, low_mark, spread_x, plain = make_tiles(
         0, up_mark, coords, coords_prev, coords_after
     )
-    tiles_high, high_mark = make_tiles(half // 2, low_mark, coords, spread_x)
-    direction_prev = ordered(direction_prev, high_mark)
-    direction_after = ordered(direction_after, high_mark)
+    tiles_high, high_mark = make_tiles(half // 2, low_mark, plain, spread_x)
+    direction_prev = ordered(direction_prev, high_mark, coef_prev, coef_after)
+    direction_after = ordered(direction_after, high_mark, coef_prev, coef_after)
+    paired = leaf_count == 2
+    top = call(
+        top_kernel,
+        shape((samples, rank), BF if paired else F32),
+        MIB,
+        MIB,
+        in_specs=[vmem] * (3 if paired else 1) + [anywhere],
+        out_specs=vmem,
+        vmem=4,
+    )(coef, *((coef_prev, coef_after) if paired else ()), high_mark)
+    if not paired:
+        terms = [shifted(top, "leaf", by) for by in range(1, leaf_count)]
+        top = sum(terms, top).astype(BF)
+    if blk_count <= 8:
+        others = [shifted(top, "blk", by) for by in range(1, blk_count)]
+    else:
+        others = lax.all_gather(top[None], "blk", axis=0, tiled=True)
+        places = jnp.mod(lax.axis_index("blk") - jnp.arange(blk_count, dtype=jnp.int32), blk_count)
+        others = list(others[places][1:])
     kept, given, near_mark = call(
         near_kernel,
         (shape((half, samples, points), F32), shape((half, samples, points), BF), token),
         4 * half * entries * samples * points * points,
         half * entries * points * points * 2,
-        in_specs=[hbm] + [anywhere] * 6 + [vmem] * 2,
+        in_specs=[hbm] + [anywhere] * 6 + [vmem] * 2 + [anywhere] * len(others),
         out_specs=(vmem,) * 3,
         scratch_shapes=[
             pltpu.VMEM((3 * leaves, 2 * samples, points), BF),
@@ -493,31 +516,13 @@
         partner(direction_after),
         tiles_low,
         tiles_high,
-    )
-
-    paired = leaf_count == 2
-    top = call(
-        top_kernel,
-        shape((samples, rank), BF if paired else F32),
-        MIB,
-        MIB,
-        in_specs=[vmem] * (3 if paired else 1) + [anywhere],
-        out_specs=vmem,
-        vmem=4,
-    )(coef, *((coef_prev, coef_after) if paired else ()), near_mark)
-    if not paired:
-        terms = [shifted(top, "leaf", by) for by in range(1, leaf_count)]
-        top = sum(terms, top).astype(BF)
-    if blk_count <= 8:
-        others = [shifted(top, "blk", by) for by in range(1, blk_count)]
-    else:
-        others = lax.all_gather(top[None], "blk", axis=0, tiled=True)
-        places = jnp.mod(lax.axis_index("blk") - jnp.arange(blk_count, dtype=jnp.int32), blk_count)
-        others = list(others[places][1:])
+        *others,
+    )
+
     tops = jnp.stack([top] + others)
     arrays = (
         top_list,
-        coupling_list,
+        coupling_list.T,
         top_coupling,
         node_transfer,
         leaf_transfer,

time: 70.3 us -> 74.2 us (1.055)
  blocking collectives: 10.6 us -> 12.2 us
  waiting for transfers between devices: 8.13 us -> 9.47 us
  starting transfers between devices: 20.3 us -> 21.5 us
    all_to_all x1, blocking collectives: 10.6 us -> 12.2 us  [on_device(): norms = lax.all_to_all(norms, RING, 0, 0)]
    ppermute x9, waiting for transfers between devices: 8.12 us -> 9.46 us  [shifted(): lax.ppermute(array, axis, [(i, (i + by) % count) for i in range(count)])]
    ppermute x9, starting transfers between devices: 19.7 us -> 21 us  [shifted(): lax.ppermute(array, axis, [(i, (i + by) % count) for i in range(count)])]
  transfers between devices with their start and end apart: 13 -> 13, of which waited for: 5 -> 5; matrix products, arithmetic and copies ran while one was open for 1% -> 0% of each run, Pallas kernels for 38% -> 30%
where the time goes in v5:
time: 74.2 us; the launch traced here: 73.8 us
  Pallas kernels  29.1 us (39%)
  starting transfers between devices  21.5 us (29%)
  blocking collectives  12.2 us (16%)
  waiting for transfers between devices  9.47 us (13%)
  between operations  0.76 us (1%)
  local copies, waits for them, and re-layouts  0.75 us (1%)
    ppermute x9, starting transfers between devices, shifted(): lax.ppermute(array, axis, [(i, (i + by) % count) for i in range(count)])  21 us
    all_to_all x1, blocking collectives, on_device(): norms = lax.all_to_all(norms, RING, 0, 0)  12.2 us
    pallas_call x2, Pallas kernels, make_tiles(): call(functools.partial(tile_kernel, start), outs, 40 * count * entries *...  11.6 us
    ppermute x9, waiting for transfers between devices, shifted(): lax.ppermute(array, axis, [(i, (i + by) % count) for i in range(count)])  9.46 us
    pallas_call x1, Pallas kernels, on_device(): call(up_kernel, (pltpu.HBM((leaves, rank, points), BF), shape((leaves //...  5.94 us
    pallas_call x1, Pallas kernels, on_device(): call(down_kernel, (whole, whole), 2 * leaves * samples * rank * (points +...  4.83 us
    pallas_call x1, Pallas kernels, on_device(): call(near_kernel, (shape((half, samples, points), F32), shape((half, samp...  4.46 us
  transfers between devices with their start and end apart: 13, of which 5 were waited for; matrix products, arithmetic and copies ran while one was open for 0% of the time, Pallas kernels for 30%

profile of v5, /device:TPU:0, one launch (start us, length us, event | category | flops | bytes accessed | tf_op | source)
XLA Modules:
  0.0 73.8 jit_solution(5719210556040744402)
XLA Ops:
  0.6 3.0 %collective-permute-start = (bf16[3,16,256]{2,1,0:T(8,128)(2,1)}, bf16[3,16,256]{2,1,0:T(8,128)(2,1)S(1)}, u32[]{:S(2)}, u32[]{:S(2)}) collective-permute-start(bf16[3,16,256]{2,1,0:T(8,128)(2,1)} %bitcast.12), channel_id=1, source_target_pairs={{0,2},{2,4},{4,6},{6,8},{8,10},{10,12},{12,14},{14,0},{1,3},{3,5},... | collective-permute-start | bytes 73736 | tf_op jit(solution)/shard_map/ppermute | solution.py:32
  3.6 3.1 %collective-permute-start.1 = (bf16[3,16,256]{2,1,0:T(8,128)(2,1)}, bf16[3,16,256]{2,1,0:T(8,128)(2,1)S(1)}, u32[]{:S(2)}, u32[]{:S(2)}) collective-permute-start(bf16[3,16,256]{2,1,0:T(8,128)(2,1)} %bitcast.13), channel_id=1, source_target_pairs={{0,14},{2,0},{4,2},{6,4},{8,6},{10,8},{12,10},{14,12},{1,15},{3,1}... | collective-permute-start | bytes 73736 | tf_op jit(solution)/shard_map/ppermute | solution.py:32
  6.7 2.0 %collective-permute-done.refs_1_ = bf16[3,16,256]{2,1,0:T(8,128)(2,1)S(1)} collective-permute-done((bf16[3,16,256]{2,1,0:T(8,128)(2,1)}, bf16[3,16,256]{2,1,0:T(8,128)(2,1)S(1)}, u32[]{:S(2)}, u32[]{:S(2)}) %collective-permute-start) | collective-permute-done | bytes 24608 | tf_op jit(solution)/shard_map/ppermute | solution.py:32
  8.7 0.0 collective-permute-done.1.refs_2_
  8.7 4.8 %collective-permute-start.10 = (bf16[16,64,256]{2,1,0:T(8,128)(2,1)}, bf16[16,64,256]{2,1,0:T(8,128)(2,1)S(1)}, u32[]{:S(2)}, u32[]{:S(2)}) collective-permute-start(bf16[16,64,256]{2,1,0:T(8,128)(2,1)} %direction.1), channel_id=1, source_target_pairs={{0,14},{2,0},{4,2},{6,4},{8,6},{10,8},{12,10},{14,12},{1,15},{3,1}... | collective-permute-start | bytes 1572872 | tf_op jit(solution)/shard_map/ppermute | solution.py:32
  13.5 0.0 collective-permute-start.7
  13.5 5.9 %shard_map.140 = (bf16[16,64,256]{2,1,0:T(8,128)(2,1)}, bf16[10,64,128]{2,1,0:T(8,128)(2,1)S(1)}, f32[8,128]{1,0:T(8,128)S(1)}) custom-call(s32[16,256]{1,0:T(8,128)} %order_h, bf16[16,64,256]{2,1,0:T(8,128)(2,1)} %basis_h.1, bf16[16,64,256]{2,1,0:T(8,128)(2,1)} %direction.1, bf16[16,64,64]{2,1,0:T(8,128)(2,1)} %refs_8_.1, bf16[1,64,64]{2,1,0:T(8,128)(2,1)} %refs_7_.1), custom_call_target="tpu_custom_call" | custom-call | flops 268435456 | bytes 6291456 | tf_op jit(solution)/shard_map/pallas_call | solution.py:427
  19.4 0.1 collective-permute-start.2
  19.5 4.8 %collective-permute-start.3 = (bf16[10,64,128]{2,1,0:T(8,128)(2,1)S(1)}, bf16[10,64,128]{2,1,0:T(8,128)(2,1)S(1)}, u32[]{:S(2)}, u32[]{:S(2)}) collective-permute-start(bf16[10,64,128]{2,1,0:T(8,128)(2,1)S(1)} %get-tuple-element.24.own), channel_id=1, source_target_pairs={{0,14},{2,0},{4,2},{6,4},{8,6},{10,8},{12,10},{14,12},{1,15},{3,1}... | collective-permute-start | bytes 491528 | tf_op jit(solution)/shard_map/ppermute | solution.py:32
  24.2 0.7 copy-done.2
  25.0 6.1 %shard_map.141 = (bf16[4,3072,256]{2,1,0:T(8,128)(2,1)S(1)}, f32[8,128]{1,0:T(8,128)S(1)}, bf16[48,256,128]{2,1,0:T(8,128)(2,1)S(1)}, f32[3,16,256]{2,1,0:T(8,128)S(1)}) custom-call(s32[16,12]{1,0:T(8,128)} %near_h.5, f32[8,128]{1,0:T(8,128)S(1)} %get-tuple-element.25._, bf16[3,16,256]{2,1,0:T(8,128)(2,1)S(1)} %bitcast.14, ...), custom_call_target="tpu_custom_call" | custom-call | flops 125829120 | bytes 6291456 | tf_op jit(solution)/shard_map/pallas_call | solution.py:455
  31.1 5.5 %shard_map.142 = (bf16[4,3072,256]{2,1,0:T(8,128)(2,1)S(1)}, f32[8,128]{1,0:T(8,128)S(1)}) custom-call(s32[16,12]{1,0:T(8,128)} %near_h.5, f32[8,128]{1,0:T(8,128)S(1)} %get-tuple-element.26._, f32[3,16,256]{2,1,0:T(8,128)S(1)} %get-tuple-element.27.refs_0_, bf16[48,256,128]{2,1,0:T(8,128)(2,1)S(1)} %get-tuple-element.28.refs_1_), custom_call_target="tpu_custom_call" | custom-call | flops 125829120 | bytes 6291456 | tf_op jit(solution)/shard_map/pallas_call | solution.py:455
  36.6 2.6 %collective-permute-done.2.refs_0_.refs_1_ = bf16[10,64,128]{2,1,0:T(8,128)(2,1)S(1)} collective-permute-done((bf16[10,64,128]{2,1,0:T(8,128)(2,1)S(1)}, bf16[10,64,128]{2,1,0:T(8,128)(2,1)S(1)}, u32[]{:S(2)}, u32[]{:S(2)}) %collective-permute-start.2) | collective-permute-done | bytes 163872 | tf_op jit(solution)/shard_map/ppermute | solution.py:32
  39.2 0.8 %collective-permute-done.3.refs_1_.refs_2_ = bf16[10,64,128]{2,1,0:T(8,128)(2,1)S(1)} collective-permute-done((bf16[10,64,128]{2,1,0:T(8,128)(2,1)S(1)}, bf16[10,64,128]{2,1,0:T(8,128)(2,1)S(1)}, u32[]{:S(2)}, u32[]{:S(2)}) %collective-permute-start.3) | collective-permute-done | bytes 163872 | tf_op jit(solution)/shard_map/ppermute | solution.py:32
  40.0 0.0 collective-permute-start.11
  40.1 0.0 collective-permute-done.7.refs_0_
  40.1 0.5 collective-permute-start.8
  40.6 0.1 shard_map.143
  40.7 0.7 collective-permute-start.4
  41.3 3.2 %collective-permute-start.5 = (bf16[64,64]{1,0:T(8,128)(2,1)S(1)}, bf16[64,64]{1,0:T(8,128)(2,1)S(1)}, u32[]{:S(2)}, u32[]{:S(2)}) collective-permute-start(bf16[64,64]{1,0:T(8,128)(2,1)S(1)} %shard_map.143), channel_id=1, source_target_pairs={{0,8},{4,12},{8,0},{12,4},{1,9},{5,13},{9,1},{13,5},{2,10},{6,14},... | collective-permute-start | bytes 24584 | tf_op jit(solution)/shard_map/ppermute | solution.py:32
  44.5 1.8 %collective-permute-done.4.refs_8_ = bf16[64,64]{1,0:T(8,128)(2,1)S(1)} collective-permute-done((bf16[64,64]{1,0:T(8,128)(2,1)S(1)}, bf16[64,64]{1,0:T(8,128)(2,1)S(1)}, u32[]{:S(2)}, u32[]{:S(2)}) %collective-permute-start.4) | collective-permute-done | bytes 8224 | tf_op jit(solution)/shard_map/ppermute | solution.py:32
  46.2 1.4 %collective-permute-start.6 = (bf16[64,64]{1,0:T(8,128)(2,1)S(1)}, bf16[64,64]{1,0:T(8,128)(2,1)S(1)}, u32[]{:S(2)}, u32[]{:S(2)}) collective-permute-start(bf16[64,64]{1,0:T(8,128)(2,1)S(1)} %shard_map.143), channel_id=1, source_target_pairs={{0,12},{4,0},{8,4},{12,8},{1,13},{5,1},{9,5},{13,9},{2,14},{6,2},{... | collective-permute-start | bytes 24584 | tf_op jit(solution)/shard_map/ppermute | solution.py:32
  47.7 0.0 collective-permute-done.5.refs_9_
  47.7 2.3 %collective-permute-done.6.refs_10_ = bf16[64,64]{1,0:T(8,128)(2,1)S(1)} collective-permute-done((bf16[64,64]{1,0:T(8,128)(2,1)S(1)}, bf16[64,64]{1,0:T(8,128)(2,1)S(1)}, u32[]{:S(2)}, u32[]{:S(2)}) %collective-permute-start.6) | collective-permute-done | bytes 8224 | tf_op jit(solution)/shard_map/ppermute | solution.py:32
  50.0 0.0 copy-start.1
  50.0 4.5 %shard_map.144 = (f32[8,64,256]{2,1,0:T(8,128)S(1)}, bf16[8,64,256]{2,1,0:T(8,128)(2,1)S(1)}, f32[8,128]{1,0:T(8,128)S(1)}) custom-call(s32[16,12]{1,0:T(8,128)} %near_h.5, bf16[16,64,256]{2,1,0:T(8,128)(2,1)S(1)} %collective-permute-done.7.refs_0_, bf16[16,64,256]{2,1,0:T(8,128)(2,1)S(1)} %collective-permute-done.8.refs_1_, bf16[16,64,256]{2,1,0:T(8,128)(2,1)} %direction.1, ...), custom_call_target="tpu_custom_call" | custom-call | flops 1610612736 | bytes 12582912 | tf_op jit(solution)/shard_map/pallas_call | solution.py:496
  54.5 0.0 copy-start
  54.5 0.1 collective-permute-start.12
  54.6 4.8 %shard_map.145 = (f32[16,64,256]{2,1,0:T(8,128)S(1)}, f32[16,64,256]{2,1,0:T(8,128)S(1)}) custom-call(bf16[4,64,64]{2,1,0:T(8,128)(2,1)S(1)} %pad_maximum_fusion.refs_0_, bf16[10,64,128]{2,1,0:T(8,128)(2,1)S(1)} %collective-permute-done.2.refs_0_.refs_1_, bf16[10,64,128]{2,1,0:T(8,128)(2,1)S(1)} %collective-permute-done.3.refs_1_.refs_2_, ...), custom_call_target="tpu_custom_call" | custom-call | flops 109051904 | bytes 8388608 | tf_op jit(solution)/shard_map/pallas_call | solution.py:535
  59.5 1.2 %shard_map.146 = (f32[16,64,256]{2,1,0:T(8,128)}, f32[16,64,256]{2,1,0:T(8,128)S(1)}, f32[8,8,128]{2,1,0:T(8,128)S(1)}) custom-call(f32[1,64]{1,0:T(1,128)S(1)} %bitcast.11, f32[16,64,256]{2,1,0:T(8,128)S(1)} %get-tuple-element.37.base, f32[8,64,256]{2,1,0:T(8,128)S(1)} %get-tuple-element.38.kept, bf16[8,64,256]{2,1,0:T(8,128)(2,1)S(1)} %collective-permute-done.12.received, ...), custom_call_target="tpu_custom_call" | custom-call | flops 4194304 | bytes 5242880 | tf_op jit(solution)/shard_map/pallas_call | solution.py:550
  60.7 12.2 %all_to_all.5.norms = f32[8,8,128]{2,1,0:T(8,128)S(1)} all-to-all(f32[8,8,128]{2,1,0:T(8,128)S(1)} %get-tuple-element.42), channel_id=1, replica_groups=mesh['groups'=2,'blk'=4,'leaf'=2,'sample'=2] {'blk','leaf'}, dimensions={0} | all-to-all | bytes 65536 | tf_op jit(solution)/shard_map/all_to_all | solution.py:560
  72.9 0.9 %shard_map.147 = bf16[16,64,256]{2,1,0:T(8,128)(2,1)} custom-call(f32[8,8,128]{2,1,0:T(8,128)S(1)} %all_to_all.5.norms, f32[16,64,256]{2,1,0:T(8,128)S(1)} %get-tuple-element.43.updated, bf16[16,64,256]{2,1,0:T(8,128)(2,1)S(1)} %copy-done), custom_call_target="tpu_custom_call" | custom-call | flops 1048576 | bytes 2097152 | tf_op jit(solution)/shard_map/pallas_call | solution.py:561
  (10 shorter events, 0.0 us)
Async XLA Ops:
  0.6 8.0 %collective-permute-start = (bf16[3,16,256]{2,1,0:T(8,128)(2,1)}, bf16[3,16,256]{2,1,0:T(8,128)(2,1)S(1)}, u32[]{:S(2)}, u32[]{:S(2)}) collective-permute-start(bf16[3,16,256]{2,1,0:T(8,128)(2,1)} %bitcast.12), channel_id=1, source_target_pairs={{0,2},{2,4},{4,6},{6,8},{8,10},{10,12},{12,14},{14,0},{1,3},{3,5},... | collective-permute-start | bytes 73736 | tf_op jit(solution)/shard_map/ppermute | solution.py:32
  3.6 5.1 %collective-permute-start.1 = (bf16[3,16,256]{2,1,0:T(8,128)(2,1)}, bf16[3,16,256]{2,1,0:T(8,128)(2,1)S(1)}, u32[]{:S(2)}, u32[]{:S(2)}) collective-permute-start(bf16[3,16,256]{2,1,0:T(8,128)(2,1)} %bitcast.13), channel_id=1, source_target_pairs={{0,14},{2,0},{4,2},{6,4},{8,6},{10,8},{12,10},{14,12},{1,15},{3,1}... | collective-permute-start | bytes 73736 | tf_op jit(solution)/shard_map/ppermute | solution.py:32
  8.7 31.4 %collective-permute-start.10 = (bf16[16,64,256]{2,1,0:T(8,128)(2,1)}, bf16[16,64,256]{2,1,0:T(8,128)(2,1)S(1)}, u32[]{:S(2)}, u32[]{:S(2)}) collective-permute-start(bf16[16,64,256]{2,1,0:T(8,128)(2,1)} %direction.1), channel_id=1, source_target_pairs={{0,14},{2,0},{4,2},{6,4},{8,6},{10,8},{12,10},{14,12},{1,15},{3,1}... | collective-permute-start | bytes 1572872 | tf_op jit(solution)/shard_map/ppermute | solution.py:32
  13.5 26.6 %collective-permute-start.7 = (bf16[16,64,256]{2,1,0:T(8,128)(2,1)}, bf16[16,64,256]{2,1,0:T(8,128)(2,1)S(1)}, u32[]{:S(2)}, u32[]{:S(2)}) collective-permute-start(bf16[16,64,256]{2,1,0:T(8,128)(2,1)} %direction.1), channel_id=1, source_target_pairs={{0,2},{2,4},{4,6},{6,8},{8,10},{10,12},{12,14},{14,0},{1,3},{3,5},... | collective-permute-start | bytes 1572872 | tf_op jit(solution)/shard_map/ppermute | solution.py:32
  19.4 19.8 %collective-permute-start.2 = (bf16[10,64,128]{2,1,0:T(8,128)(2,1)S(1)}, bf16[10,64,128]{2,1,0:T(8,128)(2,1)S(1)}, u32[]{:S(2)}, u32[]{:S(2)}) collective-permute-start(bf16[10,64,128]{2,1,0:T(8,128)(2,1)S(1)} %get-tuple-element.24.own), channel_id=1, source_target_pairs={{0,2},{2,4},{4,6},{6,8},{8,10},{10,12},{12,14},{14,0},{1,3},{3,5},... | collective-permute-start | bytes 491528 | tf_op jit(solution)/shard_map/ppermute | solution.py:32
  19.5 20.6 %collective-permute-start.3 = (bf16[10,64,128]{2,1,0:T(8,128)(2,1)S(1)}, bf16[10,64,128]{2,1,0:T(8,128)(2,1)S(1)}, u32[]{:S(2)}, u32[]{:S(2)}) collective-permute-start(bf16[10,64,128]{2,1,0:T(8,128)(2,1)S(1)} %get-tuple-element.24.own), channel_id=1, source_target_pairs={{0,14},{2,0},{4,2},{6,4},{8,6},{10,8},{12,10},{14,12},{1,15},{3,1}... | collective-permute-start | bytes 491528 | tf_op jit(solution)/shard_map/ppermute | solution.py:32
  24.2 25.7 %collective-permute-start.9 = (bf16[16,64,256]{2,1,0:T(8,128)(2,1)}, bf16[16,64,256]{2,1,0:T(8,128)(2,1)S(1)}, u32[]{:S(2)}, u32[]{:S(2)}) collective-permute-start(bf16[16,64,256]{2,1,0:T(8,128)(2,1)} %direction.1), channel_id=1, source_target_pairs={{0,1},{1,0},{2,3},{3,2},{4,5},{5,4},{6,7},{7,6},{8,9},{9,8},{10,11... | collective-permute-start | bytes 1572872 | tf_op jit(solution)/shard_map/ppermute | solution.py:36
  24.2 0.7 copy-start.2
  40.0 9.9 %collective-permute-start.11 = (bf16[16,64,256]{2,1,0:T(8,128)(2,1)S(1)}, bf16[16,64,256]{2,1,0:T(8,128)(2,1)S(1)}, u32[]{:S(2)}, u32[]{:S(2)}) collective-permute-start(bf16[16,64,256]{2,1,0:T(8,128)(2,1)S(1)} %collective-permute-done.10.refs_4_), channel_id=1, source_target_pairs={{0,1},{1,0},{2,3},{3,2},{4,5},{5,4},{6,7},{7,6},{8,9},{9,8},{10,11... | collective-permute-start | bytes 1572872 | tf_op jit(solution)/shard_map/ppermute | solution.py:36
  40.1 9.9 %collective-permute-start.8 = (bf16[16,64,256]{2,1,0:T(8,128)(2,1)S(1)}, bf16[16,64,256]{2,1,0:T(8,128)(2,1)S(1)}, u32[]{:S(2)}, u32[]{:S(2)}) collective-permute-start(bf16[16,64,256]{2,1,0:T(8,128)(2,1)S(1)} %collective-permute-done.7.refs_0_), channel_id=1, source_target_pairs={{0,1},{1,0},{2,3},{3,2},{4,5},{5,4},{6,7},{7,6},{8,9},{9,8},{10,11... | collective-permute-start | bytes 1572872 | tf_op jit(solution)/shard_map/ppermute | solution.py:36
  40.7 5.6 %collective-permute-start.4 = (bf16[64,64]{1,0:T(8,128)(2,1)S(1)}, bf16[64,64]{1,0:T(8,128)(2,1)S(1)}, u32[]{:S(2)}, u32[]{:S(2)}) collective-permute-start(bf16[64,64]{1,0:T(8,128)(2,1)S(1)} %shard_map.143), channel_id=1, source_target_pairs={{0,4},{4,8},{8,12},{12,0},{1,5},{5,9},{9,13},{13,1},{2,6},{6,10},{... | collective-permute-start | bytes 24584 | tf_op jit(solution)/shard_map/ppermute | solution.py:32
  41.3 6.4 %collective-permute-start.5 = (bf16[64,64]{1,0:T(8,128)(2,1)S(1)}, bf16[64,64]{1,0:T(8,128)(2,1)S(1)}, u32[]{:S(2)}, u32[]{:S(2)}) collective-permute-start(bf16[64,64]{1,0:T(8,128)(2,1)S(1)} %shard_map.143), channel_id=1, source_target_pairs={{0,8},{4,12},{8,0},{12,4},{1,9},{5,13},{9,1},{13,5},{2,10},{6,14},... | collective-permute-start | bytes 24584 | tf_op jit(solution)/shard_map/ppermute | solution.py:32
  46.2 3.7 %collective-permute-start.6 = (bf16[64,64]{1,0:T(8,128)(2,1)S(1)}, bf16[64,64]{1,0:T(8,128)(2,1)S(1)}, u32[]{:S(2)}, u32[]{:S(2)}) collective-permute-start(bf16[64,64]{1,0:T(8,128)(2,1)S(1)} %shard_map.143), channel_id=1, source_target_pairs={{0,12},{4,0},{8,4},{12,8},{1,13},{5,1},{9,5},{13,9},{2,14},{6,2},{... | collective-permute-start | bytes 24584 | tf_op jit(solution)/shard_map/ppermute | solution.py:32
  50.0 9.4 %copy-start.1 = (f32[64]{0:T(128)S(1)}, f32[64]{0:T(128)}, u32[]{:S(2)}) copy-start(f32[64]{0:T(128)} %param.15) | copy-start | bytes 772
  54.5 18.4 %copy-start = (bf16[16,64,256]{2,1,0:T(8,128)(2,1)S(1)}, bf16[16,64,256]{2,1,0:T(8,128)(2,1)}, u32[]{:S(2)}) copy-start(bf16[16,64,256]{2,1,0:T(8,128)(2,1)} %direction.1) | copy-start | bytes 1572868
  54.5 4.9 %collective-permute-start.12 = (bf16[8,64,256]{2,1,0:T(8,128)(2,1)S(1)}, bf16[8,64,256]{2,1,0:T(8,128)(2,1)S(1)}, u32[]{:S(2)}, u32[]{:S(2)}) collective-permute-start(bf16[8,64,256]{2,1,0:T(8,128)(2,1)S(1)} %get-tuple-element.39), channel_id=1, source_target_pairs={{0,1},{1,0},{2,3},{3,2},{4,5},{5,4},{6,7},{7,6},{8,9},{9,8},{10,11... | collective-permute-start | bytes 786440 | tf_op jit(solution)/shard_map/ppermute | solution.py:36

commit v6 on v5

--- a/solution.py
+++ b/solution.py
@@ -34,6 +34,20 @@
 
 def partner(array):
     return lax.ppermute(array, "sample", [(0, 1), (1, 0)])
+
+
+def passed_on(array):
+    count = lax.axis_size("blk") * 2
+    pairs = [(i, (i + 2 - 4 * (i % 2)) % count) for i in range(count)]
+    return lax.ppermute(array, RING, pairs)
+
+
+def place(slot, leaves, flip):
+    if not flip:
+        return slot
+    moved = jnp.where(slot >= 2 * leaves, slot - 2 * leaves, slot)
+    moved = jnp.where(slot < leaves, slot + 2 * leaves, moved)
+    return jnp.where(lax.axis_index("leaf") == 0, moved, slot)
 
 
 def ordered(array, *first):
@@ -109,8 +123,8 @@
         if g % size == 0:
             for copy in copies[g // size]:
                 copy.wait()
-        place = jnp.where(rows == order[g : g + 1, :], 1.0, 0.0).astype(BF)
-        own = nt(basis[g], place).astype(BF)
+        spot = jnp.where(rows == order[g : g + 1, :], 1.0, 0.0).astype(BF)
+        own = nt(basis[g], spot).astype(BF)
         natural[g] = own
         weights = nt(direction[g], own).astype(BF)
         coef[g // 2, :, (g % 2) * rank : (g % 2 + 1) * rank] = weights
@@ -154,7 +168,8 @@
     ).astype(BF)
 
 
-def tile_kernel(start, near_h, _, *refs):
+def tile_kernel(start, waits, near_h, *refs):
+    refs = refs[waits:]
     if start == 0:
         own, prev, after, tiles, mark, spread_x, plain, near, sem = refs
     else:
@@ -225,12 +240,11 @@
 
     total = term(own)
     if sides:
-        low = lax.axis_index("leaf") == 0
-        total = total + jnp.where(low, term(sides[1]), term(sides[0]))
+        total = total + term(sides[0])
     top[...] = total.astype(top.dtype)
 
 
-def down_kernel(*refs):
+def down_kernel(flip, *refs):
     tops, before, after, residual_h = refs[:4]
     sources, (base, residual), targets, sems = refs[4:12], refs[13:15], refs[15:24], refs[24]
     window, targets = targets[0], targets[1:]
@@ -269,8 +283,8 @@
         copy.wait()
     incoming = jnp.zeros((samples, rank), F32)
     for e in range(top_list.shape[1]):
-        place = lax.rem(here - top_list[0, e] + clusters, clusters)
-        incoming = incoming + nt(tops[place], top_coupling[0, e])
+        index = lax.rem(here - top_list[0, e] + clusters, clusters)
+        incoming = incoming + nt(tops[index], top_coupling[0, e])
     down = nn(incoming.astype(BF), node_transfer[0]).astype(BF)
     for g in range(leaves):
         if g % size == 0:
@@ -280,6 +294,7 @@
         rows = []
         for c in range(coupling_list.shape[0]):
             slot = lax.rem(coupling_list[c, g] - anchor + 2 * total, total)
+            slot = place(slot, leaves, flip)
             slot = jnp.where(slot >= 2 * leaves, slot - leaves, slot)
             slot = jnp.minimum(slot, 2 * leaves - 1)
             rows.append(window[slot])
@@ -290,27 +305,24 @@
     ahead.wait()
 
 
-def near_kernel(near_h, *refs):
-    pieces, tiles, (kept, given, mark, window, near, sems) = refs[:6], refs[6:8], refs[-6:]
+def near_kernel(count, flip, near_h, *refs):
+    pieces, tiles = refs[:count], refs[count : count + 2]
+    kept, given, mark, window, near, sems = refs[-6:]
     mark[...] = jnp.zeros_like(mark)
     leaves = window.shape[0] // 3
     samples = kept.shape[1]
     total = leaves * lax.axis_size("blk") * lax.axis_size("leaf")
     device = lax.axis_index("blk") * lax.axis_size("leaf") + lax.axis_index("leaf")
     anchor = (device - 1) * leaves
-    copies = [pltpu.make_async_copy(near_h, near, sems.at[6])]
+    copies = [pltpu.make_async_copy(near_h, near, sems.at[count])]
+    at = 0
     for i, piece in enumerate(pieces):
-        side, columns = i // 2, i % 2
-        copies.append(
-            pltpu.make_async_copy(
-                piece,
-                window.at[
-                    side * leaves : (side + 1) * leaves,
-                    columns * samples : (columns + 1) * samples,
-                ],
-                sems.at[i],
-            )
-        )
+        columns = i % 2
+        target = window.at[
+            at : at + piece.shape[0], columns * samples : (columns + 1) * samples
+        ]
+        copies.append(pltpu.make_async_copy(piece, target, sems.at[i]))
+        at += piece.shape[0] * columns
     for copy in copies:
         copy.start()
     for copy in copies:
@@ -322,7 +334,8 @@
             g = lax.axis_index("sample") * kept.shape[0] + at + i
             values = []
             for e in range(near.shape[1]):
-                values.append(window[lax.rem(near[g, e] - anchor + 2 * total, total)])
+                slot = lax.rem(near[g, e] - anchor + 2 * total, total)
+                values.append(window[place(slot, leaves, flip)])
             field = nn(jnp.concatenate(values, axis=1), part[i]) * AMPLITUDE
             kept[at + i] = field[:samples]
             given[at + i] = field[samples:].astype(BF)
@@ -419,10 +432,13 @@
     coords = jnp.transpose(coords, (1, 0, 2))
     coords_prev = shifted(coords, RING, 1)
     coords_after = shifted(coords, RING, -1)
+    flip = leaf_count == 2
     travelling, first = lax.optimization_barrier((direction, order, coords_prev, coords_after))[:2]
-    direction_prev = shifted(travelling, RING, 1)
-    direction_after = shifted(travelling, RING, -1)
-    direction_other = partner(direction)
+    if flip:
+        near_side = [shifted(travelling[i : i + half], "leaf", 1) for i in (0, half)]
+    else:
+        near_side = [shifted(travelling, RING, 1)]
+        far_side = [shifted(travelling, RING, -1)]
 
     natural, coef, up_mark = call(
         up_kernel,
@@ -453,38 +469,46 @@
         if start == 0:
             outs += (shape((3 * leaves, points, 128), BF), shape(coords.shape, F32))
         return call(
-            functools.partial(tile_kernel, start),
+            functools.partial(tile_kernel, start, len(done)),
             outs,
             40 * count * entries * points * points,
             count * entries * points * points * 2,
-            in_specs=[hbm, anywhere] + [vmem] * len(operands),
+            in_specs=[hbm] + [anywhere] * len(done) + [vmem] * len(operands),
             out_specs=(vmem,) * len(outs),
             scratch_shapes=[
                 pltpu.SMEM(near_list.shape, jnp.int32),
                 pltpu.SemaphoreType.DMA,
             ],
             vmem=8,
-        )(*in_hbm(near_list), done, *operands)
-
-    coef_prev = shifted(coef, RING, 1)
-    coef_after = shifted(coef, RING, -1)
+        )(*in_hbm(near_list), *done, *operands)
+
+    if flip:
+        coef_near = shifted(coef, "leaf", 1)
+        coef_far = passed_on(coef_near)
+    else:
+        coef_near = shifted(coef, RING, 1)
+        coef_far = shifted(coef, RING, -1)
     tiles_low, low_mark, spread_x, plain = make_tiles(
-        0, up_mark, coords, coords_prev, coords_after
-    )
-    tiles_high, high_mark = make_tiles(half // 2, low_mark, plain, spread_x)
-    direction_prev = ordered(direction_prev, high_mark, coef_prev, coef_after)
-    direction_after = ordered(direction_after, high_mark, coef_prev, coef_after)
-    paired = leaf_count == 2
+        0, [up_mark] + near_side[:1] * flip, coords, coords_prev, coords_after
+    )
+    if flip:
+        marks = (up_mark, low_mark)
+        far_side = [passed_on(ordered(part, mark)) for part, mark in zip(near_side, marks)]
+    tiles_high, high_mark = make_tiles(
+        half // 2, [low_mark] + (near_side[1:] + far_side[:1]) * flip, plain, spread_x
+    )
+    near_side = [ordered(part, high_mark) for part in near_side]
+    far_side = [ordered(part, high_mark) for part in far_side]
     top = call(
         top_kernel,
-        shape((samples, rank), BF if paired else F32),
+        shape((samples, rank), BF if flip else F32),
         MIB,
         MIB,
-        in_specs=[vmem] * (3 if paired else 1) + [anywhere],
+        in_specs=[vmem] * (2 if flip else 1) + [anywhere],
         out_specs=vmem,
         vmem=4,
-    )(coef, *((coef_prev, coef_after) if paired else ()), high_mark)
-    if not paired:
+    )(coef, *([coef_near] if flip else []), high_mark)
+    if not flip:
         terms = [shifted(top, "leaf", by) for by in range(1, leaf_count)]
         top = sum(terms, top).astype(BF)
     if blk_count <= 8:
@@ -493,32 +517,23 @@
         others = lax.all_gather(top[None], "blk", axis=0, tiled=True)
         places = jnp.mod(lax.axis_index("blk") - jnp.arange(blk_count, dtype=jnp.int32), blk_count)
         others = list(others[places][1:])
+    pieces = []
+    for part in near_side + in_hbm(direction) + far_side:
+        pieces += [part, partner(part)]
     kept, given, near_mark = call(
-        near_kernel,
+        functools.partial(near_kernel, len(pieces), flip),
         (shape((half, samples, points), F32), shape((half, samples, points), BF), token),
         4 * half * entries * samples * points * points,
         half * entries * points * points * 2,
-        in_specs=[hbm] + [anywhere] * 6 + [vmem] * 2 + [anywhere] * len(others),
+        in_specs=[hbm] + [anywhere] * len(pieces) + [vmem] * 2 + [anywhere] * (len(others) + 1),
         out_specs=(vmem,) * 3,
         scratch_shapes=[
             pltpu.VMEM((3 * leaves, 2 * samples, points), BF),
             pltpu.SMEM(near_list.shape, jnp.int32),
-            pltpu.SemaphoreType.DMA((7,)),
+            pltpu.SemaphoreType.DMA((len(pieces) + 1,)),
         ],
         vmem=8,
-    )(
-        *in_hbm(near_list),
-        direction_prev,
-        partner(direction_prev),
-        *in_hbm(direction),
-        direction_other,
-        direction_after,
-        partner(direction_after),
-        tiles_low,
-        tiles_high,
-        *others,
-    )
-
+    )(*in_hbm(near_list), *pieces, tiles_low, tiles_high, *others, coef_far)
     tops = jnp.stack([top] + others)
     arrays = (
         top_list,
@@ -533,7 +548,7 @@
     spaces = (pltpu.SMEM,) * 2 + (pltpu.VMEM,) * 6
     whole = shape((leaves, samples, points), F32)
     base, residual_here = call(
-        down_kernel,
+        functools.partial(down_kernel, flip),
         (whole, whole),
         2 * leaves * samples * rank * (points + 9 * rank),
         8 * MIB,
@@ -543,7 +558,7 @@
         + [space(array.shape, array.dtype) for space, array in zip(spaces, arrays)]
         + [pltpu.SemaphoreType.DMA((5, 7))],
         vmem=10,
-    )(tops, coef_prev, coef_after, *in_hbm(residual, *arrays), near_mark)
+    )(tops, coef_near, coef_far, *in_hbm(residual, *arrays), near_mark)
     received = partner(given)
 
     devices = blk_count * leaf_count

time: 74.2 us -> 77.8 us (1.049)
  waiting for transfers between devices: 9.47 us -> 20.2 us
  starting transfers between devices: 21.5 us -> 15.4 us
  blocking collectives: 12.2 us -> 9.89 us
  local copies, waits for them, and re-layouts: 0.75 us -> 1.82 us
    ppermute x9 -> x8, starting transfers between devices: 21 us -> 9.74 us  [shifted(): lax.ppermute(array, axis, [(i, (i + by) % count) for i in range(count)])]
    ppermute x9 -> x8, waiting for transfers between devices: 9.46 us -> 15.9 us  [shifted(): lax.ppermute(array, axis, [(i, (i + by) % count) for i in range(count)])]
    ppermute x0 -> x3, starting transfers between devices: none -> 5.1 us  [passed_on(): return lax.ppermute(array, RING, pairs)]
    ppermute x0 -> x3, waiting for transfers between devices: none -> 4.32 us  [passed_on(): return lax.ppermute(array, RING, pairs)]
    all_to_all x1, blocking collectives: 12.2 us -> 9.89 us  [on_device(): norms = lax.all_to_all(norms, RING, 0, 0)]
    slice x0 -> x1, local copies, waits for them, and re-layouts: none -> 1.06 us  [on_device(): near_side = [shifted(travelling[i:i + half], 'leaf', 1) for i in (0, half)]]
  transfers between devices with their start and end apart: 13 -> 17, of which waited for: 5 -> 6; matrix products, arithmetic and copies ran while one was open for 0% -> 0% of each run, Pallas kernels for 30% -> 29%
where the time goes in v6:
time: 77.8 us; the launch traced here: 77.4 us
  Pallas kernels  29.3 us (38%)
  waiting for transfers between devices  20.2 us (26%)
  starting transfers between devices  15.4 us (20%)
  blocking collectives  9.89 us (13%)
  local copies, waits for them, and re-layouts  1.82 us (2%)
  between operations  0.8 us (1%)
    ppermute x8, waiting for transfers between devices, shifted(): lax.ppermute(array, axis, [(i, (i + by) % count) for i in range(count)])  15.9 us
    pallas_call x2, Pallas kernels, make_tiles(): call(functools.partial(tile_kernel, start, len(done)), outs, 40 * count *...  11.6 us
    all_to_all x1, blocking collectives, on_device(): norms = lax.all_to_all(norms, RING, 0, 0)  9.89 us
    ppermute x8, starting transfers between devices, shifted(): lax.ppermute(array, axis, [(i, (i + by) % count) for i in range(count)])  9.74 us
    pallas_call x1, Pallas kernels, on_device(): call(up_kernel, (pltpu.HBM((leaves, rank, points), BF), shape((leaves //...  5.93 us
    ppermute x3, starting transfers between devices, passed_on(): return lax.ppermute(array, RING, pairs)  5.1 us
    pallas_call x1, Pallas kernels, on_device(): call(functools.partial(down_kernel, flip), (whole, whole), 2 * leaves * s...  4.84 us
    pallas_call x1, Pallas kernels, on_device(): call(functools.partial(near_kernel, len(pieces), flip), (shape((half, sam...  4.65 us
  transfers between devices with their start and end apart: 17, of which 6 were waited for; matrix products, arithmetic and copies ran while one was open for 0% of the time, Pallas kernels for 29%

profile of v6, /device:TPU:0, one launch (start us, length us, event | category | flops | bytes accessed | tf_op | source)
XLA Modules:
  0.0 77.4 jit_solution(7909397435209017786)
XLA Ops:
  0.6 3.0 %collective-permute-start = (bf16[3,16,256]{2,1,0:T(8,128)(2,1)}, bf16[3,16,256]{2,1,0:T(8,128)(2,1)S(1)}, u32[]{:S(2)}, u32[]{:S(2)}) collective-permute-start(bf16[3,16,256]{2,1,0:T(8,128)(2,1)} %bitcast.12), channel_id=1, source_target_pairs={{0,2},{2,4},{4,6},{6,8},{8,10},{10,12},{12,14},{14,0},{1,3},{3,5},... | collective-permute-start | bytes 73736 | tf_op jit(solution)/shard_map/ppermute | solution.py:32
  3.6 3.1 %collective-permute-start.1 = (bf16[3,16,256]{2,1,0:T(8,128)(2,1)}, bf16[3,16,256]{2,1,0:T(8,128)(2,1)S(1)}, u32[]{:S(2)}, u32[]{:S(2)}) collective-permute-start(bf16[3,16,256]{2,1,0:T(8,128)(2,1)} %bitcast.13), channel_id=1, source_target_pairs={{0,14},{2,0},{4,2},{6,4},{8,6},{10,8},{12,10},{14,12},{1,15},{3,1}... | collective-permute-start | bytes 73736 | tf_op jit(solution)/shard_map/ppermute | solution.py:32
  6.7 2.0 %collective-permute-done.refs_3_ = bf16[3,16,256]{2,1,0:T(8,128)(2,1)S(1)} collective-permute-done((bf16[3,16,256]{2,1,0:T(8,128)(2,1)}, bf16[3,16,256]{2,1,0:T(8,128)(2,1)S(1)}, u32[]{:S(2)}, u32[]{:S(2)}) %collective-permute-start) | collective-permute-done | bytes 24608 | tf_op jit(solution)/shard_map/ppermute | solution.py:32
  8.7 1.1 %fusion = (bf16[8,64,256]{2,1,0:T(8,128)(2,1)S(1)}, bf16[8,64,256]{2,1,0:T(8,128)(2,1)S(1)}) fusion(bf16[16,64,256]{2,1,0:T(8,128)(2,1)} %direction.1), kind=kLoop, calls=%fused_computation.1 | loop fusion | bytes 1048576 | tf_op jit(solution)/shard_map/slice | solution.py:438
  9.8 1.5 %collective-permute-start.3 = (bf16[8,64,256]{2,1,0:T(8,128)(2,1)S(1)}, bf16[8,64,256]{2,1,0:T(8,128)(2,1)S(1)}, u32[]{:S(2)}, u32[]{:S(2)}) collective-permute-start(bf16[8,64,256]{2,1,0:T(8,128)(2,1)S(1)} %get-tuple-element.53), channel_id=1, source_target_pairs={{0,2},{2,0},{1,3},{3,1},{4,6},{6,4},{5,7},{7,5},{8,10},{10,8},{9,1... | collective-permute-start | bytes 786440 | tf_op jit(solution)/shard_map/ppermute | solution.py:32
  11.2 0.6 collective-permute-start.4
  11.8 5.9 %shard_map.140 = (bf16[16,64,256]{2,1,0:T(8,128)(2,1)}, bf16[10,64,128]{2,1,0:T(8,128)(2,1)S(1)}, f32[8,128]{1,0:T(8,128)S(1)}) custom-call(s32[16,256]{1,0:T(8,128)} %order_h, bf16[16,64,256]{2,1,0:T(8,128)(2,1)} %basis_h.1, bf16[16,64,256]{2,1,0:T(8,128)(2,1)} %direction.1, bf16[16,64,64]{2,1,0:T(8,128)(2,1)} %refs_8_.1, bf16[1,64,64]{2,1,0:T(8,128)(2,1)} %refs_7_.1), custom_call_target="tpu_custom_call" | custom-call | flops 268435456 | bytes 6291456 | tf_op jit(solution)/shard_map/pallas_call | solution.py:443
  17.8 1.5 %collective-permute-start.2 = (bf16[10,64,128]{2,1,0:T(8,128)(2,1)S(1)}, bf16[10,64,128]{2,1,0:T(8,128)(2,1)S(1)}, u32[]{:S(2)}, u32[]{:S(2)}) collective-permute-start(bf16[10,64,128]{2,1,0:T(8,128)(2,1)S(1)} %get-tuple-element.28.own), channel_id=1, source_target_pairs={{0,2},{2,0},{1,3},{3,1},{4,6},{6,4},{5,7},{7,5},{8,10},{10,8},{9,1... | collective-permute-start | bytes 491528 | tf_op jit(solution)/shard_map/ppermute | solution.py:32
  19.3 1.6 %collective-permute-start.5 = (bf16[8,64,256]{2,1,0:T(8,128)(2,1)S(1)}, bf16[8,64,256]{2,1,0:T(8,128)(2,1)S(1)}, u32[]{:S(2)}, u32[]{:S(2)}) collective-permute-start(bf16[8,64,256]{2,1,0:T(8,128)(2,1)S(1)} %collective-permute-done.3.refs_1_.refs_0_), channel_id=1, source_target_pairs={{0,4},{2,14},{4,8},{6,2},{8,12},{10,6},{12,0},{14,10},{1,5},{3,15}... | collective-permute-start | bytes 786440 | tf_op jit(solution)/shard_map/ppermute | solution.py:42
  20.9 0.7 copy-done.2
  21.6 6.1 %shard_map.141 = (bf16[4,3072,256]{2,1,0:T(8,128)(2,1)S(1)}, f32[8,128]{1,0:T(8,128)S(1)}, bf16[48,256,128]{2,1,0:T(8,128)(2,1)S(1)}, f32[3,16,256]{2,1,0:T(8,128)S(1)}) custom-call(s32[16,12]{1,0:T(8,128)} %near_h.5, f32[8,128]{1,0:T(8,128)S(1)} %get-tuple-element.29.refs_0_, bf16[8,64,256]{2,1,0:T(8,128)(2,1)S(1)} %collective-permute-done.3.refs_1_.refs_0_, ...), custom_call_target="tpu_custom_call" | custom-call | flops 125829120 | bytes 6291456 | tf_op jit(solution)/shard_map/pallas_call | solution.py:471
  27.7 1.6 %collective-permute-start.14 = (bf16[8,64,256]{2,1,0:T(8,128)(2,1)S(1)}, bf16[8,64,256]{2,1,0:T(8,128)(2,1)S(1)}, u32[]{:S(2)}, u32[]{:S(2)}) collective-permute-start(bf16[8,64,256]{2,1,0:T(8,128)(2,1)S(1)} %collective-permute-done.4.refs_1_.refs_2_), channel_id=1, source_target_pairs={{0,4},{2,14},{4,8},{6,2},{8,12},{10,6},{12,0},{14,10},{1,5},{3,15}... | collective-permute-start | bytes 786440 | tf_op jit(solution)/shard_map/ppermute | solution.py:42
  29.4 1.9 %collective-permute-start.9 = (bf16[10,64,128]{2,1,0:T(8,128)(2,1)S(1)}, bf16[10,64,128]{2,1,0:T(8,128)(2,1)S(1)}, u32[]{:S(2)}, u32[]{:S(2)}) collective-permute-start(bf16[10,64,128]{2,1,0:T(8,128)(2,1)S(1)} %collective-permute-done.2.refs_0_.refs_1_), channel_id=1, source_target_pairs={{0,4},{2,14},{4,8},{6,2},{8,12},{10,6},{12,0},{14,10},{1,5},{3,15}... | collective-permute-start | bytes 491528 | tf_op jit(solution)/shard_map/ppermute | solution.py:42
  31.3 5.5 %shard_map.142 = (bf16[4,3072,256]{2,1,0:T(8,128)(2,1)S(1)}, f32[8,128]{1,0:T(8,128)S(1)}) custom-call(s32[16,12]{1,0:T(8,128)} %near_h.5, f32[8,128]{1,0:T(8,128)S(1)} %get-tuple-element.31.refs_0_, bf16[8,64,256]{2,1,0:T(8,128)(2,1)S(1)} %collective-permute-done.4.refs_1_.refs_2_, bf16[8,64,256]{2,1,0:T(8,128)(2,1)S(1)} %collective-permute-done.5.refs_2_.refs_6_, ...), custom_call_target="tpu_custom_call" | custom-call | flops 125829120 | bytes 6291456 | tf_op jit(solution)/shard_map/pallas_call | solution.py:471
  36.7 2.0 %collective-permute-done.14.refs_8_ = bf16[8,64,256]{2,1,0:T(8,128)(2,1)S(1)} collective-permute-done((bf16[8,64,256]{2,1,0:T(8,128)(2,1)S(1)}, bf16[8,64,256]{2,1,0:T(8,128)(2,1)S(1)}, u32[]{:S(2)}, u32[]{:S(2)}) %collective-permute-start.14) | collective-permute-done | bytes 262176 | tf_op jit(solution)/shard_map/ppermute | solution.py:42
  38.7 0.5 collective-permute-start.13
  39.2 0.0 collective-permute-start.11
  39.2 2.3 %collective-permute-done.9.refs_15_.refs_2_ = bf16[10,64,128]{2,1,0:T(8,128)(2,1)S(1)} collective-permute-done((bf16[10,64,128]{2,1,0:T(8,128)(2,1)S(1)}, bf16[10,64,128]{2,1,0:T(8,128)(2,1)S(1)}, u32[]{:S(2)}, u32[]{:S(2)}) %collective-permute-start.9) | collective-permute-done | bytes 163872 | tf_op jit(solution)/shard_map/ppermute | solution.py:42
  41.6 0.1 shard_map.143
  41.7 0.0 copy-start.3
  41.7 0.1 collective-permute-start.6
  41.7 5.5 %collective-permute-done.6.refs_12_ = bf16[64,64]{1,0:T(8,128)(2,1)S(1)} collective-permute-done((bf16[64,64]{1,0:T(8,128)(2,1)S(1)}, bf16[64,64]{1,0:T(8,128)(2,1)S(1)}, u32[]{:S(2)}, u32[]{:S(2)}) %collective-permute-start.6) | collective-permute-done | bytes 8224 | tf_op jit(solution)/shard_map/ppermute | solution.py:32
  47.3 4.6 %collective-permute-done.7.refs_13_ = bf16[64,64]{1,0:T(8,128)(2,1)S(1)} collective-permute-done((bf16[64,64]{1,0:T(8,128)(2,1)S(1)}, bf16[64,64]{1,0:T(8,128)(2,1)S(1)}, u32[]{:S(2)}, u32[]{:S(2)}) %collective-permute-start.7) | collective-permute-done | bytes 8224 | tf_op jit(solution)/shard_map/ppermute | solution.py:32
  51.9 3.7 %collective-permute-done.8.refs_14_ = bf16[64,64]{1,0:T(8,128)(2,1)S(1)} collective-permute-done((bf16[64,64]{1,0:T(8,128)(2,1)S(1)}, bf16[64,64]{1,0:T(8,128)(2,1)S(1)}, u32[]{:S(2)}, u32[]{:S(2)}) %collective-permute-start.8) | collective-permute-done | bytes 8224 | tf_op jit(solution)/shard_map/ppermute | solution.py:32
  55.7 0.0 copy-start.1
  55.7 4.7 %shard_map.144 = (f32[8,64,256]{2,1,0:T(8,128)S(1)}, bf16[8,64,256]{2,1,0:T(8,128)(2,1)S(1)}, f32[8,128]{1,0:T(8,128)S(1)}) custom-call(s32[16,12]{1,0:T(8,128)} %near_h.5, bf16[8,64,256]{2,1,0:T(8,128)(2,1)S(1)} %collective-permute-done.3.refs_1_.refs_0_, bf16[8,64,256]{2,1,0:T(8,128)(2,1)S(1)} %collective-permute-done.10.refs_1_, ...), custom_call_target="tpu_custom_call" | custom-call | flops 1610612736 | bytes 12582912 | tf_op jit(solution)/shard_map/pallas_call | solution.py:523
  60.3 0.0 copy-start
  60.4 0.1 collective-permute-start.16
  60.5 4.8 %shard_map.145 = (f32[16,64,256]{2,1,0:T(8,128)S(1)}, f32[16,64,256]{2,1,0:T(8,128)S(1)}) custom-call(bf16[4,64,64]{2,1,0:T(8,128)(2,1)S(1)} %pad_maximum_fusion.refs_0_, bf16[10,64,128]{2,1,0:T(8,128)(2,1)S(1)} %collective-permute-done.2.refs_0_.refs_1_, bf16[10,64,128]{2,1,0:T(8,128)(2,1)S(1)} %collective-permute-done.9.refs_15_.refs_2_, ...), custom_call_target="tpu_custom_call" | custom-call | flops 109051904 | bytes 8388608 | tf_op jit(solution)/shard_map/pallas_call | solution.py:550
  65.3 1.2 %shard_map.146 = (f32[16,64,256]{2,1,0:T(8,128)}, f32[16,64,256]{2,1,0:T(8,128)S(1)}, f32[8,8,128]{2,1,0:T(8,128)S(1)}) custom-call(f32[1,64]{1,0:T(1,128)S(1)} %bitcast.11, f32[16,64,256]{2,1,0:T(8,128)S(1)} %get-tuple-element.45.base, f32[8,64,256]{2,1,0:T(8,128)S(1)} %get-tuple-element.46.kept, bf16[8,64,256]{2,1,0:T(8,128)(2,1)S(1)} %collective-permute-done.16.received, ...), custom_call_target="tpu_custom_call" | custom-call | flops 4194304 | bytes 5242880 | tf_op jit(solution)/shard_map/pallas_call | solution.py:565
  66.6 9.9 %all_to_all.5.norms = f32[8,8,128]{2,1,0:T(8,128)S(1)} all-to-all(f32[8,8,128]{2,1,0:T(8,128)S(1)} %get-tuple-element.50), channel_id=1, replica_groups=mesh['groups'=2,'blk'=4,'leaf'=2,'sample'=2] {'blk','leaf'}, dimensions={0} | all-to-all | bytes 65536 | tf_op jit(solution)/shard_map/all_to_all | solution.py:575
  76.5 0.9 %shard_map.147 = bf16[16,64,256]{2,1,0:T(8,128)(2,1)} custom-call(f32[8,8,128]{2,1,0:T(8,128)S(1)} %all_to_all.5.norms, f32[16,64,256]{2,1,0:T(8,128)S(1)} %get-tuple-element.51.updated, bf16[16,64,256]{2,1,0:T(8,128)(2,1)S(1)} %copy-done), custom_call_target="tpu_custom_call" | custom-call | flops 1048576 | bytes 2097152 | tf_op jit(solution)/shard_map/pallas_call | solution.py:576
  (21 shorter events, 0.1 us)
Async XLA Ops:
  0.6 8.0 %collective-permute-start = (bf16[3,16,256]{2,1,0:T(8,128)(2,1)}, bf16[3,16,256]{2,1,0:T(8,128)(2,1)S(1)}, u32[]{:S(2)}, u32[]{:S(2)}) collective-permute-start(bf16[3,16,256]{2,1,0:T(8,128)(2,1)} %bitcast.12), channel_id=1, source_target_pairs={{0,2},{2,4},{4,6},{6,8},{8,10},{10,12},{12,14},{14,0},{1,3},{3,5},... | collective-permute-start | bytes 73736 | tf_op jit(solution)/shard_map/ppermute | solution.py:32
  3.6 5.1 %collective-permute-start.1 = (bf16[3,16,256]{2,1,0:T(8,128)(2,1)}, bf16[3,16,256]{2,1,0:T(8,128)(2,1)S(1)}, u32[]{:S(2)}, u32[]{:S(2)}) collective-permute-start(bf16[3,16,256]{2,1,0:T(8,128)(2,1)} %bitcast.13), channel_id=1, source_target_pairs={{0,14},{2,0},{4,2},{6,4},{8,6},{10,8},{12,10},{14,12},{1,15},{3,1}... | collective-permute-start | bytes 73736 | tf_op jit(solution)/shard_map/ppermute | solution.py:32
  9.8 9.5 %collective-permute-start.3 = (bf16[8,64,256]{2,1,0:T(8,128)(2,1)S(1)}, bf16[8,64,256]{2,1,0:T(8,128)(2,1)S(1)}, u32[]{:S(2)}, u32[]{:S(2)}) collective-permute-start(bf16[8,64,256]{2,1,0:T(8,128)(2,1)S(1)} %get-tuple-element.53), channel_id=1, source_target_pairs={{0,2},{2,0},{1,3},{3,1},{4,6},{6,4},{5,7},{7,5},{8,10},{10,8},{9,1... | collective-permute-start | bytes 786440 | tf_op jit(solution)/shard_map/ppermute | solution.py:32
  11.2 16.5 %collective-permute-start.4 = (bf16[8,64,256]{2,1,0:T(8,128)(2,1)S(1)}, bf16[8,64,256]{2,1,0:T(8,128)(2,1)S(1)}, u32[]{:S(2)}, u32[]{:S(2)}) collective-permute-start(bf16[8,64,256]{2,1,0:T(8,128)(2,1)S(1)} %get-tuple-element.52), channel_id=1, source_target_pairs={{0,2},{2,0},{1,3},{3,1},{4,6},{6,4},{5,7},{7,5},{8,10},{10,8},{9,1... | collective-permute-start | bytes 786440 | tf_op jit(solution)/shard_map/ppermute | solution.py:32
  17.8 11.6 %collective-permute-start.2 = (bf16[10,64,128]{2,1,0:T(8,128)(2,1)S(1)}, bf16[10,64,128]{2,1,0:T(8,128)(2,1)S(1)}, u32[]{:S(2)}, u32[]{:S(2)}) collective-permute-start(bf16[10,64,128]{2,1,0:T(8,128)(2,1)S(1)} %get-tuple-element.28.own), channel_id=1, source_target_pairs={{0,2},{2,0},{1,3},{3,1},{4,6},{6,4},{5,7},{7,5},{8,10},{10,8},{9,1... | collective-permute-start | bytes 491528 | tf_op jit(solution)/shard_map/ppermute | solution.py:32
  19.3 22.4 %collective-permute-start.12 = (bf16[16,64,256]{2,1,0:T(8,128)(2,1)}, bf16[16,64,256]{2,1,0:T(8,128)(2,1)S(1)}, u32[]{:S(2)}, u32[]{:S(2)}) collective-permute-start(bf16[16,64,256]{2,1,0:T(8,128)(2,1)} %direction.1), channel_id=1, source_target_pairs={{0,1},{1,0},{2,3},{3,2},{4,5},{5,4},{6,7},{7,6},{8,9},{9,8},{10,11... | collective-permute-start | bytes 1572872 | tf_op jit(solution)/shard_map/ppermute | solution.py:36
  19.3 12.0 %collective-permute-start.5 = (bf16[8,64,256]{2,1,0:T(8,128)(2,1)S(1)}, bf16[8,64,256]{2,1,0:T(8,128)(2,1)S(1)}, u32[]{:S(2)}, u32[]{:S(2)}) collective-permute-start(bf16[8,64,256]{2,1,0:T(8,128)(2,1)S(1)} %collective-permute-done.3.refs_1_.refs_0_), channel_id=1, source_target_pairs={{0,4},{2,14},{4,8},{6,2},{8,12},{10,6},{12,0},{14,10},{1,5},{3,15}... | collective-permute-start | bytes 786440 | tf_op jit(solution)/shard_map/ppermute | solution.py:42
  20.9 0.7 copy-start.2
  27.7 11.0 %collective-permute-start.14 = (bf16[8,64,256]{2,1,0:T(8,128)(2,1)S(1)}, bf16[8,64,256]{2,1,0:T(8,128)(2,1)S(1)}, u32[]{:S(2)}, u32[]{:S(2)}) collective-permute-start(bf16[8,64,256]{2,1,0:T(8,128)(2,1)S(1)} %collective-permute-done.4.refs_1_.refs_2_), channel_id=1, source_target_pairs={{0,4},{2,14},{4,8},{6,2},{8,12},{10,6},{12,0},{14,10},{1,5},{3,15}... | collective-permute-start | bytes 786440 | tf_op jit(solution)/shard_map/ppermute | solution.py:42
  29.4 12.2 %collective-permute-start.9 = (bf16[10,64,128]{2,1,0:T(8,128)(2,1)S(1)}, bf16[10,64,128]{2,1,0:T(8,128)(2,1)S(1)}, u32[]{:S(2)}, u32[]{:S(2)}) collective-permute-start(bf16[10,64,128]{2,1,0:T(8,128)(2,1)S(1)} %collective-permute-done.2.refs_0_.refs_1_), channel_id=1, source_target_pairs={{0,4},{2,14},{4,8},{6,2},{8,12},{10,6},{12,0},{14,10},{1,5},{3,15}... | collective-permute-start | bytes 491528 | tf_op jit(solution)/shard_map/ppermute | solution.py:42
  38.7 16.9 %collective-permute-start.15 = (bf16[8,64,256]{2,1,0:T(8,128)(2,1)S(1)}, bf16[8,64,256]{2,1,0:T(8,128)(2,1)S(1)}, u32[]{:S(2)}, u32[]{:S(2)}) collective-permute-start(bf16[8,64,256]{2,1,0:T(8,128)(2,1)S(1)} %collective-permute-done.14.refs_8_), channel_id=1, source_target_pairs={{0,1},{1,0},{2,3},{3,2},{4,5},{5,4},{6,7},{7,6},{8,9},{9,8},{10,11... | collective-permute-start | bytes 786440 | tf_op jit(solution)/shard_map/ppermute | solution.py:36
  38.7 16.9 %collective-permute-start.13 = (bf16[8,64,256]{2,1,0:T(8,128)(2,1)S(1)}, bf16[8,64,256]{2,1,0:T(8,128)(2,1)S(1)}, u32[]{:S(2)}, u32[]{:S(2)}) collective-permute-start(bf16[8,64,256]{2,1,0:T(8,128)(2,1)S(1)} %collective-permute-done.5.refs_2_.refs_6_), channel_id=1, source_target_pairs={{0,1},{1,0},{2,3},{3,2},{4,5},{5,4},{6,7},{7,6},{8,9},{9,8},{10,11... | collective-permute-start | bytes 786440 | tf_op jit(solution)/shard_map/ppermute | solution.py:36
  39.2 16.4 %collective-permute-start.11 = (bf16[8,64,256]{2,1,0:T(8,128)(2,1)S(1)}, bf16[8,64,256]{2,1,0:T(8,128)(2,1)S(1)}, u32[]{:S(2)}, u32[]{:S(2)}) collective-permute-start(bf16[8,64,256]{2,1,0:T(8,128)(2,1)S(1)} %collective-permute-done.4.refs_1_.refs_2_), channel_id=1, source_target_pairs={{0,1},{1,0},{2,3},{3,2},{4,5},{5,4},{6,7},{7,6},{8,9},{9,8},{10,11... | collective-permute-start | bytes 786440 | tf_op jit(solution)/shard_map/ppermute | solution.py:36
  41.6 14.1 %collective-permute-start.10 = (bf16[8,64,256]{2,1,0:T(8,128)(2,1)S(1)}, bf16[8,64,256]{2,1,0:T(8,128)(2,1)S(1)}, u32[]{:S(2)}, u32[]{:S(2)}) collective-permute-start(bf16[8,64,256]{2,1,0:T(8,128)(2,1)S(1)} %collective-permute-done.3.refs_1_.refs_0_), channel_id=1, source_target_pairs={{0,1},{1,0},{2,3},{3,2},{4,5},{5,4},{6,7},{7,6},{8,9},{9,8},{10,11... | collective-permute-start | bytes 786440 | tf_op jit(solution)/shard_map/ppermute | solution.py:36
  41.7 14.0 %copy-start.3 = (bf16[16,64,256]{2,1,0:T(8,128)(2,1)}, bf16[16,64,256]{2,1,0:T(8,128)(2,1)S(1)}, u32[]{:S(2)}) copy-start(bf16[16,64,256]{2,1,0:T(8,128)(2,1)S(1)} %collective-permute-done.12.refs_5_) | copy-start | bytes 1572868
  41.7 5.6 %collective-permute-start.6 = (bf16[64,64]{1,0:T(8,128)(2,1)S(1)}, bf16[64,64]{1,0:T(8,128)(2,1)S(1)}, u32[]{:S(2)}, u32[]{:S(2)}) collective-permute-start(bf16[64,64]{1,0:T(8,128)(2,1)S(1)} %shard_map.143), channel_id=1, source_target_pairs={{0,4},{4,8},{8,12},{12,0},{1,5},{5,9},{9,13},{13,1},{2,6},{6,10},{... | collective-permute-start | bytes 24584 | tf_op jit(solution)/shard_map/ppermute | solution.py:32
  47.3 4.6 %collective-permute-start.7 = (bf16[64,64]{1,0:T(8,128)(2,1)S(1)}, bf16[64,64]{1,0:T(8,128)(2,1)S(1)}, u32[]{:S(2)}, u32[]{:S(2)}) collective-permute-start(bf16[64,64]{1,0:T(8,128)(2,1)S(1)} %shard_map.143), channel_id=1, source_target_pairs={{0,8},{4,12},{8,0},{12,4},{1,9},{5,13},{9,1},{13,5},{2,10},{6,14},... | collective-permute-start | bytes 24584 | tf_op jit(solution)/shard_map/ppermute | solution.py:32
  51.9 3.7 %collective-permute-start.8 = (bf16[64,64]{1,0:T(8,128)(2,1)S(1)}, bf16[64,64]{1,0:T(8,128)(2,1)S(1)}, u32[]{:S(2)}, u32[]{:S(2)}) collective-permute-start(bf16[64,64]{1,0:T(8,128)(2,1)S(1)} %shard_map.143), channel_id=1, source_target_pairs={{0,12},{4,0},{8,4},{12,8},{1,13},{5,1},{9,5},{13,9},{2,14},{6,2},{... | collective-permute-start | bytes 24584 | tf_op jit(solution)/shard_map/ppermute | solution.py:32
  55.7 9.6 %copy-start.1 = (f32[64]{0:T(128)S(1)}, f32[64]{0:T(128)}, u32[]{:S(2)}) copy-start(f32[64]{0:T(128)} %param.15) | copy-start | bytes 772
  60.3 16.1 %copy-start = (bf16[16,64,256]{2,1,0:T(8,128)(2,1)S(1)}, bf16[16,64,256]{2,1,0:T(8,128)(2,1)}, u32[]{:S(2)}) copy-start(bf16[16,64,256]{2,1,0:T(8,128)(2,1)} %direction.1) | copy-start | bytes 1572868
  60.4 5.0 %collective-permute-start.16 = (bf16[8,64,256]{2,1,0:T(8,128)(2,1)S(1)}, bf16[8,64,256]{2,1,0:T(8,128)(2,1)S(1)}, u32[]{:S(2)}, u32[]{:S(2)}) collective-permute-start(bf16[8,64,256]{2,1,0:T(8,128)(2,1)S(1)} %get-tuple-element.47), channel_id=1, source_target_pairs={{0,1},{1,0},{2,3},{3,2},{4,5},{5,4},{6,7},{7,6},{8,9},{9,8},{10,11... | collective-permute-start | bytes 786440 | tf_op jit(solution)/shard_map/ppermute | solution.py:36

commit v7 on v4

--- a/solution.py
+++ b/solution.py
@@ -130,7 +130,7 @@
 
 
 def features(offsets):
-    x, y, z = (offsets[i : i + 1, :] for i in range(3))
+    x, y, z = (offsets[i : i + 1] for i in range(3))
     square = thirds(KAPPA * (x * x + y * y + z * z))
     row = lax.broadcasted_iota(jnp.int32, (8, x.shape[1]), 0)
     packed = jnp.zeros((8, x.shape[1]), F32)
@@ -154,33 +154,39 @@
     ).astype(BF)
 
 
-def tile_kernel(start, near_h, _, own, *refs):
+def tile_kernel(start, near_h, _, *refs):
     if start == 0:
-        prev, after, tiles, mark, spread_x, near, sem = refs
+        own_h, prev, after, tiles, mark, spread_x, plain, own, near, sem = refs
+        offered = pltpu.make_async_copy(own_h, own, sem.at[1])
+        offered.start()
     else:
-        spread_x, tiles, mark, near, sem = refs
-    listed = pltpu.make_async_copy(near_h, near, sem)
+        plain, spread_x, tiles, mark, near, sem = refs
+        own = plain
+    listed = pltpu.make_async_copy(near_h, near, sem.at[0])
     listed.start()
     mark[...] = jnp.zeros_like(mark)
     count = tiles.shape[0]
     entries = near.shape[1]
     points = own.shape[2]
-    leaves = own.shape[0]
+    leaves = own.shape[1]
     total = leaves * lax.axis_size("blk") * lax.axis_size("leaf")
     device = lax.axis_index("blk") * lax.axis_size("leaf") + lax.axis_index("leaf")
     anchor = (device - 1) * leaves
     if start == 0:
+        offered.wait()
         for side, ref in enumerate((prev, own, after)):
+            offsets = ref[...].astype(F32)
             for j in range(leaves):
-                spread_x[side * leaves + j] = spread_features(ref[j].astype(F32))
+                spread_x[side * leaves + j] = spread_features(offsets[:, j])
+            if side == 1:
+                plain[...] = offsets
     listed.wait()
     row = lax.broadcasted_iota(jnp.int32, (16, points), 0)
     lane = lax.broadcasted_iota(jnp.int32, (1, 128), 1)
 
     def leaf(i, carry):
         g = lax.axis_index("sample") * (leaves // 2) + start + i
-        offsets = own[g].astype(F32)
-        x, y, z = (offsets[k : k + 1, :] for k in range(3))
+        x, y, z = (plain[k, pl.ds(g, 1), :] for k in range(3))
         first = jnp.where((row >= 9) & (row < 12), 1.0, jnp.zeros((16, points), F32))
         at = 0
         for value in (x, y, z):
@@ -228,41 +234,26 @@
 
 
 def down_kernel(*refs):
-    tops, before, after, residual_h = refs[:4]
-    sources, (base, residual), targets, sems = refs[4:12], refs[13:15], refs[15:24], refs[24]
-    window, targets = targets[0], targets[1:]
-    top_list, coupling_list, top_coupling, node_transfer = targets[:4]
-    leaf_transfer, coupling, natural, direction = targets[4:]
+    tops, before, after, leaf_transfer, coupling, natural, direction = refs[:7]
+    sources, base, window, targets, sems = refs[7:11], refs[12], refs[13], refs[14:18], refs[18]
+    top_list, coupling_list, top_coupling, node_transfer = targets
     leaves, samples, points = direction.shape
     rank = natural.shape[1]
     clusters = lax.axis_size("blk")
     here = lax.axis_index("blk")
     total = leaves * clusters * lax.axis_size("leaf")
     anchor = (here * lax.axis_size("leaf") + lax.axis_index("leaf") - 1) * leaves
-    pairs = list(zip(sources[:4], targets[:4]))
-    whole = [
-        pltpu.make_async_copy(source, target, sems.at[0, i])
-        for i, (source, target) in enumerate(pairs)
+    copies = [
+        pltpu.make_async_copy(source, target, sems.at[i])
+        for i, (source, target) in enumerate(zip(sources, targets))
     ]
-    chunks = 4
-    size = leaves // chunks
-    parts = []
-    for c in range(chunks):
-        part = pl.ds(c * size, size)
-        parts.append(
-            [
-                pltpu.make_async_copy(source.at[part], target.at[part], sems.at[1 + c, i])
-                for i, (source, target) in enumerate(zip(sources[4:], targets[4:]))
-            ]
-        )
-    ahead = pltpu.make_async_copy(residual_h, residual, sems.at[0, 6])
-    for copy in whole + sum(parts, []) + [ahead]:
+    for copy in copies:
         copy.start()
     for side, packed in enumerate((before, after)):
         for g in range(leaves):
             part = packed[g // 2, :, (g % 2) * rank : (g % 2 + 1) * rank]
             window[side * leaves + g] = part
-    for copy in whole:
+    for copy in copies:
         copy.wait()
     incoming = jnp.zeros((samples, rank), F32)
     for e in range(top_list.shape[1]):
@@ -270,21 +261,17 @@
         incoming = incoming + nt(tops[place], top_coupling[0, e])
     down = nn(incoming.astype(BF), node_transfer[0]).astype(BF)
     for g in range(leaves):
-        if g % size == 0:
-            for copy in parts[g // size]:
-                copy.wait()
         inward = nn(down, leaf_transfer[g])
         rows = []
-        for c in range(coupling_list.shape[1]):
-            slot = lax.rem(coupling_list[g, c] - anchor + 2 * total, total)
+        for c in range(coupling_list.shape[0]):
+            slot = lax.rem(coupling_list[c, g] - anchor + 2 * total, total)
             slot = jnp.where(slot >= 2 * leaves, slot - leaves, slot)
             slot = jnp.minimum(slot, 2 * leaves - 1)
             rows.append(window[slot])
-        columns = [coupling[g, c] for c in range(coupling_list.shape[1])]
+        columns = [coupling[g, c] for c in range(coupling_list.shape[0])]
         inward = inward + nt(jnp.concatenate(rows, axis=1), jnp.concatenate(columns, axis=1))
         far = nn(inward.astype(BF), natural[g])
         base[g] = NUGGET * direction[g].astype(F32) + far
-    ahead.wait()
 
 
 def near_kernel(near_h, *refs):
@@ -413,6 +400,7 @@
     anywhere = pl.BlockSpec(memory_space=pl.ANY)
     hbm = pl.BlockSpec(memory_space=pltpu.HBM)
 
+    coords = jnp.transpose(coords, (1, 0, 2))
     coords_prev = shifted(coords, RING, 1)
     coords_after = shifted(coords, RING, -1)
     travelling, first = lax.optimization_barrier((direction, order, coords_prev, coords_after))[:2]
@@ -447,34 +435,32 @@
         count = half // 2
         outs = (pltpu.VMEM((count, entries * points, points), BF), token)
         if start == 0:
-            outs += (shape((3 * leaves, points, 128), BF),)
+            outs += (shape((3 * leaves, points, 128), BF), shape(coords.shape, F32))
         return call(
             functools.partial(tile_kernel, start),
             outs,
             40 * count * entries * points * points,
-            count * entries * points * points * 2,
-            in_specs=[hbm, anywhere] + [vmem] * len(operands),
+            count * entries * points * points * (16 if start == 0 else 1),
+            in_specs=[hbm, anywhere, hbm if start == 0 else vmem] + [vmem] * (len(operands) - 1),
             out_specs=(vmem,) * len(outs),
-            scratch_shapes=[
-                pltpu.SMEM(near_list.shape, jnp.int32),
-                pltpu.SemaphoreType.DMA,
-            ],
+            scratch_shapes=[pltpu.VMEM(coords.shape, BF)] * (start == 0)
+            + [pltpu.SMEM(near_list.shape, jnp.int32), pltpu.SemaphoreType.DMA((2,))],
             vmem=8,
         )(*in_hbm(near_list), done, *operands)
 
     coef_prev = shifted(coef, RING, 1)
     coef_after = shifted(coef, RING, -1)
-    tiles_low, low_mark, spread_x = make_tiles(
-        0, up_mark, coords, coords_prev, coords_after
-    )
-    tiles_high, high_mark = make_tiles(half // 2, low_mark, coords, spread_x)
+    tiles_low, low_mark, spread_x, plain = make_tiles(
+        0, up_mark, *in_hbm(coords), coords_prev, coords_after
+    )
+    tiles_high, high_mark = make_tiles(half // 2, low_mark, plain, spread_x)
     direction_prev = ordered(direction_prev, high_mark)
     direction_after = ordered(direction_after, high_mark)
     kept, given, near_mark = call(
         near_kernel,
         (shape((half, samples, points), F32), shape((half, samples, points), BF), token),
-        4 * half * entries * samples * points * points,
-        half * entries * points * points * 2,
+        MIB,
+        MIB,
         in_specs=[hbm] + [anywhere] * 6 + [vmem] * 2,
         out_specs=(vmem,) * 3,
         scratch_shapes=[
@@ -515,30 +501,31 @@
         places = jnp.mod(lax.axis_index("blk") - jnp.arange(blk_count, dtype=jnp.int32), blk_count)
         others = list(others[places][1:])
     tops = jnp.stack([top] + others)
-    arrays = (
-        top_list,
-        coupling_list,
-        top_coupling,
-        node_transfer,
+    arrays = (top_list, coupling_list.T, top_coupling, node_transfer)
+    spaces = (pltpu.SMEM,) * 2 + (pltpu.VMEM,) * 2
+    whole = shape((leaves, samples, points), F32)
+    base = call(
+        down_kernel,
+        whole,
+        2 * leaves * samples * rank * (points + 9 * rank),
+        8 * MIB,
+        in_specs=[vmem] * 7 + [hbm] * 4 + [anywhere],
+        out_specs=vmem,
+        scratch_shapes=[pltpu.VMEM((2 * leaves, samples, rank), BF)]
+        + [space(array.shape, array.dtype) for space, array in zip(spaces, arrays)]
+        + [pltpu.SemaphoreType.DMA((4,))],
+        vmem=10,
+    )(
+        tops,
+        coef_prev,
+        coef_after,
         leaf_transfer,
         coupling,
         natural,
         direction,
-    )
-    spaces = (pltpu.SMEM,) * 2 + (pltpu.VMEM,) * 6
-    whole = shape((leaves, samples, points), F32)
-    base, residual_here = call(
-        down_kernel,
-        (whole, whole),
-        2 * leaves * samples * rank * (points + 9 * rank),
-        8 * MIB,
-        in_specs=[vmem] * 3 + [hbm] * 9 + [anywhere],
-        out_specs=(vmem, vmem),
-        scratch_shapes=[pltpu.VMEM((2 * leaves, samples, rank), BF)]
-        + [space(array.shape, array.dtype) for space, array in zip(spaces, arrays)]
-        + [pltpu.SemaphoreType.DMA((5, 7))],
-        vmem=10,
-    )(tops, coef_prev, coef_after, *in_hbm(residual, *arrays), near_mark)
+        *in_hbm(*arrays),
+        near_mark,
+    )
     received = partner(given)
 
     devices = blk_count * leaf_count
@@ -551,7 +538,7 @@
         out_specs=(hbm, vmem, vmem),
         scratch_shapes=[pltpu.SemaphoreType.DMA((2, 4))],
         vmem=8,
-    )(step[None, :], base, kept, received, residual_here)
+    )(step[None, :], base, kept, received, residual)
     norms = lax.all_to_all(norms, RING, 0, 0)
     direction_next = call(
         direction_kernel,

time: 70.3 us -> 68.7 us (0.977)
  local copies, waits for them, and re-layouts: 1.44 us -> 0.04 us
    unnamed x8 -> x12, local copies, waits for them, and re-layouts: 1.44 us -> 0.04 us
    pallas_call x1, Pallas kernels: 4.79 us -> 3.75 us  [on_device(): call(down_kernel, whole, 2 * leaves * samples * rank * (points + 9 * rank...]
    pallas_call x2, Pallas kernels: 11.3 us -> 12 us  [make_tiles(): call(functools.partial(tile_kernel, start), outs, 40 * count * entries *...]
  transfers between devices with their start and end apart: 13 -> 13, of which waited for: 5 -> 5; matrix products, arithmetic and copies ran while one was open for 1% -> 0% of each run, Pallas kernels for 38% -> 39%
where the time goes in v7:
time: 68.7 us; the launch traced here: 68.3 us
  Pallas kernels  28.6 us (42%)
  starting transfers between devices  20.3 us (30%)
  blocking collectives  10.6 us (15%)
  waiting for transfers between devices  8.02 us (12%)
  between operations  0.82 us (1%)
    ppermute x9, starting transfers between devices, shifted(): lax.ppermute(array, axis, [(i, (i + by) % count) for i in range(count)])  19.7 us
    pallas_call x2, Pallas kernels, make_tiles(): call(functools.partial(tile_kernel, start), outs, 40 * count * entries *...  12 us
    all_to_all x1, blocking collectives, on_device(): norms = lax.all_to_all(norms, RING, 0, 0)  10.6 us
    ppermute x9, waiting for transfers between devices, shifted(): lax.ppermute(array, axis, [(i, (i + by) % count) for i in range(count)])  8.01 us
    pallas_call x1, Pallas kernels, on_device(): call(up_kernel, (pltpu.HBM((leaves, rank, points), BF), shape((leaves //...  5.94 us
    pallas_call x1, Pallas kernels, on_device(): call(near_kernel, (shape((half, samples, points), F32), shape((half, samp...  4.61 us
    pallas_call x1, Pallas kernels, on_device(): call(down_kernel, whole, 2 * leaves * samples * rank * (points + 9 * rank...  3.75 us
  transfers between devices with their start and end apart: 13, of which 5 were waited for; matrix products, arithmetic and copies ran while one was open for 0% of the time, Pallas kernels for 39%

profile of v7, /device:TPU:0, one launch (start us, length us, event | category | flops | bytes accessed | tf_op | source)
XLA Modules:
  0.0 68.3 jit_solution(8786138049973068646)
XLA Ops:
  0.6 3.0 %collective-permute-start = (bf16[3,16,256]{2,1,0:T(8,128)(2,1)}, bf16[3,16,256]{2,1,0:T(8,128)(2,1)S(1)}, u32[]{:S(2)}, u32[]{:S(2)}) collective-permute-start(bf16[3,16,256]{2,1,0:T(8,128)(2,1)} %bitcast.13), channel_id=1, source_target_pairs={{0,2},{2,4},{4,6},{6,8},{8,10},{10,12},{12,14},{14,0},{1,3},{3,5},... | collective-permute-start | bytes 73736 | tf_op jit(solution)/shard_map/ppermute | solution.py:32
  3.6 3.1 %collective-permute-start.1 = (bf16[3,16,256]{2,1,0:T(8,128)(2,1)}, bf16[3,16,256]{2,1,0:T(8,128)(2,1)S(1)}, u32[]{:S(2)}, u32[]{:S(2)}) collective-permute-start(bf16[3,16,256]{2,1,0:T(8,128)(2,1)} %bitcast.14), channel_id=1, source_target_pairs={{0,14},{2,0},{4,2},{6,4},{8,6},{10,8},{12,10},{14,12},{1,15},{3,1}... | collective-permute-start | bytes 73736 | tf_op jit(solution)/shard_map/ppermute | solution.py:32
  6.7 2.0 %collective-permute-done.refs_1_ = bf16[3,16,256]{2,1,0:T(8,128)(2,1)S(1)} collective-permute-done((bf16[3,16,256]{2,1,0:T(8,128)(2,1)}, bf16[3,16,256]{2,1,0:T(8,128)(2,1)S(1)}, u32[]{:S(2)}, u32[]{:S(2)}) %collective-permute-start) | collective-permute-done | bytes 24608 | tf_op jit(solution)/shard_map/ppermute | solution.py:32
  8.7 0.0 collective-permute-done.1.refs_2_
  8.7 4.8 %collective-permute-start.7 = (bf16[16,64,256]{2,1,0:T(8,128)(2,1)}, bf16[16,64,256]{2,1,0:T(8,128)(2,1)S(1)}, u32[]{:S(2)}, u32[]{:S(2)}) collective-permute-start(bf16[16,64,256]{2,1,0:T(8,128)(2,1)} %direction.1), channel_id=1, source_target_pairs={{0,14},{2,0},{4,2},{6,4},{8,6},{10,8},{12,10},{14,12},{1,15},{3,1}... | collective-permute-start | bytes 1572872 | tf_op jit(solution)/shard_map/ppermute | solution.py:32
  13.5 0.0 collective-permute-start.6
  13.5 5.9 %shard_map.140 = (bf16[16,64,256]{2,1,0:T(8,128)(2,1)}, bf16[10,64,128]{2,1,0:T(8,128)(2,1)S(1)}, f32[8,128]{1,0:T(8,128)S(1)}) custom-call(s32[16,256]{1,0:T(8,128)} %order_h, bf16[16,64,256]{2,1,0:T(8,128)(2,1)} %basis_h.1, bf16[16,64,256]{2,1,0:T(8,128)(2,1)} %direction.1, bf16[16,64,64]{2,1,0:T(8,128)(2,1)} %refs_3_.1, bf16[1,64,64]{2,1,0:T(8,128)(2,1)} %refs_10_.1), custom_call_target="tpu_custom_call" | custom-call | flops 268435456 | bytes 6291456 | tf_op jit(solution)/shard_map/pallas_call | solution.py:411
  19.4 6.5 %shard_map.141 = (bf16[4,3072,256]{2,1,0:T(8,128)(2,1)S(1)}, f32[8,128]{1,0:T(8,128)S(1)}, bf16[48,256,128]{2,1,0:T(8,128)(2,1)S(1)}, f32[3,16,256]{2,1,0:T(8,128)S(1)}) custom-call(s32[16,12]{1,0:T(8,128)} %near_h.5, f32[8,128]{1,0:T(8,128)S(1)} %get-tuple-element.24._, bf16[3,16,256]{2,1,0:T(8,128)(2,1)} %bitcast.15, ...), custom_call_target="tpu_custom_call" | custom-call | flops 125829120 | bytes 50331648 | tf_op jit(solution)/shard_map/pallas_call | solution.py:439
  25.9 5.5 %shard_map.142 = (bf16[4,3072,256]{2,1,0:T(8,128)(2,1)S(1)}, f32[8,128]{1,0:T(8,128)}) custom-call(s32[16,12]{1,0:T(8,128)} %near_h.5, f32[8,128]{1,0:T(8,128)S(1)} %get-tuple-element.25._, f32[3,16,256]{2,1,0:T(8,128)S(1)} %get-tuple-element.26.refs_0_, bf16[48,256,128]{2,1,0:T(8,128)(2,1)S(1)} %get-tuple-element.27.refs_1_), custom_call_target="tpu_custom_call" | custom-call | flops 125829120 | bytes 3145728 | tf_op jit(solution)/shard_map/pallas_call | solution.py:439
  31.4 1.6 %collective-permute-done.7.refs_4_ = bf16[16,64,256]{2,1,0:T(8,128)(2,1)S(1)} collective-permute-done((bf16[16,64,256]{2,1,0:T(8,128)(2,1)}, bf16[16,64,256]{2,1,0:T(8,128)(2,1)S(1)}, u32[]{:S(2)}, u32[]{:S(2)}) %collective-permute-start.7) | collective-permute-done | bytes 524320 | tf_op jit(solution)/shard_map/ppermute | solution.py:32
  33.0 0.5 collective-permute-start.5
  33.5 1.2 %collective-permute-start.2 = (bf16[10,64,128]{2,1,0:T(8,128)(2,1)S(1)}, bf16[10,64,128]{2,1,0:T(8,128)(2,1)S(1)}, u32[]{:S(2)}, u32[]{:S(2)}) collective-permute-start(bf16[10,64,128]{2,1,0:T(8,128)(2,1)S(1)} %get-tuple-element.22.own), channel_id=1, source_target_pairs={{0,2},{2,4},{4,6},{6,8},{8,10},{10,12},{12,14},{14,0},{1,3},{3,5},... | collective-permute-start | bytes 491528 | tf_op jit(solution)/shard_map/ppermute | solution.py:32
  34.7 3.6 %collective-permute-start.3 = (bf16[10,64,128]{2,1,0:T(8,128)(2,1)S(1)}, bf16[10,64,128]{2,1,0:T(8,128)(2,1)S(1)}, u32[]{:S(2)}, u32[]{:S(2)}) collective-permute-start(bf16[10,64,128]{2,1,0:T(8,128)(2,1)S(1)} %get-tuple-element.22.own), channel_id=1, source_target_pairs={{0,14},{2,0},{4,2},{6,4},{8,6},{10,8},{12,10},{14,12},{1,15},{3,1}... | collective-permute-start | bytes 491528 | tf_op jit(solution)/shard_map/ppermute | solution.py:32
  38.3 0.0 copy-start
  38.3 0.0 copy-start.1
  38.3 0.0 copy-start.3
  38.3 0.0 copy-start.4
  38.3 0.0 copy-start.5
  38.3 4.6 %shard_map.143 = (f32[8,64,256]{2,1,0:T(8,128)S(1)}, bf16[8,64,256]{2,1,0:T(8,128)(2,1)S(1)}, f32[8,128]{1,0:T(8,128)S(1)}) custom-call(s32[16,12]{1,0:T(8,128)} %near_h.5, bf16[16,64,256]{2,1,0:T(8,128)(2,1)S(1)} %collective-permute-done.4.refs_0_, bf16[16,64,256]{2,1,0:T(8,128)(2,1)S(1)} %collective-permute-done.5.refs_1_, bf16[16,64,256]{2,1,0:T(8,128)(2,1)} %direction.1, ...), custom_call_target="tpu_custom_call" | custom-call | flops 1048576 | bytes 1048576 | tf_op jit(solution)/shard_map/pallas_call | solution.py:459
  42.9 0.0 copy-start.2
  43.0 0.1 collective-permute-start.12
  43.1 1.5 %collective-permute-done.3.refs_1_.refs_2_ = bf16[10,64,128]{2,1,0:T(8,128)(2,1)S(1)} collective-permute-done((bf16[10,64,128]{2,1,0:T(8,128)(2,1)S(1)}, bf16[10,64,128]{2,1,0:T(8,128)(2,1)S(1)}, u32[]{:S(2)}, u32[]{:S(2)}) %collective-permute-start.3) | collective-permute-done | bytes 163872 | tf_op jit(solution)/shard_map/ppermute | solution.py:32
  44.5 0.1 shard_map.144
  44.6 0.2 collective-permute-start.9
  44.8 3.2 %collective-permute-start.10 = (bf16[64,64]{1,0:T(8,128)(2,1)S(1)}, bf16[64,64]{1,0:T(8,128)(2,1)S(1)}, u32[]{:S(2)}, u32[]{:S(2)}) collective-permute-start(bf16[64,64]{1,0:T(8,128)(2,1)S(1)} %shard_map.144), channel_id=1, source_target_pairs={{0,8},{4,12},{8,0},{12,4},{1,9},{5,13},{9,1},{13,5},{2,10},{6,14},... | collective-permute-start | bytes 24584 | tf_op jit(solution)/shard_map/ppermute | solution.py:32
  48.0 0.8 %collective-permute-start.11 = (bf16[64,64]{1,0:T(8,128)(2,1)S(1)}, bf16[64,64]{1,0:T(8,128)(2,1)S(1)}, u32[]{:S(2)}, u32[]{:S(2)}) collective-permute-start(bf16[64,64]{1,0:T(8,128)(2,1)S(1)} %shard_map.144), channel_id=1, source_target_pairs={{0,12},{4,0},{8,4},{12,8},{1,13},{5,1},{9,5},{13,9},{2,14},{6,2},{... | collective-permute-start | bytes 24584 | tf_op jit(solution)/shard_map/ppermute | solution.py:32
  48.7 1.6 %collective-permute-done.9 = bf16[64,64]{1,0:T(8,128)(2,1)S(1)} collective-permute-done((bf16[64,64]{1,0:T(8,128)(2,1)S(1)}, bf16[64,64]{1,0:T(8,128)(2,1)S(1)}, u32[]{:S(2)}, u32[]{:S(2)}) %collective-permute-start.9) | collective-permute-done | bytes 8224 | tf_op jit(solution)/shard_map/ppermute | solution.py:32
  50.4 1.3 %collective-permute-done.11 = bf16[64,64]{1,0:T(8,128)(2,1)S(1)} collective-permute-done((bf16[64,64]{1,0:T(8,128)(2,1)S(1)}, bf16[64,64]{1,0:T(8,128)(2,1)S(1)}, u32[]{:S(2)}, u32[]{:S(2)}) %collective-permute-start.11) | collective-permute-done | bytes 8224 | tf_op jit(solution)/shard_map/ppermute | solution.py:32
  51.8 3.8 %shard_map.145.base = f32[16,64,256]{2,1,0:T(8,128)S(1)} custom-call(bf16[4,64,64]{2,1,0:T(8,128)(2,1)S(1)} %pad_maximum_fusion.refs_0_, bf16[10,64,128]{2,1,0:T(8,128)(2,1)S(1)} %collective-permute-done.2.refs_0_.refs_1_, bf16[10,64,128]{2,1,0:T(8,128)(2,1)S(1)} %collective-permute-done.3.refs_1_.refs_2_, bf16[16,64,64]{2,1,0:T(8,128)(2,1)S(1)} %copy-done.3, ...), custom_call_target="tpu_custom_call" | custom-call | flops 109051904 | bytes 8388608 | tf_op jit(solution)/shard_map/pallas_call | solution.py:507
  55.6 1.2 %shard_map.146 = (f32[16,64,256]{2,1,0:T(8,128)}, f32[16,64,256]{2,1,0:T(8,128)S(1)}, f32[8,8,128]{2,1,0:T(8,128)S(1)}) custom-call(f32[1,64]{1,0:T(1,128)S(1)} %bitcast.8, f32[16,64,256]{2,1,0:T(8,128)S(1)} %shard_map.145.base, f32[8,64,256]{2,1,0:T(8,128)S(1)} %get-tuple-element.35.kept, bf16[8,64,256]{2,1,0:T(8,128)(2,1)S(1)} %collective-permute-done.12.received, ...), custom_call_target="tpu_custom_call" | custom-call | flops 4194304 | bytes 5242880 | tf_op jit(solution)/shard_map/pallas_call | solution.py:532
  56.8 10.6 %all_to_all.5.norms = f32[8,8,128]{2,1,0:T(8,128)S(1)} all-to-all(f32[8,8,128]{2,1,0:T(8,128)S(1)} %get-tuple-element.38), channel_id=1, replica_groups=mesh['groups'=2,'blk'=4,'leaf'=2,'sample'=2] {'blk','leaf'}, dimensions={0} | all-to-all | bytes 65536 | tf_op jit(solution)/shard_map/all_to_all | solution.py:542
  67.4 0.9 %shard_map.147 = bf16[16,64,256]{2,1,0:T(8,128)(2,1)} custom-call(f32[8,8,128]{2,1,0:T(8,128)S(1)} %all_to_all.5.norms, f32[16,64,256]{2,1,0:T(8,128)S(1)} %get-tuple-element.39.updated, bf16[16,64,256]{2,1,0:T(8,128)(2,1)S(1)} %copy-done), custom_call_target="tpu_custom_call" | custom-call | flops 1048576 | bytes 2097152 | tf_op jit(solution)/shard_map/pallas_call | solution.py:543
  (16 shorter events, 0.1 us)
Async XLA Ops:
  0.6 8.0 %collective-permute-start = (bf16[3,16,256]{2,1,0:T(8,128)(2,1)}, bf16[3,16,256]{2,1,0:T(8,128)(2,1)S(1)}, u32[]{:S(2)}, u32[]{:S(2)}) collective-permute-start(bf16[3,16,256]{2,1,0:T(8,128)(2,1)} %bitcast.13), channel_id=1, source_target_pairs={{0,2},{2,4},{4,6},{6,8},{8,10},{10,12},{12,14},{14,0},{1,3},{3,5},... | collective-permute-start | bytes 73736 | tf_op jit(solution)/shard_map/ppermute | solution.py:32
  3.6 5.1 %collective-permute-start.1 = (bf16[3,16,256]{2,1,0:T(8,128)(2,1)}, bf16[3,16,256]{2,1,0:T(8,128)(2,1)S(1)}, u32[]{:S(2)}, u32[]{:S(2)}) collective-permute-start(bf16[3,16,256]{2,1,0:T(8,128)(2,1)} %bitcast.14), channel_id=1, source_target_pairs={{0,14},{2,0},{4,2},{6,4},{8,6},{10,8},{12,10},{14,12},{1,15},{3,1}... | collective-permute-start | bytes 73736 | tf_op jit(solution)/shard_map/ppermute | solution.py:32
  8.7 24.3 %collective-permute-start.7 = (bf16[16,64,256]{2,1,0:T(8,128)(2,1)}, bf16[16,64,256]{2,1,0:T(8,128)(2,1)S(1)}, u32[]{:S(2)}, u32[]{:S(2)}) collective-permute-start(bf16[16,64,256]{2,1,0:T(8,128)(2,1)} %direction.1), channel_id=1, source_target_pairs={{0,14},{2,0},{4,2},{6,4},{8,6},{10,8},{12,10},{14,12},{1,15},{3,1}... | collective-permute-start | bytes 1572872 | tf_op jit(solution)/shard_map/ppermute | solution.py:32
  13.5 19.6 %collective-permute-start.4 = (bf16[16,64,256]{2,1,0:T(8,128)(2,1)}, bf16[16,64,256]{2,1,0:T(8,128)(2,1)S(1)}, u32[]{:S(2)}, u32[]{:S(2)}) collective-permute-start(bf16[16,64,256]{2,1,0:T(8,128)(2,1)} %direction.1), channel_id=1, source_target_pairs={{0,2},{2,4},{4,6},{6,8},{8,10},{10,12},{12,14},{14,0},{1,3},{3,5},... | collective-permute-start | bytes 1572872 | tf_op jit(solution)/shard_map/ppermute | solution.py:32
  13.5 24.8 %collective-permute-start.6 = (bf16[16,64,256]{2,1,0:T(8,128)(2,1)}, bf16[16,64,256]{2,1,0:T(8,128)(2,1)S(1)}, u32[]{:S(2)}, u32[]{:S(2)}) collective-permute-start(bf16[16,64,256]{2,1,0:T(8,128)(2,1)} %direction.1), channel_id=1, source_target_pairs={{0,1},{1,0},{2,3},{3,2},{4,5},{5,4},{6,7},{7,6},{8,9},{9,8},{10,11... | collective-permute-start | bytes 1572872 | tf_op jit(solution)/shard_map/ppermute | solution.py:36
  33.0 5.2 %collective-permute-start.8 = (bf16[16,64,256]{2,1,0:T(8,128)(2,1)S(1)}, bf16[16,64,256]{2,1,0:T(8,128)(2,1)S(1)}, u32[]{:S(2)}, u32[]{:S(2)}) collective-permute-start(bf16[16,64,256]{2,1,0:T(8,128)(2,1)S(1)} %collective-permute-done.7.refs_4_), channel_id=1, source_target_pairs={{0,1},{1,0},{2,3},{3,2},{4,5},{5,4},{6,7},{7,6},{8,9},{9,8},{10,11... | collective-permute-start | bytes 1572872 | tf_op jit(solution)/shard_map/ppermute | solution.py:36
  33.0 5.2 %collective-permute-start.5 = (bf16[16,64,256]{2,1,0:T(8,128)(2,1)S(1)}, bf16[16,64,256]{2,1,0:T(8,128)(2,1)S(1)}, u32[]{:S(2)}, u32[]{:S(2)}) collective-permute-start(bf16[16,64,256]{2,1,0:T(8,128)(2,1)S(1)} %collective-permute-done.4.refs_0_), channel_id=1, source_target_pairs={{0,1},{1,0},{2,3},{3,2},{4,5},{5,4},{6,7},{7,6},{8,9},{9,8},{10,11... | collective-permute-start | bytes 1572872 | tf_op jit(solution)/shard_map/ppermute | solution.py:36
  33.5 9.5 %collective-permute-start.2 = (bf16[10,64,128]{2,1,0:T(8,128)(2,1)S(1)}, bf16[10,64,128]{2,1,0:T(8,128)(2,1)S(1)}, u32[]{:S(2)}, u32[]{:S(2)}) collective-permute-start(bf16[10,64,128]{2,1,0:T(8,128)(2,1)S(1)} %get-tuple-element.22.own), channel_id=1, source_target_pairs={{0,2},{2,4},{4,6},{6,8},{8,10},{10,12},{12,14},{14,0},{1,3},{3,5},... | collective-permute-start | bytes 491528 | tf_op jit(solution)/shard_map/ppermute | solution.py:32
  34.7 9.8 %collective-permute-start.3 = (bf16[10,64,128]{2,1,0:T(8,128)(2,1)S(1)}, bf16[10,64,128]{2,1,0:T(8,128)(2,1)S(1)}, u32[]{:S(2)}, u32[]{:S(2)}) collective-permute-start(bf16[10,64,128]{2,1,0:T(8,128)(2,1)S(1)} %get-tuple-element.22.own), channel_id=1, source_target_pairs={{0,14},{2,0},{4,2},{6,4},{8,6},{10,8},{12,10},{14,12},{1,15},{3,1}... | collective-permute-start | bytes 491528 | tf_op jit(solution)/shard_map/ppermute | solution.py:32
  38.3 13.5 %copy-start = (bf16[16,64,256]{2,1,0:T(8,128)(2,1)S(1)}, bf16[16,64,256]{2,1,0:T(8,128)(2,1)}, u32[]{:S(2)}) copy-start(bf16[16,64,256]{2,1,0:T(8,128)(2,1)} %direction.1) | copy-start | bytes 1572868
  38.3 13.5 %copy-start.1 = (bf16[16,8,64,64]{3,2,1,0:T(8,128)(2,1)S(1)}, bf16[16,8,64,64]{3,2,1,0:T(8,128)(2,1)}, u32[]{:S(2)}) copy-start(bf16[16,8,64,64]{3,2,1,0:T(8,128)(2,1)} %refs_4_.1) | copy-start | bytes 3145732
  38.3 13.5 %copy-start.3 = (bf16[16,64,64]{2,1,0:T(8,128)(2,1)S(1)}, bf16[16,64,64]{2,1,0:T(8,128)(2,1)}, u32[]{:S(2)}) copy-start(bf16[16,64,64]{2,1,0:T(8,128)(2,1)} %refs_3_.1) | copy-start | bytes 393220
  38.3 13.5 %copy-start.4 = (bf16[16,64,256]{2,1,0:T(8,128)(2,1)S(1)}, bf16[16,64,256]{2,1,0:T(8,128)(2,1)}, u32[]{:S(2)}) copy-start(bf16[16,64,256]{2,1,0:T(8,128)(2,1)} %get-tuple-element.34.refs_5_) | copy-start | bytes 1572868
  38.3 17.2 %copy-start.5 = (f32[64]{0:T(128)S(1)}, f32[64]{0:T(128)}, u32[]{:S(2)}) copy-start(f32[64]{0:T(128)} %param.15) | copy-start | bytes 772
  42.9 12.6 %copy-start.2 = (f32[16,64,256]{2,1,0:T(8,128)S(1)}, f32[16,64,256]{2,1,0:T(8,128)}, u32[]{:S(2)}) copy-start(f32[16,64,256]{2,1,0:T(8,128)} %residual.1) | copy-start | bytes 3145732
  43.0 12.6 %collective-permute-start.12 = (bf16[8,64,256]{2,1,0:T(8,128)(2,1)S(1)}, bf16[8,64,256]{2,1,0:T(8,128)(2,1)S(1)}, u32[]{:S(2)}, u32[]{:S(2)}) collective-permute-start(bf16[8,64,256]{2,1,0:T(8,128)(2,1)S(1)} %get-tuple-element.36), channel_id=1, source_target_pairs={{0,1},{1,0},{2,3},{3,2},{4,5},{5,4},{6,7},{7,6},{8,9},{9,8},{10,11... | collective-permute-start | bytes 786440 | tf_op jit(solution)/shard_map/ppermute | solution.py:36
  44.6 5.8 %collective-permute-start.9 = (bf16[64,64]{1,0:T(8,128)(2,1)S(1)}, bf16[64,64]{1,0:T(8,128)(2,1)S(1)}, u32[]{:S(2)}, u32[]{:S(2)}) collective-permute-start(bf16[64,64]{1,0:T(8,128)(2,1)S(1)} %shard_map.144), channel_id=1, source_target_pairs={{0,4},{4,8},{8,12},{12,0},{1,5},{5,9},{9,13},{13,1},{2,6},{6,10},{... | collective-permute-start | bytes 24584 | tf_op jit(solution)/shard_map/ppermute | solution.py:32
  44.8 5.6 %collective-permute-start.10 = (bf16[64,64]{1,0:T(8,128)(2,1)S(1)}, bf16[64,64]{1,0:T(8,128)(2,1)S(1)}, u32[]{:S(2)}, u32[]{:S(2)}) collective-permute-start(bf16[64,64]{1,0:T(8,128)(2,1)S(1)} %shard_map.144), channel_id=1, source_target_pairs={{0,8},{4,12},{8,0},{12,4},{1,9},{5,13},{9,1},{13,5},{2,10},{6,14},... | collective-permute-start | bytes 24584 | tf_op jit(solution)/shard_map/ppermute | solution.py:32
  48.0 3.7 %collective-permute-start.11 = (bf16[64,64]{1,0:T(8,128)(2,1)S(1)}, bf16[64,64]{1,0:T(8,128)(2,1)S(1)}, u32[]{:S(2)}, u32[]{:S(2)}) collective-permute-start(bf16[64,64]{1,0:T(8,128)(2,1)S(1)} %shard_map.144), channel_id=1, source_target_pairs={{0,12},{4,0},{8,4},{12,8},{1,13},{5,1},{9,5},{13,9},{2,14},{6,2},{... | collective-permute-start | bytes 24584 | tf_op jit(solution)/shard_map/ppermute | solution.py:32

commit v8 on v7

--- a/solution.py
+++ b/solution.py
@@ -76,7 +76,7 @@
     )
 
 
-def up_kernel(order_h, basis_h, direction_h, transfer_h, node_h, natural_h, coef, mark, *scratch):
+def up_kernel(order_h, basis_h, direction_h, transfer_h, node_h, natural_h, coef, lifted, mark, *scratch):
     mark[...] = jnp.zeros_like(mark)
     order, basis, direction, leaf_transfer, node_transfer, natural, sems = scratch
     leaves, rank, points = basis.shape
@@ -122,9 +122,7 @@
             )
             copy.start()
             leaving.append(copy)
-    for i, part in enumerate(thirds(nt(node.astype(BF), node_transfer[0]))):
-        at = leaves + i
-        coef[at // 2, :, (at % 2) * rank : (at % 2 + 1) * rank] = part.astype(BF)
+    lifted[...] = nt(node.astype(BF), node_transfer[0])
     for copy in leaving:
         copy.wait()
 
@@ -217,29 +215,34 @@
     lax.fori_loop(0, count, leaf, 0)
 
 
-def top_kernel(own, *refs):
-    sides, top = refs[:-2], refs[-1]
-    samples, rank = top.shape
-    at = own.shape[0] - 2
-
-    def term(ref):
-        first, second = ref[at].astype(F32), ref[at + 1].astype(F32)
-        return first[:, :rank] + first[:, rank:] + second[:, :rank]
-
-    total = term(own)
-    if sides:
-        low = lax.axis_index("leaf") == 0
-        total = total + jnp.where(low, term(sides[1]), term(sides[0]))
+def top_kernel(_, *refs):
+    terms, top = refs[:-1], refs[-1]
+    total = terms[0][...]
+    for term in terms[1:]:
+        total = total + term[...]
     top[...] = total.astype(top.dtype)
 
 
+def window_kernel(given, before, after, window, sent):
+    sent[...] = given[...]
+    rows, _, lanes = before.shape
+    rank = lanes // 2
+    for side, packed in enumerate((before, after)):
+        for g in range(2 * rows):
+            part = packed[g // 2, :, (g % 2) * rank : (g % 2 + 1) * rank]
+            window[side * 2 * rows + g] = part
+
+
 def down_kernel(*refs):
-    tops, before, after, leaf_transfer, coupling, natural, direction = refs[:7]
-    sources, base, window, targets, sems = refs[7:11], refs[12], refs[13], refs[14:18], refs[18]
+    clusters = lax.axis_size("blk")
+    each, refs = refs[:clusters], refs[clusters:]
+    window, leaf_transfer, coupling, natural, direction = refs[:5]
+    sources, base, targets, tops, sems = refs[5:9], refs[9], refs[10:14], refs[14], refs[15]
+    for i, top in enumerate(each):
+        tops[i] = top[...]
     top_list, coupling_list, top_coupling, node_transfer = targets
     leaves, samples, points = direction.shape
     rank = natural.shape[1]
-    clusters = lax.axis_size("blk")
     here = lax.axis_index("blk")
     total = leaves * clusters * lax.axis_size("leaf")
     anchor = (here * lax.axis_size("leaf") + lax.axis_index("leaf") - 1) * leaves
@@ -249,10 +252,6 @@
     ]
     for copy in copies:
         copy.start()
-    for side, packed in enumerate((before, after)):
-        for g in range(leaves):
-            part = packed[g // 2, :, (g % 2) * rank : (g % 2 + 1) * rank]
-            window[side * leaves + g] = part
     for copy in copies:
         copy.wait()
     incoming = jnp.zeros((samples, rank), F32)
@@ -403,22 +402,18 @@
     coords = jnp.transpose(coords, (1, 0, 2))
     coords_prev = shifted(coords, RING, 1)
     coords_after = shifted(coords, RING, -1)
-    travelling, first = lax.optimization_barrier((direction, order, coords_prev, coords_after))[:2]
-    direction_prev = shifted(travelling, RING, 1)
-    direction_after = shifted(travelling, RING, -1)
-    direction_other = partner(direction)
-
-    natural, coef, up_mark = call(
+    natural, coef, lifted, up_mark = call(
         up_kernel,
         (
             pltpu.HBM((leaves, rank, points), BF),
-            shape((leaves // 2 + 2, samples, 2 * rank), BF),
+            shape((leaves // 2, samples, 2 * rank), BF),
+            shape((samples, rank), F32),
             token,
         ),
         4 * leaves * rank * points * points,
         6 * MIB,
         in_specs=[hbm] * 5,
-        out_specs=(hbm, vmem, vmem),
+        out_specs=(hbm, vmem, vmem, vmem),
         scratch_shapes=[
             pltpu.VMEM(order.shape, jnp.int32),
             pltpu.VMEM(basis.shape, BF),
@@ -429,7 +424,7 @@
             pltpu.SemaphoreType.DMA((5, 4)),
         ],
         vmem=8,
-    )(*in_hbm(first, basis, direction, leaf_transfer, node_transfer))
+    )(*in_hbm(order, basis, direction, leaf_transfer, node_transfer))
 
     def make_tiles(start, done, *operands):
         count = half // 2
@@ -448,14 +443,34 @@
             vmem=8,
         )(*in_hbm(near_list), done, *operands)
 
+    terms = [shifted(lifted, "leaf", by) for by in range(1, leaf_count)]
+    travelling = ordered(direction, coords_prev, coords_after, *terms)
+    direction_prev = shifted(travelling, RING, 1)
+    direction_after = shifted(travelling, RING, -1)
+    direction_other = partner(direction)
     coef_prev = shifted(coef, RING, 1)
     coef_after = shifted(coef, RING, -1)
     tiles_low, low_mark, spread_x, plain = make_tiles(
         0, up_mark, *in_hbm(coords), coords_prev, coords_after
     )
+    top = call(
+        top_kernel,
+        shape((samples, rank), BF),
+        MIB,
+        MIB,
+        in_specs=[anywhere] + [vmem] * leaf_count,
+        out_specs=vmem,
+        vmem=4,
+    )(low_mark, lifted, *terms)
+    if blk_count <= 8:
+        others = [shifted(top, "blk", by) for by in range(1, blk_count)]
+    else:
+        others = lax.all_gather(top[None], "blk", axis=0, tiled=True)
+        places = jnp.mod(lax.axis_index("blk") - jnp.arange(blk_count, dtype=jnp.int32), blk_count)
+        others = list(others[places][1:])
     tiles_high, high_mark = make_tiles(half // 2, low_mark, plain, spread_x)
-    direction_prev = ordered(direction_prev, high_mark)
-    direction_after = ordered(direction_after, high_mark)
+    direction_prev = ordered(direction_prev, high_mark, *others)
+    direction_after = ordered(direction_after, high_mark, *others)
     kept, given, near_mark = call(
         near_kernel,
         (shape((half, samples, points), F32), shape((half, samples, points), BF), token),
@@ -481,26 +496,15 @@
         tiles_high,
     )
 
-    paired = leaf_count == 2
-    top = call(
-        top_kernel,
-        shape((samples, rank), BF if paired else F32),
-        MIB,
-        MIB,
-        in_specs=[vmem] * (3 if paired else 1) + [anywhere],
-        out_specs=vmem,
+    coef_window, given = call(
+        window_kernel,
+        (shape((2 * leaves, samples, rank), BF), shape((half, samples, points), BF)),
+        MIB,
+        MIB,
+        in_specs=[vmem] * 3,
+        out_specs=(vmem, vmem),
         vmem=4,
-    )(coef, *((coef_prev, coef_after) if paired else ()), near_mark)
-    if not paired:
-        terms = [shifted(top, "leaf", by) for by in range(1, leaf_count)]
-        top = sum(terms, top).astype(BF)
-    if blk_count <= 8:
-        others = [shifted(top, "blk", by) for by in range(1, blk_count)]
-    else:
-        others = lax.all_gather(top[None], "blk", axis=0, tiled=True)
-        places = jnp.mod(lax.axis_index("blk") - jnp.arange(blk_count, dtype=jnp.int32), blk_count)
-        others = list(others[places][1:])
-    tops = jnp.stack([top] + others)
+    )(given, coef_prev, coef_after)
     arrays = (top_list, coupling_list.T, top_coupling, node_transfer)
     spaces = (pltpu.SMEM,) * 2 + (pltpu.VMEM,) * 2
     whole = shape((leaves, samples, points), F32)
@@ -509,22 +513,20 @@
         whole,
         2 * leaves * samples * rank * (points + 9 * rank),
         8 * MIB,
-        in_specs=[vmem] * 7 + [hbm] * 4 + [anywhere],
+        in_specs=[vmem] * (5 + blk_count) + [hbm] * 4,
         out_specs=vmem,
-        scratch_shapes=[pltpu.VMEM((2 * leaves, samples, rank), BF)]
-        + [space(array.shape, array.dtype) for space, array in zip(spaces, arrays)]
-        + [pltpu.SemaphoreType.DMA((4,))],
+        scratch_shapes=[space(array.shape, array.dtype) for space, array in zip(spaces, arrays)]
+        + [pltpu.VMEM((blk_count, samples, rank), BF), pltpu.SemaphoreType.DMA((4,))],
         vmem=10,
     )(
-        tops,
-        coef_prev,
-        coef_after,
+        top,
+        *others,
+        coef_window,
         leaf_transfer,
         coupling,
         natural,
         direction,
         *in_hbm(*arrays),
-        near_mark,
     )
     received = partner(given)
 

time: 68.7 us -> 68 us (0.990)
  starting transfers between devices: 20.3 us -> 17.5 us
  waiting for transfers between devices: 8.02 us -> 9.52 us
  Pallas kernels: 28.6 us -> 29.3 us
    ppermute x9 -> x10, starting transfers between devices: 19.7 us -> 16.8 us  [shifted(): lax.ppermute(array, axis, [(i, (i + by) % count) for i in range(count)])]
    ppermute x9 -> x10, waiting for transfers between devices: 8.01 us -> 9.51 us  [shifted(): lax.ppermute(array, axis, [(i, (i + by) % count) for i in range(count)])]
  transfers between devices with their start and end apart: 13 -> 14, of which waited for: 5 -> 2; matrix products, arithmetic and copies ran while one was open for 0% -> 0% of each run, Pallas kernels for 39% -> 40%
where the time goes in v8:
time: 68 us; the launch traced here: 67.6 us
  Pallas kernels  29.3 us (43%)
  starting transfers between devices  17.5 us (26%)
  blocking collectives  10.4 us (15%)
  waiting for transfers between devices  9.52 us (14%)
  between operations  0.87 us (1%)
    ppermute x10, starting transfers between devices, shifted(): lax.ppermute(array, axis, [(i, (i + by) % count) for i in range(count)])  16.8 us
    pallas_call x2, Pallas kernels, make_tiles(): call(functools.partial(tile_kernel, start), outs, 40 * count * entries *...  12 us
    all_to_all x1, blocking collectives, on_device(): norms = lax.all_to_all(norms, RING, 0, 0)  10.4 us
    ppermute x10, waiting for transfers between devices, shifted(): lax.ppermute(array, axis, [(i, (i + by) % count) for i in range(count)])  9.51 us
    pallas_call x1, Pallas kernels, on_device(): call(up_kernel, (pltpu.HBM((leaves, rank, points), BF), shape((leaves //...  6.13 us
    pallas_call x1, Pallas kernels, on_device(): call(near_kernel, (shape((half, samples, points), F32), shape((half, samp...  5.04 us
    pallas_call x1, Pallas kernels, on_device(): call(down_kernel, whole, 2 * leaves * samples * rank * (points + 9 * rank...  3.74 us
  transfers between devices with their start and end apart: 14, of which 2 were waited for; matrix products, arithmetic and copies ran while one was open for 0% of the time, Pallas kernels for 40%

profile of v8, /device:TPU:0, one launch (start us, length us, event | category | flops | bytes accessed | tf_op | source)
XLA Modules:
  0.0 67.6 jit_solution(7964537448064101129)
XLA Ops:
  0.6 3.0 %collective-permute-start = (bf16[3,16,256]{2,1,0:T(8,128)(2,1)}, bf16[3,16,256]{2,1,0:T(8,128)(2,1)S(1)}, u32[]{:S(2)}, u32[]{:S(2)}) collective-permute-start(bf16[3,16,256]{2,1,0:T(8,128)(2,1)} %bitcast.5), channel_id=1, source_target_pairs={{0,2},{2,4},{4,6},{6,8},{8,10},{10,12},{12,14},{14,0},{1,3},{3,5},... | collective-permute-start | bytes 73736 | tf_op jit(solution)/shard_map/ppermute | solution.py:32
  3.6 3.1 %collective-permute-start.1 = (bf16[3,16,256]{2,1,0:T(8,128)(2,1)}, bf16[3,16,256]{2,1,0:T(8,128)(2,1)S(1)}, u32[]{:S(2)}, u32[]{:S(2)}) collective-permute-start(bf16[3,16,256]{2,1,0:T(8,128)(2,1)} %bitcast.6), channel_id=1, source_target_pairs={{0,14},{2,0},{4,2},{6,4},{8,6},{10,8},{12,10},{14,12},{1,15},{3,1}... | collective-permute-start | bytes 73736 | tf_op jit(solution)/shard_map/ppermute | solution.py:32
  6.7 6.1 %shard_map.140 = (bf16[16,64,256]{2,1,0:T(8,128)(2,1)}, bf16[8,64,128]{2,1,0:T(8,128)(2,1)S(1)}, f32[64,64]{1,0:T(8,128)S(1)}, f32[8,128]{1,0:T(8,128)S(1)}) custom-call(s32[16,256]{1,0:T(8,128)} %order_h.1, bf16[16,64,256]{2,1,0:T(8,128)(2,1)} %basis_h.1, bf16[16,64,256]{2,1,0:T(8,128)(2,1)} %direction.1, bf16[16,64,64]{2,1,0:T(8,128)(2,1)} %refs_5_.1, ...), custom_call_target="tpu_custom_call" | custom-call | flops 268435456 | bytes 6291456 | tf_op jit(solution)/shard_map/pallas_call | solution.py:405
  12.9 0.1 collective-permute-start.2
  12.9 3.9 %collective-permute-done.2.refs_1_ = f32[64,64]{1,0:T(8,128)S(1)} collective-permute-done((f32[64,64]{1,0:T(8,128)S(1)}, f32[64,64]{1,0:T(8,128)S(1)}, u32[]{:S(2)}, u32[]{:S(2)}) %collective-permute-start.2) | collective-permute-done | bytes 16416 | tf_op jit(solution)/shard_map/ppermute | solution.py:32
  16.8 0.0 collective-permute-done.refs_1_
  16.9 0.0 collective-permute-done.1.refs_2_
  16.9 2.0 %collective-permute-start.9 = (bf16[16,64,256]{2,1,0:T(8,128)(2,1)}, bf16[16,64,256]{2,1,0:T(8,128)(2,1)S(1)}, u32[]{:S(2)}, u32[]{:S(2)}) collective-permute-start(bf16[16,64,256]{2,1,0:T(8,128)(2,1)} %direction.1), channel_id=1, source_target_pairs={{0,14},{2,0},{4,2},{6,4},{8,6},{10,8},{12,10},{14,12},{1,15},{3,1}... | collective-permute-start | bytes 1572872 | tf_op jit(solution)/shard_map/ppermute | solution.py:32
  18.8 0.1 collective-permute-start.6
  18.9 6.5 %shard_map.141 = (bf16[4,3072,256]{2,1,0:T(8,128)(2,1)S(1)}, f32[8,128]{1,0:T(8,128)S(1)}, bf16[48,256,128]{2,1,0:T(8,128)(2,1)S(1)}, f32[3,16,256]{2,1,0:T(8,128)S(1)}) custom-call(s32[16,12]{1,0:T(8,128)} %near_h.5, f32[8,128]{1,0:T(8,128)S(1)} %get-tuple-element.22._, bf16[3,16,256]{2,1,0:T(8,128)(2,1)} %bitcast.7, ...), custom_call_target="tpu_custom_call" | custom-call | flops 125829120 | bytes 50331648 | tf_op jit(solution)/shard_map/pallas_call | solution.py:434
  25.4 0.1 collective-permute-start.3
  25.5 2.5 %collective-permute-start.4 = (bf16[64,64]{1,0:T(8,128)(2,1)S(1)}, bf16[64,64]{1,0:T(8,128)(2,1)S(1)}, u32[]{:S(2)}, u32[]{:S(2)}) collective-permute-start(bf16[64,64]{1,0:T(8,128)(2,1)S(1)} %shard_map.142.refs_0_), channel_id=1, source_target_pairs={{0,8},{4,12},{8,0},{12,4},{1,9},{5,13},{9,1},{13,5},{2,10},{6,14},... | collective-permute-start | bytes 24584 | tf_op jit(solution)/shard_map/ppermute | solution.py:32
  28.0 1.3 %collective-permute-start.5 = (bf16[64,64]{1,0:T(8,128)(2,1)S(1)}, bf16[64,64]{1,0:T(8,128)(2,1)S(1)}, u32[]{:S(2)}, u32[]{:S(2)}) collective-permute-start(bf16[64,64]{1,0:T(8,128)(2,1)S(1)} %shard_map.142.refs_0_), channel_id=1, source_target_pairs={{0,12},{4,0},{8,4},{12,8},{1,13},{5,1},{9,5},{13,9},{2,14},{6,2},{... | collective-permute-start | bytes 24584 | tf_op jit(solution)/shard_map/ppermute | solution.py:32
  29.3 5.5 %shard_map.143 = (bf16[4,3072,256]{2,1,0:T(8,128)(2,1)S(1)}, f32[8,128]{1,0:T(8,128)}) custom-call(s32[16,12]{1,0:T(8,128)} %near_h.5, f32[8,128]{1,0:T(8,128)S(1)} %get-tuple-element.23._, f32[3,16,256]{2,1,0:T(8,128)S(1)} %get-tuple-element.26.refs_0_, bf16[48,256,128]{2,1,0:T(8,128)(2,1)S(1)} %get-tuple-element.27.refs_1_), custom_call_target="tpu_custom_call" | custom-call | flops 125829120 | bytes 3145728 | tf_op jit(solution)/shard_map/pallas_call | solution.py:434
  34.8 0.1 collective-permute-start.8
  34.9 5.6 %collective-permute-done.9.refs_4_ = bf16[16,64,256]{2,1,0:T(8,128)(2,1)S(1)} collective-permute-done((bf16[16,64,256]{2,1,0:T(8,128)(2,1)}, bf16[16,64,256]{2,1,0:T(8,128)(2,1)S(1)}, u32[]{:S(2)}, u32[]{:S(2)}) %collective-permute-start.9) | collective-permute-done | bytes 524320 | tf_op jit(solution)/shard_map/ppermute | solution.py:32
  40.5 0.5 collective-permute-start.7
  41.1 0.7 %collective-permute-start.11 = (bf16[8,64,128]{2,1,0:T(8,128)(2,1)S(1)}, bf16[8,64,128]{2,1,0:T(8,128)(2,1)S(1)}, u32[]{:S(2)}, u32[]{:S(2)}) collective-permute-start(bf16[8,64,128]{2,1,0:T(8,128)(2,1)S(1)} %get-tuple-element.34), channel_id=1, source_target_pairs={{0,2},{2,4},{4,6},{6,8},{8,10},{10,12},{12,14},{14,0},{1,3},{3,5},... | collective-permute-start | bytes 393224 | tf_op jit(solution)/shard_map/ppermute | solution.py:32
  41.7 4.0 %collective-permute-start.12 = (bf16[8,64,128]{2,1,0:T(8,128)(2,1)S(1)}, bf16[8,64,128]{2,1,0:T(8,128)(2,1)S(1)}, u32[]{:S(2)}, u32[]{:S(2)}) collective-permute-start(bf16[8,64,128]{2,1,0:T(8,128)(2,1)S(1)} %get-tuple-element.34), channel_id=1, source_target_pairs={{0,14},{2,0},{4,2},{6,4},{8,6},{10,8},{12,10},{14,12},{1,15},{3,1}... | collective-permute-start | bytes 393224 | tf_op jit(solution)/shard_map/ppermute | solution.py:32
  45.8 0.0 copy-start
  45.8 0.0 copy-start.1
  45.8 0.0 copy-start.3
  45.8 0.0 copy-start.4
  45.8 0.0 copy-start.5
  45.8 5.0 %shard_map.144 = (f32[8,64,256]{2,1,0:T(8,128)S(1)}, bf16[8,64,256]{2,1,0:T(8,128)(2,1)S(1)}, f32[8,128]{1,0:T(8,128)}) custom-call(s32[16,12]{1,0:T(8,128)} %near_h.5, bf16[16,64,256]{2,1,0:T(8,128)(2,1)S(1)} %collective-permute-done.6.refs_0_, bf16[16,64,256]{2,1,0:T(8,128)(2,1)S(1)} %collective-permute-done.7.refs_1_, bf16[16,64,256]{2,1,0:T(8,128)(2,1)} %direction.1, ...), custom_call_target="tpu_custom_call" | custom-call | flops 1048576 | bytes 1048576 | tf_op jit(solution)/shard_map/pallas_call | solution.py:474
  50.9 0.0 copy-start.2
  50.9 0.2 shard_map.145
  51.1 0.1 collective-permute-start.13
  51.2 3.7 %shard_map.146.base = f32[16,64,256]{2,1,0:T(8,128)S(1)} custom-call(bf16[64,64]{1,0:T(8,128)(2,1)S(1)} %shard_map.142.refs_0_, bf16[64,64]{1,0:T(8,128)(2,1)S(1)} %collective-permute-done.3.refs_1_, bf16[64,64]{1,0:T(8,128)(2,1)S(1)} %collective-permute-done.4.refs_2_, bf16[64,64]{1,0:T(8,128)(2,1)S(1)} %collective-permute-done.5.refs_3_, ...), custom_call_target="tpu_custom_call" | custom-call | flops 109051904 | bytes 8388608 | tf_op jit(solution)/shard_map/pallas_call | solution.py:511
  55.0 1.2 %shard_map.147 = (f32[16,64,256]{2,1,0:T(8,128)}, f32[16,64,256]{2,1,0:T(8,128)S(1)}, f32[8,8,128]{2,1,0:T(8,128)S(1)}) custom-call(f32[1,64]{1,0:T(1,128)S(1)} %bitcast.3, f32[16,64,256]{2,1,0:T(8,128)S(1)} %shard_map.146.base, f32[8,64,256]{2,1,0:T(8,128)S(1)} %get-tuple-element.37.kept, bf16[8,64,256]{2,1,0:T(8,128)(2,1)S(1)} %collective-permute-done.13.received, ...), custom_call_target="tpu_custom_call" | custom-call | flops 4194304 | bytes 5242880 | tf_op jit(solution)/shard_map/pallas_call | solution.py:534
  56.2 10.4 %all_to_all.5.norms = f32[8,8,128]{2,1,0:T(8,128)S(1)} all-to-all(f32[8,8,128]{2,1,0:T(8,128)S(1)} %get-tuple-element.40), channel_id=1, replica_groups=mesh['groups'=2,'blk'=4,'leaf'=2,'sample'=2] {'blk','leaf'}, dimensions={0} | all-to-all | bytes 65536 | tf_op jit(solution)/shard_map/all_to_all | solution.py:544
  66.7 0.9 %shard_map.148 = bf16[16,64,256]{2,1,0:T(8,128)(2,1)} custom-call(f32[8,8,128]{2,1,0:T(8,128)S(1)} %all_to_all.5.norms, f32[16,64,256]{2,1,0:T(8,128)S(1)} %get-tuple-element.41.updated, bf16[16,64,256]{2,1,0:T(8,128)(2,1)S(1)} %copy-done), custom_call_target="tpu_custom_call" | custom-call | flops 1048576 | bytes 2097152 | tf_op jit(solution)/shard_map/pallas_call | solution.py:545
  (18 shorter events, 0.0 us)
Async XLA Ops:
  0.6 16.2 %collective-permute-start = (bf16[3,16,256]{2,1,0:T(8,128)(2,1)}, bf16[3,16,256]{2,1,0:T(8,128)(2,1)S(1)}, u32[]{:S(2)}, u32[]{:S(2)}) collective-permute-start(bf16[3,16,256]{2,1,0:T(8,128)(2,1)} %bitcast.5), channel_id=1, source_target_pairs={{0,2},{2,4},{4,6},{6,8},{8,10},{10,12},{12,14},{14,0},{1,3},{3,5},... | collective-permute-start | bytes 73736 | tf_op jit(solution)/shard_map/ppermute | solution.py:32
  3.6 13.2 %collective-permute-start.1 = (bf16[3,16,256]{2,1,0:T(8,128)(2,1)}, bf16[3,16,256]{2,1,0:T(8,128)(2,1)S(1)}, u32[]{:S(2)}, u32[]{:S(2)}) collective-permute-start(bf16[3,16,256]{2,1,0:T(8,128)(2,1)} %bitcast.6), channel_id=1, source_target_pairs={{0,14},{2,0},{4,2},{6,4},{8,6},{10,8},{12,10},{14,12},{1,15},{3,1}... | collective-permute-start | bytes 73736 | tf_op jit(solution)/shard_map/ppermute | solution.py:32
  12.9 4.0 %collective-permute-start.2 = (f32[64,64]{1,0:T(8,128)S(1)}, f32[64,64]{1,0:T(8,128)S(1)}, u32[]{:S(2)}, u32[]{:S(2)}) collective-permute-start(f32[64,64]{1,0:T(8,128)S(1)} %get-tuple-element.24.refs_0_), channel_id=1, source_target_pairs={{0,2},{2,0},{1,3},{3,1},{4,6},{6,4},{5,7},{7,5},{8,10},{10,8},{9,1... | collective-permute-start | bytes 49160 | tf_op jit(solution)/shard_map/ppermute | solution.py:32
  16.9 23.7 %collective-permute-start.9 = (bf16[16,64,256]{2,1,0:T(8,128)(2,1)}, bf16[16,64,256]{2,1,0:T(8,128)(2,1)S(1)}, u32[]{:S(2)}, u32[]{:S(2)}) collective-permute-start(bf16[16,64,256]{2,1,0:T(8,128)(2,1)} %direction.1), channel_id=1, source_target_pairs={{0,14},{2,0},{4,2},{6,4},{8,6},{10,8},{12,10},{14,12},{1,15},{3,1}... | collective-permute-start | bytes 1572872 | tf_op jit(solution)/shard_map/ppermute | solution.py:32
  18.8 21.7 %collective-permute-start.6 = (bf16[16,64,256]{2,1,0:T(8,128)(2,1)}, bf16[16,64,256]{2,1,0:T(8,128)(2,1)S(1)}, u32[]{:S(2)}, u32[]{:S(2)}) collective-permute-start(bf16[16,64,256]{2,1,0:T(8,128)(2,1)} %direction.1), channel_id=1, source_target_pairs={{0,2},{2,4},{4,6},{6,8},{8,10},{10,12},{12,14},{14,0},{1,3},{3,5},... | collective-permute-start | bytes 1572872 | tf_op jit(solution)/shard_map/ppermute | solution.py:32
  25.4 9.4 %collective-permute-start.3 = (bf16[64,64]{1,0:T(8,128)(2,1)S(1)}, bf16[64,64]{1,0:T(8,128)(2,1)S(1)}, u32[]{:S(2)}, u32[]{:S(2)}) collective-permute-start(bf16[64,64]{1,0:T(8,128)(2,1)S(1)} %shard_map.142.refs_0_), channel_id=1, source_target_pairs={{0,4},{4,8},{8,12},{12,0},{1,5},{5,9},{9,13},{13,1},{2,6},{6,10},{... | collective-permute-start | bytes 24584 | tf_op jit(solution)/shard_map/ppermute | solution.py:32
  25.5 9.4 %collective-permute-start.4 = (bf16[64,64]{1,0:T(8,128)(2,1)S(1)}, bf16[64,64]{1,0:T(8,128)(2,1)S(1)}, u32[]{:S(2)}, u32[]{:S(2)}) collective-permute-start(bf16[64,64]{1,0:T(8,128)(2,1)S(1)} %shard_map.142.refs_0_), channel_id=1, source_target_pairs={{0,8},{4,12},{8,0},{12,4},{1,9},{5,13},{9,1},{13,5},{2,10},{6,14},... | collective-permute-start | bytes 24584 | tf_op jit(solution)/shard_map/ppermute | solution.py:32
  28.0 7.0 %collective-permute-start.5 = (bf16[64,64]{1,0:T(8,128)(2,1)S(1)}, bf16[64,64]{1,0:T(8,128)(2,1)S(1)}, u32[]{:S(2)}, u32[]{:S(2)}) collective-permute-start(bf16[64,64]{1,0:T(8,128)(2,1)S(1)} %shard_map.142.refs_0_), channel_id=1, source_target_pairs={{0,12},{4,0},{8,4},{12,8},{1,13},{5,1},{9,5},{13,9},{2,14},{6,2},{... | collective-permute-start | bytes 24584 | tf_op jit(solution)/shard_map/ppermute | solution.py:32
  34.8 10.9 %collective-permute-start.8 = (bf16[16,64,256]{2,1,0:T(8,128)(2,1)}, bf16[16,64,256]{2,1,0:T(8,128)(2,1)S(1)}, u32[]{:S(2)}, u32[]{:S(2)}) collective-permute-start(bf16[16,64,256]{2,1,0:T(8,128)(2,1)} %direction.1), channel_id=1, source_target_pairs={{0,1},{1,0},{2,3},{3,2},{4,5},{5,4},{6,7},{7,6},{8,9},{9,8},{10,11... | collective-permute-start | bytes 1572872 | tf_op jit(solution)/shard_map/ppermute | solution.py:36
  40.5 5.2 %collective-permute-start.10 = (bf16[16,64,256]{2,1,0:T(8,128)(2,1)S(1)}, bf16[16,64,256]{2,1,0:T(8,128)(2,1)S(1)}, u32[]{:S(2)}, u32[]{:S(2)}) collective-permute-start(bf16[16,64,256]{2,1,0:T(8,128)(2,1)S(1)} %collective-permute-done.9.refs_4_), channel_id=1, source_target_pairs={{0,1},{1,0},{2,3},{3,2},{4,5},{5,4},{6,7},{7,6},{8,9},{9,8},{10,11... | collective-permute-start | bytes 1572872 | tf_op jit(solution)/shard_map/ppermute | solution.py:36
  40.5 5.2 %collective-permute-start.7 = (bf16[16,64,256]{2,1,0:T(8,128)(2,1)S(1)}, bf16[16,64,256]{2,1,0:T(8,128)(2,1)S(1)}, u32[]{:S(2)}, u32[]{:S(2)}) collective-permute-start(bf16[16,64,256]{2,1,0:T(8,128)(2,1)S(1)} %collective-permute-done.6.refs_0_), channel_id=1, source_target_pairs={{0,1},{1,0},{2,3},{3,2},{4,5},{5,4},{6,7},{7,6},{8,9},{9,8},{10,11... | collective-permute-start | bytes 1572872 | tf_op jit(solution)/shard_map/ppermute | solution.py:36
  41.1 9.9 %collective-permute-start.11 = (bf16[8,64,128]{2,1,0:T(8,128)(2,1)S(1)}, bf16[8,64,128]{2,1,0:T(8,128)(2,1)S(1)}, u32[]{:S(2)}, u32[]{:S(2)}) collective-permute-start(bf16[8,64,128]{2,1,0:T(8,128)(2,1)S(1)} %get-tuple-element.34), channel_id=1, source_target_pairs={{0,2},{2,4},{4,6},{6,8},{8,10},{10,12},{12,14},{14,0},{1,3},{3,5},... | collective-permute-start | bytes 393224 | tf_op jit(solution)/shard_map/ppermute | solution.py:32
  41.7 9.2 %collective-permute-start.12 = (bf16[8,64,128]{2,1,0:T(8,128)(2,1)S(1)}, bf16[8,64,128]{2,1,0:T(8,128)(2,1)S(1)}, u32[]{:S(2)}, u32[]{:S(2)}) collective-permute-start(bf16[8,64,128]{2,1,0:T(8,128)(2,1)S(1)} %get-tuple-element.34), channel_id=1, source_target_pairs={{0,14},{2,0},{4,2},{6,4},{8,6},{10,8},{12,10},{14,12},{1,15},{3,1}... | collective-permute-start | bytes 393224 | tf_op jit(solution)/shard_map/ppermute | solution.py:32
  45.8 5.4 %copy-start = (bf16[16,64,256]{2,1,0:T(8,128)(2,1)S(1)}, bf16[16,64,256]{2,1,0:T(8,128)(2,1)}, u32[]{:S(2)}) copy-start(bf16[16,64,256]{2,1,0:T(8,128)(2,1)} %direction.1) | copy-start | bytes 1572868
  45.8 5.4 %copy-start.1 = (bf16[16,8,64,64]{3,2,1,0:T(8,128)(2,1)S(1)}, bf16[16,8,64,64]{3,2,1,0:T(8,128)(2,1)}, u32[]{:S(2)}) copy-start(bf16[16,8,64,64]{3,2,1,0:T(8,128)(2,1)} %refs_6_.1) | copy-start | bytes 3145732
  45.8 5.4 %copy-start.3 = (bf16[16,64,64]{2,1,0:T(8,128)(2,1)S(1)}, bf16[16,64,64]{2,1,0:T(8,128)(2,1)}, u32[]{:S(2)}) copy-start(bf16[16,64,64]{2,1,0:T(8,128)(2,1)} %refs_5_.1) | copy-start | bytes 393220
  45.8 5.4 %copy-start.4 = (bf16[16,64,256]{2,1,0:T(8,128)(2,1)S(1)}, bf16[16,64,256]{2,1,0:T(8,128)(2,1)}, u32[]{:S(2)}) copy-start(bf16[16,64,256]{2,1,0:T(8,128)(2,1)} %get-tuple-element.36.refs_7_) | copy-start | bytes 1572868
  45.8 9.2 %copy-start.5 = (f32[64]{0:T(128)S(1)}, f32[64]{0:T(128)}, u32[]{:S(2)}) copy-start(f32[64]{0:T(128)} %param.15) | copy-start | bytes 772
  50.9 4.1 %copy-start.2 = (f32[16,64,256]{2,1,0:T(8,128)S(1)}, f32[16,64,256]{2,1,0:T(8,128)}, u32[]{:S(2)}) copy-start(f32[16,64,256]{2,1,0:T(8,128)} %residual.1) | copy-start | bytes 3145732
  51.1 3.9 %collective-permute-start.13 = (bf16[8,64,256]{2,1,0:T(8,128)(2,1)S(1)}, bf16[8,64,256]{2,1,0:T(8,128)(2,1)S(1)}, u32[]{:S(2)}, u32[]{:S(2)}) collective-permute-start(bf16[8,64,256]{2,1,0:T(8,128)(2,1)S(1)} %get-tuple-element.38), channel_id=1, source_target_pairs={{0,1},{1,0},{2,3},{3,2},{4,5},{5,4},{6,7},{7,6},{8,9},{9,8},{10,11... | collective-permute-start | bytes 786440 | tf_op jit(solution)/shard_map/ppermute | solution.py:36

commit v9 on v8

--- a/solution.py
+++ b/solution.py
@@ -215,15 +215,22 @@
     lax.fori_loop(0, count, leaf, 0)
 
 
-def top_kernel(_, *refs):
-    terms, top = refs[:-1], refs[-1]
+def after_kernel(_, source, target):
+    target[...] = source[...]
+
+
+def collect_kernel(*refs):
+    terms, together = refs[:-1], refs[-1]
+    for i, term in enumerate(terms):
+        together[i] = term[...]
+
+
+def window_kernel(given, before, after, *refs):
+    terms, (window, sent, tops) = refs[:-3], refs[-3:]
     total = terms[0][...]
     for term in terms[1:]:
         total = total + term[...]
-    top[...] = total.astype(top.dtype)
-
-
-def window_kernel(given, before, after, window, sent):
+    tops[...] = total.astype(tops.dtype)
     sent[...] = given[...]
     rows, _, lanes = before.shape
     rank = lanes // 2
@@ -235,11 +242,8 @@
 
 def down_kernel(*refs):
     clusters = lax.axis_size("blk")
-    each, refs = refs[:clusters], refs[clusters:]
-    window, leaf_transfer, coupling, natural, direction = refs[:5]
-    sources, base, targets, tops, sems = refs[5:9], refs[9], refs[10:14], refs[14], refs[15]
-    for i, top in enumerate(each):
-        tops[i] = top[...]
+    tops, window, leaf_transfer, coupling, natural, direction = refs[:6]
+    sources, base, targets, sems = refs[6:10], refs[10], refs[11:15], refs[15]
     top_list, coupling_list, top_coupling, node_transfer = targets
     leaves, samples, points = direction.shape
     rank = natural.shape[1]
@@ -402,6 +406,9 @@
     coords = jnp.transpose(coords, (1, 0, 2))
     coords_prev = shifted(coords, RING, 1)
     coords_after = shifted(coords, RING, -1)
+    travelling, first = lax.optimization_barrier((direction, order, coords_prev, coords_after))[:2]
+    direction_prev = shifted(travelling, RING, 1)
+    direction_after = shifted(travelling, RING, -1)
     natural, coef, lifted, up_mark = call(
         up_kernel,
         (
@@ -424,7 +431,7 @@
             pltpu.SemaphoreType.DMA((5, 4)),
         ],
         vmem=8,
-    )(*in_hbm(order, basis, direction, leaf_transfer, node_transfer))
+    )(*in_hbm(first, basis, direction, leaf_transfer, node_transfer))
 
     def make_tiles(start, done, *operands):
         count = half // 2
@@ -443,34 +450,40 @@
             vmem=8,
         )(*in_hbm(near_list), done, *operands)
 
-    terms = [shifted(lifted, "leaf", by) for by in range(1, leaf_count)]
-    travelling = ordered(direction, coords_prev, coords_after, *terms)
-    direction_prev = shifted(travelling, RING, 1)
-    direction_after = shifted(travelling, RING, -1)
-    direction_other = partner(direction)
     coef_prev = shifted(coef, RING, 1)
     coef_after = shifted(coef, RING, -1)
     tiles_low, low_mark, spread_x, plain = make_tiles(
         0, up_mark, *in_hbm(coords), coords_prev, coords_after
     )
-    top = call(
-        top_kernel,
-        shape((samples, rank), BF),
-        MIB,
-        MIB,
-        in_specs=[anywhere] + [vmem] * leaf_count,
+    leaving = call(
+        after_kernel,
+        shape((samples, rank), F32),
+        MIB,
+        MIB,
+        in_specs=[anywhere, vmem],
         out_specs=vmem,
         vmem=4,
-    )(low_mark, lifted, *terms)
+    )(low_mark, lifted)
     if blk_count <= 8:
-        others = [shifted(top, "blk", by) for by in range(1, blk_count)]
+        others = [shifted(leaving, "blk", by) for by in range(1, blk_count)]
     else:
-        others = lax.all_gather(top[None], "blk", axis=0, tiled=True)
+        others = lax.all_gather(leaving[None], "blk", axis=0, tiled=True)
         places = jnp.mod(lax.axis_index("blk") - jnp.arange(blk_count, dtype=jnp.int32), blk_count)
         others = list(others[places][1:])
     tiles_high, high_mark = make_tiles(half // 2, low_mark, plain, spread_x)
+    direction_other = partner(ordered(direction, high_mark, *others))
     direction_prev = ordered(direction_prev, high_mark, *others)
     direction_after = ordered(direction_after, high_mark, *others)
+    together = call(
+        collect_kernel,
+        shape((blk_count, samples, rank), F32),
+        MIB,
+        MIB,
+        in_specs=[vmem] * blk_count,
+        out_specs=vmem,
+        vmem=4,
+    )(lifted, *others)
+    terms = [shifted(together, "leaf", by) for by in range(1, leaf_count)]
     kept, given, near_mark = call(
         near_kernel,
         (shape((half, samples, points), F32), shape((half, samples, points), BF), token),
@@ -496,15 +509,19 @@
         tiles_high,
     )
 
-    coef_window, given = call(
+    coef_window, given, tops = call(
         window_kernel,
-        (shape((2 * leaves, samples, rank), BF), shape((half, samples, points), BF)),
-        MIB,
-        MIB,
-        in_specs=[vmem] * 3,
-        out_specs=(vmem, vmem),
-        vmem=4,
-    )(given, coef_prev, coef_after)
+        (
+            shape((2 * leaves, samples, rank), BF),
+            shape((half, samples, points), BF),
+            shape((blk_count, samples, rank), BF),
+        ),
+        MIB,
+        MIB,
+        in_specs=[vmem] * (3 + leaf_count),
+        out_specs=(vmem,) * 3,
+        vmem=8,
+    )(given, coef_prev, coef_after, together, *terms)
     arrays = (top_list, coupling_list.T, top_coupling, node_transfer)
     spaces = (pltpu.SMEM,) * 2 + (pltpu.VMEM,) * 2
     whole = shape((leaves, samples, points), F32)
@@ -513,14 +530,13 @@
         whole,
         2 * leaves * samples * rank * (points + 9 * rank),
         8 * MIB,
-        in_specs=[vmem] * (5 + blk_count) + [hbm] * 4,
+        in_specs=[vmem] * 6 + [hbm] * 4,
         out_specs=vmem,
         scratch_shapes=[space(array.shape, array.dtype) for space, array in zip(spaces, arrays)]
-        + [pltpu.VMEM((blk_count, samples, rank), BF), pltpu.SemaphoreType.DMA((4,))],
+        + [pltpu.SemaphoreType.DMA((4,))],
         vmem=10,
     )(
-        top,
-        *others,
+        tops,
         coef_window,
         leaf_transfer,
         coupling,

time: 68 us -> 65.6 us (0.965)
  waiting for transfers between devices: 9.52 us -> 5.22 us
  starting transfers between devices: 17.5 us -> 20.3 us
  blocking collectives: 10.4 us -> 9.5 us
    ppermute x10, waiting for transfers between devices: 9.51 us -> 5.21 us  [shifted(): lax.ppermute(array, axis, [(i, (i + by) % count) for i in range(count)])]
    ppermute x10, starting transfers between devices: 16.8 us -> 19.5 us  [shifted(): lax.ppermute(array, axis, [(i, (i + by) % count) for i in range(count)])]
    all_to_all x1, blocking collectives: 10.4 us -> 9.5 us  [on_device(): norms = lax.all_to_all(norms, RING, 0, 0)]
  transfers between devices with their start and end apart: 14 -> 14, of which waited for: 2 -> 2; matrix products, arithmetic and copies ran while one was open for 0% -> 0% of each run, Pallas kernels for 40% -> 41%
where the time goes in v9:
time: 65.6 us; the launch traced here: 65.2 us
  Pallas kernels  29.3 us (45%)
  starting transfers between devices  20.3 us (31%)
  blocking collectives  9.5 us (14%)
  waiting for transfers between devices  5.22 us (8%)
  between operations  0.89 us (1%)
    ppermute x10, starting transfers between devices, shifted(): lax.ppermute(array, axis, [(i, (i + by) % count) for i in range(count)])  19.5 us
    pallas_call x2, Pallas kernels, make_tiles(): call(functools.partial(tile_kernel, start), outs, 40 * count * entries *...  12 us
    all_to_all x1, blocking collectives, on_device(): norms = lax.all_to_all(norms, RING, 0, 0)  9.5 us
    pallas_call x1, Pallas kernels, on_device(): call(up_kernel, (pltpu.HBM((leaves, rank, points), BF), shape((leaves //...  6.14 us
    ppermute x10, waiting for transfers between devices, shifted(): lax.ppermute(array, axis, [(i, (i + by) % count) for i in range(count)])  5.21 us
    pallas_call x1, Pallas kernels, on_device(): call(near_kernel, (shape((half, samples, points), F32), shape((half, samp...  5.02 us
    pallas_call x1, Pallas kernels, on_device(): call(down_kernel, whole, 2 * leaves * samples * rank * (points + 9 * rank...  3.73 us
  transfers between devices with their start and end apart: 14, of which 2 were waited for; matrix products, arithmetic and copies ran while one was open for 0% of the time, Pallas kernels for 41%

profile of v9, /device:TPU:0, one launch (start us, length us, event | category | flops | bytes accessed | tf_op | source)
XLA Modules:
  0.0 65.2 jit_solution(11378403959155730303)
XLA Ops:
  0.6 3.0 %collective-permute-start = (bf16[3,16,256]{2,1,0:T(8,128)(2,1)}, bf16[3,16,256]{2,1,0:T(8,128)(2,1)S(1)}, u32[]{:S(2)}, u32[]{:S(2)}) collective-permute-start(bf16[3,16,256]{2,1,0:T(8,128)(2,1)} %bitcast.5), channel_id=1, source_target_pairs={{0,2},{2,4},{4,6},{6,8},{8,10},{10,12},{12,14},{14,0},{1,3},{3,5},... | collective-permute-start | bytes 73736 | tf_op jit(solution)/shard_map/ppermute | solution.py:32
  3.6 3.1 %collective-permute-start.1 = (bf16[3,16,256]{2,1,0:T(8,128)(2,1)}, bf16[3,16,256]{2,1,0:T(8,128)(2,1)S(1)}, u32[]{:S(2)}, u32[]{:S(2)}) collective-permute-start(bf16[3,16,256]{2,1,0:T(8,128)(2,1)} %bitcast.6), channel_id=1, source_target_pairs={{0,14},{2,0},{4,2},{6,4},{8,6},{10,8},{12,10},{14,12},{1,15},{3,1}... | collective-permute-start | bytes 73736 | tf_op jit(solution)/shard_map/ppermute | solution.py:32
  6.7 2.0 %collective-permute-done.refs_1_ = bf16[3,16,256]{2,1,0:T(8,128)(2,1)S(1)} collective-permute-done((bf16[3,16,256]{2,1,0:T(8,128)(2,1)}, bf16[3,16,256]{2,1,0:T(8,128)(2,1)S(1)}, u32[]{:S(2)}, u32[]{:S(2)}) %collective-permute-start) | collective-permute-done | bytes 24608 | tf_op jit(solution)/shard_map/ppermute | solution.py:32
  8.7 0.0 collective-permute-done.1.refs_2_
  8.7 4.8 %collective-permute-start.8 = (bf16[16,64,256]{2,1,0:T(8,128)(2,1)}, bf16[16,64,256]{2,1,0:T(8,128)(2,1)S(1)}, u32[]{:S(2)}, u32[]{:S(2)}) collective-permute-start(bf16[16,64,256]{2,1,0:T(8,128)(2,1)} %direction.1), channel_id=1, source_target_pairs={{0,14},{2,0},{4,2},{6,4},{8,6},{10,8},{12,10},{14,12},{1,15},{3,1}... | collective-permute-start | bytes 1572872 | tf_op jit(solution)/shard_map/ppermute | solution.py:32
  13.5 0.0 collective-permute-start.2
  13.5 6.1 %shard_map.140 = (bf16[16,64,256]{2,1,0:T(8,128)(2,1)}, bf16[8,64,128]{2,1,0:T(8,128)(2,1)S(1)}, f32[64,64]{1,0:T(8,128)S(1)}, f32[8,128]{1,0:T(8,128)S(1)}) custom-call(s32[16,256]{1,0:T(8,128)} %order_h, bf16[16,64,256]{2,1,0:T(8,128)(2,1)} %basis_h.1, bf16[16,64,256]{2,1,0:T(8,128)(2,1)} %direction.1, bf16[16,64,64]{2,1,0:T(8,128)(2,1)} %refs_2_.3, ...), custom_call_target="tpu_custom_call" | custom-call | flops 268435456 | bytes 6291456 | tf_op jit(solution)/shard_map/pallas_call | solution.py:412
  19.6 6.5 %shard_map.141 = (bf16[4,3072,256]{2,1,0:T(8,128)(2,1)S(1)}, f32[8,128]{1,0:T(8,128)S(1)}, bf16[48,256,128]{2,1,0:T(8,128)(2,1)S(1)}, f32[3,16,256]{2,1,0:T(8,128)S(1)}) custom-call(s32[16,12]{1,0:T(8,128)} %near_h.5, f32[8,128]{1,0:T(8,128)S(1)} %get-tuple-element.27._, bf16[3,16,256]{2,1,0:T(8,128)(2,1)} %bitcast.7, ...), custom_call_target="tpu_custom_call" | custom-call | flops 125829120 | bytes 50331648 | tf_op jit(solution)/shard_map/pallas_call | solution.py:441
  26.1 0.1 collective-permute-start.3
  26.2 1.1 %collective-permute-start.4 = (f32[64,64]{1,0:T(8,128)S(1)}, f32[64,64]{1,0:T(8,128)S(1)}, u32[]{:S(2)}, u32[]{:S(2)}) collective-permute-start(f32[64,64]{1,0:T(8,128)S(1)} %shard_map.143), channel_id=1, source_target_pairs={{0,8},{4,12},{8,0},{12,4},{1,9},{5,13},{9,1},{13,5},{2,10},{6,14},... | collective-permute-start | bytes 49160 | tf_op jit(solution)/shard_map/ppermute | solution.py:32
  27.3 2.7 %collective-permute-start.5 = (f32[64,64]{1,0:T(8,128)S(1)}, f32[64,64]{1,0:T(8,128)S(1)}, u32[]{:S(2)}, u32[]{:S(2)}) collective-permute-start(f32[64,64]{1,0:T(8,128)S(1)} %shard_map.143), channel_id=1, source_target_pairs={{0,12},{4,0},{8,4},{12,8},{1,13},{5,1},{9,5},{13,9},{2,14},{6,2},{... | collective-permute-start | bytes 49160 | tf_op jit(solution)/shard_map/ppermute | solution.py:32
  30.0 5.5 %shard_map.142 = (bf16[4,3072,256]{2,1,0:T(8,128)(2,1)S(1)}, f32[8,128]{1,0:T(8,128)}) custom-call(s32[16,12]{1,0:T(8,128)} %near_h.5, f32[8,128]{1,0:T(8,128)S(1)} %get-tuple-element.28._, f32[3,16,256]{2,1,0:T(8,128)S(1)} %get-tuple-element.29.refs_0_, bf16[48,256,128]{2,1,0:T(8,128)(2,1)S(1)} %get-tuple-element.30.refs_1_), custom_call_target="tpu_custom_call" | custom-call | flops 125829120 | bytes 3145728 | tf_op jit(solution)/shard_map/pallas_call | solution.py:441
  35.6 0.1 collective-permute-start.7
  35.7 0.5 collective-permute-start.9
  36.2 0.1 collective-permute-start.6
  36.3 2.0 %collective-permute-start.10 = (bf16[8,64,128]{2,1,0:T(8,128)(2,1)S(1)}, bf16[8,64,128]{2,1,0:T(8,128)(2,1)S(1)}, u32[]{:S(2)}, u32[]{:S(2)}) collective-permute-start(bf16[8,64,128]{2,1,0:T(8,128)(2,1)S(1)} %get-tuple-element.39), channel_id=1, source_target_pairs={{0,2},{2,4},{4,6},{6,8},{8,10},{10,12},{12,14},{14,0},{1,3},{3,5},... | collective-permute-start | bytes 393224 | tf_op jit(solution)/shard_map/ppermute | solution.py:32
  38.3 2.7 %collective-permute-start.11 = (bf16[8,64,128]{2,1,0:T(8,128)(2,1)S(1)}, bf16[8,64,128]{2,1,0:T(8,128)(2,1)S(1)}, u32[]{:S(2)}, u32[]{:S(2)}) collective-permute-start(bf16[8,64,128]{2,1,0:T(8,128)(2,1)S(1)} %get-tuple-element.39), channel_id=1, source_target_pairs={{0,14},{2,0},{4,2},{6,4},{8,6},{10,8},{12,10},{14,12},{1,15},{3,1}... | collective-permute-start | bytes 393224 | tf_op jit(solution)/shard_map/ppermute | solution.py:32
  41.0 0.1 collective-permute-start.12
  41.1 0.0 copy-start
  41.1 0.0 copy-start.1
  41.1 0.0 copy-start.3
  41.1 0.0 copy-start.4
  41.2 0.0 copy-start.5
  41.2 5.0 %shard_map.144 = (f32[8,64,256]{2,1,0:T(8,128)S(1)}, bf16[8,64,256]{2,1,0:T(8,128)(2,1)S(1)}, f32[8,128]{1,0:T(8,128)}) custom-call(s32[16,12]{1,0:T(8,128)} %near_h.5, bf16[16,64,256]{2,1,0:T(8,128)(2,1)S(1)} %collective-permute-done.2.refs_0_, bf16[16,64,256]{2,1,0:T(8,128)(2,1)S(1)} %collective-permute-done.6.refs_1_, bf16[16,64,256]{2,1,0:T(8,128)(2,1)} %direction.1, ...), custom_call_target="tpu_custom_call" | custom-call | flops 1048576 | bytes 1048576 | tf_op jit(solution)/shard_map/pallas_call | solution.py:487
  46.2 0.0 copy-start.2
  46.2 3.2 %collective-permute-done.12.refs_1_ = f32[4,64,64]{2,1,0:T(8,128)S(1)} collective-permute-done((f32[4,64,64]{2,1,0:T(8,128)S(1)}, f32[4,64,64]{2,1,0:T(8,128)S(1)}, u32[]{:S(2)}, u32[]{:S(2)}) %collective-permute-start.12) | collective-permute-done | bytes 65568 | tf_op jit(solution)/shard_map/ppermute | solution.py:32
  49.5 0.2 shard_map.146
  49.7 0.1 collective-permute-start.13
  49.8 3.7 %shard_map.147.base = f32[16,64,256]{2,1,0:T(8,128)S(1)} custom-call(bf16[4,64,64]{2,1,0:T(8,128)(2,1)S(1)} %get-tuple-element.40.refs_0_, bf16[32,64,64]{2,1,0:T(8,128)(2,1)S(1)} %get-tuple-element.41.refs_1_, bf16[16,64,64]{2,1,0:T(8,128)(2,1)S(1)} %copy-done.3, bf16[16,8,64,64]{3,2,1,0:T(8,128)(2,1)S(1)} %copy-done.1, bf16[16,64,256]{2,1,0:T(8,128)(2,1)S(1)} %copy-done.4, ...), custom_call_target="tpu_custom_call" | custom-call | flops 109051904 | bytes 8388608 | tf_op jit(solution)/shard_map/pallas_call | solution.py:528
  53.6 1.2 %shard_map.148 = (f32[16,64,256]{2,1,0:T(8,128)}, f32[16,64,256]{2,1,0:T(8,128)S(1)}, f32[8,8,128]{2,1,0:T(8,128)S(1)}) custom-call(f32[1,64]{1,0:T(1,128)S(1)} %bitcast.3, f32[16,64,256]{2,1,0:T(8,128)S(1)} %shard_map.147.base, f32[8,64,256]{2,1,0:T(8,128)S(1)} %get-tuple-element.43.kept, bf16[8,64,256]{2,1,0:T(8,128)(2,1)S(1)} %collective-permute-done.13.received, ...), custom_call_target="tpu_custom_call" | custom-call | flops 4194304 | bytes 5242880 | tf_op jit(solution)/shard_map/pallas_call | solution.py:550
  54.8 9.5 %all_to_all.5.norms = f32[8,8,128]{2,1,0:T(8,128)S(1)} all-to-all(f32[8,8,128]{2,1,0:T(8,128)S(1)} %get-tuple-element.46), channel_id=1, replica_groups=mesh['groups'=2,'blk'=4,'leaf'=2,'sample'=2] {'blk','leaf'}, dimensions={0} | all-to-all | bytes 65536 | tf_op jit(solution)/shard_map/all_to_all | solution.py:560
  64.3 0.9 %shard_map.149 = bf16[16,64,256]{2,1,0:T(8,128)(2,1)} custom-call(f32[8,8,128]{2,1,0:T(8,128)S(1)} %all_to_all.5.norms, f32[16,64,256]{2,1,0:T(8,128)S(1)} %get-tuple-element.47.updated, bf16[16,64,256]{2,1,0:T(8,128)(2,1)S(1)} %copy-done), custom_call_target="tpu_custom_call" | custom-call | flops 1048576 | bytes 2097152 | tf_op jit(solution)/shard_map/pallas_call | solution.py:561
  (19 shorter events, 0.1 us)
Async XLA Ops:
  0.6 8.0 %collective-permute-start = (bf16[3,16,256]{2,1,0:T(8,128)(2,1)}, bf16[3,16,256]{2,1,0:T(8,128)(2,1)S(1)}, u32[]{:S(2)}, u32[]{:S(2)}) collective-permute-start(bf16[3,16,256]{2,1,0:T(8,128)(2,1)} %bitcast.5), channel_id=1, source_target_pairs={{0,2},{2,4},{4,6},{6,8},{8,10},{10,12},{12,14},{14,0},{1,3},{3,5},... | collective-permute-start | bytes 73736 | tf_op jit(solution)/shard_map/ppermute | solution.py:32
  3.6 5.1 %collective-permute-start.1 = (bf16[3,16,256]{2,1,0:T(8,128)(2,1)}, bf16[3,16,256]{2,1,0:T(8,128)(2,1)S(1)}, u32[]{:S(2)}, u32[]{:S(2)}) collective-permute-start(bf16[3,16,256]{2,1,0:T(8,128)(2,1)} %bitcast.6), channel_id=1, source_target_pairs={{0,14},{2,0},{4,2},{6,4},{8,6},{10,8},{12,10},{14,12},{1,15},{3,1}... | collective-permute-start | bytes 73736 | tf_op jit(solution)/shard_map/ppermute | solution.py:32
  8.7 27.0 %collective-permute-start.8 = (bf16[16,64,256]{2,1,0:T(8,128)(2,1)}, bf16[16,64,256]{2,1,0:T(8,128)(2,1)S(1)}, u32[]{:S(2)}, u32[]{:S(2)}) collective-permute-start(bf16[16,64,256]{2,1,0:T(8,128)(2,1)} %direction.1), channel_id=1, source_target_pairs={{0,14},{2,0},{4,2},{6,4},{8,6},{10,8},{12,10},{14,12},{1,15},{3,1}... | collective-permute-start | bytes 1572872 | tf_op jit(solution)/shard_map/ppermute | solution.py:32
  13.5 22.7 %collective-permute-start.2 = (bf16[16,64,256]{2,1,0:T(8,128)(2,1)}, bf16[16,64,256]{2,1,0:T(8,128)(2,1)S(1)}, u32[]{:S(2)}, u32[]{:S(2)}) collective-permute-start(bf16[16,64,256]{2,1,0:T(8,128)(2,1)} %direction.1), channel_id=1, source_target_pairs={{0,2},{2,4},{4,6},{6,8},{8,10},{10,12},{12,14},{14,0},{1,3},{3,5},... | collective-permute-start | bytes 1572872 | tf_op jit(solution)/shard_map/ppermute | solution.py:32
  26.1 9.4 %collective-permute-start.3 = (f32[64,64]{1,0:T(8,128)S(1)}, f32[64,64]{1,0:T(8,128)S(1)}, u32[]{:S(2)}, u32[]{:S(2)}) collective-permute-start(f32[64,64]{1,0:T(8,128)S(1)} %shard_map.143), channel_id=1, source_target_pairs={{0,4},{4,8},{8,12},{12,0},{1,5},{5,9},{9,13},{13,1},{2,6},{6,10},{... | collective-permute-start | bytes 49160 | tf_op jit(solution)/shard_map/ppermute | solution.py:32
  26.2 9.4 %collective-permute-start.4 = (f32[64,64]{1,0:T(8,128)S(1)}, f32[64,64]{1,0:T(8,128)S(1)}, u32[]{:S(2)}, u32[]{:S(2)}) collective-permute-start(f32[64,64]{1,0:T(8,128)S(1)} %shard_map.143), channel_id=1, source_target_pairs={{0,8},{4,12},{8,0},{12,4},{1,9},{5,13},{9,1},{13,5},{2,10},{6,14},... | collective-permute-start | bytes 49160 | tf_op jit(solution)/shard_map/ppermute | solution.py:32
  27.3 8.3 %collective-permute-start.5 = (f32[64,64]{1,0:T(8,128)S(1)}, f32[64,64]{1,0:T(8,128)S(1)}, u32[]{:S(2)}, u32[]{:S(2)}) collective-permute-start(f32[64,64]{1,0:T(8,128)S(1)} %shard_map.143), channel_id=1, source_target_pairs={{0,12},{4,0},{8,4},{12,8},{1,13},{5,1},{9,5},{13,9},{2,14},{6,2},{... | collective-permute-start | bytes 49160 | tf_op jit(solution)/shard_map/ppermute | solution.py:32
  35.6 5.4 %collective-permute-start.7 = (bf16[16,64,256]{2,1,0:T(8,128)(2,1)}, bf16[16,64,256]{2,1,0:T(8,128)(2,1)S(1)}, u32[]{:S(2)}, u32[]{:S(2)}) collective-permute-start(bf16[16,64,256]{2,1,0:T(8,128)(2,1)} %direction.1), channel_id=1, source_target_pairs={{0,1},{1,0},{2,3},{3,2},{4,5},{5,4},{6,7},{7,6},{8,9},{9,8},{10,11... | collective-permute-start | bytes 1572872 | tf_op jit(solution)/shard_map/ppermute | solution.py:36
  35.7 5.4 %collective-permute-start.9 = (bf16[16,64,256]{2,1,0:T(8,128)(2,1)S(1)}, bf16[16,64,256]{2,1,0:T(8,128)(2,1)S(1)}, u32[]{:S(2)}, u32[]{:S(2)}) collective-permute-start(bf16[16,64,256]{2,1,0:T(8,128)(2,1)S(1)} %collective-permute-done.8.refs_4_), channel_id=1, source_target_pairs={{0,1},{1,0},{2,3},{3,2},{4,5},{5,4},{6,7},{7,6},{8,9},{9,8},{10,11... | collective-permute-start | bytes 1572872 | tf_op jit(solution)/shard_map/ppermute | solution.py:36
  36.2 4.9 %collective-permute-start.6 = (bf16[16,64,256]{2,1,0:T(8,128)(2,1)S(1)}, bf16[16,64,256]{2,1,0:T(8,128)(2,1)S(1)}, u32[]{:S(2)}, u32[]{:S(2)}) collective-permute-start(bf16[16,64,256]{2,1,0:T(8,128)(2,1)S(1)} %collective-permute-done.2.refs_0_), channel_id=1, source_target_pairs={{0,1},{1,0},{2,3},{3,2},{4,5},{5,4},{6,7},{7,6},{8,9},{9,8},{10,11... | collective-permute-start | bytes 1572872 | tf_op jit(solution)/shard_map/ppermute | solution.py:36
  36.3 13.2 %collective-permute-start.10 = (bf16[8,64,128]{2,1,0:T(8,128)(2,1)S(1)}, bf16[8,64,128]{2,1,0:T(8,128)(2,1)S(1)}, u32[]{:S(2)}, u32[]{:S(2)}) collective-permute-start(bf16[8,64,128]{2,1,0:T(8,128)(2,1)S(1)} %get-tuple-element.39), channel_id=1, source_target_pairs={{0,2},{2,4},{4,6},{6,8},{8,10},{10,12},{12,14},{14,0},{1,3},{3,5},... | collective-permute-start | bytes 393224 | tf_op jit(solution)/shard_map/ppermute | solution.py:32
  38.3 11.2 %collective-permute-start.11 = (bf16[8,64,128]{2,1,0:T(8,128)(2,1)S(1)}, bf16[8,64,128]{2,1,0:T(8,128)(2,1)S(1)}, u32[]{:S(2)}, u32[]{:S(2)}) collective-permute-start(bf16[8,64,128]{2,1,0:T(8,128)(2,1)S(1)} %get-tuple-element.39), channel_id=1, source_target_pairs={{0,14},{2,0},{4,2},{6,4},{8,6},{10,8},{12,10},{14,12},{1,15},{3,1}... | collective-permute-start | bytes 393224 | tf_op jit(solution)/shard_map/ppermute | solution.py:32
  41.0 8.4 %collective-permute-start.12 = (f32[4,64,64]{2,1,0:T(8,128)S(1)}, f32[4,64,64]{2,1,0:T(8,128)S(1)}, u32[]{:S(2)}, u32[]{:S(2)}) collective-permute-start(f32[4,64,64]{2,1,0:T(8,128)S(1)} %shard_map.145.refs_0_), channel_id=1, source_target_pairs={{0,2},{2,0},{1,3},{3,1},{4,6},{6,4},{5,7},{7,5},{8,10},{10,8},{9,1... | collective-permute-start | bytes 196616 | tf_op jit(solution)/shard_map/ppermute | solution.py:32
  41.1 8.6 %copy-start = (bf16[16,64,256]{2,1,0:T(8,128)(2,1)S(1)}, bf16[16,64,256]{2,1,0:T(8,128)(2,1)}, u32[]{:S(2)}) copy-start(bf16[16,64,256]{2,1,0:T(8,128)(2,1)} %direction.1) | copy-start | bytes 1572868
  41.1 8.6 %copy-start.1 = (bf16[16,8,64,64]{3,2,1,0:T(8,128)(2,1)S(1)}, bf16[16,8,64,64]{3,2,1,0:T(8,128)(2,1)}, u32[]{:S(2)}) copy-start(bf16[16,8,64,64]{3,2,1,0:T(8,128)(2,1)} %refs_3_.1) | copy-start | bytes 3145732
  41.1 8.6 %copy-start.3 = (bf16[16,64,64]{2,1,0:T(8,128)(2,1)S(1)}, bf16[16,64,64]{2,1,0:T(8,128)(2,1)}, u32[]{:S(2)}) copy-start(bf16[16,64,64]{2,1,0:T(8,128)(2,1)} %refs_2_.3) | copy-start | bytes 393220
  41.1 8.6 %copy-start.4 = (bf16[16,64,256]{2,1,0:T(8,128)(2,1)S(1)}, bf16[16,64,256]{2,1,0:T(8,128)(2,1)}, u32[]{:S(2)}) copy-start(bf16[16,64,256]{2,1,0:T(8,128)(2,1)} %get-tuple-element.42.refs_4_) | copy-start | bytes 1572868
  41.2 12.4 %copy-start.5 = (f32[64]{0:T(128)S(1)}, f32[64]{0:T(128)}, u32[]{:S(2)}) copy-start(f32[64]{0:T(128)} %param.15) | copy-start | bytes 772
  46.2 7.4 %copy-start.2 = (f32[16,64,256]{2,1,0:T(8,128)S(1)}, f32[16,64,256]{2,1,0:T(8,128)}, u32[]{:S(2)}) copy-start(f32[16,64,256]{2,1,0:T(8,128)} %residual.1) | copy-start | bytes 3145732
  49.7 3.9 %collective-permute-start.13 = (bf16[8,64,256]{2,1,0:T(8,128)(2,1)S(1)}, bf16[8,64,256]{2,1,0:T(8,128)(2,1)S(1)}, u32[]{:S(2)}, u32[]{:S(2)}) collective-permute-start(bf16[8,64,256]{2,1,0:T(8,128)(2,1)S(1)} %get-tuple-element.44), channel_id=1, source_target_pairs={{0,1},{1,0},{2,3},{3,2},{4,5},{5,4},{6,7},{7,6},{8,9},{9,8},{10,11... | collective-permute-start | bytes 786440 | tf_op jit(solution)/shard_map/ppermute | solution.py:36

commit v10 on v9

--- a/solution.py
+++ b/solution.py
@@ -216,7 +216,9 @@
 
 
 def after_kernel(_, source, target):
-    target[...] = source[...]
+    rank = source.shape[1]
+    for i, part in enumerate(thirds(source[...])[:2]):
+        target[:, i * rank : (i + 1) * rank] = part.astype(target.dtype)
 
 
 def collect_kernel(*refs):
@@ -225,12 +227,7 @@
         together[i] = term[...]
 
 
-def window_kernel(given, before, after, *refs):
-    terms, (window, sent, tops) = refs[:-3], refs[-3:]
-    total = terms[0][...]
-    for term in terms[1:]:
-        total = total + term[...]
-    tops[...] = total.astype(tops.dtype)
+def window_kernel(given, before, after, window, sent):
     sent[...] = given[...]
     rows, _, lanes = before.shape
     rank = lanes // 2
@@ -240,39 +237,53 @@
             window[side * 2 * rows + g] = part
 
 
+def couple_kernel(window, coupling, list_h, part, coupling_list, sem):
+    copy = pltpu.make_async_copy(list_h, coupling_list, sem)
+    copy.start()
+    leaves, count = coupling.shape[:2]
+    total = leaves * lax.axis_size("blk") * lax.axis_size("leaf")
+    device = lax.axis_index("blk") * lax.axis_size("leaf") + lax.axis_index("leaf")
+    anchor = (device - 1) * leaves
+    copy.wait()
+    for g in range(leaves):
+        rows = []
+        for c in range(count):
+            slot = lax.rem(coupling_list[c, g] - anchor + 2 * total, total)
+            slot = jnp.where(slot >= 2 * leaves, slot - leaves, slot)
+            slot = jnp.minimum(slot, 2 * leaves - 1)
+            rows.append(window[slot])
+        columns = [coupling[g, c] for c in range(count)]
+        part[g] = nt(jnp.concatenate(rows, axis=1), jnp.concatenate(columns, axis=1))
+
+
 def down_kernel(*refs):
-    clusters = lax.axis_size("blk")
-    tops, window, leaf_transfer, coupling, natural, direction = refs[:6]
-    sources, base, targets, sems = refs[6:10], refs[10], refs[11:15], refs[15]
-    top_list, coupling_list, top_coupling, node_transfer = targets
-    leaves, samples, points = direction.shape
-    rank = natural.shape[1]
-    here = lax.axis_index("blk")
-    total = leaves * clusters * lax.axis_size("leaf")
-    anchor = (here * lax.axis_size("leaf") + lax.axis_index("leaf") - 1) * leaves
+    terms, refs = refs[: lax.axis_size("leaf")], refs[lax.axis_size("leaf") :]
+    part, leaf_transfer, natural, direction = refs[:4]
+    sources, base, targets, (tops, sems) = refs[4:7], refs[7], refs[8:11], refs[11:]
+    top_list, top_coupling, node_transfer = targets
     copies = [
         pltpu.make_async_copy(source, target, sems.at[i])
         for i, (source, target) in enumerate(zip(sources, targets))
     ]
     for copy in copies:
         copy.start()
+    leaves, samples, points = direction.shape
+    rank = natural.shape[1]
+    clusters = lax.axis_size("blk")
+    here = lax.axis_index("blk")
+    together = terms[0][...].astype(F32)
+    for term in terms[1:]:
+        together = together + term[...].astype(F32)
+    tops[...] = (together[:, :, :rank] + together[:, :, rank:]).astype(tops.dtype)
     for copy in copies:
         copy.wait()
     incoming = jnp.zeros((samples, rank), F32)
     for e in range(top_list.shape[1]):
-        place = lax.rem(here - top_list[0, e] + clusters, clusters)
-        incoming = incoming + nt(tops[place], top_coupling[0, e])
+        index = lax.rem(here - top_list[0, e] + clusters, clusters)
+        incoming = incoming + nt(tops[index], top_coupling[0, e])
     down = nn(incoming.astype(BF), node_transfer[0]).astype(BF)
     for g in range(leaves):
-        inward = nn(down, leaf_transfer[g])
-        rows = []
-        for c in range(coupling_list.shape[0]):
-            slot = lax.rem(coupling_list[c, g] - anchor + 2 * total, total)
-            slot = jnp.where(slot >= 2 * leaves, slot - leaves, slot)
-            slot = jnp.minimum(slot, 2 * leaves - 1)
-            rows.append(window[slot])
-        columns = [coupling[g, c] for c in range(coupling_list.shape[0])]
-        inward = inward + nt(jnp.concatenate(rows, axis=1), jnp.concatenate(columns, axis=1))
+        inward = nn(down, leaf_transfer[g]) + part[g]
         far = nn(inward.astype(BF), natural[g])
         base[g] = NUGGET * direction[g].astype(F32) + far
 
@@ -457,7 +468,7 @@
     )
     leaving = call(
         after_kernel,
-        shape((samples, rank), F32),
+        shape((samples, 2 * rank), BF),
         MIB,
         MIB,
         in_specs=[anywhere, vmem],
@@ -476,13 +487,13 @@
     direction_after = ordered(direction_after, high_mark, *others)
     together = call(
         collect_kernel,
-        shape((blk_count, samples, rank), F32),
+        shape((blk_count, samples, 2 * rank), BF),
         MIB,
         MIB,
         in_specs=[vmem] * blk_count,
         out_specs=vmem,
         vmem=4,
-    )(lifted, *others)
+    )(leaving, *others)
     terms = [shifted(together, "leaf", by) for by in range(1, leaf_count)]
     kept, given, near_mark = call(
         near_kernel,
@@ -509,44 +520,45 @@
         tiles_high,
     )
 
-    coef_window, given, tops = call(
+    coef_window, given = call(
         window_kernel,
-        (
-            shape((2 * leaves, samples, rank), BF),
-            shape((half, samples, points), BF),
-            shape((blk_count, samples, rank), BF),
-        ),
-        MIB,
-        MIB,
-        in_specs=[vmem] * (3 + leaf_count),
-        out_specs=(vmem,) * 3,
+        (shape((2 * leaves, samples, rank), BF), shape((half, samples, points), BF)),
+        MIB,
+        MIB,
+        in_specs=[vmem] * 3,
+        out_specs=(vmem, vmem),
+        vmem=4,
+    )(given, coef_prev, coef_after)
+    part = call(
+        couple_kernel,
+        shape((leaves, samples, rank), F32),
+        2 * leaves * samples * rank * rank * 8,
+        4 * MIB,
+        in_specs=[vmem] * 2 + [hbm],
+        out_specs=vmem,
+        scratch_shapes=[
+            pltpu.SMEM(coupling_list.shape[::-1], jnp.int32),
+            pltpu.SemaphoreType.DMA,
+        ],
         vmem=8,
-    )(given, coef_prev, coef_after, together, *terms)
-    arrays = (top_list, coupling_list.T, top_coupling, node_transfer)
-    spaces = (pltpu.SMEM,) * 2 + (pltpu.VMEM,) * 2
-    whole = shape((leaves, samples, points), F32)
+    )(coef_window, coupling, *in_hbm(coupling_list.T))
+    arrays = (top_list, top_coupling, node_transfer)
+    spaces = (pltpu.SMEM, pltpu.VMEM, pltpu.VMEM)
     base = call(
         down_kernel,
-        whole,
-        2 * leaves * samples * rank * (points + 9 * rank),
-        8 * MIB,
-        in_specs=[vmem] * 6 + [hbm] * 4,
+        shape((leaves, samples, points), F32),
+        2 * leaves * samples * rank * (points + rank),
+        4 * MIB,
+        in_specs=[vmem] * (4 + leaf_count) + [hbm] * 3,
         out_specs=vmem,
         scratch_shapes=[space(array.shape, array.dtype) for space, array in zip(spaces, arrays)]
-        + [pltpu.SemaphoreType.DMA((4,))],
+        + [pltpu.VMEM((blk_count, samples, rank), BF), pltpu.SemaphoreType.DMA((3,))],
         vmem=10,
-    )(
-        tops,
-        coef_window,
-        leaf_transfer,
-        coupling,
-        natural,
-        direction,
-        *in_hbm(*arrays),
-    )
+    )(together, *terms, part, leaf_transfer, natural, direction, *in_hbm(*arrays))
     received = partner(given)
 
     devices = blk_count * leaf_count
+    whole = shape((leaves, samples, points), F32)
     residual_next, updated, norms = call(
         residual_kernel,
         (whole, whole, shape((devices, 8, 128), F32)),

time: 65.6 us -> 67 us (1.021)
  blocking collectives: 9.5 us -> 10.4 us
    all_to_all x1, blocking collectives: 9.5 us -> 10.4 us  [on_device(): norms = lax.all_to_all(norms, RING, 0, 0)]
    pallas_call x3 -> x4, Pallas kernels: 3.75 us -> 4.18 us  [the longest x1 2.58 us: on_device(): call(down_kernel, shape((leaves, samples, points), F32), 2 * leaves * sam...]
  transfers between devices with their start and end apart: 14 -> 14, of which waited for: 2 -> 3; matrix products, arithmetic and copies ran while one was open for 0% -> 0% of each run, Pallas kernels for 41% -> 41%
where the time goes in v10:
time: 67 us; the launch traced here: 66.6 us
  Pallas kernels  29.7 us (44%)
  starting transfers between devices  20.5 us (31%)
  blocking collectives  10.4 us (16%)
  waiting for transfers between devices  5.12 us (8%)
  between operations  0.85 us (1%)
    ppermute x10, starting transfers between devices, shifted(): lax.ppermute(array, axis, [(i, (i + by) % count) for i in range(count)])  19.8 us
    pallas_call x2, Pallas kernels, make_tiles(): call(functools.partial(tile_kernel, start), outs, 40 * count * entries *...  12 us
    all_to_all x1, blocking collectives, on_device(): norms = lax.all_to_all(norms, RING, 0, 0)  10.4 us
    pallas_call x1, Pallas kernels, on_device(): call(up_kernel, (pltpu.HBM((leaves, rank, points), BF), shape((leaves //...  6.14 us
    ppermute x10, waiting for transfers between devices, shifted(): lax.ppermute(array, axis, [(i, (i + by) % count) for i in range(count)])  5.11 us
    pallas_call x1, Pallas kernels, on_device(): call(near_kernel, (shape((half, samples, points), F32), shape((half, samp...  5.03 us
    pallas_call x1, Pallas kernels, on_device(): call(down_kernel, shape((leaves, samples, points), F32), 2 * leaves * sam...  2.58 us
    pallas_call x1, Pallas kernels, on_device(): call(couple_kernel, shape((leaves, samples, rank), F32), 2 * leaves * sam...  1.52 us
  transfers between devices with their start and end apart: 14, of which 3 were waited for; matrix products, arithmetic and copies ran while one was open for 0% of the time, Pallas kernels for 41%

profile of v10, /device:TPU:0, one launch (start us, length us, event | category | flops | bytes accessed | tf_op | source)
XLA Modules:
  0.0 66.6 jit_solution(7853309144320051110)
XLA Ops:
  0.6 3.0 %collective-permute-start = (bf16[3,16,256]{2,1,0:T(8,128)(2,1)}, bf16[3,16,256]{2,1,0:T(8,128)(2,1)S(1)}, u32[]{:S(2)}, u32[]{:S(2)}) collective-permute-start(bf16[3,16,256]{2,1,0:T(8,128)(2,1)} %bitcast.5), channel_id=1, source_target_pairs={{0,2},{2,4},{4,6},{6,8},{8,10},{10,12},{12,14},{14,0},{1,3},{3,5},... | collective-permute-start | bytes 73736 | tf_op jit(solution)/shard_map/ppermute | solution.py:32
  3.6 3.1 %collective-permute-start.1 = (bf16[3,16,256]{2,1,0:T(8,128)(2,1)}, bf16[3,16,256]{2,1,0:T(8,128)(2,1)S(1)}, u32[]{:S(2)}, u32[]{:S(2)}) collective-permute-start(bf16[3,16,256]{2,1,0:T(8,128)(2,1)} %bitcast.6), channel_id=1, source_target_pairs={{0,14},{2,0},{4,2},{6,4},{8,6},{10,8},{12,10},{14,12},{1,15},{3,1}... | collective-permute-start | bytes 73736 | tf_op jit(solution)/shard_map/ppermute | solution.py:32
  6.7 2.0 %collective-permute-done.refs_1_ = bf16[3,16,256]{2,1,0:T(8,128)(2,1)S(1)} collective-permute-done((bf16[3,16,256]{2,1,0:T(8,128)(2,1)}, bf16[3,16,256]{2,1,0:T(8,128)(2,1)S(1)}, u32[]{:S(2)}, u32[]{:S(2)}) %collective-permute-start) | collective-permute-done | bytes 24608 | tf_op jit(solution)/shard_map/ppermute | solution.py:32
  8.7 4.8 %collective-permute-start.9 = (bf16[16,64,256]{2,1,0:T(8,128)(2,1)}, bf16[16,64,256]{2,1,0:T(8,128)(2,1)S(1)}, u32[]{:S(2)}, u32[]{:S(2)}) collective-permute-start(bf16[16,64,256]{2,1,0:T(8,128)(2,1)} %direction.1), channel_id=1, source_target_pairs={{0,14},{2,0},{4,2},{6,4},{8,6},{10,8},{12,10},{14,12},{1,15},{3,1}... | collective-permute-start | bytes 1572872 | tf_op jit(solution)/shard_map/ppermute | solution.py:32
  13.5 6.1 %shard_map.140 = (bf16[16,64,256]{2,1,0:T(8,128)(2,1)}, bf16[8,64,128]{2,1,0:T(8,128)(2,1)S(1)}, f32[64,64]{1,0:T(8,128)S(1)}, f32[8,128]{1,0:T(8,128)S(1)}) custom-call(s32[16,256]{1,0:T(8,128)} %order_h, bf16[16,64,256]{2,1,0:T(8,128)(2,1)} %basis_h.1, bf16[16,64,256]{2,1,0:T(8,128)(2,1)} %direction.1, bf16[16,64,64]{2,1,0:T(8,128)(2,1)} %refs_3_.1, ...), custom_call_target="tpu_custom_call" | custom-call | flops 268435456 | bytes 6291456 | tf_op jit(solution)/shard_map/pallas_call | solution.py:423
  19.6 6.5 %shard_map.141 = (bf16[4,3072,256]{2,1,0:T(8,128)(2,1)S(1)}, f32[8,128]{1,0:T(8,128)S(1)}, bf16[48,256,128]{2,1,0:T(8,128)(2,1)S(1)}, f32[3,16,256]{2,1,0:T(8,128)S(1)}) custom-call(s32[16,12]{1,0:T(8,128)} %near_h.5, f32[8,128]{1,0:T(8,128)S(1)} %get-tuple-element.25._, bf16[3,16,256]{2,1,0:T(8,128)(2,1)} %bitcast.7, ...), custom_call_target="tpu_custom_call" | custom-call | flops 125829120 | bytes 50331648 | tf_op jit(solution)/shard_map/pallas_call | solution.py:452
  26.1 0.1 shard_map.142.refs_0_
  26.2 0.0 collective-permute-start.2
  26.2 1.1 %collective-permute-start.3 = (bf16[64,128]{1,0:T(8,128)(2,1)S(1)}, bf16[64,128]{1,0:T(8,128)(2,1)S(1)}, u32[]{:S(2)}, u32[]{:S(2)}) collective-permute-start(bf16[64,128]{1,0:T(8,128)(2,1)S(1)} %shard_map.142.refs_0_), channel_id=1, source_target_pairs={{0,8},{4,12},{8,0},{12,4},{1,9},{5,13},{9,1},{13,5},{2,10},{6,14},... | collective-permute-start | bytes 49160 | tf_op jit(solution)/shard_map/ppermute | solution.py:32
  27.3 2.7 %collective-permute-start.4 = (bf16[64,128]{1,0:T(8,128)(2,1)S(1)}, bf16[64,128]{1,0:T(8,128)(2,1)S(1)}, u32[]{:S(2)}, u32[]{:S(2)}) collective-permute-start(bf16[64,128]{1,0:T(8,128)(2,1)S(1)} %shard_map.142.refs_0_), channel_id=1, source_target_pairs={{0,12},{4,0},{8,4},{12,8},{1,13},{5,1},{9,5},{13,9},{2,14},{6,2},{... | collective-permute-start | bytes 49160 | tf_op jit(solution)/shard_map/ppermute | solution.py:32
  30.0 5.5 %shard_map.144 = (bf16[4,3072,256]{2,1,0:T(8,128)(2,1)S(1)}, f32[8,128]{1,0:T(8,128)}) custom-call(s32[16,12]{1,0:T(8,128)} %near_h.5, f32[8,128]{1,0:T(8,128)S(1)} %get-tuple-element.26._, f32[3,16,256]{2,1,0:T(8,128)S(1)} %get-tuple-element.29.refs_0_, bf16[48,256,128]{2,1,0:T(8,128)(2,1)S(1)} %get-tuple-element.30.refs_1_), custom_call_target="tpu_custom_call" | custom-call | flops 125829120 | bytes 3145728 | tf_op jit(solution)/shard_map/pallas_call | solution.py:452
  35.6 0.1 collective-permute-start.8
  35.7 0.5 collective-permute-start.10
  36.2 0.1 collective-permute-start.7
  36.3 2.0 %collective-permute-start.11 = (bf16[8,64,128]{2,1,0:T(8,128)(2,1)S(1)}, bf16[8,64,128]{2,1,0:T(8,128)(2,1)S(1)}, u32[]{:S(2)}, u32[]{:S(2)}) collective-permute-start(bf16[8,64,128]{2,1,0:T(8,128)(2,1)S(1)} %get-tuple-element.38), channel_id=1, source_target_pairs={{0,2},{2,4},{4,6},{6,8},{8,10},{10,12},{12,14},{14,0},{1,3},{3,5},... | collective-permute-start | bytes 393224 | tf_op jit(solution)/shard_map/ppermute | solution.py:32
  38.3 2.7 %collective-permute-start.12 = (bf16[8,64,128]{2,1,0:T(8,128)(2,1)S(1)}, bf16[8,64,128]{2,1,0:T(8,128)(2,1)S(1)}, u32[]{:S(2)}, u32[]{:S(2)}) collective-permute-start(bf16[8,64,128]{2,1,0:T(8,128)(2,1)S(1)} %get-tuple-element.38), channel_id=1, source_target_pairs={{0,14},{2,0},{4,2},{6,4},{8,6},{10,8},{12,10},{14,12},{1,15},{3,1}... | collective-permute-start | bytes 393224 | tf_op jit(solution)/shard_map/ppermute | solution.py:32
  41.0 0.0 copy-start.1
  41.0 0.0 copy-start
  41.0 0.0 copy-start.4
  41.1 5.0 %shard_map.145 = (f32[8,64,256]{2,1,0:T(8,128)S(1)}, bf16[8,64,256]{2,1,0:T(8,128)(2,1)S(1)}, f32[8,128]{1,0:T(8,128)}) custom-call(s32[16,12]{1,0:T(8,128)} %near_h.5, bf16[16,64,256]{2,1,0:T(8,128)(2,1)S(1)} %collective-permute-done.6.refs_0_, bf16[16,64,256]{2,1,0:T(8,128)(2,1)S(1)} %collective-permute-done.7.refs_1_, bf16[16,64,256]{2,1,0:T(8,128)(2,1)} %direction.1, ...), custom_call_target="tpu_custom_call" | custom-call | flops 1048576 | bytes 1048576 | tf_op jit(solution)/shard_map/pallas_call | solution.py:498
  46.1 0.0 copy-start.2
  46.1 0.0 copy-start.5
  46.1 0.5 collective-permute-done.12.after
  46.7 0.2 shard_map.146
  46.9 0.1 collective-permute-start.13
  46.9 0.3 collective-permute-start.5
  47.3 1.5 %shard_map.147.refs_2_ = f32[16,64,64]{2,1,0:T(8,128)S(1)} custom-call(bf16[32,64,64]{2,1,0:T(8,128)(2,1)S(1)} %get-tuple-element.39.window, bf16[16,8,64,64]{3,2,1,0:T(8,128)(2,1)S(1)} %copy-done.1, s32[8,16]{1,0:T(8,128)} %bitcast.4), custom_call_target="tpu_custom_call" | custom-call | flops 67108864 | bytes 4194304 | tf_op jit(solution)/shard_map/pallas_call | solution.py:532
  48.8 2.6 %collective-permute-done.5.refs_1_ = bf16[4,64,128]{2,1,0:T(8,128)(2,1)S(1)} collective-permute-done((bf16[4,64,128]{2,1,0:T(8,128)(2,1)S(1)}, bf16[4,64,128]{2,1,0:T(8,128)(2,1)S(1)}, u32[]{:S(2)}, u32[]{:S(2)}) %collective-permute-start.5) | collective-permute-done | bytes 65568 | tf_op jit(solution)/shard_map/ppermute | solution.py:32
  51.5 2.6 %shard_map.148.base = f32[16,64,256]{2,1,0:T(8,128)S(1)} custom-call(bf16[4,64,128]{2,1,0:T(8,128)(2,1)S(1)} %shard_map.143.refs_0_, bf16[4,64,128]{2,1,0:T(8,128)(2,1)S(1)} %collective-permute-done.5.refs_1_, f32[16,64,64]{2,1,0:T(8,128)S(1)} %shard_map.147.refs_2_, bf16[16,64,64]{2,1,0:T(8,128)(2,1)S(1)} %copy-done.3, bf16[16,64,256]{2,1,0:T(8,128)(2,1)S(1)} %copy-done.4, ...), custom_call_target="tpu_custom_call" | custom-call | flops 41943040 | bytes 4194304 | tf_op jit(solution)/shard_map/pallas_call | solution.py:547
  54.1 1.2 %shard_map.149 = (f32[16,64,256]{2,1,0:T(8,128)}, f32[16,64,256]{2,1,0:T(8,128)S(1)}, f32[8,8,128]{2,1,0:T(8,128)S(1)}) custom-call(f32[1,64]{1,0:T(1,128)S(1)} %bitcast.3, f32[16,64,256]{2,1,0:T(8,128)S(1)} %shard_map.148.base, f32[8,64,256]{2,1,0:T(8,128)S(1)} %get-tuple-element.41.kept, bf16[8,64,256]{2,1,0:T(8,128)(2,1)S(1)} %collective-permute-done.13.received, ...), custom_call_target="tpu_custom_call" | custom-call | flops 4194304 | bytes 5242880 | tf_op jit(solution)/shard_map/pallas_call | solution.py:562
  55.3 10.4 %all_to_all.5.norms = f32[8,8,128]{2,1,0:T(8,128)S(1)} all-to-all(f32[8,8,128]{2,1,0:T(8,128)S(1)} %get-tuple-element.44), channel_id=1, replica_groups=mesh['groups'=2,'blk'=4,'leaf'=2,'sample'=2] {'blk','leaf'}, dimensions={0} | all-to-all | bytes 65536 | tf_op jit(solution)/shard_map/all_to_all | solution.py:572
  65.6 0.9 %shard_map.150 = bf16[16,64,256]{2,1,0:T(8,128)(2,1)} custom-call(f32[8,8,128]{2,1,0:T(8,128)S(1)} %all_to_all.5.norms, f32[16,64,256]{2,1,0:T(8,128)S(1)} %get-tuple-element.45.updated, bf16[16,64,256]{2,1,0:T(8,128)(2,1)S(1)} %copy-done), custom_call_target="tpu_custom_call" | custom-call | flops 1048576 | bytes 2097152 | tf_op jit(solution)/shard_map/pallas_call | solution.py:573
  (20 shorter events, 0.1 us)
Async XLA Ops:
  0.6 8.0 %collective-permute-start = (bf16[3,16,256]{2,1,0:T(8,128)(2,1)}, bf16[3,16,256]{2,1,0:T(8,128)(2,1)S(1)}, u32[]{:S(2)}, u32[]{:S(2)}) collective-permute-start(bf16[3,16,256]{2,1,0:T(8,128)(2,1)} %bitcast.5), channel_id=1, source_target_pairs={{0,2},{2,4},{4,6},{6,8},{8,10},{10,12},{12,14},{14,0},{1,3},{3,5},... | collective-permute-start | bytes 73736 | tf_op jit(solution)/shard_map/ppermute | solution.py:32
  3.6 5.1 %collective-permute-start.1 = (bf16[3,16,256]{2,1,0:T(8,128)(2,1)}, bf16[3,16,256]{2,1,0:T(8,128)(2,1)S(1)}, u32[]{:S(2)}, u32[]{:S(2)}) collective-permute-start(bf16[3,16,256]{2,1,0:T(8,128)(2,1)} %bitcast.6), channel_id=1, source_target_pairs={{0,14},{2,0},{4,2},{6,4},{8,6},{10,8},{12,10},{14,12},{1,15},{3,1}... | collective-permute-start | bytes 73736 | tf_op jit(solution)/shard_map/ppermute | solution.py:32
  8.7 27.0 %collective-permute-start.9 = (bf16[16,64,256]{2,1,0:T(8,128)(2,1)}, bf16[16,64,256]{2,1,0:T(8,128)(2,1)S(1)}, u32[]{:S(2)}, u32[]{:S(2)}) collective-permute-start(bf16[16,64,256]{2,1,0:T(8,128)(2,1)} %direction.1), channel_id=1, source_target_pairs={{0,14},{2,0},{4,2},{6,4},{8,6},{10,8},{12,10},{14,12},{1,15},{3,1}... | collective-permute-start | bytes 1572872 | tf_op jit(solution)/shard_map/ppermute | solution.py:32
  13.5 22.7 %collective-permute-start.6 = (bf16[16,64,256]{2,1,0:T(8,128)(2,1)}, bf16[16,64,256]{2,1,0:T(8,128)(2,1)S(1)}, u32[]{:S(2)}, u32[]{:S(2)}) collective-permute-start(bf16[16,64,256]{2,1,0:T(8,128)(2,1)} %direction.1), channel_id=1, source_target_pairs={{0,2},{2,4},{4,6},{6,8},{8,10},{10,12},{12,14},{14,0},{1,3},{3,5},... | collective-permute-start | bytes 1572872 | tf_op jit(solution)/shard_map/ppermute | solution.py:32
  26.2 9.4 %collective-permute-start.2 = (bf16[64,128]{1,0:T(8,128)(2,1)S(1)}, bf16[64,128]{1,0:T(8,128)(2,1)S(1)}, u32[]{:S(2)}, u32[]{:S(2)}) collective-permute-start(bf16[64,128]{1,0:T(8,128)(2,1)S(1)} %shard_map.142.refs_0_), channel_id=1, source_target_pairs={{0,4},{4,8},{8,12},{12,0},{1,5},{5,9},{9,13},{13,1},{2,6},{6,10},{... | collective-permute-start | bytes 49160 | tf_op jit(solution)/shard_map/ppermute | solution.py:32
  26.2 9.4 %collective-permute-start.3 = (bf16[64,128]{1,0:T(8,128)(2,1)S(1)}, bf16[64,128]{1,0:T(8,128)(2,1)S(1)}, u32[]{:S(2)}, u32[]{:S(2)}) collective-permute-start(bf16[64,128]{1,0:T(8,128)(2,1)S(1)} %shard_map.142.refs_0_), channel_id=1, source_target_pairs={{0,8},{4,12},{8,0},{12,4},{1,9},{5,13},{9,1},{13,5},{2,10},{6,14},... | collective-permute-start | bytes 49160 | tf_op jit(solution)/shard_map/ppermute | solution.py:32
  27.3 8.3 %collective-permute-start.4 = (bf16[64,128]{1,0:T(8,128)(2,1)S(1)}, bf16[64,128]{1,0:T(8,128)(2,1)S(1)}, u32[]{:S(2)}, u32[]{:S(2)}) collective-permute-start(bf16[64,128]{1,0:T(8,128)(2,1)S(1)} %shard_map.142.refs_0_), channel_id=1, source_target_pairs={{0,12},{4,0},{8,4},{12,8},{1,13},{5,1},{9,5},{13,9},{2,14},{6,2},{... | collective-permute-start | bytes 49160 | tf_op jit(solution)/shard_map/ppermute | solution.py:32
  35.6 5.4 %collective-permute-start.8 = (bf16[16,64,256]{2,1,0:T(8,128)(2,1)}, bf16[16,64,256]{2,1,0:T(8,128)(2,1)S(1)}, u32[]{:S(2)}, u32[]{:S(2)}) collective-permute-start(bf16[16,64,256]{2,1,0:T(8,128)(2,1)} %direction.1), channel_id=1, source_target_pairs={{0,1},{1,0},{2,3},{3,2},{4,5},{5,4},{6,7},{7,6},{8,9},{9,8},{10,11... | collective-permute-start | bytes 1572872 | tf_op jit(solution)/shard_map/ppermute | solution.py:36
  35.7 5.3 %collective-permute-start.10 = (bf16[16,64,256]{2,1,0:T(8,128)(2,1)S(1)}, bf16[16,64,256]{2,1,0:T(8,128)(2,1)S(1)}, u32[]{:S(2)}, u32[]{:S(2)}) collective-permute-start(bf16[16,64,256]{2,1,0:T(8,128)(2,1)S(1)} %collective-permute-done.9.refs_4_), channel_id=1, source_target_pairs={{0,1},{1,0},{2,3},{3,2},{4,5},{5,4},{6,7},{7,6},{8,9},{9,8},{10,11... | collective-permute-start | bytes 1572872 | tf_op jit(solution)/shard_map/ppermute | solution.py:36
  36.2 4.8 %collective-permute-start.7 = (bf16[16,64,256]{2,1,0:T(8,128)(2,1)S(1)}, bf16[16,64,256]{2,1,0:T(8,128)(2,1)S(1)}, u32[]{:S(2)}, u32[]{:S(2)}) collective-permute-start(bf16[16,64,256]{2,1,0:T(8,128)(2,1)S(1)} %collective-permute-done.6.refs_0_), channel_id=1, source_target_pairs={{0,1},{1,0},{2,3},{3,2},{4,5},{5,4},{6,7},{7,6},{8,9},{9,8},{10,11... | collective-permute-start | bytes 1572872 | tf_op jit(solution)/shard_map/ppermute | solution.py:36
  36.3 9.9 %collective-permute-start.11 = (bf16[8,64,128]{2,1,0:T(8,128)(2,1)S(1)}, bf16[8,64,128]{2,1,0:T(8,128)(2,1)S(1)}, u32[]{:S(2)}, u32[]{:S(2)}) collective-permute-start(bf16[8,64,128]{2,1,0:T(8,128)(2,1)S(1)} %get-tuple-element.38), channel_id=1, source_target_pairs={{0,2},{2,4},{4,6},{6,8},{8,10},{10,12},{12,14},{14,0},{1,3},{3,5},... | collective-permute-start | bytes 393224 | tf_op jit(solution)/shard_map/ppermute | solution.py:32
  38.3 8.4 %collective-permute-start.12 = (bf16[8,64,128]{2,1,0:T(8,128)(2,1)S(1)}, bf16[8,64,128]{2,1,0:T(8,128)(2,1)S(1)}, u32[]{:S(2)}, u32[]{:S(2)}) collective-permute-start(bf16[8,64,128]{2,1,0:T(8,128)(2,1)S(1)} %get-tuple-element.38), channel_id=1, source_target_pairs={{0,14},{2,0},{4,2},{6,4},{8,6},{10,8},{12,10},{14,12},{1,15},{3,1}... | collective-permute-start | bytes 393224 | tf_op jit(solution)/shard_map/ppermute | solution.py:32
  41.0 6.3 %copy-start.1 = (bf16[16,8,64,64]{3,2,1,0:T(8,128)(2,1)S(1)}, bf16[16,8,64,64]{3,2,1,0:T(8,128)(2,1)}, u32[]{:S(2)}) copy-start(bf16[16,8,64,64]{3,2,1,0:T(8,128)(2,1)} %coupling.1) | copy-start | bytes 3145732
  41.0 10.4 %copy-start = (bf16[16,64,256]{2,1,0:T(8,128)(2,1)S(1)}, bf16[16,64,256]{2,1,0:T(8,128)(2,1)}, u32[]{:S(2)}) copy-start(bf16[16,64,256]{2,1,0:T(8,128)(2,1)} %direction.1) | copy-start | bytes 1572868
  41.0 10.4 %copy-start.3 = (bf16[16,64,64]{2,1,0:T(8,128)(2,1)S(1)}, bf16[16,64,64]{2,1,0:T(8,128)(2,1)}, u32[]{:S(2)}) copy-start(bf16[16,64,64]{2,1,0:T(8,128)(2,1)} %refs_3_.1) | copy-start | bytes 393220
  41.0 10.4 %copy-start.4 = (bf16[16,64,256]{2,1,0:T(8,128)(2,1)S(1)}, bf16[16,64,256]{2,1,0:T(8,128)(2,1)}, u32[]{:S(2)}) copy-start(bf16[16,64,256]{2,1,0:T(8,128)(2,1)} %get-tuple-element.40.refs_4_) | copy-start | bytes 1572868
  46.1 8.0 %copy-start.2 = (f32[16,64,256]{2,1,0:T(8,128)S(1)}, f32[16,64,256]{2,1,0:T(8,128)}, u32[]{:S(2)}) copy-start(f32[16,64,256]{2,1,0:T(8,128)} %residual.1) | copy-start | bytes 3145732
  46.1 8.0 %copy-start.5 = (f32[64]{0:T(128)S(1)}, f32[64]{0:T(128)}, u32[]{:S(2)}) copy-start(f32[64]{0:T(128)} %param.15) | copy-start | bytes 772
  46.9 7.2 %collective-permute-start.13 = (bf16[8,64,256]{2,1,0:T(8,128)(2,1)S(1)}, bf16[8,64,256]{2,1,0:T(8,128)(2,1)S(1)}, u32[]{:S(2)}, u32[]{:S(2)}) collective-permute-start(bf16[8,64,256]{2,1,0:T(8,128)(2,1)S(1)} %get-tuple-element.42), channel_id=1, source_target_pairs={{0,1},{1,0},{2,3},{3,2},{4,5},{5,4},{6,7},{7,6},{8,9},{9,8},{10,11... | collective-permute-start | bytes 786440 | tf_op jit(solution)/shard_map/ppermute | solution.py:36
  46.9 4.5 %collective-permute-start.5 = (bf16[4,64,128]{2,1,0:T(8,128)(2,1)S(1)}, bf16[4,64,128]{2,1,0:T(8,128)(2,1)S(1)}, u32[]{:S(2)}, u32[]{:S(2)}) collective-permute-start(bf16[4,64,128]{2,1,0:T(8,128)(2,1)S(1)} %shard_map.143.refs_0_), channel_id=1, source_target_pairs={{0,2},{2,0},{1,3},{3,1},{4,6},{6,4},{5,7},{7,5},{8,10},{10,8},{9,1... | collective-permute-start | bytes 196616 | tf_op jit(solution)/shard_map/ppermute | solution.py:32

commit v11 on v10

--- a/solution.py
+++ b/solution.py
@@ -227,6 +227,16 @@
         together[i] = term[...]
 
 
+def top_kernel(_, given, *refs):
+    terms, (tops, sent) = refs[:-2], refs[-2:]
+    rank = tops.shape[2]
+    total = terms[0][...].astype(F32)
+    for term in terms[1:]:
+        total = total + term[...].astype(F32)
+    tops[...] = (total[:, :, :rank] + total[:, :, rank:]).astype(tops.dtype)
+    sent[...] = given[...]
+
+
 def window_kernel(given, before, after, window, sent):
     sent[...] = given[...]
     rows, _, lanes = before.shape
@@ -257,9 +267,8 @@
 
 
 def down_kernel(*refs):
-    terms, refs = refs[: lax.axis_size("leaf")], refs[lax.axis_size("leaf") :]
-    part, leaf_transfer, natural, direction = refs[:4]
-    sources, base, targets, (tops, sems) = refs[4:7], refs[7], refs[8:11], refs[11:]
+    tops, part, leaf_transfer, natural, direction = refs[:5]
+    sources, base, targets, sems = refs[5:8], refs[8], refs[9:12], refs[12]
     top_list, top_coupling, node_transfer = targets
     copies = [
         pltpu.make_async_copy(source, target, sems.at[i])
@@ -271,10 +280,6 @@
     rank = natural.shape[1]
     clusters = lax.axis_size("blk")
     here = lax.axis_index("blk")
-    together = terms[0][...].astype(F32)
-    for term in terms[1:]:
-        together = together + term[...].astype(F32)
-    tops[...] = (together[:, :, :rank] + together[:, :, rank:]).astype(tops.dtype)
     for copy in copies:
         copy.wait()
     incoming = jnp.zeros((samples, rank), F32)
@@ -542,6 +547,15 @@
         ],
         vmem=8,
     )(coef_window, coupling, *in_hbm(coupling_list.T))
+    tops, given = call(
+        top_kernel,
+        (shape((blk_count, samples, rank), BF), shape((half, samples, points), BF)),
+        MIB,
+        MIB,
+        in_specs=[anywhere] + [vmem] * (2 + len(terms)),
+        out_specs=(vmem, vmem),
+        vmem=8,
+    )(part, given, together, *terms)
     arrays = (top_list, top_coupling, node_transfer)
     spaces = (pltpu.SMEM, pltpu.VMEM, pltpu.VMEM)
     base = call(
@@ -549,12 +563,12 @@
         shape((leaves, samples, points), F32),
         2 * leaves * samples * rank * (points + rank),
         4 * MIB,
-        in_specs=[vmem] * (4 + leaf_count) + [hbm] * 3,
+        in_specs=[vmem] * 5 + [hbm] * 3,
         out_specs=vmem,
         scratch_shapes=[space(array.shape, array.dtype) for space, array in zip(spaces, arrays)]
-        + [pltpu.VMEM((blk_count, samples, rank), BF), pltpu.SemaphoreType.DMA((3,))],
+        + [pltpu.SemaphoreType.DMA((3,))],
         vmem=10,
-    )(together, *terms, part, leaf_transfer, natural, direction, *in_hbm(*arrays))
+    )(tops, part, leaf_transfer, natural, direction, *in_hbm(*arrays))
     received = partner(given)
 
     devices = blk_count * leaf_count

time: 67 us -> 64.1 us (0.957)
  waiting for transfers between devices: 5.12 us -> 3.11 us
  blocking collectives: 10.4 us -> 9.65 us
    ppermute x10, waiting for transfers between devices: 5.11 us -> 3.1 us  [shifted(): lax.ppermute(array, axis, [(i, (i + by) % count) for i in range(count)])]
    all_to_all x1, blocking collectives: 10.4 us -> 9.65 us  [on_device(): norms = lax.all_to_all(norms, RING, 0, 0)]
  transfers between devices with their start and end apart: 14 -> 14, of which waited for: 3 -> 2; matrix products, arithmetic and copies ran while one was open for 0% -> 0% of each run, Pallas kernels for 41% -> 43%
where the time goes in v11:
time: 64.1 us; the launch traced here: 63.7 us
  Pallas kernels  29.8 us (46%)
  starting transfers between devices  20.2 us (32%)
  blocking collectives  9.65 us (15%)
  waiting for transfers between devices  3.11 us (5%)
  between operations  0.9 us (1%)
    ppermute x10, starting transfers between devices, shifted(): lax.ppermute(array, axis, [(i, (i + by) % count) for i in range(count)])  19.5 us
    pallas_call x2, Pallas kernels, make_tiles(): call(functools.partial(tile_kernel, start), outs, 40 * count * entries *...  12 us
    all_to_all x1, blocking collectives, on_device(): norms = lax.all_to_all(norms, RING, 0, 0)  9.65 us
    pallas_call x1, Pallas kernels, on_device(): call(up_kernel, (pltpu.HBM((leaves, rank, points), BF), shape((leaves //...  6.14 us
    pallas_call x1, Pallas kernels, on_device(): call(near_kernel, (shape((half, samples, points), F32), shape((half, samp...  5.02 us
    ppermute x10, waiting for transfers between devices, shifted(): lax.ppermute(array, axis, [(i, (i + by) % count) for i in range(count)])  3.1 us
    pallas_call x1, Pallas kernels, on_device(): call(down_kernel, shape((leaves, samples, points), F32), 2 * leaves * sam...  2.58 us
    pallas_call x1, Pallas kernels, on_device(): call(couple_kernel, shape((leaves, samples, rank), F32), 2 * leaves * sam...  1.52 us
  transfers between devices with their start and end apart: 14, of which 2 were waited for; matrix products, arithmetic and copies ran while one was open for 0% of the time, Pallas kernels for 43%

profile of v11, /device:TPU:0, one launch (start us, length us, event | category | flops | bytes accessed | tf_op | source)
XLA Modules:
  0.0 63.7 jit_solution(3305479798731464191)
XLA Ops:
  0.6 3.0 %collective-permute-start = (bf16[3,16,256]{2,1,0:T(8,128)(2,1)}, bf16[3,16,256]{2,1,0:T(8,128)(2,1)S(1)}, u32[]{:S(2)}, u32[]{:S(2)}) collective-permute-start(bf16[3,16,256]{2,1,0:T(8,128)(2,1)} %bitcast.5), channel_id=1, source_target_pairs={{0,2},{2,4},{4,6},{6,8},{8,10},{10,12},{12,14},{14,0},{1,3},{3,5},... | collective-permute-start | bytes 73736 | tf_op jit(solution)/shard_map/ppermute | solution.py:32
  3.6 3.1 %collective-permute-start.1 = (bf16[3,16,256]{2,1,0:T(8,128)(2,1)}, bf16[3,16,256]{2,1,0:T(8,128)(2,1)S(1)}, u32[]{:S(2)}, u32[]{:S(2)}) collective-permute-start(bf16[3,16,256]{2,1,0:T(8,128)(2,1)} %bitcast.6), channel_id=1, source_target_pairs={{0,14},{2,0},{4,2},{6,4},{8,6},{10,8},{12,10},{14,12},{1,15},{3,1}... | collective-permute-start | bytes 73736 | tf_op jit(solution)/shard_map/ppermute | solution.py:32
  6.7 2.0 %collective-permute-done.refs_1_ = bf16[3,16,256]{2,1,0:T(8,128)(2,1)S(1)} collective-permute-done((bf16[3,16,256]{2,1,0:T(8,128)(2,1)}, bf16[3,16,256]{2,1,0:T(8,128)(2,1)S(1)}, u32[]{:S(2)}, u32[]{:S(2)}) %collective-permute-start) | collective-permute-done | bytes 24608 | tf_op jit(solution)/shard_map/ppermute | solution.py:32
  8.7 4.8 %collective-permute-start.8 = (bf16[16,64,256]{2,1,0:T(8,128)(2,1)}, bf16[16,64,256]{2,1,0:T(8,128)(2,1)S(1)}, u32[]{:S(2)}, u32[]{:S(2)}) collective-permute-start(bf16[16,64,256]{2,1,0:T(8,128)(2,1)} %direction.1), channel_id=1, source_target_pairs={{0,14},{2,0},{4,2},{6,4},{8,6},{10,8},{12,10},{14,12},{1,15},{3,1}... | collective-permute-start | bytes 1572872 | tf_op jit(solution)/shard_map/ppermute | solution.py:32
  13.5 6.1 %shard_map.140 = (bf16[16,64,256]{2,1,0:T(8,128)(2,1)}, bf16[8,64,128]{2,1,0:T(8,128)(2,1)S(1)}, f32[64,64]{1,0:T(8,128)S(1)}, f32[8,128]{1,0:T(8,128)S(1)}) custom-call(s32[16,256]{1,0:T(8,128)} %order_h, bf16[16,64,256]{2,1,0:T(8,128)(2,1)} %basis_h.1, bf16[16,64,256]{2,1,0:T(8,128)(2,1)} %direction.1, bf16[16,64,64]{2,1,0:T(8,128)(2,1)} %refs_2_.3, ...), custom_call_target="tpu_custom_call" | custom-call | flops 268435456 | bytes 6291456 | tf_op jit(solution)/shard_map/pallas_call | solution.py:428
  19.6 6.5 %shard_map.141 = (bf16[4,3072,256]{2,1,0:T(8,128)(2,1)S(1)}, f32[8,128]{1,0:T(8,128)S(1)}, bf16[48,256,128]{2,1,0:T(8,128)(2,1)S(1)}, f32[3,16,256]{2,1,0:T(8,128)S(1)}) custom-call(s32[16,12]{1,0:T(8,128)} %near_h.5, f32[8,128]{1,0:T(8,128)S(1)} %get-tuple-element.28._, bf16[3,16,256]{2,1,0:T(8,128)(2,1)} %bitcast.7, ...), custom_call_target="tpu_custom_call" | custom-call | flops 125829120 | bytes 50331648 | tf_op jit(solution)/shard_map/pallas_call | solution.py:457
  26.1 0.1 shard_map.143.refs_0_
  26.2 0.0 collective-permute-start.3
  26.2 1.1 %collective-permute-start.4 = (bf16[64,128]{1,0:T(8,128)(2,1)S(1)}, bf16[64,128]{1,0:T(8,128)(2,1)S(1)}, u32[]{:S(2)}, u32[]{:S(2)}) collective-permute-start(bf16[64,128]{1,0:T(8,128)(2,1)S(1)} %shard_map.143.refs_0_), channel_id=1, source_target_pairs={{0,8},{4,12},{8,0},{12,4},{1,9},{5,13},{9,1},{13,5},{2,10},{6,14},... | collective-permute-start | bytes 49160 | tf_op jit(solution)/shard_map/ppermute | solution.py:32
  27.3 2.7 %collective-permute-start.5 = (bf16[64,128]{1,0:T(8,128)(2,1)S(1)}, bf16[64,128]{1,0:T(8,128)(2,1)S(1)}, u32[]{:S(2)}, u32[]{:S(2)}) collective-permute-start(bf16[64,128]{1,0:T(8,128)(2,1)S(1)} %shard_map.143.refs_0_), channel_id=1, source_target_pairs={{0,12},{4,0},{8,4},{12,8},{1,13},{5,1},{9,5},{13,9},{2,14},{6,2},{... | collective-permute-start | bytes 49160 | tf_op jit(solution)/shard_map/ppermute | solution.py:32
  30.0 5.5 %shard_map.142 = (bf16[4,3072,256]{2,1,0:T(8,128)(2,1)S(1)}, f32[8,128]{1,0:T(8,128)}) custom-call(s32[16,12]{1,0:T(8,128)} %near_h.5, f32[8,128]{1,0:T(8,128)S(1)} %get-tuple-element.29._, f32[3,16,256]{2,1,0:T(8,128)S(1)} %get-tuple-element.30.refs_0_, bf16[48,256,128]{2,1,0:T(8,128)(2,1)S(1)} %get-tuple-element.31.refs_1_), custom_call_target="tpu_custom_call" | custom-call | flops 125829120 | bytes 3145728 | tf_op jit(solution)/shard_map/pallas_call | solution.py:457
  35.6 0.1 collective-permute-start.7
  35.7 0.5 collective-permute-start.9
  36.2 0.1 collective-permute-start.6
  36.3 2.0 %collective-permute-start.10 = (bf16[8,64,128]{2,1,0:T(8,128)(2,1)S(1)}, bf16[8,64,128]{2,1,0:T(8,128)(2,1)S(1)}, u32[]{:S(2)}, u32[]{:S(2)}) collective-permute-start(bf16[8,64,128]{2,1,0:T(8,128)(2,1)S(1)} %get-tuple-element.40), channel_id=1, source_target_pairs={{0,2},{2,4},{4,6},{6,8},{8,10},{10,12},{12,14},{14,0},{1,3},{3,5},... | collective-permute-start | bytes 393224 | tf_op jit(solution)/shard_map/ppermute | solution.py:32
  38.3 2.7 %collective-permute-start.11 = (bf16[8,64,128]{2,1,0:T(8,128)(2,1)S(1)}, bf16[8,64,128]{2,1,0:T(8,128)(2,1)S(1)}, u32[]{:S(2)}, u32[]{:S(2)}) collective-permute-start(bf16[8,64,128]{2,1,0:T(8,128)(2,1)S(1)} %get-tuple-element.40), channel_id=1, source_target_pairs={{0,14},{2,0},{4,2},{6,4},{8,6},{10,8},{12,10},{14,12},{1,15},{3,1}... | collective-permute-start | bytes 393224 | tf_op jit(solution)/shard_map/ppermute | solution.py:32
  41.0 0.1 collective-permute-start.12
  41.1 0.0 copy-start.1
  41.1 0.0 copy-start
  41.1 0.0 copy-start.3
  41.1 0.0 copy-start.4
  41.2 5.0 %shard_map.144 = (f32[8,64,256]{2,1,0:T(8,128)S(1)}, bf16[8,64,256]{2,1,0:T(8,128)(2,1)S(1)}, f32[8,128]{1,0:T(8,128)}) custom-call(s32[16,12]{1,0:T(8,128)} %near_h.5, bf16[16,64,256]{2,1,0:T(8,128)(2,1)S(1)} %collective-permute-done.2.refs_0_, bf16[16,64,256]{2,1,0:T(8,128)(2,1)S(1)} %collective-permute-done.6.refs_1_, bf16[16,64,256]{2,1,0:T(8,128)(2,1)} %direction.1, ...), custom_call_target="tpu_custom_call" | custom-call | flops 1048576 | bytes 1048576 | tf_op jit(solution)/shard_map/pallas_call | solution.py:503
  46.2 0.0 copy-start.5
  46.2 1.1 %collective-permute-done.11.after = bf16[8,64,128]{2,1,0:T(8,128)(2,1)S(1)} collective-permute-done((bf16[8,64,128]{2,1,0:T(8,128)(2,1)S(1)}, bf16[8,64,128]{2,1,0:T(8,128)(2,1)S(1)}, u32[]{:S(2)}, u32[]{:S(2)}) %collective-permute-start.11) | collective-permute-done | bytes 131104 | tf_op jit(solution)/shard_map/ppermute | solution.py:32
  47.4 0.2 shard_map.145
  47.6 1.5 %shard_map.146._.refs_1_ = f32[16,64,64]{2,1,0:T(8,128)S(1)} custom-call(bf16[32,64,64]{2,1,0:T(8,128)(2,1)S(1)} %get-tuple-element.41.window, bf16[16,8,64,64]{3,2,1,0:T(8,128)(2,1)S(1)} %copy-done.1, s32[8,16]{1,0:T(8,128)} %bitcast.4), custom_call_target="tpu_custom_call" | custom-call | flops 67108864 | bytes 4194304 | tf_op jit(solution)/shard_map/pallas_call | solution.py:537
  49.1 0.1 shard_map.148
  49.2 0.1 collective-permute-start.13
  49.3 2.6 %shard_map.149.base = f32[16,64,256]{2,1,0:T(8,128)S(1)} custom-call(bf16[4,64,64]{2,1,0:T(8,128)(2,1)S(1)} %get-tuple-element.43.refs_0_, f32[16,64,64]{2,1,0:T(8,128)S(1)} %shard_map.146._.refs_1_, bf16[16,64,64]{2,1,0:T(8,128)(2,1)S(1)} %copy-done.3, bf16[16,64,256]{2,1,0:T(8,128)(2,1)S(1)} %copy-done.4, bf16[16,64,256]{2,1,0:T(8,128)(2,1)S(1)} %copy-done, ...), custom_call_target="tpu_custom_call" | custom-call | flops 41943040 | bytes 4194304 | tf_op jit(solution)/shard_map/pallas_call | solution.py:561
  51.9 1.2 %shard_map.150 = (f32[16,64,256]{2,1,0:T(8,128)}, f32[16,64,256]{2,1,0:T(8,128)S(1)}, f32[8,8,128]{2,1,0:T(8,128)S(1)}) custom-call(f32[1,64]{1,0:T(1,128)S(1)} %bitcast.3, f32[16,64,256]{2,1,0:T(8,128)S(1)} %shard_map.149.base, f32[8,64,256]{2,1,0:T(8,128)S(1)} %get-tuple-element.45.kept, bf16[8,64,256]{2,1,0:T(8,128)(2,1)S(1)} %collective-permute-done.13.received, ...), custom_call_target="tpu_custom_call" | custom-call | flops 4194304 | bytes 5242880 | tf_op jit(solution)/shard_map/pallas_call | solution.py:576
  53.1 9.7 %all_to_all.5.norms = f32[8,8,128]{2,1,0:T(8,128)S(1)} all-to-all(f32[8,8,128]{2,1,0:T(8,128)S(1)} %get-tuple-element.48), channel_id=1, replica_groups=mesh['groups'=2,'blk'=4,'leaf'=2,'sample'=2] {'blk','leaf'}, dimensions={0} | all-to-all | bytes 65536 | tf_op jit(solution)/shard_map/all_to_all | solution.py:586
  62.8 0.9 %shard_map.151 = bf16[16,64,256]{2,1,0:T(8,128)(2,1)} custom-call(f32[8,8,128]{2,1,0:T(8,128)S(1)} %all_to_all.5.norms, f32[16,64,256]{2,1,0:T(8,128)S(1)} %get-tuple-element.49.updated, bf16[16,64,256]{2,1,0:T(8,128)(2,1)S(1)} %copy-done), custom_call_target="tpu_custom_call" | custom-call | flops 1048576 | bytes 2097152 | tf_op jit(solution)/shard_map/pallas_call | solution.py:587
  (21 shorter events, 0.1 us)
Async XLA Ops:
  0.6 8.0 %collective-permute-start = (bf16[3,16,256]{2,1,0:T(8,128)(2,1)}, bf16[3,16,256]{2,1,0:T(8,128)(2,1)S(1)}, u32[]{:S(2)}, u32[]{:S(2)}) collective-permute-start(bf16[3,16,256]{2,1,0:T(8,128)(2,1)} %bitcast.5), channel_id=1, source_target_pairs={{0,2},{2,4},{4,6},{6,8},{8,10},{10,12},{12,14},{14,0},{1,3},{3,5},... | collective-permute-start | bytes 73736 | tf_op jit(solution)/shard_map/ppermute | solution.py:32
  3.6 5.1 %collective-permute-start.1 = (bf16[3,16,256]{2,1,0:T(8,128)(2,1)}, bf16[3,16,256]{2,1,0:T(8,128)(2,1)S(1)}, u32[]{:S(2)}, u32[]{:S(2)}) collective-permute-start(bf16[3,16,256]{2,1,0:T(8,128)(2,1)} %bitcast.6), channel_id=1, source_target_pairs={{0,14},{2,0},{4,2},{6,4},{8,6},{10,8},{12,10},{14,12},{1,15},{3,1}... | collective-permute-start | bytes 73736 | tf_op jit(solution)/shard_map/ppermute | solution.py:32
  8.7 27.0 %collective-permute-start.8 = (bf16[16,64,256]{2,1,0:T(8,128)(2,1)}, bf16[16,64,256]{2,1,0:T(8,128)(2,1)S(1)}, u32[]{:S(2)}, u32[]{:S(2)}) collective-permute-start(bf16[16,64,256]{2,1,0:T(8,128)(2,1)} %direction.1), channel_id=1, source_target_pairs={{0,14},{2,0},{4,2},{6,4},{8,6},{10,8},{12,10},{14,12},{1,15},{3,1}... | collective-permute-start | bytes 1572872 | tf_op jit(solution)/shard_map/ppermute | solution.py:32
  13.5 22.7 %collective-permute-start.2 = (bf16[16,64,256]{2,1,0:T(8,128)(2,1)}, bf16[16,64,256]{2,1,0:T(8,128)(2,1)S(1)}, u32[]{:S(2)}, u32[]{:S(2)}) collective-permute-start(bf16[16,64,256]{2,1,0:T(8,128)(2,1)} %direction.1), channel_id=1, source_target_pairs={{0,2},{2,4},{4,6},{6,8},{8,10},{10,12},{12,14},{14,0},{1,3},{3,5},... | collective-permute-start | bytes 1572872 | tf_op jit(solution)/shard_map/ppermute | solution.py:32
  26.2 9.4 %collective-permute-start.3 = (bf16[64,128]{1,0:T(8,128)(2,1)S(1)}, bf16[64,128]{1,0:T(8,128)(2,1)S(1)}, u32[]{:S(2)}, u32[]{:S(2)}) collective-permute-start(bf16[64,128]{1,0:T(8,128)(2,1)S(1)} %shard_map.143.refs_0_), channel_id=1, source_target_pairs={{0,4},{4,8},{8,12},{12,0},{1,5},{5,9},{9,13},{13,1},{2,6},{6,10},{... | collective-permute-start | bytes 49160 | tf_op jit(solution)/shard_map/ppermute | solution.py:32
  26.2 9.4 %collective-permute-start.4 = (bf16[64,128]{1,0:T(8,128)(2,1)S(1)}, bf16[64,128]{1,0:T(8,128)(2,1)S(1)}, u32[]{:S(2)}, u32[]{:S(2)}) collective-permute-start(bf16[64,128]{1,0:T(8,128)(2,1)S(1)} %shard_map.143.refs_0_), channel_id=1, source_target_pairs={{0,8},{4,12},{8,0},{12,4},{1,9},{5,13},{9,1},{13,5},{2,10},{6,14},... | collective-permute-start | bytes 49160 | tf_op jit(solution)/shard_map/ppermute | solution.py:32
  27.3 8.3 %collective-permute-start.5 = (bf16[64,128]{1,0:T(8,128)(2,1)S(1)}, bf16[64,128]{1,0:T(8,128)(2,1)S(1)}, u32[]{:S(2)}, u32[]{:S(2)}) collective-permute-start(bf16[64,128]{1,0:T(8,128)(2,1)S(1)} %shard_map.143.refs_0_), channel_id=1, source_target_pairs={{0,12},{4,0},{8,4},{12,8},{1,13},{5,1},{9,5},{13,9},{2,14},{6,2},{... | collective-permute-start | bytes 49160 | tf_op jit(solution)/shard_map/ppermute | solution.py:32
  35.6 5.4 %collective-permute-start.7 = (bf16[16,64,256]{2,1,0:T(8,128)(2,1)}, bf16[16,64,256]{2,1,0:T(8,128)(2,1)S(1)}, u32[]{:S(2)}, u32[]{:S(2)}) collective-permute-start(bf16[16,64,256]{2,1,0:T(8,128)(2,1)} %direction.1), channel_id=1, source_target_pairs={{0,1},{1,0},{2,3},{3,2},{4,5},{5,4},{6,7},{7,6},{8,9},{9,8},{10,11... | collective-permute-start | bytes 1572872 | tf_op jit(solution)/shard_map/ppermute | solution.py:36
  35.7 5.4 %collective-permute-start.9 = (bf16[16,64,256]{2,1,0:T(8,128)(2,1)S(1)}, bf16[16,64,256]{2,1,0:T(8,128)(2,1)S(1)}, u32[]{:S(2)}, u32[]{:S(2)}) collective-permute-start(bf16[16,64,256]{2,1,0:T(8,128)(2,1)S(1)} %collective-permute-done.8.refs_4_), channel_id=1, source_target_pairs={{0,1},{1,0},{2,3},{3,2},{4,5},{5,4},{6,7},{7,6},{8,9},{9,8},{10,11... | collective-permute-start | bytes 1572872 | tf_op jit(solution)/shard_map/ppermute | solution.py:36
  36.2 4.9 %collective-permute-start.6 = (bf16[16,64,256]{2,1,0:T(8,128)(2,1)S(1)}, bf16[16,64,256]{2,1,0:T(8,128)(2,1)S(1)}, u32[]{:S(2)}, u32[]{:S(2)}) collective-permute-start(bf16[16,64,256]{2,1,0:T(8,128)(2,1)S(1)} %collective-permute-done.2.refs_0_), channel_id=1, source_target_pairs={{0,1},{1,0},{2,3},{3,2},{4,5},{5,4},{6,7},{7,6},{8,9},{9,8},{10,11... | collective-permute-start | bytes 1572872 | tf_op jit(solution)/shard_map/ppermute | solution.py:36
  36.3 9.9 %collective-permute-start.10 = (bf16[8,64,128]{2,1,0:T(8,128)(2,1)S(1)}, bf16[8,64,128]{2,1,0:T(8,128)(2,1)S(1)}, u32[]{:S(2)}, u32[]{:S(2)}) collective-permute-start(bf16[8,64,128]{2,1,0:T(8,128)(2,1)S(1)} %get-tuple-element.40), channel_id=1, source_target_pairs={{0,2},{2,4},{4,6},{6,8},{8,10},{10,12},{12,14},{14,0},{1,3},{3,5},... | collective-permute-start | bytes 393224 | tf_op jit(solution)/shard_map/ppermute | solution.py:32
  38.3 9.1 %collective-permute-start.11 = (bf16[8,64,128]{2,1,0:T(8,128)(2,1)S(1)}, bf16[8,64,128]{2,1,0:T(8,128)(2,1)S(1)}, u32[]{:S(2)}, u32[]{:S(2)}) collective-permute-start(bf16[8,64,128]{2,1,0:T(8,128)(2,1)S(1)} %get-tuple-element.40), channel_id=1, source_target_pairs={{0,14},{2,0},{4,2},{6,4},{8,6},{10,8},{12,10},{14,12},{1,15},{3,1}... | collective-permute-start | bytes 393224 | tf_op jit(solution)/shard_map/ppermute | solution.py:32
  41.0 8.1 %collective-permute-start.12 = (bf16[4,64,128]{2,1,0:T(8,128)(2,1)S(1)}, bf16[4,64,128]{2,1,0:T(8,128)(2,1)S(1)}, u32[]{:S(2)}, u32[]{:S(2)}) collective-permute-start(bf16[4,64,128]{2,1,0:T(8,128)(2,1)S(1)} %shard_map.147.refs_0_), channel_id=1, source_target_pairs={{0,2},{2,0},{1,3},{3,1},{4,6},{6,4},{5,7},{7,5},{8,10},{10,8},{9,1... | collective-permute-start | bytes 196616 | tf_op jit(solution)/shard_map/ppermute | solution.py:32
  41.1 6.4 %copy-start.1 = (bf16[16,8,64,64]{3,2,1,0:T(8,128)(2,1)S(1)}, bf16[16,8,64,64]{3,2,1,0:T(8,128)(2,1)}, u32[]{:S(2)}) copy-start(bf16[16,8,64,64]{3,2,1,0:T(8,128)(2,1)} %coupling.1) | copy-start | bytes 3145732
  41.1 8.2 %copy-start = (bf16[16,64,256]{2,1,0:T(8,128)(2,1)S(1)}, bf16[16,64,256]{2,1,0:T(8,128)(2,1)}, u32[]{:S(2)}) copy-start(bf16[16,64,256]{2,1,0:T(8,128)(2,1)} %direction.1) | copy-start | bytes 1572868
  41.1 8.2 %copy-start.3 = (bf16[16,64,64]{2,1,0:T(8,128)(2,1)S(1)}, bf16[16,64,64]{2,1,0:T(8,128)(2,1)}, u32[]{:S(2)}) copy-start(bf16[16,64,64]{2,1,0:T(8,128)(2,1)} %refs_2_.3) | copy-start | bytes 393220
  41.1 8.2 %copy-start.4 = (bf16[16,64,256]{2,1,0:T(8,128)(2,1)S(1)}, bf16[16,64,256]{2,1,0:T(8,128)(2,1)}, u32[]{:S(2)}) copy-start(bf16[16,64,256]{2,1,0:T(8,128)(2,1)} %get-tuple-element.44.refs_3_) | copy-start | bytes 1572868
  46.2 5.7 %copy-start.2 = (f32[16,64,256]{2,1,0:T(8,128)S(1)}, f32[16,64,256]{2,1,0:T(8,128)}, u32[]{:S(2)}) copy-start(f32[16,64,256]{2,1,0:T(8,128)} %residual.1) | copy-start | bytes 3145732
  46.2 5.7 %copy-start.5 = (f32[64]{0:T(128)S(1)}, f32[64]{0:T(128)}, u32[]{:S(2)}) copy-start(f32[64]{0:T(128)} %param.15) | copy-start | bytes 772
  49.2 2.7 %collective-permute-start.13 = (bf16[8,64,256]{2,1,0:T(8,128)(2,1)S(1)}, bf16[8,64,256]{2,1,0:T(8,128)(2,1)S(1)}, u32[]{:S(2)}, u32[]{:S(2)}) collective-permute-start(bf16[8,64,256]{2,1,0:T(8,128)(2,1)S(1)} %get-tuple-element.46), channel_id=1, source_target_pairs={{0,1},{1,0},{2,3},{3,2},{4,5},{5,4},{6,7},{7,6},{8,9},{9,8},{10,11... | collective-permute-start | bytes 786440 | tf_op jit(solution)/shard_map/ppermute | solution.py:36

commit v12 on v11

--- a/solution.py
+++ b/solution.py
@@ -76,50 +76,39 @@
     )
 
 
-def up_kernel(order_h, basis_h, direction_h, transfer_h, node_h, natural_h, coef, lifted, mark, *scratch):
+def load_kernel(*refs):
+    count = len(refs) // 2
+    sources, targets, sems = refs[:count], refs[count:-1], refs[-1]
+    copies = [
+        pltpu.make_async_copy(source, target, sems.at[i])
+        for i, (source, target) in enumerate(zip(sources, targets))
+    ]
+    for copy in copies:
+        copy.start()
+    for copy in copies:
+        copy.wait()
+
+
+def up_kernel(order, basis, direction, leaf_transfer, node_transfer, *refs):
+    natural_h, coef, lifted, mark, natural, sems = refs
     mark[...] = jnp.zeros_like(mark)
-    order, basis, direction, leaf_transfer, node_transfer, natural, sems = scratch
     leaves, rank, points = basis.shape
     samples = direction.shape[1]
-    chunks = sems.shape[1]
+    chunks = sems.shape[0]
     size = leaves // chunks
-    whole = [
-        pltpu.make_async_copy(order_h, order, sems.at[3, 0]),
-        pltpu.make_async_copy(node_h, node_transfer, sems.at[3, 1]),
-    ]
-    copies = []
-    for c in range(chunks):
-        part = pl.ds(c * size, size)
-        copies.append(
-            [
-                pltpu.make_async_copy(source.at[part], target.at[part], sems.at[i, c])
-                for i, (source, target) in enumerate(
-                    ((basis_h, basis), (direction_h, direction), (transfer_h, leaf_transfer))
-                )
-            ]
-        )
-    for copy in whole + sum(copies, []):
-        copy.start()
-    for copy in whole:
-        copy.wait()
     rows = lax.broadcasted_iota(jnp.int32, (points, points), 0)
     node = jnp.zeros((samples, rank), F32)
     leaving = []
     for g in range(leaves):
-        if g % size == 0:
-            for copy in copies[g // size]:
-                copy.wait()
-        place = jnp.where(rows == order[g : g + 1, :], 1.0, 0.0).astype(BF)
-        own = nt(basis[g], place).astype(BF)
+        spot = jnp.where(rows == order[g : g + 1, :], 1.0, 0.0).astype(BF)
+        own = nt(basis[g], spot).astype(BF)
         natural[g] = own
         weights = nt(direction[g], own).astype(BF)
         coef[g // 2, :, (g % 2) * rank : (g % 2 + 1) * rank] = weights
         node = node + nt(weights, leaf_transfer[g])
         if g % size == size - 1:
             part = pl.ds(g + 1 - size, size)
-            copy = pltpu.make_async_copy(
-                natural.at[part], natural_h.at[part], sems.at[4, g // size]
-            )
+            copy = pltpu.make_async_copy(natural.at[part], natural_h.at[part], sems.at[g // size])
             copy.start()
             leaving.append(copy)
     lifted[...] = nt(node.astype(BF), node_transfer[0])
@@ -422,7 +411,18 @@
     coords = jnp.transpose(coords, (1, 0, 2))
     coords_prev = shifted(coords, RING, 1)
     coords_after = shifted(coords, RING, -1)
-    travelling, first = lax.optimization_barrier((direction, order, coords_prev, coords_after))[:2]
+    operands = (order, basis, direction, leaf_transfer, node_transfer)
+    resident = call(
+        load_kernel,
+        tuple(shape(array.shape, array.dtype) for array in operands),
+        MIB,
+        2 * MIB,
+        in_specs=[hbm] * 5,
+        out_specs=(vmem,) * 5,
+        scratch_shapes=[pltpu.SemaphoreType.DMA((5,))],
+        vmem=4,
+    )(*in_hbm(*operands))
+    travelling = ordered(direction, coords_prev, coords_after, resident[0])
     direction_prev = shifted(travelling, RING, 1)
     direction_after = shifted(travelling, RING, -1)
     natural, coef, lifted, up_mark = call(
@@ -435,19 +435,11 @@
         ),
         4 * leaves * rank * points * points,
         6 * MIB,
-        in_specs=[hbm] * 5,
+        in_specs=[vmem] * 5,
         out_specs=(hbm, vmem, vmem, vmem),
-        scratch_shapes=[
-            pltpu.VMEM(order.shape, jnp.int32),
-            pltpu.VMEM(basis.shape, BF),
-            pltpu.VMEM(direction.shape, BF),
-            pltpu.VMEM(leaf_transfer.shape, BF),
-            pltpu.VMEM(node_transfer.shape, BF),
-            pltpu.VMEM(basis.shape, BF),
-            pltpu.SemaphoreType.DMA((5, 4)),
-        ],
+        scratch_shapes=[pltpu.VMEM(basis.shape, BF), pltpu.SemaphoreType.DMA((4,))],
         vmem=8,
-    )(*in_hbm(first, basis, direction, leaf_transfer, node_transfer))
+    )(ordered(resident[0], coords_prev, coords_after), *resident[1:])
 
     def make_tiles(start, done, *operands):
         count = half // 2

time: 64.1 us -> 62.3 us (0.972)
  waiting for transfers between devices: 3.11 us -> 1.79 us
    pallas_call x1, Pallas kernels: 6.14 us -> 4.24 us  [on_device(): call(up_kernel, (pltpu.HBM((leaves, rank, points), BF), shape((leaves //...]
    pallas_call x0 -> x1, Pallas kernels: none -> 1.33 us  [on_device(): call(load_kernel, tuple((shape(array.shape, array.dtype) for array in ope...]
    ppermute x10, waiting for transfers between devices: 3.1 us -> 1.78 us  [shifted(): lax.ppermute(array, axis, [(i, (i + by) % count) for i in range(count)])]
  transfers between devices with their start and end apart: 14 -> 14, of which waited for: 2 -> 2; matrix products, arithmetic and copies ran while one was open for 0% -> 0% of each run, Pallas kernels for 43% -> 44%
where the time goes in v12:
time: 62.3 us; the launch traced here: 62 us
  Pallas kernels  29.3 us (47%)
  starting transfers between devices  20.2 us (32%)
  blocking collectives  9.75 us (16%)
  waiting for transfers between devices  1.79 us (3%)
  between operations  0.92 us (1%)
    ppermute x10, starting transfers between devices, shifted(): lax.ppermute(array, axis, [(i, (i + by) % count) for i in range(count)])  19.5 us
    pallas_call x2, Pallas kernels, make_tiles(): call(functools.partial(tile_kernel, start), outs, 40 * count * entries *...  12 us
    all_to_all x1, blocking collectives, on_device(): norms = lax.all_to_all(norms, RING, 0, 0)  9.75 us
    pallas_call x1, Pallas kernels, on_device(): call(near_kernel, (shape((half, samples, points), F32), shape((half, samp...  5.03 us
    pallas_call x1, Pallas kernels, on_device(): call(up_kernel, (pltpu.HBM((leaves, rank, points), BF), shape((leaves //...  4.24 us
    pallas_call x1, Pallas kernels, on_device(): call(down_kernel, shape((leaves, samples, points), F32), 2 * leaves * sam...  2.58 us
    ppermute x10, waiting for transfers between devices, shifted(): lax.ppermute(array, axis, [(i, (i + by) % count) for i in range(count)])  1.78 us
    pallas_call x1, Pallas kernels, on_device(): call(couple_kernel, shape((leaves, samples, rank), F32), 2 * leaves * sam...  1.52 us
  transfers between devices with their start and end apart: 14, of which 2 were waited for; matrix products, arithmetic and copies ran while one was open for 0% of the time, Pallas kernels for 44%

profile of v12, /device:TPU:0, one launch (start us, length us, event | category | flops | bytes accessed | tf_op | source)
XLA Modules:
  0.0 62.0 jit_solution(4437911865143572298)
XLA Ops:
  0.6 0.0 copy-start
  0.6 3.0 %collective-permute-start = (bf16[3,16,256]{2,1,0:T(8,128)(2,1)}, bf16[3,16,256]{2,1,0:T(8,128)(2,1)S(1)}, u32[]{:S(2)}, u32[]{:S(2)}) collective-permute-start(bf16[3,16,256]{2,1,0:T(8,128)(2,1)} %bitcast.5), channel_id=1, source_target_pairs={{0,2},{2,4},{4,6},{6,8},{8,10},{10,12},{12,14},{14,0},{1,3},{3,5},... | collective-permute-start | bytes 73736 | tf_op jit(solution)/shard_map/ppermute | solution.py:32
  3.6 3.1 %collective-permute-start.1 = (bf16[3,16,256]{2,1,0:T(8,128)(2,1)}, bf16[3,16,256]{2,1,0:T(8,128)(2,1)S(1)}, u32[]{:S(2)}, u32[]{:S(2)}) collective-permute-start(bf16[3,16,256]{2,1,0:T(8,128)(2,1)} %bitcast.6), channel_id=1, source_target_pairs={{0,14},{2,0},{4,2},{6,4},{8,6},{10,8},{12,10},{14,12},{1,15},{3,1}... | collective-permute-start | bytes 73736 | tf_op jit(solution)/shard_map/ppermute | solution.py:32
  6.7 1.3 %shard_map.140 = (s32[16,256]{1,0:T(8,128)S(1)}, bf16[16,64,256]{2,1,0:T(8,128)(2,1)S(1)}, bf16[16,64,256]{2,1,0:T(8,128)(2,1)S(1)}, bf16[16,64,64]{2,1,0:T(8,128)(2,1)S(1)}, bf16[1,64,64]{2,1,0:T(8,128)(2,1)S(1)}) custom-call(s32[16,256]{1,0:T(8,128)} %refs_0_.1, bf16[16,64,256]{2,1,0:T(8,128)(2,1)} %refs_1_.1, bf16[16,64,256]{2,1,0:T(8,128)(2,1)} %direction.1, ...), custom_call_target="tpu_custom_call" | custom-call | flops 1048576 | bytes 2097152 | tf_op jit(solution)/shard_map/pallas_call | solution.py:415
  8.1 0.6 collective-permute-done.refs_1_
  8.7 4.8 %collective-permute-start.8 = (bf16[16,64,256]{2,1,0:T(8,128)(2,1)}, bf16[16,64,256]{2,1,0:T(8,128)(2,1)S(1)}, u32[]{:S(2)}, u32[]{:S(2)}) collective-permute-start(bf16[16,64,256]{2,1,0:T(8,128)(2,1)} %direction.1), channel_id=1, source_target_pairs={{0,14},{2,0},{4,2},{6,4},{8,6},{10,8},{12,10},{14,12},{1,15},{3,1}... | collective-permute-start | bytes 1572872 | tf_op jit(solution)/shard_map/ppermute | solution.py:32
  13.5 4.2 %shard_map.141 = (bf16[16,64,256]{2,1,0:T(8,128)(2,1)}, bf16[8,64,128]{2,1,0:T(8,128)(2,1)S(1)}, f32[64,64]{1,0:T(8,128)S(1)}, f32[8,128]{1,0:T(8,128)S(1)}) custom-call(s32[16,256]{1,0:T(8,128)S(1)} %get-tuple-element.33.order, bf16[16,64,256]{2,1,0:T(8,128)(2,1)S(1)} %get-tuple-element.34.basis, bf16[16,64,256]{2,1,0:T(8,128)(2,1)S(1)} %get-tuple-element.35.direction, ...), custom_call_target="tpu_custom_call" | custom-call | flops 268435456 | bytes 6291456 | tf_op jit(solution)/shard_map/pallas_call | solution.py:428
  17.7 6.5 %shard_map.142 = (bf16[4,3072,256]{2,1,0:T(8,128)(2,1)S(1)}, f32[8,128]{1,0:T(8,128)S(1)}, bf16[48,256,128]{2,1,0:T(8,128)(2,1)S(1)}, f32[3,16,256]{2,1,0:T(8,128)S(1)}) custom-call(s32[16,12]{1,0:T(8,128)} %near_h.5, f32[8,128]{1,0:T(8,128)S(1)} %get-tuple-element.38._, bf16[3,16,256]{2,1,0:T(8,128)(2,1)} %bitcast.7, ...), custom_call_target="tpu_custom_call" | custom-call | flops 125829120 | bytes 50331648 | tf_op jit(solution)/shard_map/pallas_call | solution.py:449
  24.3 0.1 shard_map.144.refs_0_
  24.3 0.0 collective-permute-start.3
  24.4 1.1 %collective-permute-start.4 = (bf16[64,128]{1,0:T(8,128)(2,1)S(1)}, bf16[64,128]{1,0:T(8,128)(2,1)S(1)}, u32[]{:S(2)}, u32[]{:S(2)}) collective-permute-start(bf16[64,128]{1,0:T(8,128)(2,1)S(1)} %shard_map.144.refs_0_), channel_id=1, source_target_pairs={{0,8},{4,12},{8,0},{12,4},{1,9},{5,13},{9,1},{13,5},{2,10},{6,14},... | collective-permute-start | bytes 49160 | tf_op jit(solution)/shard_map/ppermute | solution.py:32
  25.5 2.7 %collective-permute-start.5 = (bf16[64,128]{1,0:T(8,128)(2,1)S(1)}, bf16[64,128]{1,0:T(8,128)(2,1)S(1)}, u32[]{:S(2)}, u32[]{:S(2)}) collective-permute-start(bf16[64,128]{1,0:T(8,128)(2,1)S(1)} %shard_map.144.refs_0_), channel_id=1, source_target_pairs={{0,12},{4,0},{8,4},{12,8},{1,13},{5,1},{9,5},{13,9},{2,14},{6,2},{... | collective-permute-start | bytes 49160 | tf_op jit(solution)/shard_map/ppermute | solution.py:32
  28.2 5.5 %shard_map.143 = (bf16[4,3072,256]{2,1,0:T(8,128)(2,1)S(1)}, f32[8,128]{1,0:T(8,128)}) custom-call(s32[16,12]{1,0:T(8,128)} %near_h.5, f32[8,128]{1,0:T(8,128)S(1)} %get-tuple-element.39._, f32[3,16,256]{2,1,0:T(8,128)S(1)} %get-tuple-element.40.refs_0_, bf16[48,256,128]{2,1,0:T(8,128)(2,1)S(1)} %get-tuple-element.41.refs_1_), custom_call_target="tpu_custom_call" | custom-call | flops 125829120 | bytes 3145728 | tf_op jit(solution)/shard_map/pallas_call | solution.py:449
  33.7 0.1 collective-permute-start.7
  33.8 0.5 collective-permute-start.9
  34.3 0.1 collective-permute-start.6
  34.4 2.0 %collective-permute-start.10 = (bf16[8,64,128]{2,1,0:T(8,128)(2,1)S(1)}, bf16[8,64,128]{2,1,0:T(8,128)(2,1)S(1)}, u32[]{:S(2)}, u32[]{:S(2)}) collective-permute-start(bf16[8,64,128]{2,1,0:T(8,128)(2,1)S(1)} %get-tuple-element.50), channel_id=1, source_target_pairs={{0,2},{2,4},{4,6},{6,8},{8,10},{10,12},{12,14},{14,0},{1,3},{3,5},... | collective-permute-start | bytes 393224 | tf_op jit(solution)/shard_map/ppermute | solution.py:32
  36.4 2.7 %collective-permute-start.11 = (bf16[8,64,128]{2,1,0:T(8,128)(2,1)S(1)}, bf16[8,64,128]{2,1,0:T(8,128)(2,1)S(1)}, u32[]{:S(2)}, u32[]{:S(2)}) collective-permute-start(bf16[8,64,128]{2,1,0:T(8,128)(2,1)S(1)} %get-tuple-element.50), channel_id=1, source_target_pairs={{0,14},{2,0},{4,2},{6,4},{8,6},{10,8},{12,10},{14,12},{1,15},{3,1}... | collective-permute-start | bytes 393224 | tf_op jit(solution)/shard_map/ppermute | solution.py:32
  39.1 0.1 collective-permute-start.12
  39.2 0.0 copy-start.2
  39.2 0.0 copy-start.1
  39.3 0.0 copy-start.5
  39.3 5.0 %shard_map.145 = (f32[8,64,256]{2,1,0:T(8,128)S(1)}, bf16[8,64,256]{2,1,0:T(8,128)(2,1)S(1)}, f32[8,128]{1,0:T(8,128)}) custom-call(s32[16,12]{1,0:T(8,128)} %near_h.5, bf16[16,64,256]{2,1,0:T(8,128)(2,1)S(1)} %collective-permute-done.2.refs_0_, bf16[16,64,256]{2,1,0:T(8,128)(2,1)S(1)} %collective-permute-done.6.refs_1_, bf16[16,64,256]{2,1,0:T(8,128)(2,1)} %direction.1, ...), custom_call_target="tpu_custom_call" | custom-call | flops 1048576 | bytes 1048576 | tf_op jit(solution)/shard_map/pallas_call | solution.py:495
  44.4 1.1 %collective-permute-done.11.after = bf16[8,64,128]{2,1,0:T(8,128)(2,1)S(1)} collective-permute-done((bf16[8,64,128]{2,1,0:T(8,128)(2,1)S(1)}, bf16[8,64,128]{2,1,0:T(8,128)(2,1)S(1)}, u32[]{:S(2)}, u32[]{:S(2)}) %collective-permute-start.11) | collective-permute-done | bytes 131104 | tf_op jit(solution)/shard_map/ppermute | solution.py:32
  45.5 0.2 shard_map.146
  45.7 1.5 %shard_map.147._.refs_1_ = f32[16,64,64]{2,1,0:T(8,128)S(1)} custom-call(bf16[32,64,64]{2,1,0:T(8,128)(2,1)S(1)} %get-tuple-element.51.window, bf16[16,8,64,64]{3,2,1,0:T(8,128)(2,1)S(1)} %copy-done.2, s32[8,16]{1,0:T(8,128)} %bitcast.4), custom_call_target="tpu_custom_call" | custom-call | flops 67108864 | bytes 4194304 | tf_op jit(solution)/shard_map/pallas_call | solution.py:529
  47.2 0.1 shard_map.149
  47.4 0.1 collective-permute-start.13
  47.5 2.6 %shard_map.150.base = f32[16,64,256]{2,1,0:T(8,128)S(1)} custom-call(bf16[4,64,64]{2,1,0:T(8,128)(2,1)S(1)} %get-tuple-element.53.refs_0_, f32[16,64,64]{2,1,0:T(8,128)S(1)} %shard_map.147._.refs_1_, bf16[16,64,64]{2,1,0:T(8,128)(2,1)S(1)} %copy-done.4, bf16[16,64,256]{2,1,0:T(8,128)(2,1)S(1)} %copy-done.5, bf16[16,64,256]{2,1,0:T(8,128)(2,1)S(1)} %copy-done.1, ...), custom_call_target="tpu_custom_call" | custom-call | flops 41943040 | bytes 4194304 | tf_op jit(solution)/shard_map/pallas_call | solution.py:553
  50.1 1.2 %shard_map.151 = (f32[16,64,256]{2,1,0:T(8,128)}, f32[16,64,256]{2,1,0:T(8,128)S(1)}, f32[8,8,128]{2,1,0:T(8,128)S(1)}) custom-call(f32[1,64]{1,0:T(1,128)S(1)} %bitcast.3, f32[16,64,256]{2,1,0:T(8,128)S(1)} %shard_map.150.base, f32[8,64,256]{2,1,0:T(8,128)S(1)} %get-tuple-element.55.kept, bf16[8,64,256]{2,1,0:T(8,128)(2,1)S(1)} %collective-permute-done.13.received, ...), custom_call_target="tpu_custom_call" | custom-call | flops 4194304 | bytes 5242880 | tf_op jit(solution)/shard_map/pallas_call | solution.py:568
  51.3 9.7 %all_to_all.5.norms = f32[8,8,128]{2,1,0:T(8,128)S(1)} all-to-all(f32[8,8,128]{2,1,0:T(8,128)S(1)} %get-tuple-element.58), channel_id=1, replica_groups=mesh['groups'=2,'blk'=4,'leaf'=2,'sample'=2] {'blk','leaf'}, dimensions={0} | all-to-all | bytes 65536 | tf_op jit(solution)/shard_map/all_to_all | solution.py:578
  61.0 0.9 %shard_map.152 = bf16[16,64,256]{2,1,0:T(8,128)(2,1)} custom-call(f32[8,8,128]{2,1,0:T(8,128)S(1)} %all_to_all.5.norms, f32[16,64,256]{2,1,0:T(8,128)S(1)} %get-tuple-element.59.updated, bf16[16,64,256]{2,1,0:T(8,128)(2,1)S(1)} %copy-done.1), custom_call_target="tpu_custom_call" | custom-call | flops 1048576 | bytes 2097152 | tf_op jit(solution)/shard_map/pallas_call | solution.py:579
  (24 shorter events, 0.1 us)
Async XLA Ops:
  0.6 33.1 %copy-start = (bf16[16,64,256]{2,1,0:T(8,128)(2,1)S(1)}, bf16[16,64,256]{2,1,0:T(8,128)(2,1)}, u32[]{:S(2)}) copy-start(bf16[16,64,256]{2,1,0:T(8,128)(2,1)} %direction.1) | copy-start | bytes 1572868
  0.6 8.0 %collective-permute-start = (bf16[3,16,256]{2,1,0:T(8,128)(2,1)}, bf16[3,16,256]{2,1,0:T(8,128)(2,1)S(1)}, u32[]{:S(2)}, u32[]{:S(2)}) collective-permute-start(bf16[3,16,256]{2,1,0:T(8,128)(2,1)} %bitcast.5), channel_id=1, source_target_pairs={{0,2},{2,4},{4,6},{6,8},{8,10},{10,12},{12,14},{14,0},{1,3},{3,5},... | collective-permute-start | bytes 73736 | tf_op jit(solution)/shard_map/ppermute | solution.py:32
  3.6 5.1 %collective-permute-start.1 = (bf16[3,16,256]{2,1,0:T(8,128)(2,1)}, bf16[3,16,256]{2,1,0:T(8,128)(2,1)S(1)}, u32[]{:S(2)}, u32[]{:S(2)}) collective-permute-start(bf16[3,16,256]{2,1,0:T(8,128)(2,1)} %bitcast.6), channel_id=1, source_target_pairs={{0,14},{2,0},{4,2},{6,4},{8,6},{10,8},{12,10},{14,12},{1,15},{3,1}... | collective-permute-start | bytes 73736 | tf_op jit(solution)/shard_map/ppermute | solution.py:32
  8.7 25.1 %collective-permute-start.8 = (bf16[16,64,256]{2,1,0:T(8,128)(2,1)}, bf16[16,64,256]{2,1,0:T(8,128)(2,1)S(1)}, u32[]{:S(2)}, u32[]{:S(2)}) collective-permute-start(bf16[16,64,256]{2,1,0:T(8,128)(2,1)} %direction.1), channel_id=1, source_target_pairs={{0,14},{2,0},{4,2},{6,4},{8,6},{10,8},{12,10},{14,12},{1,15},{3,1}... | collective-permute-start | bytes 1572872 | tf_op jit(solution)/shard_map/ppermute | solution.py:32
  13.5 20.8 %collective-permute-start.2 = (bf16[16,64,256]{2,1,0:T(8,128)(2,1)}, bf16[16,64,256]{2,1,0:T(8,128)(2,1)S(1)}, u32[]{:S(2)}, u32[]{:S(2)}) collective-permute-start(bf16[16,64,256]{2,1,0:T(8,128)(2,1)} %direction.1), channel_id=1, source_target_pairs={{0,2},{2,4},{4,6},{6,8},{8,10},{10,12},{12,14},{14,0},{1,3},{3,5},... | collective-permute-start | bytes 1572872 | tf_op jit(solution)/shard_map/ppermute | solution.py:32
  24.3 9.3 %collective-permute-start.3 = (bf16[64,128]{1,0:T(8,128)(2,1)S(1)}, bf16[64,128]{1,0:T(8,128)(2,1)S(1)}, u32[]{:S(2)}, u32[]{:S(2)}) collective-permute-start(bf16[64,128]{1,0:T(8,128)(2,1)S(1)} %shard_map.144.refs_0_), channel_id=1, source_target_pairs={{0,4},{4,8},{8,12},{12,0},{1,5},{5,9},{9,13},{13,1},{2,6},{6,10},{... | collective-permute-start | bytes 49160 | tf_op jit(solution)/shard_map/ppermute | solution.py:32
  24.4 9.3 %collective-permute-start.4 = (bf16[64,128]{1,0:T(8,128)(2,1)S(1)}, bf16[64,128]{1,0:T(8,128)(2,1)S(1)}, u32[]{:S(2)}, u32[]{:S(2)}) collective-permute-start(bf16[64,128]{1,0:T(8,128)(2,1)S(1)} %shard_map.144.refs_0_), channel_id=1, source_target_pairs={{0,8},{4,12},{8,0},{12,4},{1,9},{5,13},{9,1},{13,5},{2,10},{6,14},... | collective-permute-start | bytes 49160 | tf_op jit(solution)/shard_map/ppermute | solution.py:32
  25.5 8.2 %collective-permute-start.5 = (bf16[64,128]{1,0:T(8,128)(2,1)S(1)}, bf16[64,128]{1,0:T(8,128)(2,1)S(1)}, u32[]{:S(2)}, u32[]{:S(2)}) collective-permute-start(bf16[64,128]{1,0:T(8,128)(2,1)S(1)} %shard_map.144.refs_0_), channel_id=1, source_target_pairs={{0,12},{4,0},{8,4},{12,8},{1,13},{5,1},{9,5},{13,9},{2,14},{6,2},{... | collective-permute-start | bytes 49160 | tf_op jit(solution)/shard_map/ppermute | solution.py:32
  33.7 5.4 %collective-permute-start.7 = (bf16[16,64,256]{2,1,0:T(8,128)(2,1)S(1)}, bf16[16,64,256]{2,1,0:T(8,128)(2,1)S(1)}, u32[]{:S(2)}, u32[]{:S(2)}) collective-permute-start(bf16[16,64,256]{2,1,0:T(8,128)(2,1)S(1)} %copy-done), channel_id=1, source_target_pairs={{0,1},{1,0},{2,3},{3,2},{4,5},{5,4},{6,7},{7,6},{8,9},{9,8},{10,11... | collective-permute-start | bytes 1572872 | tf_op jit(solution)/shard_map/ppermute | solution.py:36
  33.8 5.4 %collective-permute-start.9 = (bf16[16,64,256]{2,1,0:T(8,128)(2,1)S(1)}, bf16[16,64,256]{2,1,0:T(8,128)(2,1)S(1)}, u32[]{:S(2)}, u32[]{:S(2)}) collective-permute-start(bf16[16,64,256]{2,1,0:T(8,128)(2,1)S(1)} %collective-permute-done.8.refs_4_), channel_id=1, source_target_pairs={{0,1},{1,0},{2,3},{3,2},{4,5},{5,4},{6,7},{7,6},{8,9},{9,8},{10,11... | collective-permute-start | bytes 1572872 | tf_op jit(solution)/shard_map/ppermute | solution.py:36
  34.3 4.9 %collective-permute-start.6 = (bf16[16,64,256]{2,1,0:T(8,128)(2,1)S(1)}, bf16[16,64,256]{2,1,0:T(8,128)(2,1)S(1)}, u32[]{:S(2)}, u32[]{:S(2)}) collective-permute-start(bf16[16,64,256]{2,1,0:T(8,128)(2,1)S(1)} %collective-permute-done.2.refs_0_), channel_id=1, source_target_pairs={{0,1},{1,0},{2,3},{3,2},{4,5},{5,4},{6,7},{7,6},{8,9},{9,8},{10,11... | collective-permute-start | bytes 1572872 | tf_op jit(solution)/shard_map/ppermute | solution.py:36
  34.4 9.9 %collective-permute-start.10 = (bf16[8,64,128]{2,1,0:T(8,128)(2,1)S(1)}, bf16[8,64,128]{2,1,0:T(8,128)(2,1)S(1)}, u32[]{:S(2)}, u32[]{:S(2)}) collective-permute-start(bf16[8,64,128]{2,1,0:T(8,128)(2,1)S(1)} %get-tuple-element.50), channel_id=1, source_target_pairs={{0,2},{2,4},{4,6},{6,8},{8,10},{10,12},{12,14},{14,0},{1,3},{3,5},... | collective-permute-start | bytes 393224 | tf_op jit(solution)/shard_map/ppermute | solution.py:32
  36.4 9.1 %collective-permute-start.11 = (bf16[8,64,128]{2,1,0:T(8,128)(2,1)S(1)}, bf16[8,64,128]{2,1,0:T(8,128)(2,1)S(1)}, u32[]{:S(2)}, u32[]{:S(2)}) collective-permute-start(bf16[8,64,128]{2,1,0:T(8,128)(2,1)S(1)} %get-tuple-element.50), channel_id=1, source_target_pairs={{0,14},{2,0},{4,2},{6,4},{8,6},{10,8},{12,10},{14,12},{1,15},{3,1}... | collective-permute-start | bytes 393224 | tf_op jit(solution)/shard_map/ppermute | solution.py:32
  39.1 8.1 %collective-permute-start.12 = (bf16[4,64,128]{2,1,0:T(8,128)(2,1)S(1)}, bf16[4,64,128]{2,1,0:T(8,128)(2,1)S(1)}, u32[]{:S(2)}, u32[]{:S(2)}) collective-permute-start(bf16[4,64,128]{2,1,0:T(8,128)(2,1)S(1)} %shard_map.148.refs_0_), channel_id=1, source_target_pairs={{0,2},{2,0},{1,3},{3,1},{4,6},{6,4},{5,7},{7,5},{8,10},{10,8},{9,1... | collective-permute-start | bytes 196616 | tf_op jit(solution)/shard_map/ppermute | solution.py:32
  39.2 6.5 %copy-start.2 = (bf16[16,8,64,64]{3,2,1,0:T(8,128)(2,1)S(1)}, bf16[16,8,64,64]{3,2,1,0:T(8,128)(2,1)}, u32[]{:S(2)}) copy-start(bf16[16,8,64,64]{3,2,1,0:T(8,128)(2,1)} %coupling.1) | copy-start | bytes 3145732
  39.2 8.2 %copy-start.1 = (bf16[16,64,256]{2,1,0:T(8,128)(2,1)S(1)}, bf16[16,64,256]{2,1,0:T(8,128)(2,1)}, u32[]{:S(2)}) copy-start(bf16[16,64,256]{2,1,0:T(8,128)(2,1)} %direction.1) | copy-start | bytes 1572868
  39.3 8.2 %copy-start.4 = (bf16[16,64,64]{2,1,0:T(8,128)(2,1)S(1)}, bf16[16,64,64]{2,1,0:T(8,128)(2,1)}, u32[]{:S(2)}) copy-start(bf16[16,64,64]{2,1,0:T(8,128)(2,1)} %refs_2_.5) | copy-start | bytes 393220
  39.3 8.2 %copy-start.5 = (bf16[16,64,256]{2,1,0:T(8,128)(2,1)S(1)}, bf16[16,64,256]{2,1,0:T(8,128)(2,1)}, u32[]{:S(2)}) copy-start(bf16[16,64,256]{2,1,0:T(8,128)(2,1)} %get-tuple-element.54.refs_3_) | copy-start | bytes 1572868
  44.3 5.7 %copy-start.3 = (f32[16,64,256]{2,1,0:T(8,128)S(1)}, f32[16,64,256]{2,1,0:T(8,128)}, u32[]{:S(2)}) copy-start(f32[16,64,256]{2,1,0:T(8,128)} %residual.1) | copy-start | bytes 3145732
  44.3 5.7 %copy-start.6 = (f32[64]{0:T(128)S(1)}, f32[64]{0:T(128)}, u32[]{:S(2)}) copy-start(f32[64]{0:T(128)} %param.15) | copy-start | bytes 772
  47.4 2.7 %collective-permute-start.13 = (bf16[8,64,256]{2,1,0:T(8,128)(2,1)S(1)}, bf16[8,64,256]{2,1,0:T(8,128)(2,1)S(1)}, u32[]{:S(2)}, u32[]{:S(2)}) collective-permute-start(bf16[8,64,256]{2,1,0:T(8,128)(2,1)S(1)} %get-tuple-element.56), channel_id=1, source_target_pairs={{0,1},{1,0},{2,3},{3,2},{4,5},{5,4},{6,7},{7,6},{8,9},{9,8},{10,11... | collective-permute-start | bytes 786440 | tf_op jit(solution)/shard_map/ppermute | solution.py:36

commit v13 on v12

--- a/solution.py
+++ b/solution.py
@@ -212,8 +212,14 @@
 
 def collect_kernel(*refs):
     terms, together = refs[:-1], refs[-1]
-    for i, term in enumerate(terms):
-        together[i] = term[...]
+    at = 0
+    for term in terms:
+        if len(term.shape) == 2:
+            together[at] = term[...]
+            at += 1
+        else:
+            together[at : at + term.shape[0]] = term[...]
+            at += term.shape[0]
 
 
 def top_kernel(_, given, *refs):
@@ -274,6 +280,8 @@
     incoming = jnp.zeros((samples, rank), F32)
     for e in range(top_list.shape[1]):
         index = lax.rem(here - top_list[0, e] + clusters, clusters)
+        if clusters == 4:
+            index = here ^ top_list[0, e]
         incoming = incoming + nt(tops[index], top_coupling[0, e])
     down = nn(incoming.astype(BF), node_transfer[0]).astype(BF)
     for g in range(leaves):
@@ -472,7 +480,9 @@
         out_specs=vmem,
         vmem=4,
     )(low_mark, lifted)
-    if blk_count <= 8:
+    if blk_count == 4:
+        others = [lax.ppermute(leaving, "blk", [(i, i ^ 1) for i in range(4)])]
+    elif blk_count <= 8:
         others = [shifted(leaving, "blk", by) for by in range(1, blk_count)]
     else:
         others = lax.all_gather(leaving[None], "blk", axis=0, tiled=True)
@@ -482,15 +492,22 @@
     direction_other = partner(ordered(direction, high_mark, *others))
     direction_prev = ordered(direction_prev, high_mark, *others)
     direction_after = ordered(direction_after, high_mark, *others)
-    together = call(
-        collect_kernel,
-        shape((blk_count, samples, 2 * rank), BF),
-        MIB,
-        MIB,
-        in_specs=[vmem] * blk_count,
-        out_specs=vmem,
-        vmem=4,
-    )(leaving, *others)
+    def collect(parts):
+        count = sum(1 if part.ndim == 2 else part.shape[0] for part in parts)
+        return call(
+            collect_kernel,
+            shape((count, samples, 2 * rank), BF),
+            MIB,
+            MIB,
+            in_specs=[vmem] * len(parts),
+            out_specs=vmem,
+            vmem=4,
+        )(*parts)
+
+    together = collect([leaving] + others)
+    if blk_count == 4:
+        beyond = lax.ppermute(together, "blk", [(i, i ^ 2) for i in range(4)])
+        together = collect([together, beyond])
     terms = [shifted(together, "leaf", by) for by in range(1, leaf_count)]
     kept, given, near_mark = call(
         near_kernel,

time: 62.3 us -> 65.1 us (1.045)
  waiting for transfers between devices: 1.79 us -> 6 us
  starting transfers between devices: 20.2 us -> 18.4 us
    ppermute x10 -> x7, starting transfers between devices: 19.5 us -> 16.1 us  [shifted(): lax.ppermute(array, axis, [(i, (i + by) % count) for i in range(count)])]
    ppermute x0 -> x2, waiting for transfers between devices: none -> 2.31 us  [the longest x1 2.31 us: on_device(): beyond = lax.ppermute(together, 'blk', [(i, i ^ 2) for i in range(4)])]
    ppermute x10 -> x7, waiting for transfers between devices: 1.78 us -> 3.68 us  [shifted(): lax.ppermute(array, axis, [(i, (i + by) % count) for i in range(count)])]
    ppermute x0 -> x2, starting transfers between devices: none -> 1.63 us  [the longest x1 1.61 us: on_device(): beyond = lax.ppermute(together, 'blk', [(i, i ^ 2) for i in range(4)])]
  transfers between devices with their start and end apart: 14 -> 13, of which waited for: 2 -> 3; matrix products, arithmetic and copies ran while one was open for 0% -> 0% of each run, Pallas kernels for 44% -> 42%
where the time goes in v13:
time: 65.1 us; the launch traced here: 64.8 us
  Pallas kernels  29.4 us (45%)
  starting transfers between devices  18.4 us (28%)
  blocking collectives  10.1 us (16%)
  waiting for transfers between devices  6 us (9%)
  between operations  0.91 us (1%)
    ppermute x7, starting transfers between devices, shifted(): lax.ppermute(array, axis, [(i, (i + by) % count) for i in range(count)])  16.1 us
    pallas_call x2, Pallas kernels, make_tiles(): call(functools.partial(tile_kernel, start), outs, 40 * count * entries *...  12 us
    all_to_all x1, blocking collectives, on_device(): norms = lax.all_to_all(norms, RING, 0, 0)  10.1 us
    pallas_call x1, Pallas kernels, on_device(): call(near_kernel, (shape((half, samples, points), F32), shape((half, samp...  5.02 us
    pallas_call x1, Pallas kernels, on_device(): call(up_kernel, (pltpu.HBM((leaves, rank, points), BF), shape((leaves //...  4.24 us
    ppermute x7, waiting for transfers between devices, shifted(): lax.ppermute(array, axis, [(i, (i + by) % count) for i in range(count)])  3.68 us
    pallas_call x1, Pallas kernels, on_device(): call(down_kernel, shape((leaves, samples, points), F32), 2 * leaves * sam...  2.58 us
    ppermute x1, waiting for transfers between devices, on_device(): beyond = lax.ppermute(together, 'blk', [(i, i ^ 2) for i in range(4)])  2.31 us
  transfers between devices with their start and end apart: 13, of which 3 were waited for; matrix products, arithmetic and copies ran while one was open for 0% of the time, Pallas kernels for 42%

profile of v13, /device:TPU:0, one launch (start us, length us, event | category | flops | bytes accessed | tf_op | source)
XLA Modules:
  0.0 64.8 jit_solution(5757467682453753913)
XLA Ops:
  0.6 0.0 copy-start
  0.6 3.0 %collective-permute-start = (bf16[3,16,256]{2,1,0:T(8,128)(2,1)}, bf16[3,16,256]{2,1,0:T(8,128)(2,1)S(1)}, u32[]{:S(2)}, u32[]{:S(2)}) collective-permute-start(bf16[3,16,256]{2,1,0:T(8,128)(2,1)} %bitcast.5), channel_id=1, source_target_pairs={{0,2},{2,4},{4,6},{6,8},{8,10},{10,12},{12,14},{14,0},{1,3},{3,5},... | collective-permute-start | bytes 73736 | tf_op jit(solution)/shard_map/ppermute | solution.py:32
  3.6 3.1 %collective-permute-start.1 = (bf16[3,16,256]{2,1,0:T(8,128)(2,1)}, bf16[3,16,256]{2,1,0:T(8,128)(2,1)S(1)}, u32[]{:S(2)}, u32[]{:S(2)}) collective-permute-start(bf16[3,16,256]{2,1,0:T(8,128)(2,1)} %bitcast.6), channel_id=1, source_target_pairs={{0,14},{2,0},{4,2},{6,4},{8,6},{10,8},{12,10},{14,12},{1,15},{3,1}... | collective-permute-start | bytes 73736 | tf_op jit(solution)/shard_map/ppermute | solution.py:32
  6.7 1.3 %shard_map.140 = (s32[16,256]{1,0:T(8,128)S(1)}, bf16[16,64,256]{2,1,0:T(8,128)(2,1)S(1)}, bf16[16,64,256]{2,1,0:T(8,128)(2,1)S(1)}, bf16[16,64,64]{2,1,0:T(8,128)(2,1)S(1)}, bf16[1,64,64]{2,1,0:T(8,128)(2,1)S(1)}) custom-call(s32[16,256]{1,0:T(8,128)} %refs_0_.1, bf16[16,64,256]{2,1,0:T(8,128)(2,1)} %refs_1_.1, bf16[16,64,256]{2,1,0:T(8,128)(2,1)} %direction.1, ...), custom_call_target="tpu_custom_call" | custom-call | flops 1048576 | bytes 2097152 | tf_op jit(solution)/shard_map/pallas_call | solution.py:423
  8.1 0.6 collective-permute-done.refs_1_
  8.7 4.8 %collective-permute-start.6 = (bf16[16,64,256]{2,1,0:T(8,128)(2,1)}, bf16[16,64,256]{2,1,0:T(8,128)(2,1)S(1)}, u32[]{:S(2)}, u32[]{:S(2)}) collective-permute-start(bf16[16,64,256]{2,1,0:T(8,128)(2,1)} %direction.1), channel_id=1, source_target_pairs={{0,14},{2,0},{4,2},{6,4},{8,6},{10,8},{12,10},{14,12},{1,15},{3,1}... | collective-permute-start | bytes 1572872 | tf_op jit(solution)/shard_map/ppermute | solution.py:32
  13.5 4.2 %shard_map.141 = (bf16[16,64,256]{2,1,0:T(8,128)(2,1)}, bf16[8,64,128]{2,1,0:T(8,128)(2,1)S(1)}, f32[64,64]{1,0:T(8,128)S(1)}, f32[8,128]{1,0:T(8,128)S(1)}) custom-call(s32[16,256]{1,0:T(8,128)S(1)} %get-tuple-element.33.order, bf16[16,64,256]{2,1,0:T(8,128)(2,1)S(1)} %get-tuple-element.34.basis, bf16[16,64,256]{2,1,0:T(8,128)(2,1)S(1)} %get-tuple-element.35.direction, ...), custom_call_target="tpu_custom_call" | custom-call | flops 268435456 | bytes 6291456 | tf_op jit(solution)/shard_map/pallas_call | solution.py:436
  17.7 6.5 %shard_map.142 = (bf16[4,3072,256]{2,1,0:T(8,128)(2,1)S(1)}, f32[8,128]{1,0:T(8,128)S(1)}, bf16[48,256,128]{2,1,0:T(8,128)(2,1)S(1)}, f32[3,16,256]{2,1,0:T(8,128)S(1)}) custom-call(s32[16,12]{1,0:T(8,128)} %near_h.5, f32[8,128]{1,0:T(8,128)S(1)} %get-tuple-element.38._, bf16[3,16,256]{2,1,0:T(8,128)(2,1)} %bitcast.7, ...), custom_call_target="tpu_custom_call" | custom-call | flops 125829120 | bytes 50331648 | tf_op jit(solution)/shard_map/pallas_call | solution.py:457
  24.3 0.1 shard_map.144.refs_0_
  24.3 0.0 collective-permute-start.3
  24.4 5.5 %shard_map.143 = (bf16[4,3072,256]{2,1,0:T(8,128)(2,1)S(1)}, f32[8,128]{1,0:T(8,128)}) custom-call(s32[16,12]{1,0:T(8,128)} %near_h.5, f32[8,128]{1,0:T(8,128)S(1)} %get-tuple-element.39._, f32[3,16,256]{2,1,0:T(8,128)S(1)} %get-tuple-element.40.refs_0_, bf16[48,256,128]{2,1,0:T(8,128)(2,1)S(1)} %get-tuple-element.41.refs_1_), custom_call_target="tpu_custom_call" | custom-call | flops 125829120 | bytes 3145728 | tf_op jit(solution)/shard_map/pallas_call | solution.py:457
  29.9 0.1 collective-permute-start.5
  30.0 3.1 %collective-permute-done.6.refs_4_ = bf16[16,64,256]{2,1,0:T(8,128)(2,1)S(1)} collective-permute-done((bf16[16,64,256]{2,1,0:T(8,128)(2,1)}, bf16[16,64,256]{2,1,0:T(8,128)(2,1)S(1)}, u32[]{:S(2)}, u32[]{:S(2)}) %collective-permute-start.6) | collective-permute-done | bytes 524320 | tf_op jit(solution)/shard_map/ppermute | solution.py:32
  33.0 0.5 collective-permute-start.4
  33.6 1.6 %collective-permute-start.10 = (bf16[2,64,128]{2,1,0:T(8,128)(2,1)S(1)}, bf16[2,64,128]{2,1,0:T(8,128)(2,1)S(1)}, u32[]{:S(2)}, u32[]{:S(2)}) collective-permute-start(bf16[2,64,128]{2,1,0:T(8,128)(2,1)S(1)} %shard_map.148.refs_0_), channel_id=1, source_target_pairs={{0,8},{4,12},{8,0},{12,4},{1,9},{5,13},{9,1},{13,5},{2,10},{6,14},... | collective-permute-start | bytes 98312 | tf_op jit(solution)/shard_map/ppermute | solution.py:509
  35.2 1.3 %collective-permute-start.8 = (bf16[8,64,128]{2,1,0:T(8,128)(2,1)S(1)}, bf16[8,64,128]{2,1,0:T(8,128)(2,1)S(1)}, u32[]{:S(2)}, u32[]{:S(2)}) collective-permute-start(bf16[8,64,128]{2,1,0:T(8,128)(2,1)S(1)} %get-tuple-element.50), channel_id=1, source_target_pairs={{0,2},{2,4},{4,6},{6,8},{8,10},{10,12},{12,14},{14,0},{1,3},{3,5},... | collective-permute-start | bytes 393224 | tf_op jit(solution)/shard_map/ppermute | solution.py:32
  36.4 2.3 %collective-permute-done.10.refs_1_ = bf16[2,64,128]{2,1,0:T(8,128)(2,1)S(1)} collective-permute-done((bf16[2,64,128]{2,1,0:T(8,128)(2,1)S(1)}, bf16[2,64,128]{2,1,0:T(8,128)(2,1)S(1)}, u32[]{:S(2)}, u32[]{:S(2)}) %collective-permute-start.10) | collective-permute-done | bytes 32800 | tf_op jit(solution)/shard_map/ppermute | solution.py:509
  38.8 3.9 %collective-permute-start.9 = (bf16[8,64,128]{2,1,0:T(8,128)(2,1)S(1)}, bf16[8,64,128]{2,1,0:T(8,128)(2,1)S(1)}, u32[]{:S(2)}, u32[]{:S(2)}) collective-permute-start(bf16[8,64,128]{2,1,0:T(8,128)(2,1)S(1)} %get-tuple-element.50), channel_id=1, source_target_pairs={{0,14},{2,0},{4,2},{6,4},{8,6},{10,8},{12,10},{14,12},{1,15},{3,1}... | collective-permute-start | bytes 393224 | tf_op jit(solution)/shard_map/ppermute | solution.py:32
  42.6 0.1 collective-permute-start.11
  42.7 0.0 copy-start.2
  42.7 0.0 copy-start.1
  42.8 0.0 copy-start.4
  42.8 5.0 %shard_map.145 = (f32[8,64,256]{2,1,0:T(8,128)S(1)}, bf16[8,64,256]{2,1,0:T(8,128)(2,1)S(1)}, f32[8,128]{1,0:T(8,128)}) custom-call(s32[16,12]{1,0:T(8,128)} %near_h.5, bf16[16,64,256]{2,1,0:T(8,128)(2,1)S(1)} %collective-permute-done.2.refs_0_, bf16[16,64,256]{2,1,0:T(8,128)(2,1)S(1)} %collective-permute-done.4.refs_1_, bf16[16,64,256]{2,1,0:T(8,128)(2,1)} %direction.1, ...), custom_call_target="tpu_custom_call" | custom-call | flops 1048576 | bytes 1048576 | tf_op jit(solution)/shard_map/pallas_call | solution.py:512
  47.8 0.0 copy-start.3
  47.8 0.2 shard_map.146
  48.1 1.7 %shard_map.147._.refs_1_ = f32[16,64,64]{2,1,0:T(8,128)S(1)} custom-call(bf16[32,64,64]{2,1,0:T(8,128)(2,1)S(1)} %get-tuple-element.51.window, bf16[16,8,64,64]{3,2,1,0:T(8,128)(2,1)S(1)} %copy-done.2, s32[8,16]{1,0:T(8,128)} %bitcast.4), custom_call_target="tpu_custom_call" | custom-call | flops 67108864 | bytes 4194304 | tf_op jit(solution)/shard_map/pallas_call | solution.py:546
  49.7 0.1 shard_map.150
  49.8 0.1 collective-permute-start.12
  49.9 2.6 %shard_map.151.base = f32[16,64,256]{2,1,0:T(8,128)S(1)} custom-call(bf16[4,64,64]{2,1,0:T(8,128)(2,1)S(1)} %get-tuple-element.53.refs_0_, f32[16,64,64]{2,1,0:T(8,128)S(1)} %shard_map.147._.refs_1_, bf16[16,64,64]{2,1,0:T(8,128)(2,1)S(1)} %copy-done.4, bf16[16,64,256]{2,1,0:T(8,128)(2,1)S(1)} %copy-done.5, bf16[16,64,256]{2,1,0:T(8,128)(2,1)S(1)} %copy-done.1, ...), custom_call_target="tpu_custom_call" | custom-call | flops 41943040 | bytes 4194304 | tf_op jit(solution)/shard_map/pallas_call | solution.py:570
  52.6 1.2 %shard_map.152 = (f32[16,64,256]{2,1,0:T(8,128)}, f32[16,64,256]{2,1,0:T(8,128)S(1)}, f32[8,8,128]{2,1,0:T(8,128)S(1)}) custom-call(f32[1,64]{1,0:T(1,128)S(1)} %bitcast.3, f32[16,64,256]{2,1,0:T(8,128)S(1)} %shard_map.151.base, f32[8,64,256]{2,1,0:T(8,128)S(1)} %get-tuple-element.55.kept, bf16[8,64,256]{2,1,0:T(8,128)(2,1)S(1)} %collective-permute-done.12.received, ...), custom_call_target="tpu_custom_call" | custom-call | flops 4194304 | bytes 5242880 | tf_op jit(solution)/shard_map/pallas_call | solution.py:585
  53.8 10.1 %all_to_all.5.norms = f32[8,8,128]{2,1,0:T(8,128)S(1)} all-to-all(f32[8,8,128]{2,1,0:T(8,128)S(1)} %get-tuple-element.58), channel_id=1, replica_groups=mesh['groups'=2,'blk'=4,'leaf'=2,'sample'=2] {'blk','leaf'}, dimensions={0} | all-to-all | bytes 65536 | tf_op jit(solution)/shard_map/all_to_all | solution.py:595
  63.8 0.9 %shard_map.153 = bf16[16,64,256]{2,1,0:T(8,128)(2,1)} custom-call(f32[8,8,128]{2,1,0:T(8,128)S(1)} %all_to_all.5.norms, f32[16,64,256]{2,1,0:T(8,128)S(1)} %get-tuple-element.59.updated, bf16[16,64,256]{2,1,0:T(8,128)(2,1)S(1)} %copy-done.1), custom_call_target="tpu_custom_call" | custom-call | flops 1048576 | bytes 2097152 | tf_op jit(solution)/shard_map/pallas_call | solution.py:596
  (23 shorter events, 0.1 us)
Async XLA Ops:
  0.6 29.3 %copy-start = (bf16[16,64,256]{2,1,0:T(8,128)(2,1)S(1)}, bf16[16,64,256]{2,1,0:T(8,128)(2,1)}, u32[]{:S(2)}) copy-start(bf16[16,64,256]{2,1,0:T(8,128)(2,1)} %direction.1) | copy-start | bytes 1572868
  0.6 8.0 %collective-permute-start = (bf16[3,16,256]{2,1,0:T(8,128)(2,1)}, bf16[3,16,256]{2,1,0:T(8,128)(2,1)S(1)}, u32[]{:S(2)}, u32[]{:S(2)}) collective-permute-start(bf16[3,16,256]{2,1,0:T(8,128)(2,1)} %bitcast.5), channel_id=1, source_target_pairs={{0,2},{2,4},{4,6},{6,8},{8,10},{10,12},{12,14},{14,0},{1,3},{3,5},... | collective-permute-start | bytes 73736 | tf_op jit(solution)/shard_map/ppermute | solution.py:32
  3.6 5.1 %collective-permute-start.1 = (bf16[3,16,256]{2,1,0:T(8,128)(2,1)}, bf16[3,16,256]{2,1,0:T(8,128)(2,1)S(1)}, u32[]{:S(2)}, u32[]{:S(2)}) collective-permute-start(bf16[3,16,256]{2,1,0:T(8,128)(2,1)} %bitcast.6), channel_id=1, source_target_pairs={{0,14},{2,0},{4,2},{6,4},{8,6},{10,8},{12,10},{14,12},{1,15},{3,1}... | collective-permute-start | bytes 73736 | tf_op jit(solution)/shard_map/ppermute | solution.py:32
  8.7 24.3 %collective-permute-start.6 = (bf16[16,64,256]{2,1,0:T(8,128)(2,1)}, bf16[16,64,256]{2,1,0:T(8,128)(2,1)S(1)}, u32[]{:S(2)}, u32[]{:S(2)}) collective-permute-start(bf16[16,64,256]{2,1,0:T(8,128)(2,1)} %direction.1), channel_id=1, source_target_pairs={{0,14},{2,0},{4,2},{6,4},{8,6},{10,8},{12,10},{14,12},{1,15},{3,1}... | collective-permute-start | bytes 1572872 | tf_op jit(solution)/shard_map/ppermute | solution.py:32
  13.5 19.6 %collective-permute-start.2 = (bf16[16,64,256]{2,1,0:T(8,128)(2,1)}, bf16[16,64,256]{2,1,0:T(8,128)(2,1)S(1)}, u32[]{:S(2)}, u32[]{:S(2)}) collective-permute-start(bf16[16,64,256]{2,1,0:T(8,128)(2,1)} %direction.1), channel_id=1, source_target_pairs={{0,2},{2,4},{4,6},{6,8},{8,10},{10,12},{12,14},{14,0},{1,3},{3,5},... | collective-permute-start | bytes 1572872 | tf_op jit(solution)/shard_map/ppermute | solution.py:32
  24.3 5.5 %collective-permute-start.3 = (bf16[64,128]{1,0:T(8,128)(2,1)S(1)}, bf16[64,128]{1,0:T(8,128)(2,1)S(1)}, u32[]{:S(2)}, u32[]{:S(2)}) collective-permute-start(bf16[64,128]{1,0:T(8,128)(2,1)S(1)} %shard_map.144.refs_0_), channel_id=1, source_target_pairs={{0,4},{4,0},{8,12},{12,8},{1,5},{5,1},{9,13},{13,9},{2,6},{6,2},{1... | collective-permute-start | bytes 49160 | tf_op jit(solution)/shard_map/ppermute | solution.py:484
  29.9 12.7 %collective-permute-start.5 = (bf16[16,64,256]{2,1,0:T(8,128)(2,1)S(1)}, bf16[16,64,256]{2,1,0:T(8,128)(2,1)S(1)}, u32[]{:S(2)}, u32[]{:S(2)}) collective-permute-start(bf16[16,64,256]{2,1,0:T(8,128)(2,1)S(1)} %copy-done), channel_id=1, source_target_pairs={{0,1},{1,0},{2,3},{3,2},{4,5},{5,4},{6,7},{7,6},{8,9},{9,8},{10,11... | collective-permute-start | bytes 1572872 | tf_op jit(solution)/shard_map/ppermute | solution.py:36
  33.0 9.7 %collective-permute-start.7 = (bf16[16,64,256]{2,1,0:T(8,128)(2,1)S(1)}, bf16[16,64,256]{2,1,0:T(8,128)(2,1)S(1)}, u32[]{:S(2)}, u32[]{:S(2)}) collective-permute-start(bf16[16,64,256]{2,1,0:T(8,128)(2,1)S(1)} %collective-permute-done.6.refs_4_), channel_id=1, source_target_pairs={{0,1},{1,0},{2,3},{3,2},{4,5},{5,4},{6,7},{7,6},{8,9},{9,8},{10,11... | collective-permute-start | bytes 1572872 | tf_op jit(solution)/shard_map/ppermute | solution.py:36
  33.0 9.7 %collective-permute-start.4 = (bf16[16,64,256]{2,1,0:T(8,128)(2,1)S(1)}, bf16[16,64,256]{2,1,0:T(8,128)(2,1)S(1)}, u32[]{:S(2)}, u32[]{:S(2)}) collective-permute-start(bf16[16,64,256]{2,1,0:T(8,128)(2,1)S(1)} %collective-permute-done.2.refs_0_), channel_id=1, source_target_pairs={{0,1},{1,0},{2,3},{3,2},{4,5},{5,4},{6,7},{7,6},{8,9},{9,8},{10,11... | collective-permute-start | bytes 1572872 | tf_op jit(solution)/shard_map/ppermute | solution.py:36
  33.6 5.2 %collective-permute-start.10 = (bf16[2,64,128]{2,1,0:T(8,128)(2,1)S(1)}, bf16[2,64,128]{2,1,0:T(8,128)(2,1)S(1)}, u32[]{:S(2)}, u32[]{:S(2)}) collective-permute-start(bf16[2,64,128]{2,1,0:T(8,128)(2,1)S(1)} %shard_map.148.refs_0_), channel_id=1, source_target_pairs={{0,8},{4,12},{8,0},{12,4},{1,9},{5,13},{9,1},{13,5},{2,10},{6,14},... | collective-permute-start | bytes 98312 | tf_op jit(solution)/shard_map/ppermute | solution.py:509
  35.2 12.7 %collective-permute-start.8 = (bf16[8,64,128]{2,1,0:T(8,128)(2,1)S(1)}, bf16[8,64,128]{2,1,0:T(8,128)(2,1)S(1)}, u32[]{:S(2)}, u32[]{:S(2)}) collective-permute-start(bf16[8,64,128]{2,1,0:T(8,128)(2,1)S(1)} %get-tuple-element.50), channel_id=1, source_target_pairs={{0,2},{2,4},{4,6},{6,8},{8,10},{10,12},{12,14},{14,0},{1,3},{3,5},... | collective-permute-start | bytes 393224 | tf_op jit(solution)/shard_map/ppermute | solution.py:32
  38.8 9.1 %collective-permute-start.9 = (bf16[8,64,128]{2,1,0:T(8,128)(2,1)S(1)}, bf16[8,64,128]{2,1,0:T(8,128)(2,1)S(1)}, u32[]{:S(2)}, u32[]{:S(2)}) collective-permute-start(bf16[8,64,128]{2,1,0:T(8,128)(2,1)S(1)} %get-tuple-element.50), channel_id=1, source_target_pairs={{0,14},{2,0},{4,2},{6,4},{8,6},{10,8},{12,10},{14,12},{1,15},{3,1}... | collective-permute-start | bytes 393224 | tf_op jit(solution)/shard_map/ppermute | solution.py:32
  42.6 7.1 %collective-permute-start.11 = (bf16[4,64,128]{2,1,0:T(8,128)(2,1)S(1)}, bf16[4,64,128]{2,1,0:T(8,128)(2,1)S(1)}, u32[]{:S(2)}, u32[]{:S(2)}) collective-permute-start(bf16[4,64,128]{2,1,0:T(8,128)(2,1)S(1)} %shard_map.149.refs_0_), channel_id=1, source_target_pairs={{0,2},{2,0},{1,3},{3,1},{4,6},{6,4},{5,7},{7,5},{8,10},{10,8},{9,1... | collective-permute-start | bytes 196616 | tf_op jit(solution)/shard_map/ppermute | solution.py:32
  42.7 5.3 %copy-start.2 = (bf16[16,8,64,64]{3,2,1,0:T(8,128)(2,1)S(1)}, bf16[16,8,64,64]{3,2,1,0:T(8,128)(2,1)}, u32[]{:S(2)}) copy-start(bf16[16,8,64,64]{3,2,1,0:T(8,128)(2,1)} %coupling.1) | copy-start | bytes 3145732
  42.7 7.2 %copy-start.1 = (bf16[16,64,256]{2,1,0:T(8,128)(2,1)S(1)}, bf16[16,64,256]{2,1,0:T(8,128)(2,1)}, u32[]{:S(2)}) copy-start(bf16[16,64,256]{2,1,0:T(8,128)(2,1)} %direction.1) | copy-start | bytes 1572868
  42.8 7.2 %copy-start.4 = (bf16[16,64,64]{2,1,0:T(8,128)(2,1)S(1)}, bf16[16,64,64]{2,1,0:T(8,128)(2,1)}, u32[]{:S(2)}) copy-start(bf16[16,64,64]{2,1,0:T(8,128)(2,1)} %refs_2_.5) | copy-start | bytes 393220
  42.8 7.2 %copy-start.5 = (bf16[16,64,256]{2,1,0:T(8,128)(2,1)S(1)}, bf16[16,64,256]{2,1,0:T(8,128)(2,1)}, u32[]{:S(2)}) copy-start(bf16[16,64,256]{2,1,0:T(8,128)(2,1)} %get-tuple-element.54.refs_3_) | copy-start | bytes 1572868
  47.8 4.7 %copy-start.3 = (f32[16,64,256]{2,1,0:T(8,128)S(1)}, f32[16,64,256]{2,1,0:T(8,128)}, u32[]{:S(2)}) copy-start(f32[16,64,256]{2,1,0:T(8,128)} %residual.1) | copy-start | bytes 3145732
  47.8 4.7 %copy-start.6 = (f32[64]{0:T(128)S(1)}, f32[64]{0:T(128)}, u32[]{:S(2)}) copy-start(f32[64]{0:T(128)} %param.15) | copy-start | bytes 772
  49.8 2.7 %collective-permute-start.12 = (bf16[8,64,256]{2,1,0:T(8,128)(2,1)S(1)}, bf16[8,64,256]{2,1,0:T(8,128)(2,1)S(1)}, u32[]{:S(2)}, u32[]{:S(2)}) collective-permute-start(bf16[8,64,256]{2,1,0:T(8,128)(2,1)S(1)} %get-tuple-element.56), channel_id=1, source_target_pairs={{0,1},{1,0},{2,3},{3,2},{4,5},{5,4},{6,7},{7,6},{8,9},{9,8},{10,11... | collective-permute-start | bytes 786440 | tf_op jit(solution)/shard_map/ppermute | solution.py:36

commit v14 on v12

--- a/solution.py
+++ b/solution.py
@@ -255,26 +255,21 @@
         part[g] = nt(jnp.concatenate(rows, axis=1), jnp.concatenate(columns, axis=1))
 
 
-def down_kernel(*refs):
-    tops, part, leaf_transfer, natural, direction = refs[:5]
-    sources, base, targets, sems = refs[5:8], refs[8], refs[9:12], refs[12]
-    top_list, top_coupling, node_transfer = targets
-    copies = [
-        pltpu.make_async_copy(source, target, sems.at[i])
-        for i, (source, target) in enumerate(zip(sources, targets))
-    ]
-    for copy in copies:
-        copy.start()
+def down_kernel(
+    tops, part, leaf_transfer, natural, direction, top_list, top_coupling, node_transfer, base
+):
     leaves, samples, points = direction.shape
     rank = natural.shape[1]
     clusters = lax.axis_size("blk")
     here = lax.axis_index("blk")
-    for copy in copies:
-        copy.wait()
+    behind = here - top_list[...]
+    behind = jnp.where(behind < 0, behind + clusters, behind)
     incoming = jnp.zeros((samples, rank), F32)
     for e in range(top_list.shape[1]):
-        index = lax.rem(here - top_list[0, e] + clusters, clusters)
-        incoming = incoming + nt(tops[index], top_coupling[0, e])
+        chosen = jnp.zeros((samples, rank), F32)
+        for i in range(clusters):
+            chosen = jnp.where(behind[:, e : e + 1] == i, tops[i].astype(F32), chosen)
+        incoming = incoming + nt(chosen.astype(BF), top_coupling[0, e])
     down = nn(incoming.astype(BF), node_transfer[0]).astype(BF)
     for g in range(leaves):
         inward = nn(down, leaf_transfer[g]) + part[g]
@@ -548,19 +543,24 @@
         out_specs=(vmem, vmem),
         vmem=8,
     )(part, given, together, *terms)
-    arrays = (top_list, top_coupling, node_transfer)
-    spaces = (pltpu.SMEM, pltpu.VMEM, pltpu.VMEM)
     base = call(
         down_kernel,
         shape((leaves, samples, points), F32),
         2 * leaves * samples * rank * (points + rank),
         4 * MIB,
-        in_specs=[vmem] * 5 + [hbm] * 3,
+        in_specs=[vmem] * 8,
         out_specs=vmem,
-        scratch_shapes=[space(array.shape, array.dtype) for space, array in zip(spaces, arrays)]
-        + [pltpu.SemaphoreType.DMA((3,))],
         vmem=10,
-    )(tops, part, leaf_transfer, natural, direction, *in_hbm(*arrays))
+    )(
+        tops,
+        part,
+        leaf_transfer,
+        natural,
+        direction,
+        top_list,
+        top_coupling,
+        node_transfer,
+    )
     received = partner(given)
 
     devices = blk_count * leaf_count

time: 62.3 us -> 61.6 us (0.989)
  Pallas kernels: 29.3 us -> 28.5 us
    pallas_call x1, Pallas kernels: 2.58 us -> 1.78 us  [on_device(): call(down_kernel, shape((leaves, samples, points), F32), 2 * leaves * sam...]
  transfers between devices with their start and end apart: 14 -> 14, of which waited for: 2 -> 2; matrix products, arithmetic and copies ran while one was open for 0% -> 0% of each run, Pallas kernels for 44% -> 43%
where the time goes in v14:
time: 61.6 us; the launch traced here: 61.2 us
  Pallas kernels  28.5 us (46%)
  starting transfers between devices  20.2 us (33%)
  blocking collectives  9.75 us (16%)
  waiting for transfers between devices  1.77 us (3%)
  between operations  0.96 us (2%)
    ppermute x10, starting transfers between devices, shifted(): lax.ppermute(array, axis, [(i, (i + by) % count) for i in range(count)])  19.5 us
    pallas_call x2, Pallas kernels, make_tiles(): call(functools.partial(tile_kernel, start), outs, 40 * count * entries *...  12 us
    all_to_all x1, blocking collectives, on_device(): norms = lax.all_to_all(norms, RING, 0, 0)  9.75 us
    pallas_call x1, Pallas kernels, on_device(): call(near_kernel, (shape((half, samples, points), F32), shape((half, samp...  5.02 us
    pallas_call x1, Pallas kernels, on_device(): call(up_kernel, (pltpu.HBM((leaves, rank, points), BF), shape((leaves //...  4.24 us
    pallas_call x1, Pallas kernels, on_device(): call(down_kernel, shape((leaves, samples, points), F32), 2 * leaves * sam...  1.78 us
    ppermute x10, waiting for transfers between devices, shifted(): lax.ppermute(array, axis, [(i, (i + by) % count) for i in range(count)])  1.76 us
    pallas_call x1, Pallas kernels, on_device(): call(couple_kernel, shape((leaves, samples, rank), F32), 2 * leaves * sam...  1.52 us
  transfers between devices with their start and end apart: 14, of which 2 were waited for; matrix products, arithmetic and copies ran while one was open for 0% of the time, Pallas kernels for 43%

profile of v14, /device:TPU:0, one launch (start us, length us, event | category | flops | bytes accessed | tf_op | source)
XLA Modules:
  0.0 61.2 jit_solution(8127577585885118006)
XLA Ops:
  0.6 3.0 %collective-permute-start = (bf16[3,16,256]{2,1,0:T(8,128)(2,1)}, bf16[3,16,256]{2,1,0:T(8,128)(2,1)S(1)}, u32[]{:S(2)}, u32[]{:S(2)}) collective-permute-start(bf16[3,16,256]{2,1,0:T(8,128)(2,1)} %bitcast.5), channel_id=1, source_target_pairs={{0,2},{2,4},{4,6},{6,8},{8,10},{10,12},{12,14},{14,0},{1,3},{3,5},... | collective-permute-start | bytes 73736 | tf_op jit(solution)/shard_map/ppermute | solution.py:32
  3.6 3.1 %collective-permute-start.1 = (bf16[3,16,256]{2,1,0:T(8,128)(2,1)}, bf16[3,16,256]{2,1,0:T(8,128)(2,1)S(1)}, u32[]{:S(2)}, u32[]{:S(2)}) collective-permute-start(bf16[3,16,256]{2,1,0:T(8,128)(2,1)} %bitcast.6), channel_id=1, source_target_pairs={{0,14},{2,0},{4,2},{6,4},{8,6},{10,8},{12,10},{14,12},{1,15},{3,1}... | collective-permute-start | bytes 73736 | tf_op jit(solution)/shard_map/ppermute | solution.py:32
  6.7 1.3 %shard_map.140 = (s32[16,256]{1,0:T(8,128)S(1)}, bf16[16,64,256]{2,1,0:T(8,128)(2,1)S(1)}, bf16[16,64,256]{2,1,0:T(8,128)(2,1)S(1)}, bf16[16,64,64]{2,1,0:T(8,128)(2,1)S(1)}, bf16[1,64,64]{2,1,0:T(8,128)(2,1)S(1)}) custom-call(s32[16,256]{1,0:T(8,128)} %refs_0_.1, bf16[16,64,256]{2,1,0:T(8,128)(2,1)} %refs_1_.1, bf16[16,64,256]{2,1,0:T(8,128)(2,1)} %direction.3, ...), custom_call_target="tpu_custom_call" | custom-call | flops 1048576 | bytes 2097152 | tf_op jit(solution)/shard_map/pallas_call | solution.py:410
  8.1 0.6 %collective-permute-done.refs_1_ = bf16[3,16,256]{2,1,0:T(8,128)(2,1)S(1)} collective-permute-done((bf16[3,16,256]{2,1,0:T(8,128)(2,1)}, bf16[3,16,256]{2,1,0:T(8,128)(2,1)S(1)}, u32[]{:S(2)}, u32[]{:S(2)}) %collective-permute-start) | collective-permute-done | bytes 24608 | tf_op jit(solution)/shard_map/ppermute | solution.py:32
  8.7 4.8 %collective-permute-start.8 = (bf16[16,64,256]{2,1,0:T(8,128)(2,1)}, bf16[16,64,256]{2,1,0:T(8,128)(2,1)S(1)}, u32[]{:S(2)}, u32[]{:S(2)}) collective-permute-start(bf16[16,64,256]{2,1,0:T(8,128)(2,1)} %direction.3), channel_id=1, source_target_pairs={{0,14},{2,0},{4,2},{6,4},{8,6},{10,8},{12,10},{14,12},{1,15},{3,1}... | collective-permute-start | bytes 1572872 | tf_op jit(solution)/shard_map/ppermute | solution.py:32
  13.5 4.2 %shard_map.141 = (bf16[16,64,256]{2,1,0:T(8,128)(2,1)}, bf16[8,64,128]{2,1,0:T(8,128)(2,1)S(1)}, f32[64,64]{1,0:T(8,128)S(1)}, f32[8,128]{1,0:T(8,128)S(1)}) custom-call(s32[16,256]{1,0:T(8,128)S(1)} %get-tuple-element.33.order, bf16[16,64,256]{2,1,0:T(8,128)(2,1)S(1)} %get-tuple-element.34.basis, bf16[16,64,256]{2,1,0:T(8,128)(2,1)S(1)} %get-tuple-element.35.direction, ...), custom_call_target="tpu_custom_call" | custom-call | flops 268435456 | bytes 6291456 | tf_op jit(solution)/shard_map/pallas_call | solution.py:423
  17.7 6.5 %shard_map.142 = (bf16[4,3072,256]{2,1,0:T(8,128)(2,1)S(1)}, f32[8,128]{1,0:T(8,128)S(1)}, bf16[48,256,128]{2,1,0:T(8,128)(2,1)S(1)}, f32[3,16,256]{2,1,0:T(8,128)S(1)}) custom-call(s32[16,12]{1,0:T(8,128)} %near_h.5, f32[8,128]{1,0:T(8,128)S(1)} %get-tuple-element.38._, bf16[3,16,256]{2,1,0:T(8,128)(2,1)} %bitcast.7, ...), custom_call_target="tpu_custom_call" | custom-call | flops 125829120 | bytes 50331648 | tf_op jit(solution)/shard_map/pallas_call | solution.py:444
  24.3 0.1 shard_map.144.refs_0_
  24.3 0.0 collective-permute-start.3
  24.4 1.1 %collective-permute-start.4 = (bf16[64,128]{1,0:T(8,128)(2,1)S(1)}, bf16[64,128]{1,0:T(8,128)(2,1)S(1)}, u32[]{:S(2)}, u32[]{:S(2)}) collective-permute-start(bf16[64,128]{1,0:T(8,128)(2,1)S(1)} %shard_map.144.refs_0_), channel_id=1, source_target_pairs={{0,8},{4,12},{8,0},{12,4},{1,9},{5,13},{9,1},{13,5},{2,10},{6,14},... | collective-permute-start | bytes 49160 | tf_op jit(solution)/shard_map/ppermute | solution.py:32
  25.5 2.7 %collective-permute-start.5 = (bf16[64,128]{1,0:T(8,128)(2,1)S(1)}, bf16[64,128]{1,0:T(8,128)(2,1)S(1)}, u32[]{:S(2)}, u32[]{:S(2)}) collective-permute-start(bf16[64,128]{1,0:T(8,128)(2,1)S(1)} %shard_map.144.refs_0_), channel_id=1, source_target_pairs={{0,12},{4,0},{8,4},{12,8},{1,13},{5,1},{9,5},{13,9},{2,14},{6,2},{... | collective-permute-start | bytes 49160 | tf_op jit(solution)/shard_map/ppermute | solution.py:32
  28.2 5.5 %shard_map.143 = (bf16[4,3072,256]{2,1,0:T(8,128)(2,1)S(1)}, f32[8,128]{1,0:T(8,128)}) custom-call(s32[16,12]{1,0:T(8,128)} %near_h.5, f32[8,128]{1,0:T(8,128)S(1)} %get-tuple-element.39._, f32[3,16,256]{2,1,0:T(8,128)S(1)} %get-tuple-element.40.refs_0_, bf16[48,256,128]{2,1,0:T(8,128)(2,1)S(1)} %get-tuple-element.41.refs_1_), custom_call_target="tpu_custom_call" | custom-call | flops 125829120 | bytes 3145728 | tf_op jit(solution)/shard_map/pallas_call | solution.py:444
  33.7 0.1 collective-permute-start.7
  33.8 0.5 collective-permute-start.9
  34.3 0.1 collective-permute-start.6
  34.4 2.0 %collective-permute-start.10 = (bf16[8,64,128]{2,1,0:T(8,128)(2,1)S(1)}, bf16[8,64,128]{2,1,0:T(8,128)(2,1)S(1)}, u32[]{:S(2)}, u32[]{:S(2)}) collective-permute-start(bf16[8,64,128]{2,1,0:T(8,128)(2,1)S(1)} %get-tuple-element.50), channel_id=1, source_target_pairs={{0,2},{2,4},{4,6},{6,8},{8,10},{10,12},{12,14},{14,0},{1,3},{3,5},... | collective-permute-start | bytes 393224 | tf_op jit(solution)/shard_map/ppermute | solution.py:32
  36.4 2.7 %collective-permute-start.11 = (bf16[8,64,128]{2,1,0:T(8,128)(2,1)S(1)}, bf16[8,64,128]{2,1,0:T(8,128)(2,1)S(1)}, u32[]{:S(2)}, u32[]{:S(2)}) collective-permute-start(bf16[8,64,128]{2,1,0:T(8,128)(2,1)S(1)} %get-tuple-element.50), channel_id=1, source_target_pairs={{0,14},{2,0},{4,2},{6,4},{8,6},{10,8},{12,10},{14,12},{1,15},{3,1}... | collective-permute-start | bytes 393224 | tf_op jit(solution)/shard_map/ppermute | solution.py:32
  39.1 0.1 collective-permute-start.12
  39.2 0.0 copy-start.1
  39.3 0.0 copy-start.4
  39.3 0.0 copy-start.7
  39.3 0.0 copy-start.8
  39.3 5.0 %shard_map.145 = (f32[8,64,256]{2,1,0:T(8,128)S(1)}, bf16[8,64,256]{2,1,0:T(8,128)(2,1)S(1)}, f32[8,128]{1,0:T(8,128)}) custom-call(s32[16,12]{1,0:T(8,128)} %near_h.5, bf16[16,64,256]{2,1,0:T(8,128)(2,1)S(1)} %collective-permute-done.2.refs_0_, bf16[16,64,256]{2,1,0:T(8,128)(2,1)S(1)} %collective-permute-done.6.refs_1_, bf16[16,64,256]{2,1,0:T(8,128)(2,1)} %direction.3, ...), custom_call_target="tpu_custom_call" | custom-call | flops 1048576 | bytes 1048576 | tf_op jit(solution)/shard_map/pallas_call | solution.py:490
  44.4 1.1 %collective-permute-done.11.after = bf16[8,64,128]{2,1,0:T(8,128)(2,1)S(1)} collective-permute-done((bf16[8,64,128]{2,1,0:T(8,128)(2,1)S(1)}, bf16[8,64,128]{2,1,0:T(8,128)(2,1)S(1)}, u32[]{:S(2)}, u32[]{:S(2)}) %collective-permute-start.11) | collective-permute-done | bytes 131104 | tf_op jit(solution)/shard_map/ppermute | solution.py:32
  45.5 0.2 shard_map.146
  45.7 1.5 %shard_map.147._.part = f32[16,64,64]{2,1,0:T(8,128)S(1)} custom-call(bf16[32,64,64]{2,1,0:T(8,128)(2,1)S(1)} %get-tuple-element.51.window, bf16[16,8,64,64]{3,2,1,0:T(8,128)(2,1)S(1)} %copy-done.2, s32[8,16]{1,0:T(8,128)} %bitcast.4), custom_call_target="tpu_custom_call" | custom-call | flops 67108864 | bytes 4194304 | tf_op jit(solution)/shard_map/pallas_call | solution.py:524
  47.2 0.1 shard_map.149
  47.4 0.1 collective-permute-start.13
  47.5 1.8 %shard_map.150.base = f32[16,64,256]{2,1,0:T(8,128)S(1)} custom-call(bf16[4,64,64]{2,1,0:T(8,128)(2,1)S(1)} %get-tuple-element.53.tops, f32[16,64,64]{2,1,0:T(8,128)S(1)} %shard_map.147._.part, bf16[16,64,64]{2,1,0:T(8,128)(2,1)S(1)} %copy-done.4, bf16[16,64,256]{2,1,0:T(8,128)(2,1)S(1)} %copy-done.5, bf16[16,64,256]{2,1,0:T(8,128)(2,1)S(1)} %copy-done.1, ...), custom_call_target="tpu_custom_call" | custom-call | flops 41943040 | bytes 4194304 | tf_op jit(solution)/shard_map/pallas_call | solution.py:546
  49.3 1.2 %shard_map.151 = (f32[16,64,256]{2,1,0:T(8,128)}, f32[16,64,256]{2,1,0:T(8,128)S(1)}, f32[8,8,128]{2,1,0:T(8,128)S(1)}) custom-call(f32[1,64]{1,0:T(1,128)S(1)} %bitcast.3, f32[16,64,256]{2,1,0:T(8,128)S(1)} %shard_map.150.base, f32[8,64,256]{2,1,0:T(8,128)S(1)} %get-tuple-element.55.kept, bf16[8,64,256]{2,1,0:T(8,128)(2,1)S(1)} %collective-permute-done.13.received, ...), custom_call_target="tpu_custom_call" | custom-call | flops 4194304 | bytes 5242880 | tf_op jit(solution)/shard_map/pallas_call | solution.py:568
  50.6 9.7 %all_to_all.5.norms = f32[8,8,128]{2,1,0:T(8,128)S(1)} all-to-all(f32[8,8,128]{2,1,0:T(8,128)S(1)} %get-tuple-element.58), channel_id=1, replica_groups=mesh['groups'=2,'blk'=4,'leaf'=2,'sample'=2] {'blk','leaf'}, dimensions={0} | all-to-all | bytes 65536 | tf_op jit(solution)/shard_map/all_to_all | solution.py:578
  60.3 0.9 %shard_map.152 = bf16[16,64,256]{2,1,0:T(8,128)(2,1)} custom-call(f32[8,8,128]{2,1,0:T(8,128)S(1)} %all_to_all.5.norms, f32[16,64,256]{2,1,0:T(8,128)S(1)} %get-tuple-element.59.updated, bf16[16,64,256]{2,1,0:T(8,128)(2,1)S(1)} %copy-done.1), custom_call_target="tpu_custom_call" | custom-call | flops 1048576 | bytes 2097152 | tf_op jit(solution)/shard_map/pallas_call | solution.py:579
  (30 shorter events, 0.1 us)
Async XLA Ops:
  0.6 33.1 %copy-start = (bf16[16,64,256]{2,1,0:T(8,128)(2,1)S(1)}, bf16[16,64,256]{2,1,0:T(8,128)(2,1)}, u32[]{:S(2)}) copy-start(bf16[16,64,256]{2,1,0:T(8,128)(2,1)} %direction.3) | copy-start | bytes 1572868
  0.6 8.0 %collective-permute-start = (bf16[3,16,256]{2,1,0:T(8,128)(2,1)}, bf16[3,16,256]{2,1,0:T(8,128)(2,1)S(1)}, u32[]{:S(2)}, u32[]{:S(2)}) collective-permute-start(bf16[3,16,256]{2,1,0:T(8,128)(2,1)} %bitcast.5), channel_id=1, source_target_pairs={{0,2},{2,4},{4,6},{6,8},{8,10},{10,12},{12,14},{14,0},{1,3},{3,5},... | collective-permute-start | bytes 73736 | tf_op jit(solution)/shard_map/ppermute | solution.py:32
  3.6 5.1 %collective-permute-start.1 = (bf16[3,16,256]{2,1,0:T(8,128)(2,1)}, bf16[3,16,256]{2,1,0:T(8,128)(2,1)S(1)}, u32[]{:S(2)}, u32[]{:S(2)}) collective-permute-start(bf16[3,16,256]{2,1,0:T(8,128)(2,1)} %bitcast.6), channel_id=1, source_target_pairs={{0,14},{2,0},{4,2},{6,4},{8,6},{10,8},{12,10},{14,12},{1,15},{3,1}... | collective-permute-start | bytes 73736 | tf_op jit(solution)/shard_map/ppermute | solution.py:32
  8.7 25.1 %collective-permute-start.8 = (bf16[16,64,256]{2,1,0:T(8,128)(2,1)}, bf16[16,64,256]{2,1,0:T(8,128)(2,1)S(1)}, u32[]{:S(2)}, u32[]{:S(2)}) collective-permute-start(bf16[16,64,256]{2,1,0:T(8,128)(2,1)} %direction.3), channel_id=1, source_target_pairs={{0,14},{2,0},{4,2},{6,4},{8,6},{10,8},{12,10},{14,12},{1,15},{3,1}... | collective-permute-start | bytes 1572872 | tf_op jit(solution)/shard_map/ppermute | solution.py:32
  13.5 20.8 %collective-permute-start.2 = (bf16[16,64,256]{2,1,0:T(8,128)(2,1)}, bf16[16,64,256]{2,1,0:T(8,128)(2,1)S(1)}, u32[]{:S(2)}, u32[]{:S(2)}) collective-permute-start(bf16[16,64,256]{2,1,0:T(8,128)(2,1)} %direction.3), channel_id=1, source_target_pairs={{0,2},{2,4},{4,6},{6,8},{8,10},{10,12},{12,14},{14,0},{1,3},{3,5},... | collective-permute-start | bytes 1572872 | tf_op jit(solution)/shard_map/ppermute | solution.py:32
  24.3 9.3 %collective-permute-start.3 = (bf16[64,128]{1,0:T(8,128)(2,1)S(1)}, bf16[64,128]{1,0:T(8,128)(2,1)S(1)}, u32[]{:S(2)}, u32[]{:S(2)}) collective-permute-start(bf16[64,128]{1,0:T(8,128)(2,1)S(1)} %shard_map.144.refs_0_), channel_id=1, source_target_pairs={{0,4},{4,8},{8,12},{12,0},{1,5},{5,9},{9,13},{13,1},{2,6},{6,10},{... | collective-permute-start | bytes 49160 | tf_op jit(solution)/shard_map/ppermute | solution.py:32
  24.4 9.3 %collective-permute-start.4 = (bf16[64,128]{1,0:T(8,128)(2,1)S(1)}, bf16[64,128]{1,0:T(8,128)(2,1)S(1)}, u32[]{:S(2)}, u32[]{:S(2)}) collective-permute-start(bf16[64,128]{1,0:T(8,128)(2,1)S(1)} %shard_map.144.refs_0_), channel_id=1, source_target_pairs={{0,8},{4,12},{8,0},{12,4},{1,9},{5,13},{9,1},{13,5},{2,10},{6,14},... | collective-permute-start | bytes 49160 | tf_op jit(solution)/shard_map/ppermute | solution.py:32
  25.5 8.2 %collective-permute-start.5 = (bf16[64,128]{1,0:T(8,128)(2,1)S(1)}, bf16[64,128]{1,0:T(8,128)(2,1)S(1)}, u32[]{:S(2)}, u32[]{:S(2)}) collective-permute-start(bf16[64,128]{1,0:T(8,128)(2,1)S(1)} %shard_map.144.refs_0_), channel_id=1, source_target_pairs={{0,12},{4,0},{8,4},{12,8},{1,13},{5,1},{9,5},{13,9},{2,14},{6,2},{... | collective-permute-start | bytes 49160 | tf_op jit(solution)/shard_map/ppermute | solution.py:32
  33.7 5.4 %collective-permute-start.7 = (bf16[16,64,256]{2,1,0:T(8,128)(2,1)S(1)}, bf16[16,64,256]{2,1,0:T(8,128)(2,1)S(1)}, u32[]{:S(2)}, u32[]{:S(2)}) collective-permute-start(bf16[16,64,256]{2,1,0:T(8,128)(2,1)S(1)} %copy-done), channel_id=1, source_target_pairs={{0,1},{1,0},{2,3},{3,2},{4,5},{5,4},{6,7},{7,6},{8,9},{9,8},{10,11... | collective-permute-start | bytes 1572872 | tf_op jit(solution)/shard_map/ppermute | solution.py:36
  33.8 5.4 %collective-permute-start.9 = (bf16[16,64,256]{2,1,0:T(8,128)(2,1)S(1)}, bf16[16,64,256]{2,1,0:T(8,128)(2,1)S(1)}, u32[]{:S(2)}, u32[]{:S(2)}) collective-permute-start(bf16[16,64,256]{2,1,0:T(8,128)(2,1)S(1)} %collective-permute-done.8.refs_4_), channel_id=1, source_target_pairs={{0,1},{1,0},{2,3},{3,2},{4,5},{5,4},{6,7},{7,6},{8,9},{9,8},{10,11... | collective-permute-start | bytes 1572872 | tf_op jit(solution)/shard_map/ppermute | solution.py:36
  34.3 4.9 %collective-permute-start.6 = (bf16[16,64,256]{2,1,0:T(8,128)(2,1)S(1)}, bf16[16,64,256]{2,1,0:T(8,128)(2,1)S(1)}, u32[]{:S(2)}, u32[]{:S(2)}) collective-permute-start(bf16[16,64,256]{2,1,0:T(8,128)(2,1)S(1)} %collective-permute-done.2.refs_0_), channel_id=1, source_target_pairs={{0,1},{1,0},{2,3},{3,2},{4,5},{5,4},{6,7},{7,6},{8,9},{9,8},{10,11... | collective-permute-start | bytes 1572872 | tf_op jit(solution)/shard_map/ppermute | solution.py:36
  34.4 10.0 %collective-permute-start.10 = (bf16[8,64,128]{2,1,0:T(8,128)(2,1)S(1)}, bf16[8,64,128]{2,1,0:T(8,128)(2,1)S(1)}, u32[]{:S(2)}, u32[]{:S(2)}) collective-permute-start(bf16[8,64,128]{2,1,0:T(8,128)(2,1)S(1)} %get-tuple-element.50), channel_id=1, source_target_pairs={{0,2},{2,4},{4,6},{6,8},{8,10},{10,12},{12,14},{14,0},{1,3},{3,5},... | collective-permute-start | bytes 393224 | tf_op jit(solution)/shard_map/ppermute | solution.py:32
  36.4 9.1 %collective-permute-start.11 = (bf16[8,64,128]{2,1,0:T(8,128)(2,1)S(1)}, bf16[8,64,128]{2,1,0:T(8,128)(2,1)S(1)}, u32[]{:S(2)}, u32[]{:S(2)}) collective-permute-start(bf16[8,64,128]{2,1,0:T(8,128)(2,1)S(1)} %get-tuple-element.50), channel_id=1, source_target_pairs={{0,14},{2,0},{4,2},{6,4},{8,6},{10,8},{12,10},{14,12},{1,15},{3,1}... | collective-permute-start | bytes 393224 | tf_op jit(solution)/shard_map/ppermute | solution.py:32
  39.1 8.1 %collective-permute-start.12 = (bf16[4,64,128]{2,1,0:T(8,128)(2,1)S(1)}, bf16[4,64,128]{2,1,0:T(8,128)(2,1)S(1)}, u32[]{:S(2)}, u32[]{:S(2)}) collective-permute-start(bf16[4,64,128]{2,1,0:T(8,128)(2,1)S(1)} %shard_map.148.refs_0_), channel_id=1, source_target_pairs={{0,2},{2,0},{1,3},{3,1},{4,6},{6,4},{5,7},{7,5},{8,10},{10,8},{9,1... | collective-permute-start | bytes 196616 | tf_op jit(solution)/shard_map/ppermute | solution.py:32
  39.2 6.5 %copy-start.2 = (bf16[16,8,64,64]{3,2,1,0:T(8,128)(2,1)S(1)}, bf16[16,8,64,64]{3,2,1,0:T(8,128)(2,1)}, u32[]{:S(2)}) copy-start(bf16[16,8,64,64]{3,2,1,0:T(8,128)(2,1)} %coupling.1) | copy-start | bytes 3145732
  39.2 8.2 %copy-start.1 = (bf16[16,64,256]{2,1,0:T(8,128)(2,1)S(1)}, bf16[16,64,256]{2,1,0:T(8,128)(2,1)}, u32[]{:S(2)}) copy-start(bf16[16,64,256]{2,1,0:T(8,128)(2,1)} %direction.3) | copy-start | bytes 1572868
  39.3 8.2 %copy-start.4 = (bf16[16,64,64]{2,1,0:T(8,128)(2,1)S(1)}, bf16[16,64,64]{2,1,0:T(8,128)(2,1)}, u32[]{:S(2)}) copy-start(bf16[16,64,64]{2,1,0:T(8,128)(2,1)} %leaf_transfer.1) | copy-start | bytes 393220
  39.3 8.2 %copy-start.5 = (bf16[16,64,256]{2,1,0:T(8,128)(2,1)S(1)}, bf16[16,64,256]{2,1,0:T(8,128)(2,1)}, u32[]{:S(2)}) copy-start(bf16[16,64,256]{2,1,0:T(8,128)(2,1)} %get-tuple-element.54.natural) | copy-start | bytes 1572868
  39.3 8.2 %copy-start.6 = (bf16[1,64,64]{2,1,0:T(8,128)(2,1)S(1)}, bf16[1,64,64]{2,1,0:T(8,128)(2,1)}, u32[]{:S(2)}) copy-start(bf16[1,64,64]{2,1,0:T(8,128)(2,1)} %node_transfer.1) | copy-start | bytes 24580
  39.3 8.2 %copy-start.7 = (bf16[1,4,64,64]{3,2,1,0:T(8,128)(2,1)S(1)}, bf16[1,4,64,64]{3,2,1,0:T(8,128)(2,1)}, u32[]{:S(2)}) copy-start(bf16[1,4,64,64]{3,2,1,0:T(8,128)(2,1)} %top_coupling.1) | copy-start | bytes 98308
  39.3 8.2 %copy-start.8 = (s32[1,4]{1,0:T(1,128)S(1)}, s32[1,4]{1,0:T(1,128)}, u32[]{:S(2)}) copy-start(s32[1,4]{1,0:T(1,128)} %top_list.1) | copy-start | bytes 52
  44.3 4.9 %copy-start.3 = (f32[16,64,256]{2,1,0:T(8,128)S(1)}, f32[16,64,256]{2,1,0:T(8,128)}, u32[]{:S(2)}) copy-start(f32[16,64,256]{2,1,0:T(8,128)} %residual.1) | copy-start | bytes 3145732
  44.4 4.9 %copy-start.9 = (f32[64]{0:T(128)S(1)}, f32[64]{0:T(128)}, u32[]{:S(2)}) copy-start(f32[64]{0:T(128)} %param.15) | copy-start | bytes 772
  47.4 1.9 %collective-permute-start.13 = (bf16[8,64,256]{2,1,0:T(8,128)(2,1)S(1)}, bf16[8,64,256]{2,1,0:T(8,128)(2,1)S(1)}, u32[]{:S(2)}, u32[]{:S(2)}) collective-permute-start(bf16[8,64,256]{2,1,0:T(8,128)(2,1)S(1)} %get-tuple-element.56), channel_id=1, source_target_pairs={{0,1},{1,0},{2,3},{3,2},{4,5},{5,4},{6,7},{7,6},{8,9},{9,8},{10,11... | collective-permute-start | bytes 786440 | tf_op jit(solution)/shard_map/ppermute | solution.py:36

commit v15 on v14

--- a/solution.py
+++ b/solution.py
@@ -226,19 +226,18 @@
     sent[...] = given[...]
 
 
-def window_kernel(given, before, after, window, sent):
+def couple_kernel(
+    given, before, after, coupling, list_h, part, sent, window, coupling_list, sem
+):
+    copy = pltpu.make_async_copy(list_h, coupling_list, sem)
+    copy.start()
     sent[...] = given[...]
     rows, _, lanes = before.shape
     rank = lanes // 2
     for side, packed in enumerate((before, after)):
         for g in range(2 * rows):
-            part = packed[g // 2, :, (g % 2) * rank : (g % 2 + 1) * rank]
-            window[side * 2 * rows + g] = part
-
-
-def couple_kernel(window, coupling, list_h, part, coupling_list, sem):
-    copy = pltpu.make_async_copy(list_h, coupling_list, sem)
-    copy.start()
+            piece = packed[g // 2, :, (g % 2) * rank : (g % 2 + 1) * rank]
+            window[side * 2 * rows + g] = piece
     leaves, count = coupling.shape[:2]
     total = leaves * lax.axis_size("blk") * lax.axis_size("leaf")
     device = lax.axis_index("blk") * lax.axis_size("leaf") + lax.axis_index("leaf")
@@ -512,28 +511,20 @@
         tiles_high,
     )
 
-    coef_window, given = call(
-        window_kernel,
-        (shape((2 * leaves, samples, rank), BF), shape((half, samples, points), BF)),
-        MIB,
-        MIB,
-        in_specs=[vmem] * 3,
-        out_specs=(vmem, vmem),
-        vmem=4,
-    )(given, coef_prev, coef_after)
-    part = call(
+    part, given = call(
         couple_kernel,
-        shape((leaves, samples, rank), F32),
+        (shape((leaves, samples, rank), F32), shape((half, samples, points), BF)),
         2 * leaves * samples * rank * rank * 8,
         4 * MIB,
-        in_specs=[vmem] * 2 + [hbm],
-        out_specs=vmem,
+        in_specs=[vmem] * 4 + [hbm],
+        out_specs=(vmem, vmem),
         scratch_shapes=[
+            pltpu.VMEM((2 * leaves, samples, rank), BF),
             pltpu.SMEM(coupling_list.shape[::-1], jnp.int32),
             pltpu.SemaphoreType.DMA,
         ],
         vmem=8,
-    )(coef_window, coupling, *in_hbm(coupling_list.T))
+    )(given, coef_prev, coef_after, coupling, *in_hbm(coupling_list.T))
     tops, given = call(
         top_kernel,
         (shape((blk_count, samples, rank), BF), shape((half, samples, points), BF)),

time: 61.6 us -> 61.4 us (level)
    pallas_call x2 -> x1, Pallas kernels: 1.72 us -> 1.54 us  [on_device(): call(couple_kernel, (shape((leaves, samples, rank), F32), shape((half, sa...]
where the time goes in v15:
time: 61.4 us; the launch traced here: 61 us
  Pallas kernels  28.3 us (46%)
  starting transfers between devices  20.2 us (33%)
  blocking collectives  9.75 us (16%)
  waiting for transfers between devices  1.77 us (3%)
  between operations  0.96 us (2%)
    ppermute x10, starting transfers between devices, shifted(): lax.ppermute(array, axis, [(i, (i + by) % count) for i in range(count)])  19.5 us
    pallas_call x2, Pallas kernels, make_tiles(): call(functools.partial(tile_kernel, start), outs, 40 * count * entries *...  12 us
    all_to_all x1, blocking collectives, on_device(): norms = lax.all_to_all(norms, RING, 0, 0)  9.75 us
    pallas_call x1, Pallas kernels, on_device(): call(near_kernel, (shape((half, samples, points), F32), shape((half, samp...  5.02 us
    pallas_call x1, Pallas kernels, on_device(): call(up_kernel, (pltpu.HBM((leaves, rank, points), BF), shape((leaves //...  4.24 us
    pallas_call x1, Pallas kernels, on_device(): call(down_kernel, shape((leaves, samples, points), F32), 2 * leaves * sam...  1.77 us
    ppermute x10, waiting for transfers between devices, shifted(): lax.ppermute(array, axis, [(i, (i + by) % count) for i in range(count)])  1.76 us
    pallas_call x1, Pallas kernels, on_device(): call(couple_kernel, (shape((leaves, samples, rank), F32), shape((half, sa...  1.54 us
  transfers between devices with their start and end apart: 14, of which 2 were waited for; matrix products, arithmetic and copies ran while one was open for 0% of the time, Pallas kernels for 43%

profile of v15, /device:TPU:0, one launch (start us, length us, event | category | flops | bytes accessed | tf_op | source)
XLA Modules:
  0.0 61.0 jit_solution(2141649522946185637)
XLA Ops:
  0.6 3.0 %collective-permute-start = (bf16[3,16,256]{2,1,0:T(8,128)(2,1)}, bf16[3,16,256]{2,1,0:T(8,128)(2,1)S(1)}, u32[]{:S(2)}, u32[]{:S(2)}) collective-permute-start(bf16[3,16,256]{2,1,0:T(8,128)(2,1)} %bitcast.5), channel_id=1, source_target_pairs={{0,2},{2,4},{4,6},{6,8},{8,10},{10,12},{12,14},{14,0},{1,3},{3,5},... | collective-permute-start | bytes 73736 | tf_op jit(solution)/shard_map/ppermute | solution.py:32
  3.6 3.1 %collective-permute-start.1 = (bf16[3,16,256]{2,1,0:T(8,128)(2,1)}, bf16[3,16,256]{2,1,0:T(8,128)(2,1)S(1)}, u32[]{:S(2)}, u32[]{:S(2)}) collective-permute-start(bf16[3,16,256]{2,1,0:T(8,128)(2,1)} %bitcast.6), channel_id=1, source_target_pairs={{0,14},{2,0},{4,2},{6,4},{8,6},{10,8},{12,10},{14,12},{1,15},{3,1}... | collective-permute-start | bytes 73736 | tf_op jit(solution)/shard_map/ppermute | solution.py:32
  6.7 1.3 %shard_map.140 = (s32[16,256]{1,0:T(8,128)S(1)}, bf16[16,64,256]{2,1,0:T(8,128)(2,1)S(1)}, bf16[16,64,256]{2,1,0:T(8,128)(2,1)S(1)}, bf16[16,64,64]{2,1,0:T(8,128)(2,1)S(1)}, bf16[1,64,64]{2,1,0:T(8,128)(2,1)S(1)}) custom-call(s32[16,256]{1,0:T(8,128)} %refs_0_.1, bf16[16,64,256]{2,1,0:T(8,128)(2,1)} %refs_1_.1, bf16[16,64,256]{2,1,0:T(8,128)(2,1)} %direction.3, ...), custom_call_target="tpu_custom_call" | custom-call | flops 1048576 | bytes 2097152 | tf_op jit(solution)/shard_map/pallas_call | solution.py:409
  8.1 0.6 %collective-permute-done.refs_1_ = bf16[3,16,256]{2,1,0:T(8,128)(2,1)S(1)} collective-permute-done((bf16[3,16,256]{2,1,0:T(8,128)(2,1)}, bf16[3,16,256]{2,1,0:T(8,128)(2,1)S(1)}, u32[]{:S(2)}, u32[]{:S(2)}) %collective-permute-start) | collective-permute-done | bytes 24608 | tf_op jit(solution)/shard_map/ppermute | solution.py:32
  8.7 4.8 %collective-permute-start.8 = (bf16[16,64,256]{2,1,0:T(8,128)(2,1)}, bf16[16,64,256]{2,1,0:T(8,128)(2,1)S(1)}, u32[]{:S(2)}, u32[]{:S(2)}) collective-permute-start(bf16[16,64,256]{2,1,0:T(8,128)(2,1)} %direction.3), channel_id=1, source_target_pairs={{0,14},{2,0},{4,2},{6,4},{8,6},{10,8},{12,10},{14,12},{1,15},{3,1}... | collective-permute-start | bytes 1572872 | tf_op jit(solution)/shard_map/ppermute | solution.py:32
  13.5 4.2 %shard_map.141 = (bf16[16,64,256]{2,1,0:T(8,128)(2,1)}, bf16[8,64,128]{2,1,0:T(8,128)(2,1)S(1)}, f32[64,64]{1,0:T(8,128)S(1)}, f32[8,128]{1,0:T(8,128)S(1)}) custom-call(s32[16,256]{1,0:T(8,128)S(1)} %get-tuple-element.33.order, bf16[16,64,256]{2,1,0:T(8,128)(2,1)S(1)} %get-tuple-element.34.basis, bf16[16,64,256]{2,1,0:T(8,128)(2,1)S(1)} %get-tuple-element.35.direction, ...), custom_call_target="tpu_custom_call" | custom-call | flops 268435456 | bytes 6291456 | tf_op jit(solution)/shard_map/pallas_call | solution.py:422
  17.7 6.5 %shard_map.142 = (bf16[4,3072,256]{2,1,0:T(8,128)(2,1)S(1)}, f32[8,128]{1,0:T(8,128)S(1)}, bf16[48,256,128]{2,1,0:T(8,128)(2,1)S(1)}, f32[3,16,256]{2,1,0:T(8,128)S(1)}) custom-call(s32[16,12]{1,0:T(8,128)} %near_h.5, f32[8,128]{1,0:T(8,128)S(1)} %get-tuple-element.38._, bf16[3,16,256]{2,1,0:T(8,128)(2,1)} %bitcast.7, ...), custom_call_target="tpu_custom_call" | custom-call | flops 125829120 | bytes 50331648 | tf_op jit(solution)/shard_map/pallas_call | solution.py:443
  24.3 0.1 shard_map.144.refs_0_
  24.3 0.0 collective-permute-start.3
  24.4 1.1 %collective-permute-start.4 = (bf16[64,128]{1,0:T(8,128)(2,1)S(1)}, bf16[64,128]{1,0:T(8,128)(2,1)S(1)}, u32[]{:S(2)}, u32[]{:S(2)}) collective-permute-start(bf16[64,128]{1,0:T(8,128)(2,1)S(1)} %shard_map.144.refs_0_), channel_id=1, source_target_pairs={{0,8},{4,12},{8,0},{12,4},{1,9},{5,13},{9,1},{13,5},{2,10},{6,14},... | collective-permute-start | bytes 49160 | tf_op jit(solution)/shard_map/ppermute | solution.py:32
  25.5 2.7 %collective-permute-start.5 = (bf16[64,128]{1,0:T(8,128)(2,1)S(1)}, bf16[64,128]{1,0:T(8,128)(2,1)S(1)}, u32[]{:S(2)}, u32[]{:S(2)}) collective-permute-start(bf16[64,128]{1,0:T(8,128)(2,1)S(1)} %shard_map.144.refs_0_), channel_id=1, source_target_pairs={{0,12},{4,0},{8,4},{12,8},{1,13},{5,1},{9,5},{13,9},{2,14},{6,2},{... | collective-permute-start | bytes 49160 | tf_op jit(solution)/shard_map/ppermute | solution.py:32
  28.2 5.5 %shard_map.143 = (bf16[4,3072,256]{2,1,0:T(8,128)(2,1)S(1)}, f32[8,128]{1,0:T(8,128)}) custom-call(s32[16,12]{1,0:T(8,128)} %near_h.5, f32[8,128]{1,0:T(8,128)S(1)} %get-tuple-element.39._, f32[3,16,256]{2,1,0:T(8,128)S(1)} %get-tuple-element.40.refs_0_, bf16[48,256,128]{2,1,0:T(8,128)(2,1)S(1)} %get-tuple-element.41.refs_1_), custom_call_target="tpu_custom_call" | custom-call | flops 125829120 | bytes 3145728 | tf_op jit(solution)/shard_map/pallas_call | solution.py:443
  33.7 0.1 collective-permute-start.7
  33.8 0.5 collective-permute-start.9
  34.3 0.1 collective-permute-start.6
  34.4 2.0 %collective-permute-start.10 = (bf16[8,64,128]{2,1,0:T(8,128)(2,1)S(1)}, bf16[8,64,128]{2,1,0:T(8,128)(2,1)S(1)}, u32[]{:S(2)}, u32[]{:S(2)}) collective-permute-start(bf16[8,64,128]{2,1,0:T(8,128)(2,1)S(1)} %get-tuple-element.50), channel_id=1, source_target_pairs={{0,2},{2,4},{4,6},{6,8},{8,10},{10,12},{12,14},{14,0},{1,3},{3,5},... | collective-permute-start | bytes 393224 | tf_op jit(solution)/shard_map/ppermute | solution.py:32
  36.4 2.7 %collective-permute-start.11 = (bf16[8,64,128]{2,1,0:T(8,128)(2,1)S(1)}, bf16[8,64,128]{2,1,0:T(8,128)(2,1)S(1)}, u32[]{:S(2)}, u32[]{:S(2)}) collective-permute-start(bf16[8,64,128]{2,1,0:T(8,128)(2,1)S(1)} %get-tuple-element.50), channel_id=1, source_target_pairs={{0,14},{2,0},{4,2},{6,4},{8,6},{10,8},{12,10},{14,12},{1,15},{3,1}... | collective-permute-start | bytes 393224 | tf_op jit(solution)/shard_map/ppermute | solution.py:32
  39.1 0.1 collective-permute-start.12
  39.3 0.0 copy-start.4
  39.3 0.0 copy-start.5
  39.3 0.0 copy-start.8
  39.3 5.0 %shard_map.145 = (f32[8,64,256]{2,1,0:T(8,128)S(1)}, bf16[8,64,256]{2,1,0:T(8,128)(2,1)S(1)}, f32[8,128]{1,0:T(8,128)}) custom-call(s32[16,12]{1,0:T(8,128)} %near_h.5, bf16[16,64,256]{2,1,0:T(8,128)(2,1)S(1)} %collective-permute-done.2.refs_0_, bf16[16,64,256]{2,1,0:T(8,128)(2,1)S(1)} %collective-permute-done.6.refs_1_, bf16[16,64,256]{2,1,0:T(8,128)(2,1)} %direction.3, ...), custom_call_target="tpu_custom_call" | custom-call | flops 1048576 | bytes 1048576 | tf_op jit(solution)/shard_map/pallas_call | solution.py:489
  44.3 0.0 copy-start.3
  44.4 0.0 copy-start.9
  44.4 1.1 %collective-permute-done.11.after = bf16[8,64,128]{2,1,0:T(8,128)(2,1)S(1)} collective-permute-done((bf16[8,64,128]{2,1,0:T(8,128)(2,1)S(1)}, bf16[8,64,128]{2,1,0:T(8,128)(2,1)S(1)}, u32[]{:S(2)}, u32[]{:S(2)}) %collective-permute-start.11) | collective-permute-done | bytes 131104 | tf_op jit(solution)/shard_map/ppermute | solution.py:32
  45.5 1.5 %shard_map.146 = (f32[16,64,64]{2,1,0:T(8,128)S(1)}, bf16[8,64,256]{2,1,0:T(8,128)(2,1)S(1)}) custom-call(bf16[8,64,256]{2,1,0:T(8,128)(2,1)S(1)} %get-tuple-element.49.given, bf16[8,64,128]{2,1,0:T(8,128)(2,1)S(1)} %collective-permute-done.10.before, bf16[8,64,128]{2,1,0:T(8,128)(2,1)S(1)} %collective-permute-done.11.after, ...), custom_call_target="tpu_custom_call" | custom-call | flops 67108864 | bytes 4194304 | tf_op jit(solution)/shard_map/pallas_call | solution.py:514
  47.1 0.1 shard_map.148
  47.2 0.1 collective-permute-start.13
  47.3 1.8 %shard_map.149.base = f32[16,64,256]{2,1,0:T(8,128)S(1)} custom-call(bf16[4,64,64]{2,1,0:T(8,128)(2,1)S(1)} %get-tuple-element.53.tops, f32[16,64,64]{2,1,0:T(8,128)S(1)} %get-tuple-element.51._.part, bf16[16,64,64]{2,1,0:T(8,128)(2,1)S(1)} %copy-done.4, bf16[16,64,256]{2,1,0:T(8,128)(2,1)S(1)} %copy-done.5, bf16[16,64,256]{2,1,0:T(8,128)(2,1)S(1)} %copy-done.1, ...), custom_call_target="tpu_custom_call" | custom-call | flops 41943040 | bytes 4194304 | tf_op jit(solution)/shard_map/pallas_call | solution.py:537
  49.1 1.2 %shard_map.150 = (f32[16,64,256]{2,1,0:T(8,128)}, f32[16,64,256]{2,1,0:T(8,128)S(1)}, f32[8,8,128]{2,1,0:T(8,128)S(1)}) custom-call(f32[1,64]{1,0:T(1,128)S(1)} %bitcast.3, f32[16,64,256]{2,1,0:T(8,128)S(1)} %shard_map.149.base, f32[8,64,256]{2,1,0:T(8,128)S(1)} %get-tuple-element.55.kept, bf16[8,64,256]{2,1,0:T(8,128)(2,1)S(1)} %collective-permute-done.13.received, ...), custom_call_target="tpu_custom_call" | custom-call | flops 4194304 | bytes 5242880 | tf_op jit(solution)/shard_map/pallas_call | solution.py:559
  50.4 9.7 %all_to_all.5.norms = f32[8,8,128]{2,1,0:T(8,128)S(1)} all-to-all(f32[8,8,128]{2,1,0:T(8,128)S(1)} %get-tuple-element.58), channel_id=1, replica_groups=mesh['groups'=2,'blk'=4,'leaf'=2,'sample'=2] {'blk','leaf'}, dimensions={0} | all-to-all | bytes 65536 | tf_op jit(solution)/shard_map/all_to_all | solution.py:569
  60.1 0.9 %shard_map.151 = bf16[16,64,256]{2,1,0:T(8,128)(2,1)} custom-call(f32[8,8,128]{2,1,0:T(8,128)S(1)} %all_to_all.5.norms, f32[16,64,256]{2,1,0:T(8,128)S(1)} %get-tuple-element.59.updated, bf16[16,64,256]{2,1,0:T(8,128)(2,1)S(1)} %copy-done.1), custom_call_target="tpu_custom_call" | custom-call | flops 1048576 | bytes 2097152 | tf_op jit(solution)/shard_map/pallas_call | solution.py:570
  (29 shorter events, 0.1 us)
Async XLA Ops:
  0.6 33.1 %copy-start = (bf16[16,64,256]{2,1,0:T(8,128)(2,1)S(1)}, bf16[16,64,256]{2,1,0:T(8,128)(2,1)}, u32[]{:S(2)}) copy-start(bf16[16,64,256]{2,1,0:T(8,128)(2,1)} %direction.3) | copy-start | bytes 1572868
  0.6 8.0 %collective-permute-start = (bf16[3,16,256]{2,1,0:T(8,128)(2,1)}, bf16[3,16,256]{2,1,0:T(8,128)(2,1)S(1)}, u32[]{:S(2)}, u32[]{:S(2)}) collective-permute-start(bf16[3,16,256]{2,1,0:T(8,128)(2,1)} %bitcast.5), channel_id=1, source_target_pairs={{0,2},{2,4},{4,6},{6,8},{8,10},{10,12},{12,14},{14,0},{1,3},{3,5},... | collective-permute-start | bytes 73736 | tf_op jit(solution)/shard_map/ppermute | solution.py:32
  3.6 5.1 %collective-permute-start.1 = (bf16[3,16,256]{2,1,0:T(8,128)(2,1)}, bf16[3,16,256]{2,1,0:T(8,128)(2,1)S(1)}, u32[]{:S(2)}, u32[]{:S(2)}) collective-permute-start(bf16[3,16,256]{2,1,0:T(8,128)(2,1)} %bitcast.6), channel_id=1, source_target_pairs={{0,14},{2,0},{4,2},{6,4},{8,6},{10,8},{12,10},{14,12},{1,15},{3,1}... | collective-permute-start | bytes 73736 | tf_op jit(solution)/shard_map/ppermute | solution.py:32
  8.7 25.1 %collective-permute-start.8 = (bf16[16,64,256]{2,1,0:T(8,128)(2,1)}, bf16[16,64,256]{2,1,0:T(8,128)(2,1)S(1)}, u32[]{:S(2)}, u32[]{:S(2)}) collective-permute-start(bf16[16,64,256]{2,1,0:T(8,128)(2,1)} %direction.3), channel_id=1, source_target_pairs={{0,14},{2,0},{4,2},{6,4},{8,6},{10,8},{12,10},{14,12},{1,15},{3,1}... | collective-permute-start | bytes 1572872 | tf_op jit(solution)/shard_map/ppermute | solution.py:32
  13.5 20.8 %collective-permute-start.2 = (bf16[16,64,256]{2,1,0:T(8,128)(2,1)}, bf16[16,64,256]{2,1,0:T(8,128)(2,1)S(1)}, u32[]{:S(2)}, u32[]{:S(2)}) collective-permute-start(bf16[16,64,256]{2,1,0:T(8,128)(2,1)} %direction.3), channel_id=1, source_target_pairs={{0,2},{2,4},{4,6},{6,8},{8,10},{10,12},{12,14},{14,0},{1,3},{3,5},... | collective-permute-start | bytes 1572872 | tf_op jit(solution)/shard_map/ppermute | solution.py:32
  24.3 9.3 %collective-permute-start.3 = (bf16[64,128]{1,0:T(8,128)(2,1)S(1)}, bf16[64,128]{1,0:T(8,128)(2,1)S(1)}, u32[]{:S(2)}, u32[]{:S(2)}) collective-permute-start(bf16[64,128]{1,0:T(8,128)(2,1)S(1)} %shard_map.144.refs_0_), channel_id=1, source_target_pairs={{0,4},{4,8},{8,12},{12,0},{1,5},{5,9},{9,13},{13,1},{2,6},{6,10},{... | collective-permute-start | bytes 49160 | tf_op jit(solution)/shard_map/ppermute | solution.py:32
  24.4 9.3 %collective-permute-start.4 = (bf16[64,128]{1,0:T(8,128)(2,1)S(1)}, bf16[64,128]{1,0:T(8,128)(2,1)S(1)}, u32[]{:S(2)}, u32[]{:S(2)}) collective-permute-start(bf16[64,128]{1,0:T(8,128)(2,1)S(1)} %shard_map.144.refs_0_), channel_id=1, source_target_pairs={{0,8},{4,12},{8,0},{12,4},{1,9},{5,13},{9,1},{13,5},{2,10},{6,14},... | collective-permute-start | bytes 49160 | tf_op jit(solution)/shard_map/ppermute | solution.py:32
  25.5 8.2 %collective-permute-start.5 = (bf16[64,128]{1,0:T(8,128)(2,1)S(1)}, bf16[64,128]{1,0:T(8,128)(2,1)S(1)}, u32[]{:S(2)}, u32[]{:S(2)}) collective-permute-start(bf16[64,128]{1,0:T(8,128)(2,1)S(1)} %shard_map.144.refs_0_), channel_id=1, source_target_pairs={{0,12},{4,0},{8,4},{12,8},{1,13},{5,1},{9,5},{13,9},{2,14},{6,2},{... | collective-permute-start | bytes 49160 | tf_op jit(solution)/shard_map/ppermute | solution.py:32
  33.7 5.4 %collective-permute-start.7 = (bf16[16,64,256]{2,1,0:T(8,128)(2,1)S(1)}, bf16[16,64,256]{2,1,0:T(8,128)(2,1)S(1)}, u32[]{:S(2)}, u32[]{:S(2)}) collective-permute-start(bf16[16,64,256]{2,1,0:T(8,128)(2,1)S(1)} %copy-done), channel_id=1, source_target_pairs={{0,1},{1,0},{2,3},{3,2},{4,5},{5,4},{6,7},{7,6},{8,9},{9,8},{10,11... | collective-permute-start | bytes 1572872 | tf_op jit(solution)/shard_map/ppermute | solution.py:36
  33.8 5.4 %collective-permute-start.9 = (bf16[16,64,256]{2,1,0:T(8,128)(2,1)S(1)}, bf16[16,64,256]{2,1,0:T(8,128)(2,1)S(1)}, u32[]{:S(2)}, u32[]{:S(2)}) collective-permute-start(bf16[16,64,256]{2,1,0:T(8,128)(2,1)S(1)} %collective-permute-done.8.refs_4_), channel_id=1, source_target_pairs={{0,1},{1,0},{2,3},{3,2},{4,5},{5,4},{6,7},{7,6},{8,9},{9,8},{10,11... | collective-permute-start | bytes 1572872 | tf_op jit(solution)/shard_map/ppermute | solution.py:36
  34.3 4.9 %collective-permute-start.6 = (bf16[16,64,256]{2,1,0:T(8,128)(2,1)S(1)}, bf16[16,64,256]{2,1,0:T(8,128)(2,1)S(1)}, u32[]{:S(2)}, u32[]{:S(2)}) collective-permute-start(bf16[16,64,256]{2,1,0:T(8,128)(2,1)S(1)} %collective-permute-done.2.refs_0_), channel_id=1, source_target_pairs={{0,1},{1,0},{2,3},{3,2},{4,5},{5,4},{6,7},{7,6},{8,9},{9,8},{10,11... | collective-permute-start | bytes 1572872 | tf_op jit(solution)/shard_map/ppermute | solution.py:36
  34.4 10.0 %collective-permute-start.10 = (bf16[8,64,128]{2,1,0:T(8,128)(2,1)S(1)}, bf16[8,64,128]{2,1,0:T(8,128)(2,1)S(1)}, u32[]{:S(2)}, u32[]{:S(2)}) collective-permute-start(bf16[8,64,128]{2,1,0:T(8,128)(2,1)S(1)} %get-tuple-element.50), channel_id=1, source_target_pairs={{0,2},{2,4},{4,6},{6,8},{8,10},{10,12},{12,14},{14,0},{1,3},{3,5},... | collective-permute-start | bytes 393224 | tf_op jit(solution)/shard_map/ppermute | solution.py:32
  36.4 9.1 %collective-permute-start.11 = (bf16[8,64,128]{2,1,0:T(8,128)(2,1)S(1)}, bf16[8,64,128]{2,1,0:T(8,128)(2,1)S(1)}, u32[]{:S(2)}, u32[]{:S(2)}) collective-permute-start(bf16[8,64,128]{2,1,0:T(8,128)(2,1)S(1)} %get-tuple-element.50), channel_id=1, source_target_pairs={{0,14},{2,0},{4,2},{6,4},{8,6},{10,8},{12,10},{14,12},{1,15},{3,1}... | collective-permute-start | bytes 393224 | tf_op jit(solution)/shard_map/ppermute | solution.py:32
  39.1 7.9 %collective-permute-start.12 = (bf16[4,64,128]{2,1,0:T(8,128)(2,1)S(1)}, bf16[4,64,128]{2,1,0:T(8,128)(2,1)S(1)}, u32[]{:S(2)}, u32[]{:S(2)}) collective-permute-start(bf16[4,64,128]{2,1,0:T(8,128)(2,1)S(1)} %shard_map.147.refs_0_), channel_id=1, source_target_pairs={{0,2},{2,0},{1,3},{3,1},{4,6},{6,4},{5,7},{7,5},{8,10},{10,8},{9,1... | collective-permute-start | bytes 196616 | tf_op jit(solution)/shard_map/ppermute | solution.py:32
  39.2 6.3 %copy-start.2 = (bf16[16,8,64,64]{3,2,1,0:T(8,128)(2,1)S(1)}, bf16[16,8,64,64]{3,2,1,0:T(8,128)(2,1)}, u32[]{:S(2)}) copy-start(bf16[16,8,64,64]{3,2,1,0:T(8,128)(2,1)} %coupling.1) | copy-start | bytes 3145732
  39.2 8.0 %copy-start.1 = (bf16[16,64,256]{2,1,0:T(8,128)(2,1)S(1)}, bf16[16,64,256]{2,1,0:T(8,128)(2,1)}, u32[]{:S(2)}) copy-start(bf16[16,64,256]{2,1,0:T(8,128)(2,1)} %direction.3) | copy-start | bytes 1572868
  39.3 8.0 %copy-start.4 = (bf16[16,64,64]{2,1,0:T(8,128)(2,1)S(1)}, bf16[16,64,64]{2,1,0:T(8,128)(2,1)}, u32[]{:S(2)}) copy-start(bf16[16,64,64]{2,1,0:T(8,128)(2,1)} %leaf_transfer.1) | copy-start | bytes 393220
  39.3 8.0 %copy-start.5 = (bf16[16,64,256]{2,1,0:T(8,128)(2,1)S(1)}, bf16[16,64,256]{2,1,0:T(8,128)(2,1)}, u32[]{:S(2)}) copy-start(bf16[16,64,256]{2,1,0:T(8,128)(2,1)} %get-tuple-element.54.natural) | copy-start | bytes 1572868
  39.3 8.0 %copy-start.6 = (bf16[1,64,64]{2,1,0:T(8,128)(2,1)S(1)}, bf16[1,64,64]{2,1,0:T(8,128)(2,1)}, u32[]{:S(2)}) copy-start(bf16[1,64,64]{2,1,0:T(8,128)(2,1)} %node_transfer.1) | copy-start | bytes 24580
  39.3 8.0 %copy-start.7 = (bf16[1,4,64,64]{3,2,1,0:T(8,128)(2,1)S(1)}, bf16[1,4,64,64]{3,2,1,0:T(8,128)(2,1)}, u32[]{:S(2)}) copy-start(bf16[1,4,64,64]{3,2,1,0:T(8,128)(2,1)} %top_coupling.1) | copy-start | bytes 98308
  39.3 8.0 %copy-start.8 = (s32[1,4]{1,0:T(1,128)S(1)}, s32[1,4]{1,0:T(1,128)}, u32[]{:S(2)}) copy-start(s32[1,4]{1,0:T(1,128)} %top_list.1) | copy-start | bytes 52
  44.3 4.7 %copy-start.3 = (f32[16,64,256]{2,1,0:T(8,128)S(1)}, f32[16,64,256]{2,1,0:T(8,128)}, u32[]{:S(2)}) copy-start(f32[16,64,256]{2,1,0:T(8,128)} %residual.1) | copy-start | bytes 3145732
  44.4 4.7 %copy-start.9 = (f32[64]{0:T(128)S(1)}, f32[64]{0:T(128)}, u32[]{:S(2)}) copy-start(f32[64]{0:T(128)} %param.15) | copy-start | bytes 772
  47.2 1.9 %collective-permute-start.13 = (bf16[8,64,256]{2,1,0:T(8,128)(2,1)S(1)}, bf16[8,64,256]{2,1,0:T(8,128)(2,1)S(1)}, u32[]{:S(2)}, u32[]{:S(2)}) collective-permute-start(bf16[8,64,256]{2,1,0:T(8,128)(2,1)S(1)} %get-tuple-element.56), channel_id=1, source_target_pairs={{0,1},{1,0},{2,3},{3,2},{4,5},{5,4},{6,7},{7,6},{8,9},{9,8},{10,11... | collective-permute-start | bytes 786440 | tf_op jit(solution)/shard_map/ppermute | solution.py:36

commit v16 on v15

--- a/solution.py
+++ b/solution.py
@@ -143,7 +143,9 @@
 
 def tile_kernel(start, near_h, _, *refs):
     if start == 0:
-        own_h, prev, after, tiles, mark, spread_x, plain, own, near, sem = refs
+        own_h, prev, after, tiles, mark, spread_x, plain, listing, own, near, sem = refs
+        handed = pltpu.make_async_copy(near_h, listing, sem.at[2])
+        handed.start()
         offered = pltpu.make_async_copy(own_h, own, sem.at[1])
         offered.start()
     else:
@@ -161,6 +163,7 @@
     anchor = (device - 1) * leaves
     if start == 0:
         offered.wait()
+        handed.wait()
         for side, ref in enumerate((prev, own, after)):
             offsets = ref[...].astype(F32)
             for j in range(leaves):
@@ -435,27 +438,29 @@
         vmem=8,
     )(ordered(resident[0], coords_prev, coords_after), *resident[1:])
 
-    def make_tiles(start, done, *operands):
+    def make_tiles(start, listing, done, *operands):
         count = half // 2
         outs = (pltpu.VMEM((count, entries * points, points), BF), token)
         if start == 0:
             outs += (shape((3 * leaves, points, 128), BF), shape(coords.shape, F32))
+            outs += (shape(near_list.shape, jnp.int32),)
         return call(
             functools.partial(tile_kernel, start),
             outs,
             40 * count * entries * points * points,
             count * entries * points * points * (16 if start == 0 else 1),
-            in_specs=[hbm, anywhere, hbm if start == 0 else vmem] + [vmem] * (len(operands) - 1),
+            in_specs=([hbm, anywhere, hbm] if start == 0 else [vmem, anywhere, vmem])
+            + [vmem] * (len(operands) - 1),
             out_specs=(vmem,) * len(outs),
             scratch_shapes=[pltpu.VMEM(coords.shape, BF)] * (start == 0)
-            + [pltpu.SMEM(near_list.shape, jnp.int32), pltpu.SemaphoreType.DMA((2,))],
+            + [pltpu.SMEM(near_list.shape, jnp.int32), pltpu.SemaphoreType.DMA((3,))],
             vmem=8,
-        )(*in_hbm(near_list), done, *operands)
+        )(listing, done, *operands)
 
     coef_prev = shifted(coef, RING, 1)
     coef_after = shifted(coef, RING, -1)
-    tiles_low, low_mark, spread_x, plain = make_tiles(
-        0, up_mark, *in_hbm(coords), coords_prev, coords_after
+    tiles_low, low_mark, spread_x, plain, listing = make_tiles(
+        0, *in_hbm(near_list), up_mark, *in_hbm(coords), coords_prev, coords_after
     )
     leaving = call(
         after_kernel,
@@ -472,7 +477,7 @@
         others = lax.all_gather(leaving[None], "blk", axis=0, tiled=True)
         places = jnp.mod(lax.axis_index("blk") - jnp.arange(blk_count, dtype=jnp.int32), blk_count)
         others = list(others[places][1:])
-    tiles_high, high_mark = make_tiles(half // 2, low_mark, plain, spread_x)
+    tiles_high, high_mark = make_tiles(half // 2, listing, low_mark, plain, spread_x)
     direction_other = partner(ordered(direction, high_mark, *others))
     direction_prev = ordered(direction_prev, high_mark, *others)
     direction_after = ordered(direction_after, high_mark, *others)

time: 61.4 us -> 61.1 us (level)
  transfers between devices with their start and end apart: 14 -> 14, of which waited for: 2 -> 2; matrix products, arithmetic and copies ran while one was open for 0% -> 0% of each run, Pallas kernels for 43% -> 42%
where the time goes in v16:
time: 61.1 us; the launch traced here: 60.9 us
  Pallas kernels  28.1 us (46%)
  starting transfers between devices  20.2 us (33%)
  blocking collectives  9.75 us (16%)
  waiting for transfers between devices  1.76 us (3%)
  between operations  0.96 us (2%)
    ppermute x10, starting transfers between devices, shifted(): lax.ppermute(array, axis, [(i, (i + by) % count) for i in range(count)])  19.5 us
    pallas_call x2, Pallas kernels, make_tiles(): call(functools.partial(tile_kernel, start), outs, 40 * count * entries *...  11.9 us
    all_to_all x1, blocking collectives, on_device(): norms = lax.all_to_all(norms, RING, 0, 0)  9.75 us
    pallas_call x1, Pallas kernels, on_device(): call(near_kernel, (shape((half, samples, points), F32), shape((half, samp...  5.03 us
    pallas_call x1, Pallas kernels, on_device(): call(up_kernel, (pltpu.HBM((leaves, rank, points), BF), shape((leaves //...  4.24 us
    pallas_call x1, Pallas kernels, on_device(): call(down_kernel, shape((leaves, samples, points), F32), 2 * leaves * sam...  1.77 us
    ppermute x10, waiting for transfers between devices, shifted(): lax.ppermute(array, axis, [(i, (i + by) % count) for i in range(count)])  1.75 us
    pallas_call x1, Pallas kernels, on_device(): call(couple_kernel, (shape((leaves, samples, rank), F32), shape((half, sa...  1.54 us
  transfers between devices with their start and end apart: 14, of which 2 were waited for; matrix products, arithmetic and copies ran while one was open for 0% of the time, Pallas kernels for 42%

profile of v16, /device:TPU:0, one launch (start us, length us, event | category | flops | bytes accessed | tf_op | source)
XLA Modules:
  0.0 60.9 jit_solution(8861428117473738937)
XLA Ops:
  0.6 3.0 %collective-permute-start = (bf16[3,16,256]{2,1,0:T(8,128)(2,1)}, bf16[3,16,256]{2,1,0:T(8,128)(2,1)S(1)}, u32[]{:S(2)}, u32[]{:S(2)}) collective-permute-start(bf16[3,16,256]{2,1,0:T(8,128)(2,1)} %bitcast.5), channel_id=1, source_target_pairs={{0,2},{2,4},{4,6},{6,8},{8,10},{10,12},{12,14},{14,0},{1,3},{3,5},... | collective-permute-start | bytes 73736 | tf_op jit(solution)/shard_map/ppermute | solution.py:32
  3.6 3.1 %collective-permute-start.1 = (bf16[3,16,256]{2,1,0:T(8,128)(2,1)}, bf16[3,16,256]{2,1,0:T(8,128)(2,1)S(1)}, u32[]{:S(2)}, u32[]{:S(2)}) collective-permute-start(bf16[3,16,256]{2,1,0:T(8,128)(2,1)} %bitcast.6), channel_id=1, source_target_pairs={{0,14},{2,0},{4,2},{6,4},{8,6},{10,8},{12,10},{14,12},{1,15},{3,1}... | collective-permute-start | bytes 73736 | tf_op jit(solution)/shard_map/ppermute | solution.py:32
  6.7 1.3 %shard_map.140 = (s32[16,256]{1,0:T(8,128)S(1)}, bf16[16,64,256]{2,1,0:T(8,128)(2,1)S(1)}, bf16[16,64,256]{2,1,0:T(8,128)(2,1)S(1)}, bf16[16,64,64]{2,1,0:T(8,128)(2,1)S(1)}, bf16[1,64,64]{2,1,0:T(8,128)(2,1)S(1)}) custom-call(s32[16,256]{1,0:T(8,128)} %refs_0_.1, bf16[16,64,256]{2,1,0:T(8,128)(2,1)} %refs_1_.1, bf16[16,64,256]{2,1,0:T(8,128)(2,1)} %direction.3, ...), custom_call_target="tpu_custom_call" | custom-call | flops 1048576 | bytes 2097152 | tf_op jit(solution)/shard_map/pallas_call | solution.py:412
  8.1 0.6 %collective-permute-done.refs_1_ = bf16[3,16,256]{2,1,0:T(8,128)(2,1)S(1)} collective-permute-done((bf16[3,16,256]{2,1,0:T(8,128)(2,1)}, bf16[3,16,256]{2,1,0:T(8,128)(2,1)S(1)}, u32[]{:S(2)}, u32[]{:S(2)}) %collective-permute-start) | collective-permute-done | bytes 24608 | tf_op jit(solution)/shard_map/ppermute | solution.py:32
  8.7 4.8 %collective-permute-start.8 = (bf16[16,64,256]{2,1,0:T(8,128)(2,1)}, bf16[16,64,256]{2,1,0:T(8,128)(2,1)S(1)}, u32[]{:S(2)}, u32[]{:S(2)}) collective-permute-start(bf16[16,64,256]{2,1,0:T(8,128)(2,1)} %direction.3), channel_id=1, source_target_pairs={{0,14},{2,0},{4,2},{6,4},{8,6},{10,8},{12,10},{14,12},{1,15},{3,1}... | collective-permute-start | bytes 1572872 | tf_op jit(solution)/shard_map/ppermute | solution.py:32
  13.5 4.2 %shard_map.141 = (bf16[16,64,256]{2,1,0:T(8,128)(2,1)}, bf16[8,64,128]{2,1,0:T(8,128)(2,1)S(1)}, f32[64,64]{1,0:T(8,128)S(1)}, f32[8,128]{1,0:T(8,128)S(1)}) custom-call(s32[16,256]{1,0:T(8,128)S(1)} %get-tuple-element.34.order, bf16[16,64,256]{2,1,0:T(8,128)(2,1)S(1)} %get-tuple-element.35.basis, bf16[16,64,256]{2,1,0:T(8,128)(2,1)S(1)} %get-tuple-element.36.direction, ...), custom_call_target="tpu_custom_call" | custom-call | flops 268435456 | bytes 6291456 | tf_op jit(solution)/shard_map/pallas_call | solution.py:425
  17.7 6.5 %shard_map.142 = (bf16[4,3072,256]{2,1,0:T(8,128)(2,1)S(1)}, f32[8,128]{1,0:T(8,128)S(1)}, bf16[48,256,128]{2,1,0:T(8,128)(2,1)S(1)}, f32[3,16,256]{2,1,0:T(8,128)S(1)}, s32[16,12]{1,0:T(8,128)S(1)}) custom-call(s32[16,12]{1,0:T(8,128)} %near_h.3, f32[8,128]{1,0:T(8,128)S(1)} %get-tuple-element.39._, bf16[3,16,256]{2,1,0:T(8,128)(2,1)} %bitcast.7, ...), custom_call_target="tpu_custom_call" | custom-call | flops 125829120 | bytes 50331648 | tf_op jit(solution)/shard_map/pallas_call | solution.py:447
  24.2 0.1 shard_map.144.refs_0_
  24.3 0.0 collective-permute-start.3
  24.3 1.1 %collective-permute-start.4 = (bf16[64,128]{1,0:T(8,128)(2,1)S(1)}, bf16[64,128]{1,0:T(8,128)(2,1)S(1)}, u32[]{:S(2)}, u32[]{:S(2)}) collective-permute-start(bf16[64,128]{1,0:T(8,128)(2,1)S(1)} %shard_map.144.refs_0_), channel_id=1, source_target_pairs={{0,8},{4,12},{8,0},{12,4},{1,9},{5,13},{9,1},{13,5},{2,10},{6,14},... | collective-permute-start | bytes 49160 | tf_op jit(solution)/shard_map/ppermute | solution.py:32
  25.4 2.7 %collective-permute-start.5 = (bf16[64,128]{1,0:T(8,128)(2,1)S(1)}, bf16[64,128]{1,0:T(8,128)(2,1)S(1)}, u32[]{:S(2)}, u32[]{:S(2)}) collective-permute-start(bf16[64,128]{1,0:T(8,128)(2,1)S(1)} %shard_map.144.refs_0_), channel_id=1, source_target_pairs={{0,12},{4,0},{8,4},{12,8},{1,13},{5,1},{9,5},{13,9},{2,14},{6,2},{... | collective-permute-start | bytes 49160 | tf_op jit(solution)/shard_map/ppermute | solution.py:32
  28.1 5.4 %shard_map.143 = (bf16[4,3072,256]{2,1,0:T(8,128)(2,1)S(1)}, f32[8,128]{1,0:T(8,128)}) custom-call(s32[16,12]{1,0:T(8,128)S(1)} %get-tuple-element.40.near_h, f32[8,128]{1,0:T(8,128)S(1)} %get-tuple-element.41._, f32[3,16,256]{2,1,0:T(8,128)S(1)} %get-tuple-element.42.refs_0_, bf16[48,256,128]{2,1,0:T(8,128)(2,1)S(1)} %get-tuple-element.43.refs_1_), custom_call_target="tpu_custom_call" | custom-call | flops 125829120 | bytes 3145728 | tf_op jit(solution)/shard_map/pallas_call | solution.py:447
  33.6 0.1 collective-permute-start.7
  33.6 0.5 collective-permute-start.9
  34.1 0.1 collective-permute-start.6
  34.2 2.0 %collective-permute-start.10 = (bf16[8,64,128]{2,1,0:T(8,128)(2,1)S(1)}, bf16[8,64,128]{2,1,0:T(8,128)(2,1)S(1)}, u32[]{:S(2)}, u32[]{:S(2)}) collective-permute-start(bf16[8,64,128]{2,1,0:T(8,128)(2,1)S(1)} %get-tuple-element.52), channel_id=1, source_target_pairs={{0,2},{2,4},{4,6},{6,8},{8,10},{10,12},{12,14},{14,0},{1,3},{3,5},... | collective-permute-start | bytes 393224 | tf_op jit(solution)/shard_map/ppermute | solution.py:32
  36.2 2.7 %collective-permute-start.11 = (bf16[8,64,128]{2,1,0:T(8,128)(2,1)S(1)}, bf16[8,64,128]{2,1,0:T(8,128)(2,1)S(1)}, u32[]{:S(2)}, u32[]{:S(2)}) collective-permute-start(bf16[8,64,128]{2,1,0:T(8,128)(2,1)S(1)} %get-tuple-element.52), channel_id=1, source_target_pairs={{0,14},{2,0},{4,2},{6,4},{8,6},{10,8},{12,10},{14,12},{1,15},{3,1}... | collective-permute-start | bytes 393224 | tf_op jit(solution)/shard_map/ppermute | solution.py:32
  39.0 0.1 collective-permute-start.12
  39.1 0.0 copy-start.2
  39.1 0.0 copy-start.5
  39.1 0.0 copy-start.6
  39.1 5.0 %shard_map.145 = (f32[8,64,256]{2,1,0:T(8,128)S(1)}, bf16[8,64,256]{2,1,0:T(8,128)(2,1)S(1)}, f32[8,128]{1,0:T(8,128)}) custom-call(s32[16,12]{1,0:T(8,128)} %near_h.3, bf16[16,64,256]{2,1,0:T(8,128)(2,1)S(1)} %collective-permute-done.2.refs_0_, bf16[16,64,256]{2,1,0:T(8,128)(2,1)S(1)} %collective-permute-done.6.refs_1_, bf16[16,64,256]{2,1,0:T(8,128)(2,1)} %direction.3, ...), custom_call_target="tpu_custom_call" | custom-call | flops 1048576 | bytes 1048576 | tf_op jit(solution)/shard_map/pallas_call | solution.py:494
  44.2 0.0 copy-start.3
  44.2 0.0 copy-start.9
  44.2 1.1 %collective-permute-done.11.after = bf16[8,64,128]{2,1,0:T(8,128)(2,1)S(1)} collective-permute-done((bf16[8,64,128]{2,1,0:T(8,128)(2,1)S(1)}, bf16[8,64,128]{2,1,0:T(8,128)(2,1)S(1)}, u32[]{:S(2)}, u32[]{:S(2)}) %collective-permute-start.11) | collective-permute-done | bytes 131104 | tf_op jit(solution)/shard_map/ppermute | solution.py:32
  45.3 1.5 %shard_map.146 = (f32[16,64,64]{2,1,0:T(8,128)S(1)}, bf16[8,64,256]{2,1,0:T(8,128)(2,1)S(1)}) custom-call(bf16[8,64,256]{2,1,0:T(8,128)(2,1)S(1)} %get-tuple-element.51.given, bf16[8,64,128]{2,1,0:T(8,128)(2,1)S(1)} %collective-permute-done.10.before, bf16[8,64,128]{2,1,0:T(8,128)(2,1)S(1)} %collective-permute-done.11.after, ...), custom_call_target="tpu_custom_call" | custom-call | flops 67108864 | bytes 4194304 | tf_op jit(solution)/shard_map/pallas_call | solution.py:519
  46.9 0.1 shard_map.148
  47.0 0.1 collective-permute-start.13
  47.1 1.8 %shard_map.149.base = f32[16,64,256]{2,1,0:T(8,128)S(1)} custom-call(bf16[4,64,64]{2,1,0:T(8,128)(2,1)S(1)} %get-tuple-element.55.tops, f32[16,64,64]{2,1,0:T(8,128)S(1)} %get-tuple-element.53._.part, bf16[16,64,64]{2,1,0:T(8,128)(2,1)S(1)} %copy-done.4, bf16[16,64,256]{2,1,0:T(8,128)(2,1)S(1)} %copy-done.5, bf16[16,64,256]{2,1,0:T(8,128)(2,1)S(1)} %copy-done.1, ...), custom_call_target="tpu_custom_call" | custom-call | flops 41943040 | bytes 4194304 | tf_op jit(solution)/shard_map/pallas_call | solution.py:542
  48.9 1.2 %shard_map.150 = (f32[16,64,256]{2,1,0:T(8,128)}, f32[16,64,256]{2,1,0:T(8,128)S(1)}, f32[8,8,128]{2,1,0:T(8,128)S(1)}) custom-call(f32[1,64]{1,0:T(1,128)S(1)} %bitcast.3, f32[16,64,256]{2,1,0:T(8,128)S(1)} %shard_map.149.base, f32[8,64,256]{2,1,0:T(8,128)S(1)} %get-tuple-element.57.kept, bf16[8,64,256]{2,1,0:T(8,128)(2,1)S(1)} %collective-permute-done.13.received, ...), custom_call_target="tpu_custom_call" | custom-call | flops 4194304 | bytes 5242880 | tf_op jit(solution)/shard_map/pallas_call | solution.py:564
  50.2 9.7 %all_to_all.5.norms = f32[8,8,128]{2,1,0:T(8,128)S(1)} all-to-all(f32[8,8,128]{2,1,0:T(8,128)S(1)} %get-tuple-element.60), channel_id=1, replica_groups=mesh['groups'=2,'blk'=4,'leaf'=2,'sample'=2] {'blk','leaf'}, dimensions={0} | all-to-all | bytes 65536 | tf_op jit(solution)/shard_map/all_to_all | solution.py:574
  59.9 0.9 %shard_map.151 = bf16[16,64,256]{2,1,0:T(8,128)(2,1)} custom-call(f32[8,8,128]{2,1,0:T(8,128)S(1)} %all_to_all.5.norms, f32[16,64,256]{2,1,0:T(8,128)S(1)} %get-tuple-element.61.updated, bf16[16,64,256]{2,1,0:T(8,128)(2,1)S(1)} %copy-done.1), custom_call_target="tpu_custom_call" | custom-call | flops 1048576 | bytes 2097152 | tf_op jit(solution)/shard_map/pallas_call | solution.py:575
  (29 shorter events, 0.1 us)
Async XLA Ops:
  0.6 32.9 %copy-start = (bf16[16,64,256]{2,1,0:T(8,128)(2,1)S(1)}, bf16[16,64,256]{2,1,0:T(8,128)(2,1)}, u32[]{:S(2)}) copy-start(bf16[16,64,256]{2,1,0:T(8,128)(2,1)} %direction.3) | copy-start | bytes 1572868
  0.6 8.0 %collective-permute-start = (bf16[3,16,256]{2,1,0:T(8,128)(2,1)}, bf16[3,16,256]{2,1,0:T(8,128)(2,1)S(1)}, u32[]{:S(2)}, u32[]{:S(2)}) collective-permute-start(bf16[3,16,256]{2,1,0:T(8,128)(2,1)} %bitcast.5), channel_id=1, source_target_pairs={{0,2},{2,4},{4,6},{6,8},{8,10},{10,12},{12,14},{14,0},{1,3},{3,5},... | collective-permute-start | bytes 73736 | tf_op jit(solution)/shard_map/ppermute | solution.py:32
  3.6 5.1 %collective-permute-start.1 = (bf16[3,16,256]{2,1,0:T(8,128)(2,1)}, bf16[3,16,256]{2,1,0:T(8,128)(2,1)S(1)}, u32[]{:S(2)}, u32[]{:S(2)}) collective-permute-start(bf16[3,16,256]{2,1,0:T(8,128)(2,1)} %bitcast.6), channel_id=1, source_target_pairs={{0,14},{2,0},{4,2},{6,4},{8,6},{10,8},{12,10},{14,12},{1,15},{3,1}... | collective-permute-start | bytes 73736 | tf_op jit(solution)/shard_map/ppermute | solution.py:32
  8.7 24.9 %collective-permute-start.8 = (bf16[16,64,256]{2,1,0:T(8,128)(2,1)}, bf16[16,64,256]{2,1,0:T(8,128)(2,1)S(1)}, u32[]{:S(2)}, u32[]{:S(2)}) collective-permute-start(bf16[16,64,256]{2,1,0:T(8,128)(2,1)} %direction.3), channel_id=1, source_target_pairs={{0,14},{2,0},{4,2},{6,4},{8,6},{10,8},{12,10},{14,12},{1,15},{3,1}... | collective-permute-start | bytes 1572872 | tf_op jit(solution)/shard_map/ppermute | solution.py:32
  13.5 20.7 %collective-permute-start.2 = (bf16[16,64,256]{2,1,0:T(8,128)(2,1)}, bf16[16,64,256]{2,1,0:T(8,128)(2,1)S(1)}, u32[]{:S(2)}, u32[]{:S(2)}) collective-permute-start(bf16[16,64,256]{2,1,0:T(8,128)(2,1)} %direction.3), channel_id=1, source_target_pairs={{0,2},{2,4},{4,6},{6,8},{8,10},{10,12},{12,14},{14,0},{1,3},{3,5},... | collective-permute-start | bytes 1572872 | tf_op jit(solution)/shard_map/ppermute | solution.py:32
  24.3 9.2 %collective-permute-start.3 = (bf16[64,128]{1,0:T(8,128)(2,1)S(1)}, bf16[64,128]{1,0:T(8,128)(2,1)S(1)}, u32[]{:S(2)}, u32[]{:S(2)}) collective-permute-start(bf16[64,128]{1,0:T(8,128)(2,1)S(1)} %shard_map.144.refs_0_), channel_id=1, source_target_pairs={{0,4},{4,8},{8,12},{12,0},{1,5},{5,9},{9,13},{13,1},{2,6},{6,10},{... | collective-permute-start | bytes 49160 | tf_op jit(solution)/shard_map/ppermute | solution.py:32
  24.3 9.2 %collective-permute-start.4 = (bf16[64,128]{1,0:T(8,128)(2,1)S(1)}, bf16[64,128]{1,0:T(8,128)(2,1)S(1)}, u32[]{:S(2)}, u32[]{:S(2)}) collective-permute-start(bf16[64,128]{1,0:T(8,128)(2,1)S(1)} %shard_map.144.refs_0_), channel_id=1, source_target_pairs={{0,8},{4,12},{8,0},{12,4},{1,9},{5,13},{9,1},{13,5},{2,10},{6,14},... | collective-permute-start | bytes 49160 | tf_op jit(solution)/shard_map/ppermute | solution.py:32
  25.4 8.1 %collective-permute-start.5 = (bf16[64,128]{1,0:T(8,128)(2,1)S(1)}, bf16[64,128]{1,0:T(8,128)(2,1)S(1)}, u32[]{:S(2)}, u32[]{:S(2)}) collective-permute-start(bf16[64,128]{1,0:T(8,128)(2,1)S(1)} %shard_map.144.refs_0_), channel_id=1, source_target_pairs={{0,12},{4,0},{8,4},{12,8},{1,13},{5,1},{9,5},{13,9},{2,14},{6,2},{... | collective-permute-start | bytes 49160 | tf_op jit(solution)/shard_map/ppermute | solution.py:32
  33.6 5.4 %collective-permute-start.7 = (bf16[16,64,256]{2,1,0:T(8,128)(2,1)S(1)}, bf16[16,64,256]{2,1,0:T(8,128)(2,1)S(1)}, u32[]{:S(2)}, u32[]{:S(2)}) collective-permute-start(bf16[16,64,256]{2,1,0:T(8,128)(2,1)S(1)} %copy-done), channel_id=1, source_target_pairs={{0,1},{1,0},{2,3},{3,2},{4,5},{5,4},{6,7},{7,6},{8,9},{9,8},{10,11... | collective-permute-start | bytes 1572872 | tf_op jit(solution)/shard_map/ppermute | solution.py:36
  33.6 5.4 %collective-permute-start.9 = (bf16[16,64,256]{2,1,0:T(8,128)(2,1)S(1)}, bf16[16,64,256]{2,1,0:T(8,128)(2,1)S(1)}, u32[]{:S(2)}, u32[]{:S(2)}) collective-permute-start(bf16[16,64,256]{2,1,0:T(8,128)(2,1)S(1)} %collective-permute-done.8.refs_4_), channel_id=1, source_target_pairs={{0,1},{1,0},{2,3},{3,2},{4,5},{5,4},{6,7},{7,6},{8,9},{9,8},{10,11... | collective-permute-start | bytes 1572872 | tf_op jit(solution)/shard_map/ppermute | solution.py:36
  34.1 4.9 %collective-permute-start.6 = (bf16[16,64,256]{2,1,0:T(8,128)(2,1)S(1)}, bf16[16,64,256]{2,1,0:T(8,128)(2,1)S(1)}, u32[]{:S(2)}, u32[]{:S(2)}) collective-permute-start(bf16[16,64,256]{2,1,0:T(8,128)(2,1)S(1)} %collective-permute-done.2.refs_0_), channel_id=1, source_target_pairs={{0,1},{1,0},{2,3},{3,2},{4,5},{5,4},{6,7},{7,6},{8,9},{9,8},{10,11... | collective-permute-start | bytes 1572872 | tf_op jit(solution)/shard_map/ppermute | solution.py:36
  34.2 10.0 %collective-permute-start.10 = (bf16[8,64,128]{2,1,0:T(8,128)(2,1)S(1)}, bf16[8,64,128]{2,1,0:T(8,128)(2,1)S(1)}, u32[]{:S(2)}, u32[]{:S(2)}) collective-permute-start(bf16[8,64,128]{2,1,0:T(8,128)(2,1)S(1)} %get-tuple-element.52), channel_id=1, source_target_pairs={{0,2},{2,4},{4,6},{6,8},{8,10},{10,12},{12,14},{14,0},{1,3},{3,5},... | collective-permute-start | bytes 393224 | tf_op jit(solution)/shard_map/ppermute | solution.py:32
  36.2 9.1 %collective-permute-start.11 = (bf16[8,64,128]{2,1,0:T(8,128)(2,1)S(1)}, bf16[8,64,128]{2,1,0:T(8,128)(2,1)S(1)}, u32[]{:S(2)}, u32[]{:S(2)}) collective-permute-start(bf16[8,64,128]{2,1,0:T(8,128)(2,1)S(1)} %get-tuple-element.52), channel_id=1, source_target_pairs={{0,14},{2,0},{4,2},{6,4},{8,6},{10,8},{12,10},{14,12},{1,15},{3,1}... | collective-permute-start | bytes 393224 | tf_op jit(solution)/shard_map/ppermute | solution.py:32
  39.0 7.9 %collective-permute-start.12 = (bf16[4,64,128]{2,1,0:T(8,128)(2,1)S(1)}, bf16[4,64,128]{2,1,0:T(8,128)(2,1)S(1)}, u32[]{:S(2)}, u32[]{:S(2)}) collective-permute-start(bf16[4,64,128]{2,1,0:T(8,128)(2,1)S(1)} %shard_map.147.refs_0_), channel_id=1, source_target_pairs={{0,2},{2,0},{1,3},{3,1},{4,6},{6,4},{5,7},{7,5},{8,10},{10,8},{9,1... | collective-permute-start | bytes 196616 | tf_op jit(solution)/shard_map/ppermute | solution.py:32
  39.1 6.3 %copy-start.2 = (bf16[16,8,64,64]{3,2,1,0:T(8,128)(2,1)S(1)}, bf16[16,8,64,64]{3,2,1,0:T(8,128)(2,1)}, u32[]{:S(2)}) copy-start(bf16[16,8,64,64]{3,2,1,0:T(8,128)(2,1)} %coupling.1) | copy-start | bytes 3145732
  39.1 8.0 %copy-start.1 = (bf16[16,64,256]{2,1,0:T(8,128)(2,1)S(1)}, bf16[16,64,256]{2,1,0:T(8,128)(2,1)}, u32[]{:S(2)}) copy-start(bf16[16,64,256]{2,1,0:T(8,128)(2,1)} %direction.3) | copy-start | bytes 1572868
  39.1 8.0 %copy-start.4 = (bf16[16,64,64]{2,1,0:T(8,128)(2,1)S(1)}, bf16[16,64,64]{2,1,0:T(8,128)(2,1)}, u32[]{:S(2)}) copy-start(bf16[16,64,64]{2,1,0:T(8,128)(2,1)} %leaf_transfer.1) | copy-start | bytes 393220
  39.1 8.0 %copy-start.5 = (bf16[16,64,256]{2,1,0:T(8,128)(2,1)S(1)}, bf16[16,64,256]{2,1,0:T(8,128)(2,1)}, u32[]{:S(2)}) copy-start(bf16[16,64,256]{2,1,0:T(8,128)(2,1)} %get-tuple-element.56.natural) | copy-start | bytes 1572868
  39.1 8.0 %copy-start.6 = (bf16[1,64,64]{2,1,0:T(8,128)(2,1)S(1)}, bf16[1,64,64]{2,1,0:T(8,128)(2,1)}, u32[]{:S(2)}) copy-start(bf16[1,64,64]{2,1,0:T(8,128)(2,1)} %node_transfer.1) | copy-start | bytes 24580
  39.1 8.0 %copy-start.7 = (bf16[1,4,64,64]{3,2,1,0:T(8,128)(2,1)S(1)}, bf16[1,4,64,64]{3,2,1,0:T(8,128)(2,1)}, u32[]{:S(2)}) copy-start(bf16[1,4,64,64]{3,2,1,0:T(8,128)(2,1)} %top_coupling.1) | copy-start | bytes 98308
  39.1 8.0 %copy-start.8 = (s32[1,4]{1,0:T(1,128)S(1)}, s32[1,4]{1,0:T(1,128)}, u32[]{:S(2)}) copy-start(s32[1,4]{1,0:T(1,128)} %top_list.1) | copy-start | bytes 52
  44.2 4.7 %copy-start.3 = (f32[16,64,256]{2,1,0:T(8,128)S(1)}, f32[16,64,256]{2,1,0:T(8,128)}, u32[]{:S(2)}) copy-start(f32[16,64,256]{2,1,0:T(8,128)} %residual.1) | copy-start | bytes 3145732
  44.2 4.7 %copy-start.9 = (f32[64]{0:T(128)S(1)}, f32[64]{0:T(128)}, u32[]{:S(2)}) copy-start(f32[64]{0:T(128)} %param.15) | copy-start | bytes 772
  47.0 1.9 %collective-permute-start.13 = (bf16[8,64,256]{2,1,0:T(8,128)(2,1)S(1)}, bf16[8,64,256]{2,1,0:T(8,128)(2,1)S(1)}, u32[]{:S(2)}, u32[]{:S(2)}) collective-permute-start(bf16[8,64,256]{2,1,0:T(8,128)(2,1)S(1)} %get-tuple-element.58), channel_id=1, source_target_pairs={{0,1},{1,0},{2,3},{3,2},{4,5},{5,4},{6,7},{7,6},{8,9},{9,8},{10,11... | collective-permute-start | bytes 786440 | tf_op jit(solution)/shard_map/ppermute | solution.py:36
